TPU v7x, 32 devices: a whole 2x2x4 slice. The times are simulated.
32 devices in a mesh: parts: 2 (over y), replica: 4 (over x, core), tensor: 4 (over z).
Axes of the slice: x: 2, y: 2, z: 4, core: 2. Of those that a mesh axis runs over, the one named last changes fastest.
Arguments:
- prompt_owner: int32 [8], P('parts'), parts along dimension 0, may hold values from 0 to 3, each once
- fork_map: int32 [1024], P(('parts', 'replica')), parts along dimension 0, may hold values from 0 to 3
- page_table: int32 [24], P('parts'), parts along dimension 0, may hold values from 0 to 11, each once
- prompt_length: int32 [8], P('parts'), parts along dimension 0, may hold values from 1 to 384
- span_states: bfloat16 [1024, 8192], P(('parts', 'replica'), 'tensor'), parts along dimension 0, may hold values from -6 to 6
- decode_states: bfloat16 [1024, 4, 8192], P(('parts', 'replica'), None, 'tensor'), parts along dimension 0, may hold values from -6 to 6
- decode_queries: bfloat16 [1024, 4, 4096], P(('parts', 'replica'), None, 'tensor'), parts along dimension 0, may hold values from -64 to 64
- key_weight: bfloat16 [8192, 512], P('tensor'), may hold values from -0.0625 to 0.0625
- value_weight: bfloat16 [8192, 512], P('tensor'), may hold values from -0.0625 to 0.0625
- out_weight: bfloat16 [4096, 8192], P(None, 'tensor'), may hold values from -0.09375 to 0.09375
- page_pool: bfloat16 [4, 24, 128, 256], P('tensor', 'parts'), parts along dimension 1, may hold values from -6 to 60, as said below
Outputs:
- decoded: bfloat16 [1024, 4, 8192], P(('parts', 'replica'), None, 'tensor'), parts along dimension 0
There are 2 independent parts, one for each index of `parts`. A program takes and returns all parts, laid end to end along the dimension named above; an argument that names none is the same for every part. Nothing has to cross between parts.
Inputs may be any that keep to these rules, and one draw needn't show every extreme that they name: Replica r prefills prompt prompt_owner[r]; every prompt has exactly one such replica. The cache pages of prompt p are page_table[p * 3 + c] for c below 3; every pool page belongs to exactly one prompt. page_pool[t] holds the cache of key-value head t; devices that read the same head hold equal copies.
All inputs are finite; a program needn't handle non-finite values.
Results may differ from a plain program's by a relative error of at most 0.009.
Values may be sent and summed in bfloat16 or wider, within the bound.
No kernel may reach another device: no remote copies, remote signals or barrier semaphores. Data moves between devices by JAX's collectives and lax.ppermute only.
A program may use at most 64 MiB of HBM per device.

v0:
```python
import functools
import math

import jax
import jax.numpy as jnp
from jax import lax
from jax.experimental import pallas as pl
from jax.experimental.pallas import tpu as pltpu
from jax.sharding import PartitionSpec as P


HD = 128
rope_base = 1000000.0
LOG2E = math.log2(math.e)
HIDDEN = -1e30


def rotary(vectors, places):
    half = vectors.shape[-1] // 2
    freq = rope_base ** (-(2.0 / vectors.shape[-1]) * jnp.arange(half, dtype=jnp.float32))
    angle = places.astype(jnp.float32)[..., None, None] * freq
    cosine = jnp.cos(angle)
    sine = jnp.sin(angle)
    first = vectors[..., :half]
    second = vectors[..., half:]
    return jnp.concatenate([first * cosine - second * sine, second * cosine + first * sine], -1)


def rotate_round(summed, places, kv_heads):
    number = summed.shape[0]
    turned = rotary(summed[:, : kv_heads * HD].reshape(number, kv_heads, HD), places)
    turned = turned.astype(jnp.bfloat16).reshape(number, kv_heads * HD)
    return jnp.concatenate([turned, summed[:, kv_heads * HD :].astype(jnp.bfloat16)], 1)


def own_pair(packed, head_group, kv_heads):
    key_part = lax.dynamic_slice_in_dim(packed, head_group * HD, HD, 1)
    value_part = lax.dynamic_slice_in_dim(packed, (kv_heads + head_group) * HD, HD, 1)
    return jnp.concatenate([key_part, value_part], 1)


NT = (((1,), (1,)), ((), ()))
SMALL = pltpu.CompilerParams(vmem_limit_bytes=24 << 20)
LARGE = pltpu.CompilerParams(vmem_limit_bytes=36 << 20)
SET_ROWS = 32


def in_hbm(x):
    return pltpu.with_memory_space_constraint(x, pltpu.HBM)


def lane_tiles(combine, x):
    out = x[..., :HD]
    for i in range(1, x.shape[-1] // HD):
        out = combine(out, x[..., i * HD : (i + 1) * HD])
    return out


def stacked_heads(q_ref, heads):
    m = q_ref.shape[0] * q_ref.shape[1]
    q = q_ref[...].reshape(m, heads * HD)
    return jnp.concatenate([q[:, h * HD : (h + 1) * HD] for h in range(heads)], 0)


def softmax_parts(qs, heads, parts, scale2, s_ref):
    m = qs.shape[0] // heads
    top = None
    at = 0
    for ref, bias in parts:
        n = ref.shape[0]
        s = lax.dot_general(qs, ref[:, :HD], NT, preferred_element_type=jnp.float32)
        s = s.reshape(heads, m, n) * scale2 + bias()[None]
        s_ref[:, :, at : at + n] = s
        most = lane_tiles(jnp.maximum, s)
        top = most if top is None else jnp.maximum(top, most)
        at += n
    top = jnp.max(top, -1, keepdims=True)
    total = mixed = None
    at = 0
    for ref, _ in parts:
        n = ref.shape[0]
        w = jnp.exp2(s_ref[:, :, at : at + n] - top)
        summed = lane_tiles(jnp.add, w)
        one = jnp.dot(
            w.astype(jnp.bfloat16).reshape(heads * m, n),
            ref[:, HD:],
            preferred_element_type=jnp.float32,
        ).reshape(heads, m, HD)
        total = summed if total is None else total + summed
        mixed = one if mixed is None else mixed + one
        at += n
    return top, jnp.sum(total, -1, keepdims=True), mixed


def hidden_unless(prompt, keys):
    return jnp.where(prompt == keys, 0.0, HIDDEN)


def cached_kernel(heads, scale2, q_ref, prompt_ref, keyp_ref, pool_ref, mixed_ref, stat_ref, s_ref):
    qs = stacked_heads(q_ref, heads)
    parts = ((pool_ref, lambda: hidden_unless(prompt_ref[...], keyp_ref[...])),)
    top, total, mixed = softmax_parts(qs, heads, parts, scale2, s_ref)
    mixed_ref[...] = mixed
    lane = lax.broadcasted_iota(jnp.int32, mixed.shape, 2)
    stat_ref[...] = jnp.where(lane < HD // 2, top, total)


def new_kernel(
    heads, steps, scale2, q_ref, prompt_ref, keyp_ref, span_ref, tail_ref, mixed_ref, stat_ref, o_ref, s_ref
):
    qs = stacked_heads(q_ref, heads)
    m = qs.shape[0] // heads

    def causal():
        row = lax.broadcasted_iota(jnp.int32, (m, m), 0)
        col = lax.broadcasted_iota(jnp.int32, (m, m), 1)
        return jnp.where((row // steps == col // steps) & (col <= row), 0.0, HIDDEN)

    parts = (
        (span_ref, lambda: hidden_unless(prompt_ref[...], keyp_ref[...])),
        (tail_ref, causal),
    )
    top, total, mixed = softmax_parts(qs, heads, parts, scale2, s_ref)
    old_top = stat_ref[:, :, :1]
    old_total = stat_ref[:, :, HD // 2 : HD // 2 + 1]
    both = jnp.maximum(top, old_top)
    new_share = jnp.exp2(top - both)
    old_share = jnp.exp2(old_top - both)
    total = total * new_share + old_total * old_share
    mixed = mixed * new_share + mixed_ref[...] * old_share
    out = (mixed / total).astype(jnp.bfloat16)
    for h in range(heads):
        o_ref[:, h * HD : (h + 1) * HD] = out[h]


def attend_cached(q, row_prompt, key_prompt, pool, start, count):
    steps, width = q.shape[1:]
    heads = width // HD
    block = min(SET_ROWS, q.shape[0])
    m = block * steps
    cached = pool.shape[0]
    return pl.pallas_call(
        functools.partial(cached_kernel, heads, LOG2E / math.sqrt(HD)),
        grid=(count,),
        in_specs=[
            pl.BlockSpec((block, steps, width), lambda i: (i + start, 0, 0)),
            pl.BlockSpec((m, 1), lambda i: (i + start, 0)),
            pl.BlockSpec((1, cached), lambda i: (0, 0)),
            pl.BlockSpec((cached, 2 * HD), lambda i: (0, 0)),
        ],
        out_specs=[pl.BlockSpec((heads, m, HD), lambda i: (0, i, 0))] * 2,
        out_shape=[jax.ShapeDtypeStruct((heads, m * count, HD), jnp.float32)] * 2,
        scratch_shapes=[pltpu.VMEM((heads, m, cached), jnp.float32)],
        cost_estimate=pl.CostEstimate(
            flops=4 * count * heads * m * cached * HD,
            transcendentals=count * heads * m * cached,
            bytes_accessed=8 * count * heads * m * HD,
        ),
        compiler_params=SMALL,
        name="attend_cached",
    )(q, row_prompt, key_prompt, pool)


def attend_new(q, row_prompt, key_prompt, span_pairs, tail_pairs, mixed, stat, start, count):
    steps, width = q.shape[1:]
    heads = width // HD
    block = min(SET_ROWS, q.shape[0])
    m = block * steps
    keys = span_pairs.shape[0]
    part = pl.BlockSpec((heads, m, HD), lambda i: (0, i, 0))
    return pl.pallas_call(
        functools.partial(new_kernel, heads, steps, LOG2E / math.sqrt(HD)),
        grid=(count,),
        in_specs=[
            pl.BlockSpec((block, steps, width), lambda i: (i + start, 0, 0)),
            pl.BlockSpec((m, 1), lambda i: (i + start, 0)),
            pl.BlockSpec((1, keys), lambda i: (0, 0)),
            pl.BlockSpec((keys, 2 * HD), lambda i: (0, 0)),
            pl.BlockSpec((m, 2 * HD), lambda i: (i, 0)),
            part,
            part,
        ],
        out_specs=pl.BlockSpec((m, width), lambda i: (i, 0)),
        out_shape=jax.ShapeDtypeStruct((m * count, width), jnp.bfloat16),
        scratch_shapes=[pltpu.VMEM((heads, m, keys + m), jnp.float32)],
        cost_estimate=pl.CostEstimate(
            flops=4 * count * heads * m * (keys + m) * HD,
            transcendentals=count * heads * m * (keys + m),
            bytes_accessed=10 * count * heads * m * HD,
        ),
        compiler_params=SMALL,
        name="attend_new",
    )(q, row_prompt, key_prompt, span_pairs, tail_pairs, mixed, stat)


def project_kernel(split, kept, sent, rank_ref, x_ref, *refs):
    keep_ref, send_ref, acc = refs[-3:]
    s = pl.program_id(0)
    x = x_ref[...].reshape(-1, x_ref.shape[-1])
    w = jnp.concatenate(
        [jnp.concatenate([refs[2 * i][...], refs[2 * i + 1][...]], 1) for i in range(split)], 0
    )
    one = jnp.dot(x, w, preferred_element_type=jnp.float32)

    @pl.when(s == 0)
    def _():
        acc[...] = one

    @pl.when(s > 0)
    def _():
        acc[...] += one

    @pl.when(s == pl.num_programs(0) - 1)
    def _():
        keys = acc.shape[1] // 2
        for ref, rels in ((send_ref, sent), (keep_ref, kept)):
            for i, rel in enumerate(rels):
                at = pl.multiple_of((rank_ref[0] ^ rel) * HD, HD)
                ref[i, :, :HD] = acc[:, pl.ds(at, HD)].astype(ref.dtype)
                ref[i, :, HD:] = acc[:, pl.ds(pl.multiple_of(at + keys, HD), HD)].astype(ref.dtype)


def project(rank, x, start, rows, key_weight, value_weight, kept, sent):
    width, columns = key_weight.shape
    depth, split = width // 2, 2
    lead = (rows,) + x.shape[1:-1]
    n = math.prod(lead)
    zeros = (0,) * (len(lead) - 1)
    in_specs = [
        pl.BlockSpec(
            tuple(pl.Element(d) for d in lead + (depth,)),
            lambda s, r: (start,) + zeros + (s * depth,),
        )
    ]
    for i in range(split):
        piece = pl.BlockSpec((depth // split, columns), lambda s, r, i=i: (s * split + i, 0))
        in_specs += [piece, piece]
    return pl.pallas_call(
        functools.partial(project_kernel, split, kept, sent),
        grid_spec=pltpu.PrefetchScalarGridSpec(
            num_scalar_prefetch=1,
            grid=(width // depth,),
            in_specs=in_specs,
            out_specs=[
                pl.BlockSpec((len(rels), n, 2 * HD), lambda s, r: (0, 0, 0)) for rels in (kept, sent)
            ],
            scratch_shapes=[pltpu.VMEM((n, 2 * columns), jnp.float32)],
        ),
        out_shape=[
            jax.ShapeDtypeStruct((len(kept), n, 2 * HD), jnp.float32),
            jax.ShapeDtypeStruct((len(sent), n, 2 * HD), jnp.bfloat16),
        ],
        cost_estimate=pl.CostEstimate(
            flops=4 * n * width * columns, transcendentals=0, bytes_accessed=4 * width * columns
        ),
        compiler_params=SMALL,
        name="project",
    )(rank, in_hbm(x), *([in_hbm(key_weight), in_hbm(value_weight)] * split))


def finish_kernel(keep_ref, *refs):
    cos_ref, sin_ref, o_ref = refs[-3:]
    summed = keep_ref[0]
    for ref in refs[:-3]:
        summed = summed + (ref[0] if len(ref.shape) == 3 else ref[...]).astype(jnp.float32)
    keys = summed[:, :HD]
    turned = keys * cos_ref[...] + pltpu.roll(keys, HD // 2, 1) * sin_ref[...]
    o_ref[:, :HD] = turned.astype(jnp.bfloat16)
    o_ref[:, HD:] = summed[:, HD:].astype(jnp.bfloat16)


def finish(keep, others, tables):
    n = keep.shape[1]
    first = pl.BlockSpec((1, n, 2 * HD), lambda i: (0, 0, 0))
    flat = lambda w: pl.BlockSpec((n, w), lambda i: (0, 0))
    return pl.pallas_call(
        finish_kernel,
        grid=(1,),
        in_specs=[first]
        + [first if x.ndim == 3 else flat(2 * HD) for x in others]
        + [flat(HD), flat(HD)],
        out_specs=flat(2 * HD),
        out_shape=jax.ShapeDtypeStruct((n, 2 * HD), jnp.bfloat16),
        compiler_params=SMALL,
        name="finish",
    )(keep, *others, *tables)


def turn_tables(places):
    half = HD // 2
    freq = rope_base ** (-(2.0 / HD) * jnp.arange(half, dtype=jnp.float32))
    angle = places.astype(jnp.float32)[:, None] * freq
    cosine = jnp.cos(angle)
    sine = jnp.sin(angle)
    return lax.optimization_barrier(
        (jnp.concatenate([cosine, cosine], 1), jnp.concatenate([-sine, sine], 1))
    )


def swap(x, axis, bit):
    return lax.ppermute(x, axis, [(i, i ^ bit) for i in range(lax.axis_size(axis))])


def swap_sum(keep, send, tables):
    got = swap(send, "tensor", 1)
    half = (keep[1] + got[1].astype(jnp.float32)).astype(jnp.bfloat16)
    last = swap(half, "tensor", 2)
    return finish(keep, (got, last), tables)


def chain_sum(keep, send, tables):
    one = lax.ppermute(send, "tensor", [(0, 1), (3, 2)])
    inward = jnp.stack([keep[3] + one[1].astype(jnp.float32), keep[2] + one[2].astype(jnp.float32)])
    two = lax.ppermute(inward.astype(jnp.bfloat16), "tensor", [(1, 2), (2, 1)])
    outward = (keep[1] + two[1].astype(jnp.float32)).astype(jnp.bfloat16)
    three = lax.ppermute(outward, "tensor", [(1, 0), (2, 3)])
    return finish(keep, (one, two, three), tables)


def out_kernel(rels, pick, cuts, add, final, rank_ref, *refs):
    refs = list(refs)
    pieces = [refs.pop(0) for _ in rels]
    other = refs.pop(0) if pick else None
    partial = refs.pop(0) if add else None
    w_ref, o_ref, buf, sem = refs[0], refs[-3], refs[-2], refs[-1]
    width = pieces[0].shape[1]
    depth = width // cuts
    rank = rank_ref[0]
    copies = []
    for p, rel in enumerate(rels):
        for c in range(cuts):
            row = pl.multiple_of((rank ^ rel) * width + c * depth, depth)
            slot = p * cuts + c
            copies.append(
                pltpu.make_async_copy(w_ref.at[pl.ds(row, depth), :], buf.at[slot], sem.at[slot])
            )
            copies[-1].start()
    total = partial[...] if add else None
    for p in range(len(rels)):
        a = pieces[p][...]
        if pick and p == len(rels) - 1:
            inner = (rank == 1) | (rank == 2)
            a = jnp.where(inner, a, other[...])
        for c in range(cuts):
            slot = p * cuts + c
            copies[slot].wait()
            one = jnp.dot(
                a[:, c * depth : (c + 1) * depth], buf[slot], preferred_element_type=jnp.float32
            )
            total = one if total is None else total + one
    o_ref[...] = total.reshape(o_ref.shape).astype(o_ref.dtype)


def out_project(rank, pieces, rels, weight, shape, start, pick=None, partial=None, into=None, final=True):
    m, width = pieces[0].shape
    columns = weight.shape[1]
    steps = shape[1]
    cuts = 4
    flat = lambda w: pl.BlockSpec((m, w), lambda i, r: (0, 0))
    args = list(pieces)
    in_specs = [flat(width) for _ in pieces]
    if pick is not None:
        args.append(pick)
        in_specs.append(flat(width))
    if partial is not None:
        args.append(partial)
        in_specs.append(flat(columns))
    args.append(in_hbm(weight))
    in_specs.append(pl.BlockSpec(memory_space=pl.ANY))
    aliases = {}
    if into is not None:
        args.append(into)
        in_specs.append(pl.BlockSpec(memory_space=pl.ANY))
        aliases = {len(args): 0}
    if final:
        out_spec = pl.BlockSpec(
            (pl.Element(m // steps), pl.Element(steps), pl.Element(columns)),
            lambda i, r: (start, 0, 0),
        )
        out_shape = jax.ShapeDtypeStruct(shape, jnp.bfloat16)
    else:
        out_spec = flat(columns)
        out_shape = jax.ShapeDtypeStruct((m, columns), jnp.float32)
    slots = len(rels) * cuts
    return pl.pallas_call(
        functools.partial(out_kernel, rels, pick is not None, cuts, partial is not None, final),
        grid_spec=pltpu.PrefetchScalarGridSpec(
            num_scalar_prefetch=1,
            grid=(1,),
            in_specs=in_specs,
            out_specs=out_spec,
            scratch_shapes=[
                pltpu.VMEM((slots, width // cuts, columns), jnp.bfloat16),
                pltpu.SemaphoreType.DMA((slots,)),
            ],
        ),
        out_shape=out_shape,
        input_output_aliases=aliases,
        cost_estimate=pl.CostEstimate(
            flops=2 * m * width * columns * len(rels),
            transcendentals=0,
            bytes_accessed=2 * width * columns * len(rels),
        ),
        compiler_params=LARGE,
        name="out_project",
    )(rank, *args)


def mask_tables(prompt_owner, page_table, prompt_length, page_size, span, order):
    n_replica = order.shape[0]
    prompts = jnp.arange(n_replica, dtype=jnp.int32)
    pool_pages = page_table.shape[0]
    cpages = pool_pages // n_replica
    entries = jnp.arange(pool_pages, dtype=jnp.int32)
    page_hits = page_table[None, :] == entries[:, None]
    page_prompt = jnp.sum(jnp.where(page_hits, entries[None, :] // cpages, 0), 1)
    page_slot = jnp.sum(jnp.where(page_hits, entries[None, :] % cpages, 0), 1)
    page_length = jnp.sum(
        jnp.where(page_prompt[:, None] == prompts[None, :], prompt_length[None, :], 0), 1
    )
    visible = (
        page_slot[:, None] * page_size + jnp.arange(page_size, dtype=jnp.int32)[None, :]
        < page_length[:, None]
    )
    pool_prompt = jnp.where(visible, page_prompt[:, None], -1).reshape(-1)
    owners = jnp.sum(jnp.where(order[:, None] == prompts[None, :], prompt_owner[None, :], 0), 1)
    return jnp.concatenate([pool_prompt, jnp.repeat(owners, span)])[None, :]


def gather_heads(own):
    far = swap(own, "tensor", 2)
    near = swap(own, "tensor", 1)
    across = lax.ppermute(own, "tensor", [(1, 2), (2, 1)])
    passed = lax.ppermute(far, "tensor", [(1, 0), (2, 3)])
    return far, near, across, passed


def on_device(
    prompt_owner,
    fork_map,
    page_table,
    prompt_length,
    span_states,
    decode_states,
    decode_queries,
    key_weight,
    value_weight,
    out_weight,
    page_pool,
):
    replica = lax.axis_index("replica")
    device_rank = lax.axis_index("tensor")
    n_replica = lax.axis_size("replica")
    n_tensor = lax.axis_size("tensor")
    span = span_states.shape[0]
    rows, steps, width = decode_states.shape
    kv_heads = key_weight.shape[1] // HD
    sharing = n_tensor // kv_heads
    prompts = jnp.arange(n_replica, dtype=jnp.int32)
    own_prompt = jnp.sum(jnp.where(prompts == replica, prompt_owner, 0))
    own_length = jnp.sum(jnp.where(prompts == own_prompt, prompt_length, 0))
    row_hits = fork_map[:, None] == prompts[None, :]
    row_length = jnp.sum(jnp.where(row_hits, prompt_length[None, :], 0), 1)
    span_places = own_length + jnp.arange(span, dtype=jnp.int32)
    tail_places = (
        row_length[:, None] + span + jnp.arange(steps, dtype=jnp.int32)[None, :]
    ).reshape(-1)
    row_prompt = jnp.repeat(fork_map, steps)[:, None]
    pool = page_pool.reshape(-1, 2 * HD)
    cached = pool.shape[0]
    short_line = n_tensor == kv_heads == 4 and n_replica == 4
    first = min(SET_ROWS, rows)
    blocks = rows // first

    if not short_line:
        positions = jnp.concatenate([span_places, tail_places])
        tokens = jnp.concatenate([span_states, decode_states.reshape(rows * steps, width)], 0)
        projected = jnp.dot(
            tokens,
            jnp.concatenate([key_weight, value_weight], 1),
            preferred_element_type=jnp.float32,
        )
        share = lax.psum_scatter(projected, "tensor", scatter_dimension=0, tiled=True)
        number = share.shape[0]
        places = lax.dynamic_slice_in_dim(positions, device_rank * number, number)
        turned = rotate_round(share, places, kv_heads)
        groups = jnp.stack([own_pair(turned, g, kv_heads) for g in range(kv_heads)], 0)
        outgoing = jnp.repeat(groups, sharing, axis=0)
        paired = lax.all_to_all(
            outgoing, "tensor", split_axis=0, concat_axis=1, tiled=True
        ).reshape(-1, 2 * HD)
        arrived = lax.all_gather(paired[:span], "replica", axis=0, tiled=True)
        key_prompt = mask_tables(
            prompt_owner, page_table, prompt_length, page_pool.shape[2], span, prompts
        )
        mixed, stat = attend_cached(
            decode_queries, row_prompt, key_prompt[:, :cached], pool, 0, blocks
        )
        own = attend_new(
            decode_queries, row_prompt, key_prompt[:, cached:], arrived, paired[span:], mixed, stat, 0, blocks
        )
        decoded = jnp.dot(
            lax.all_gather(own, "tensor", axis=1, tiled=True),
            out_weight,
            preferred_element_type=jnp.float32,
        )
        return decoded.astype(jnp.bfloat16).reshape(rows, steps, out_weight.shape[1])

    rank = device_rank.reshape(1).astype(jnp.int32)
    order = replica ^ prompts
    key_prompt = mask_tables(
        prompt_owner, page_table, prompt_length, page_pool.shape[2], span, order
    )
    pool_prompt, span_prompt = key_prompt[:, :cached], key_prompt[:, cached:]
    return line_of_four(
        rank, span_states, decode_states, decode_queries, key_weight, value_weight,
        out_weight, pool, row_prompt, pool_prompt, span_prompt, span_places, tail_places,
    )


def line_of_four(
    rank, span_states, decode_states, decode_queries, key_weight, value_weight,
    out_weight, pool, row_prompt, pool_prompt, span_prompt, span_places, tail_places,
):
    n_replica = lax.axis_size("replica")
    span = span_states.shape[0]
    rows, steps, _ = decode_states.shape
    first = min(SET_ROWS, rows)
    blocks = rows // first
    cut = first * steps

    def units(x, start, count, kept, sent):
        return project(rank, x, start, count, key_weight, value_weight, kept, sent)

    span_units = units(span_states, 0, span, (0, 2), (1, 3))
    first_units = units(decode_states, 0, first, (0, 2), (1, 3))
    rest_units = units(decode_states, first, rows - first, (0, 1, 2, 3), (1, 2, 3))
    span_tables = turn_tables(span_places)
    cos, sin = turn_tables(tail_places)
    own_span = swap_sum(*span_units, span_tables)
    arrived = [own_span]
    for j in range(1, n_replica):
        arrived.append(swap(own_span, "replica", j))
    arrived = jnp.concatenate(arrived, 0)
    first_tail = swap_sum(*first_units, (cos[:cut], sin[:cut]))
    rest_tail = chain_sum(*rest_units, (cos[cut:], sin[cut:]))

    def cached_part(start, count):
        return attend_cached(decode_queries, row_prompt, pool_prompt, pool, start, count)

    def new_part(tail, parts, start, count):
        return attend_new(
            decode_queries, row_prompt, span_prompt, arrived, tail, *parts, start, count
        )

    middle = blocks - 2
    shape = (rows, steps, out_weight.shape[1])
    first_own = new_part(first_tail, cached_part(0, 1), 0, 1)
    middle_own = new_part(rest_tail[: middle * cut], cached_part(1, middle), 1, middle)
    last_own = new_part(rest_tail[middle * cut :], cached_part(blocks - 1, 1), blocks - 1, 1)
    every = (0, 2, 1, 3)
    far, near, across, passed = gather_heads(first_own)
    decoded = out_project(
        rank, [first_own, far, near, across], every, out_weight, shape, 0, pick=passed
    )
    far, near, across, passed = gather_heads(middle_own)
    decoded = out_project(
        rank, [middle_own, far, near, across], every, out_weight, shape, first,
        pick=passed, into=decoded,
    )
    far, near, across, passed = gather_heads(last_own)
    partial = out_project(rank, [last_own, far], (0, 2), out_weight, shape, 0, final=False)
    return out_project(
        rank, [near, across], (1, 3), out_weight, shape, first * (blocks - 1),
        pick=passed, partial=partial, into=decoded,
    )


def solution(mesh):
    in_specs = (
        P("parts"),
        P(("parts", "replica")),
        P("parts"),
        P("parts"),
        P(("parts", "replica"), "tensor"),
        P(("parts", "replica"), None, "tensor"),
        P(("parts", "replica"), None, "tensor"),
        P("tensor", None),
        P("tensor", None),
        P(None, "tensor"),
        P("tensor", "parts", None, None),
    )
    out_specs = P(("parts", "replica"), None, "tensor")
    return jax.shard_map(
        on_device, mesh=mesh, in_specs=in_specs, out_specs=out_specs, check_vma=False
    )
```

profile of v0, /device:TPU:0, one launch (start us, length us, event | category | flops | bytes accessed | tf_op | source)
XLA Modules:
  0.0 172.9 jit_solution(17112604867162984958)
XLA Ops:
  0.0 3.5 %project.3 = (f32[2,128,256]{2,1,0:T(8,128)S(1)}, bf16[2,128,256]{2,1,0:T(8,128)(2,1)}) custom-call(s32[1]{0:T(128)} %bitcast.rank_ref, bf16[128,2048]{1,0:T(8,128)(2,1)} %x_ref.3, bf16[2048,512]{1,0:T(8,128)(2,1)} %refs_2_.7, bf16[2048,512]{1,0:T(8,128)(2,1)} %refs_3_.5, bf16[2048,512]{1,0:T(8,128)(2,1)} %refs_2_.7, bf16[2048,512]{1,0:T(8,128)(2,1)} %refs_3_.5), custom_call_target="tpu_custom_call" | custom-call | flops 536870912 | bytes 4194304 | tf_op jit(solution)/shard_map/project/pallas_call | solution.py:238
  3.5 0.7 copy-done.7
  4.2 3.1 %collective-permute-start = (bf16[2,128,256]{2,1,0:T(8,128)(2,1)}, bf16[2,128,256]{2,1,0:T(8,128)(2,1)}, u32[]{:S(2)}, u32[]{:S(2)}) collective-permute-start(bf16[2,128,256]{2,1,0:T(8,128)(2,1)} %get-tuple-element.22), channel_id=1, source_target_pairs={{0,1},{1,0},{2,3},{3,2},{4,5},{5,4},{6,7},{7,6},{8,9},{9,8},{10,11... | collective-permute-start | bytes 393224 | tf_op jit(solution)/shard_map/ppermute | solution.py:301
  7.3 3.5 %project.5 = (f32[2,128,256]{2,1,0:T(8,128)S(1)}, bf16[2,128,256]{2,1,0:T(8,128)(2,1)}) custom-call(s32[1]{0:T(128)} %bitcast.rank_ref, bf16[128,4,2048]{2,1,0:T(4,128)(2,1)} %x_ref.5, bf16[2048,512]{1,0:T(8,128)(2,1)} %refs_2_.7, bf16[2048,512]{1,0:T(8,128)(2,1)} %refs_3_.5, bf16[2048,512]{1,0:T(8,128)(2,1)} %refs_2_.7, bf16[2048,512]{1,0:T(8,128)(2,1)} %refs_3_.5), custom_call_target="tpu_custom_call" | custom-call | flops 536870912 | bytes 4194304 | tf_op jit(solution)/shard_map/project/pallas_call | solution.py:238
  11.0 5.4 %project.4 = (f32[4,384,256]{2,1,0:T(8,128)S(1)}, bf16[3,384,256]{2,1,0:T(8,128)(2,1)}) custom-call(s32[1]{0:T(128)} %bitcast.rank_ref, bf16[128,4,2048]{2,1,0:T(4,128)(2,1)} %x_ref.5, bf16[2048,512]{1,0:T(8,128)(2,1)} %refs_2_.7, bf16[2048,512]{1,0:T(8,128)(2,1)} %refs_3_.5, bf16[2048,512]{1,0:T(8,128)(2,1)} %refs_2_.7, bf16[2048,512]{1,0:T(8,128)(2,1)} %refs_3_.5), custom_call_target="tpu_custom_call" | custom-call | flops 1610612736 | bytes 4194304 | tf_op jit(solution)/shard_map/project/pallas_call | solution.py:238
  16.4 3.7 %collective-permute-start.5 = (bf16[3,384,256]{2,1,0:T(8,128)(2,1)}, bf16[3,384,256]{2,1,0:T(8,128)(2,1)S(1)}, u32[]{:S(2)}, u32[]{:S(2)}) collective-permute-start(bf16[3,384,256]{2,1,0:T(8,128)(2,1)} %get-tuple-element.26), channel_id=1, source_target_pairs={{0,1},{3,2},{4,5},{7,6},{8,9},{11,10},{12,13},{15,14},{16,17},{19,... | collective-permute-start | bytes 1769480 | tf_op jit(solution)/shard_map/ppermute | solution.py:312
  20.8 1.3 fusion.6
  22.2 0.7 add_convert_fusion.5
  23.7 1.1 copy-done.9
  24.9 8.0 %attend_cached.4 = (f32[8,256,128]{2,1,0:T(8,128)S(1)}, f32[8,256,128]{2,1,0:T(8,128)S(1)}) custom-call(bf16[128,4,1024]{2,1,0:T(4,128)(2,1)S(1)} %copy-done, s32[512,1]{1,0:T(8,128)S(1)} %broadcast_in_dim_reshape.4.prompt_ref, s32[1,1536]{1,0:T(1,128)S(1)} %slice.78.keyp_ref, bf16[1536,256]{1,0:T(8,128)(2,1)S(1)} %bitcast.13), custom_call_target="tpu_custom_call" | custom-call | flops 1610612736 | bytes 2097152 | tf_op jit(solution)/shard_map/attend_cached/pallas_call | solution.py:142
  32.9 1.0 copy-done.1
  33.9 1.0 copy-done.3
  35.4 0.7 convert_element_type.66
  36.7 0.9 fusion.4
  37.7 1.7 fusion.1
  40.3 0.9 fusion.2
  41.2 2.1 %collective-permute-start.1 = (bf16[128,256]{1,0:T(8,128)(2,1)S(1)}, bf16[128,256]{1,0:T(8,128)(2,1)S(1)}, u32[]{:S(2)}, u32[]{:S(2)}) collective-permute-start(bf16[128,256]{1,0:T(8,128)(2,1)S(1)} %fusion.2), channel_id=1, source_target_pairs={{0,2},{1,3},{2,0},{3,1},{4,6},{5,7},{6,4},{7,5},{8,10},{9,11},{10,... | collective-permute-start | bytes 196616 | tf_op jit(solution)/shard_map/ppermute | solution.py:301
  43.4 10.0 %collective-permute-done.1.refs_1_ = bf16[128,256]{1,0:T(8,128)(2,1)S(1)} collective-permute-done((bf16[128,256]{1,0:T(8,128)(2,1)S(1)}, bf16[128,256]{1,0:T(8,128)(2,1)S(1)}, u32[]{:S(2)}, u32[]{:S(2)}) %collective-permute-start.1) | collective-permute-done | bytes 65568 | tf_op jit(solution)/shard_map/ppermute | solution.py:301
  53.3 0.9 finish.3
  54.3 1.6 collective-permute-start.3
  56.2 1.5 collective-permute-start.7
  58.0 0.8 collective-permute-done.3
  58.8 1.1 collective-permute-done.4
  60.0 5.3 %collective-permute-done.7.refs_2_ = bf16[384,256]{1,0:T(8,128)(2,1)S(1)} collective-permute-done((bf16[384,256]{1,0:T(8,128)(2,1)S(1)}, bf16[384,256]{1,0:T(8,128)(2,1)S(1)}, u32[]{:S(2)}, u32[]{:S(2)}) %collective-permute-start.7) | collective-permute-done | bytes 196640 | tf_op jit(solution)/shard_map/ppermute | solution.py:316
  65.5 6.7 %attend_new.4.refs_0_ = bf16[256,1024]{1,0:T(8,128)(2,1)S(1)} custom-call(bf16[128,4,1024]{2,1,0:T(4,128)(2,1)S(1)} %copy-done, s32[512,1]{1,0:T(8,128)S(1)} %broadcast_in_dim_reshape.4.prompt_ref, s32[1,512]{1,0:T(1,128)S(1)} %slice.72.keyp_ref, bf16[512,256]{1,0:T(8,128)(2,1)S(1)} %pad_maximum_fusion.1.span_ref, bf16[256,256]{1,0:T(8,128)(2,1)S(1)} %slice.79.tail_ref, ...), custom_call_target="tpu_custom_call" | custom-call | flops 671088640 | bytes 2621440 | tf_op jit(solution)/shard_map/attend_new/pallas_call | solution.py:171
  72.2 0.8 collective-permute-start.12
  73.0 0.9 fusion.3
  73.9 2.3 %collective-permute-start.17 = (bf16[128,256]{1,0:T(8,128)(2,1)S(1)}, bf16[128,256]{1,0:T(8,128)(2,1)S(1)}, u32[]{:S(2)}, u32[]{:S(2)}) collective-permute-start(bf16[128,256]{1,0:T(8,128)(2,1)S(1)} %fusion.3), channel_id=1, source_target_pairs={{0,2},{1,3},{2,0},{3,1},{4,6},{5,7},{6,4},{7,5},{8,10},{9,11},{10,... | collective-permute-start | bytes 196616 | tf_op jit(solution)/shard_map/ppermute | solution.py:301
  76.2 4.0 %attend_cached.5 = (f32[8,128,128]{2,1,0:T(8,128)S(1)}, f32[8,128,128]{2,1,0:T(8,128)S(1)}) custom-call(bf16[128,4,1024]{2,1,0:T(4,128)(2,1)S(1)} %copy-done, s32[512,1]{1,0:T(8,128)S(1)} %broadcast_in_dim_reshape.4.prompt_ref, s32[1,1536]{1,0:T(1,128)S(1)} %slice.78.keyp_ref, bf16[1536,256]{1,0:T(8,128)(2,1)S(1)} %bitcast.14), custom_call_target="tpu_custom_call" | custom-call | flops 805306368 | bytes 1048576 | tf_op jit(solution)/shard_map/attend_cached/pallas_call | solution.py:142
  80.1 20.4 %collective-permute-done.17.refs_1_ = bf16[128,256]{1,0:T(8,128)(2,1)S(1)} collective-permute-done((bf16[128,256]{1,0:T(8,128)(2,1)S(1)}, bf16[128,256]{1,0:T(8,128)(2,1)S(1)}, u32[]{:S(2)}, u32[]{:S(2)}) %collective-permute-start.17) | collective-permute-done | bytes 65568 | tf_op jit(solution)/shard_map/ppermute | solution.py:301
  100.6 0.9 finish.5.tail_ref
  101.5 3.3 %attend_new.5.refs_0_ = bf16[128,1024]{1,0:T(8,128)(2,1)S(1)} custom-call(bf16[128,4,1024]{2,1,0:T(4,128)(2,1)S(1)} %copy-done, s32[512,1]{1,0:T(8,128)S(1)} %broadcast_in_dim_reshape.4.prompt_ref, s32[1,512]{1,0:T(1,128)S(1)} %slice.72.keyp_ref, bf16[512,256]{1,0:T(8,128)(2,1)S(1)} %pad_maximum_fusion.1.span_ref, bf16[128,256]{1,0:T(8,128)(2,1)S(1)} %finish.5.tail_ref, ...), custom_call_target="tpu_custom_call" | custom-call | flops 335544320 | bytes 1310720 | tf_op jit(solution)/shard_map/attend_new/pallas_call | solution.py:171
  104.9 2.2 %collective-permute-start.19 = (bf16[128,1024]{1,0:T(8,128)(2,1)S(1)}, bf16[128,1024]{1,0:T(8,128)(2,1)S(1)}, u32[]{:S(2)}, u32[]{:S(2)}) collective-permute-start(bf16[128,1024]{1,0:T(8,128)(2,1)S(1)} %attend_new.5.refs_0_), channel_id=1, source_target_pairs={{0,1},{1,0},{2,3},{3,2},{4,5},{5,4},{6,7},{7,6},{8,9},{9,8},{10,11... | collective-permute-start | bytes 786440 | tf_op jit(solution)/shard_map/ppermute | solution.py:301
  107.7 11.0 %collective-permute-done.18.refs_1_ = bf16[128,1024]{1,0:T(8,128)(2,1)S(1)} collective-permute-done((bf16[128,1024]{1,0:T(8,128)(2,1)S(1)}, bf16[128,1024]{1,0:T(8,128)(2,1)S(1)}, u32[]{:S(2)}, u32[]{:S(2)}) %collective-permute-start.18) | collective-permute-done | bytes 262176 | tf_op jit(solution)/shard_map/ppermute | solution.py:301
  118.7 1.3 collective-permute-start.21
  120.0 2.7 %collective-permute-start.13 = (bf16[256,1024]{1,0:T(8,128)(2,1)S(1)}, bf16[256,1024]{1,0:T(8,128)(2,1)S(1)}, u32[]{:S(2)}, u32[]{:S(2)}) collective-permute-start(bf16[256,1024]{1,0:T(8,128)(2,1)S(1)} %attend_new.4.refs_0_), channel_id=1, source_target_pairs={{0,1},{1,0},{2,3},{3,2},{4,5},{5,4},{6,7},{7,6},{8,9},{9,8},{10,11... | collective-permute-start | bytes 1572872 | tf_op jit(solution)/shard_map/ppermute | solution.py:301
  123.4 1.5 collective-permute-start.15
  125.0 4.0 %attend_cached.3 = (f32[8,128,128]{2,1,0:T(8,128)S(1)}, f32[8,128,128]{2,1,0:T(8,128)S(1)}) custom-call(bf16[128,4,1024]{2,1,0:T(4,128)(2,1)S(1)} %copy-done, s32[512,1]{1,0:T(8,128)S(1)} %broadcast_in_dim_reshape.4.prompt_ref, s32[1,1536]{1,0:T(1,128)S(1)} %slice.78.keyp_ref, bf16[1536,256]{1,0:T(8,128)(2,1)S(1)} %bitcast.15), custom_call_target="tpu_custom_call" | custom-call | flops 805306368 | bytes 1048576 | tf_op jit(solution)/shard_map/attend_cached/pallas_call | solution.py:142
  128.9 3.3 %attend_new.3.refs_0_ = bf16[128,1024]{1,0:T(8,128)(2,1)S(1)} custom-call(bf16[128,4,1024]{2,1,0:T(4,128)(2,1)S(1)} %copy-done, s32[512,1]{1,0:T(8,128)S(1)} %broadcast_in_dim_reshape.4.prompt_ref, s32[1,512]{1,0:T(1,128)S(1)} %slice.72.keyp_ref, bf16[512,256]{1,0:T(8,128)(2,1)S(1)} %pad_maximum_fusion.1.span_ref, bf16[128,256]{1,0:T(8,128)(2,1)S(1)} %slice.77.tail_ref, ...), custom_call_target="tpu_custom_call" | custom-call | flops 335544320 | bytes 1310720 | tf_op jit(solution)/shard_map/attend_new/pallas_call | solution.py:171
  132.2 3.5 %collective-permute-start.10 = (bf16[128,1024]{1,0:T(8,128)(2,1)S(1)}, bf16[128,1024]{1,0:T(8,128)(2,1)S(1)}, u32[]{:S(2)}, u32[]{:S(2)}) collective-permute-start(bf16[128,1024]{1,0:T(8,128)(2,1)S(1)} %attend_new.3.refs_0_), channel_id=1, source_target_pairs={{0,2},{1,3},{2,0},{3,1},{4,6},{5,7},{6,4},{7,5},{8,10},{9,11},{10,... | collective-permute-start | bytes 786440 | tf_op jit(solution)/shard_map/ppermute | solution.py:301
  135.7 7.1 %out_project.5.refs_6_ = bf16[128,4,2048]{2,1,0:T(4,128)(2,1)} custom-call(s32[1]{0:T(128)} %bitcast.rank_ref, bf16[128,1024]{1,0:T(8,128)(2,1)S(1)} %attend_new.5.refs_0_, bf16[128,1024]{1,0:T(8,128)(2,1)S(1)} %collective-permute-done.18.refs_1_, bf16[128,1024]{1,0:T(8,128)(2,1)S(1)} %collective-permute-done.19.refs_2_, ...), custom_call_target="tpu_custom_call" | custom-call | flops 2147483648 | bytes 16777216 | tf_op jit(solution)/shard_map/out_project/pallas_call | solution.py:385
  142.9 6.1 %collective-permute-done.10.refs_1_ = bf16[128,1024]{1,0:T(8,128)(2,1)S(1)} collective-permute-done((bf16[128,1024]{1,0:T(8,128)(2,1)S(1)}, bf16[128,1024]{1,0:T(8,128)(2,1)S(1)}, u32[]{:S(2)}, u32[]{:S(2)}) %collective-permute-start.10) | collective-permute-done | bytes 262176 | tf_op jit(solution)/shard_map/ppermute | solution.py:301
  149.6 3.8 %out_project.4.refs_3_ = f32[128,2048]{1,0:T(8,128)S(1)} custom-call(s32[1]{0:T(128)} %bitcast.rank_ref, bf16[128,1024]{1,0:T(8,128)(2,1)S(1)} %attend_new.3.refs_0_, bf16[128,1024]{1,0:T(8,128)(2,1)S(1)} %collective-permute-done.10.refs_1_, bf16[4096,2048]{1,0:T(8,128)(2,1)} %refs_4_.1), custom_call_target="tpu_custom_call" | custom-call | flops 1073741824 | bytes 8388608 | tf_op jit(solution)/shard_map/out_project/pallas_call | solution.py:385
  153.4 1.6 collective-permute-start.11
  155.0 2.9 %collective-permute-done.15.refs_4_ = bf16[256,1024]{1,0:T(8,128)(2,1)S(1)} collective-permute-done((bf16[256,1024]{1,0:T(8,128)(2,1)S(1)}, bf16[256,1024]{1,0:T(8,128)(2,1)S(1)}, u32[]{:S(2)}, u32[]{:S(2)}) %collective-permute-start.15) | collective-permute-done | bytes 524320 | tf_op jit(solution)/shard_map/ppermute | solution.py:434
  157.9 8.1 %out_project.6.refs_5_ = bf16[128,4,2048]{2,1,0:T(4,128)(2,1)} custom-call(s32[1]{0:T(128)} %bitcast.rank_ref, bf16[256,1024]{1,0:T(8,128)(2,1)S(1)} %attend_new.4.refs_0_, bf16[256,1024]{1,0:T(8,128)(2,1)S(1)} %collective-permute-done.12.refs_1_, bf16[256,1024]{1,0:T(8,128)(2,1)S(1)} %collective-permute-done.13.refs_2_, ...), custom_call_target="tpu_custom_call", output_to_operand_aliasing={{}: (7, {})} | custom-call | flops 4294967296 | bytes 16777216 | tf_op jit(solution)/shard_map/out_project/pallas_call | solution.py:385
  166.0 2.1 %collective-permute-done.11.refs_2_ = bf16[128,1024]{1,0:T(8,128)(2,1)S(1)} collective-permute-done((bf16[128,1024]{1,0:T(8,128)(2,1)S(1)}, bf16[128,1024]{1,0:T(8,128)(2,1)S(1)}, u32[]{:S(2)}, u32[]{:S(2)}) %collective-permute-start.11) | collective-permute-done | bytes 262176 | tf_op jit(solution)/shard_map/ppermute | solution.py:434
  168.1 4.6 %out_project.7 = bf16[128,4,2048]{2,1,0:T(4,128)(2,1)} custom-call(s32[1]{0:T(128)} %bitcast.rank_ref, bf16[128,1024]{1,0:T(8,128)(2,1)S(1)} %collective-permute-done.8.refs_0_, bf16[128,1024]{1,0:T(8,128)(2,1)S(1)} %collective-permute-done.9.refs_1_, bf16[128,1024]{1,0:T(8,128)(2,1)S(1)} %collective-permute-done.11.refs_2_, ...), custom_call_target="tpu_custom_call", output_to_operand_aliasing={{}: (6, {})} | custom-call | flops 1073741824 | bytes 8388608 | tf_op jit(solution)/shard_map/out_project/pallas_call | solution.py:385
  (81 shorter events, 6.9 us)
Async XLA Ops:
  3.5 0.7 copy-start.7
  4.2 36.1 %collective-permute-start = (bf16[2,128,256]{2,1,0:T(8,128)(2,1)}, bf16[2,128,256]{2,1,0:T(8,128)(2,1)}, u32[]{:S(2)}, u32[]{:S(2)}) collective-permute-start(bf16[2,128,256]{2,1,0:T(8,128)(2,1)} %get-tuple-element.22), channel_id=1, source_target_pairs={{0,1},{1,0},{2,3},{3,2},{4,5},{5,4},{6,7},{7,6},{8,9},{9,8},{10,11... | collective-permute-start | bytes 393224 | tf_op jit(solution)/shard_map/ppermute | solution.py:301
  10.8 5.5 %copy-start.5 = (f32[2,128,256]{2,1,0:T(8,128)}, f32[2,128,256]{2,1,0:T(8,128)S(1)}, u32[]{:S(2)}) copy-start(f32[2,128,256]{2,1,0:T(8,128)S(1)} %get-tuple-element.33.keep_ref) | copy-start | bytes 786436
  10.8 9.3 %copy-start.14 = (s32[4]{0:T(128)S(1)}, s32[4]{0:T(128)}, u32[]{:S(2)}) copy-start(s32[4]{0:T(128)} %param.11) | copy-start | bytes 52
  10.8 9.9 %copy-start.15 = (s32[4]{0:T(128)S(1)}, s32[4]{0:T(128)}, u32[]{:S(2)}) copy-start(s32[4]{0:T(128)} %param.14) | copy-start | bytes 52
  10.8 11.2 %copy-start.12 = (s32[128]{0:T(128)S(1)}, s32[128]{0:T(128)}, u32[]{:S(2)}) copy-start(s32[128]{0:T(128)} %param.12) | copy-start | bytes 1540
  10.9 12.1 %copy-start.13 = (s32[12]{0:T(128)S(1)}, s32[12]{0:T(128)}, u32[]{:S(2)}) copy-start(s32[12]{0:T(128)} %param.13) | copy-start | bytes 148
  10.9 12.9 %copy-start = (bf16[128,4,1024]{2,1,0:T(4,128)(2,1)S(1)}, bf16[128,4,1024]{2,1,0:T(4,128)(2,1)}, u32[]{:S(2)}) copy-start(bf16[128,4,1024]{2,1,0:T(4,128)(2,1)} %q_ref.11) | copy-start | bytes 3145732
  10.9 62.2 %collective-permute-start.16 = (bf16[2,128,256]{2,1,0:T(8,128)(2,1)}, bf16[2,128,256]{2,1,0:T(8,128)(2,1)}, u32[]{:S(2)}, u32[]{:S(2)}) collective-permute-start(bf16[2,128,256]{2,1,0:T(8,128)(2,1)} %get-tuple-element.34), channel_id=1, source_target_pairs={{0,1},{1,0},{2,3},{3,2},{4,5},{5,4},{6,7},{7,6},{8,9},{9,8},{10,11... | collective-permute-start | bytes 393224 | tf_op jit(solution)/shard_map/ppermute | solution.py:301
  16.4 23.0 %collective-permute-start.5 = (bf16[3,384,256]{2,1,0:T(8,128)(2,1)}, bf16[3,384,256]{2,1,0:T(8,128)(2,1)S(1)}, u32[]{:S(2)}, u32[]{:S(2)}) collective-permute-start(bf16[3,384,256]{2,1,0:T(8,128)(2,1)} %get-tuple-element.26), channel_id=1, source_target_pairs={{0,1},{3,2},{4,5},{7,6},{8,9},{11,10},{12,13},{15,14},{16,17},{19,... | collective-permute-start | bytes 1769480 | tf_op jit(solution)/shard_map/ppermute | solution.py:312
  23.7 1.1 copy-start.9
  24.9 10.5 %copy-start.11 = (f32[128,4]{1,0:T(8,128)S(1)}, f32[128,4]{1,0:T(8,128)}, u32[]{:S(2)}) copy-start(f32[128,4]{1,0:T(8,128)} %add_convert_fusion.5) | copy-start | bytes 6148
  32.9 1.0 copy-start.1
  33.9 1.0 copy-start.3
  36.1 4.2 %copy-start.8 = (f32[2,128,256]{2,1,0:T(8,128)S(1)}, f32[2,128,256]{2,1,0:T(8,128)}, u32[]{:S(2)}) copy-start(f32[2,128,256]{2,1,0:T(8,128)} %copy-done.7) | copy-start | bytes 786436
  39.5 16.7 %collective-permute-start.6 = (bf16[2,384,256]{2,1,0:T(8,128)(2,1)S(1)}, bf16[2,384,256]{2,1,0:T(8,128)(2,1)S(1)}, u32[]{:S(2)}, u32[]{:S(2)}) collective-permute-start(bf16[2,384,256]{2,1,0:T(8,128)(2,1)S(1)} %pad_maximum_fusion), channel_id=1, source_target_pairs={{1,2},{2,1},{5,6},{6,5},{9,10},{10,9},{13,14},{14,13},{17,18},{18,... | collective-permute-start | bytes 1179656 | tf_op jit(solution)/shard_map/ppermute | solution.py:314
  41.2 12.1 %collective-permute-start.1 = (bf16[128,256]{1,0:T(8,128)(2,1)S(1)}, bf16[128,256]{1,0:T(8,128)(2,1)S(1)}, u32[]{:S(2)}, u32[]{:S(2)}) collective-permute-start(bf16[128,256]{1,0:T(8,128)(2,1)S(1)} %fusion.2), channel_id=1, source_target_pairs={{0,2},{1,3},{2,0},{3,1},{4,6},{5,7},{6,4},{7,5},{8,10},{9,11},{10,... | collective-permute-start | bytes 196616 | tf_op jit(solution)/shard_map/ppermute | solution.py:301
  54.2 3.8 %collective-permute-start.2 = (bf16[128,256]{1,0:T(8,128)(2,1)S(1)}, bf16[128,256]{1,0:T(8,128)(2,1)S(1)}, u32[]{:S(2)}, u32[]{:S(2)}) collective-permute-start(bf16[128,256]{1,0:T(8,128)(2,1)S(1)} %finish.3), channel_id=1, source_target_pairs={{0,4},{4,0},{8,12},{12,8},{1,5},{5,1},{9,13},{13,9},{2,6},{6,2},{1... | collective-permute-start | bytes 196616 | tf_op jit(solution)/shard_map/ppermute | solution.py:301
  54.3 4.5 %collective-permute-start.3 = (bf16[128,256]{1,0:T(8,128)(2,1)S(1)}, bf16[128,256]{1,0:T(8,128)(2,1)S(1)}, u32[]{:S(2)}, u32[]{:S(2)}) collective-permute-start(bf16[128,256]{1,0:T(8,128)(2,1)S(1)} %finish.3), channel_id=1, source_target_pairs={{0,8},{4,12},{8,0},{12,4},{1,9},{5,13},{9,1},{13,5},{2,10},{6,14},... | collective-permute-start | bytes 196616 | tf_op jit(solution)/shard_map/ppermute | solution.py:301
  55.9 4.1 %collective-permute-start.4 = (bf16[128,256]{1,0:T(8,128)(2,1)S(1)}, bf16[128,256]{1,0:T(8,128)(2,1)S(1)}, u32[]{:S(2)}, u32[]{:S(2)}) collective-permute-start(bf16[128,256]{1,0:T(8,128)(2,1)S(1)} %finish.3), channel_id=1, source_target_pairs={{0,12},{4,8},{8,4},{12,0},{1,13},{5,9},{9,5},{13,1},{2,14},{6,10},... | collective-permute-start | bytes 196616 | tf_op jit(solution)/shard_map/ppermute | solution.py:301
  56.2 9.1 %collective-permute-start.7 = (bf16[384,256]{1,0:T(8,128)(2,1)S(1)}, bf16[384,256]{1,0:T(8,128)(2,1)S(1)}, u32[]{:S(2)}, u32[]{:S(2)}) collective-permute-start(bf16[384,256]{1,0:T(8,128)(2,1)S(1)} %fusion), channel_id=1, source_target_pairs={{1,0},{2,3},{5,4},{6,7},{9,8},{10,11},{13,12},{14,15},{17,16},{18,... | collective-permute-start | bytes 589832 | tf_op jit(solution)/shard_map/ppermute | solution.py:316
  58.0 7.5 %copy-start.2 = (f32[8,256,128]{2,1,0:T(8,128)S(1)}, f32[8,256,128]{2,1,0:T(8,128)}, u32[]{:S(2)}) copy-start(f32[8,256,128]{2,1,0:T(8,128)} %copy-done.1) | copy-start | bytes 3145732
  58.0 7.5 %copy-start.4 = (f32[8,256,128]{2,1,0:T(8,128)S(1)}, f32[8,256,128]{2,1,0:T(8,128)}, u32[]{:S(2)}) copy-start(f32[8,256,128]{2,1,0:T(8,128)} %copy-done.3) | copy-start | bytes 3145732
  65.5 7.6 %copy-start.6 = (f32[2,128,256]{2,1,0:T(8,128)S(1)}, f32[2,128,256]{2,1,0:T(8,128)}, u32[]{:S(2)}) copy-start(f32[2,128,256]{2,1,0:T(8,128)} %copy-done.5) | copy-start | bytes 786436
  65.5 10.7 %copy-start.10 = (bf16[1,12,128,256]{3,2,1,0:T(8,128)(2,1)S(1)}, bf16[1,12,128,256]{3,2,1,0:T(8,128)(2,1)}, u32[]{:S(2)}) copy-start(bf16[1,12,128,256]{3,2,1,0:T(8,128)(2,1)} %param.21) | copy-start | bytes 2359300
  72.2 51.2 %collective-permute-start.12 = (bf16[256,1024]{1,0:T(8,128)(2,1)S(1)}, bf16[256,1024]{1,0:T(8,128)(2,1)S(1)}, u32[]{:S(2)}, u32[]{:S(2)}) collective-permute-start(bf16[256,1024]{1,0:T(8,128)(2,1)S(1)} %attend_new.4.refs_0_), channel_id=1, source_target_pairs={{0,2},{1,3},{2,0},{3,1},{4,6},{5,7},{6,4},{7,5},{8,10},{9,11},{10,... | collective-permute-start | bytes 1572872 | tf_op jit(solution)/shard_map/ppermute | solution.py:301
  73.9 26.7 %collective-permute-start.17 = (bf16[128,256]{1,0:T(8,128)(2,1)S(1)}, bf16[128,256]{1,0:T(8,128)(2,1)S(1)}, u32[]{:S(2)}, u32[]{:S(2)}) collective-permute-start(bf16[128,256]{1,0:T(8,128)(2,1)S(1)} %fusion.3), channel_id=1, source_target_pairs={{0,2},{1,3},{2,0},{3,1},{4,6},{5,7},{6,4},{7,5},{8,10},{9,11},{10,... | collective-permute-start | bytes 196616 | tf_op jit(solution)/shard_map/ppermute | solution.py:301
  104.8 13.9 %collective-permute-start.18 = (bf16[128,1024]{1,0:T(8,128)(2,1)S(1)}, bf16[128,1024]{1,0:T(8,128)(2,1)S(1)}, u32[]{:S(2)}, u32[]{:S(2)}) collective-permute-start(bf16[128,1024]{1,0:T(8,128)(2,1)S(1)} %attend_new.5.refs_0_), channel_id=1, source_target_pairs={{0,2},{1,3},{2,0},{3,1},{4,6},{5,7},{6,4},{7,5},{8,10},{9,11},{10,... | collective-permute-start | bytes 786440 | tf_op jit(solution)/shard_map/ppermute | solution.py:301
  104.9 17.9 %collective-permute-start.19 = (bf16[128,1024]{1,0:T(8,128)(2,1)S(1)}, bf16[128,1024]{1,0:T(8,128)(2,1)S(1)}, u32[]{:S(2)}, u32[]{:S(2)}) collective-permute-start(bf16[128,1024]{1,0:T(8,128)(2,1)S(1)} %attend_new.5.refs_0_), channel_id=1, source_target_pairs={{0,1},{1,0},{2,3},{3,2},{4,5},{5,4},{6,7},{7,6},{8,9},{9,8},{10,11... | collective-permute-start | bytes 786440 | tf_op jit(solution)/shard_map/ppermute | solution.py:301
  107.1 25.2 %collective-permute-start.20 = (bf16[128,1024]{1,0:T(8,128)(2,1)S(1)}, bf16[128,1024]{1,0:T(8,128)(2,1)S(1)}, u32[]{:S(2)}, u32[]{:S(2)}) collective-permute-start(bf16[128,1024]{1,0:T(8,128)(2,1)S(1)} %attend_new.5.refs_0_), channel_id=1, source_target_pairs={{1,2},{2,1},{5,6},{6,5},{9,10},{10,9},{13,14},{14,13},{17,18},{18,... | collective-permute-start | bytes 786440 | tf_op jit(solution)/shard_map/ppermute | solution.py:433
  118.7 17.0 %collective-permute-start.21 = (bf16[128,1024]{1,0:T(8,128)(2,1)S(1)}, bf16[128,1024]{1,0:T(8,128)(2,1)S(1)}, u32[]{:S(2)}, u32[]{:S(2)}) collective-permute-start(bf16[128,1024]{1,0:T(8,128)(2,1)S(1)} %collective-permute-done.18.refs_1_), channel_id=1, source_target_pairs={{1,0},{2,3},{5,4},{6,7},{9,8},{10,11},{13,12},{14,15},{17,16},{18,... | collective-permute-start | bytes 786440 | tf_op jit(solution)/shard_map/ppermute | solution.py:434
  120.0 33.4 %collective-permute-start.13 = (bf16[256,1024]{1,0:T(8,128)(2,1)S(1)}, bf16[256,1024]{1,0:T(8,128)(2,1)S(1)}, u32[]{:S(2)}, u32[]{:S(2)}) collective-permute-start(bf16[256,1024]{1,0:T(8,128)(2,1)S(1)} %attend_new.4.refs_0_), channel_id=1, source_target_pairs={{0,1},{1,0},{2,3},{3,2},{4,5},{5,4},{6,7},{7,6},{8,9},{9,8},{10,11... | collective-permute-start | bytes 1572872 | tf_op jit(solution)/shard_map/ppermute | solution.py:301
  122.7 32.2 %collective-permute-start.14 = (bf16[256,1024]{1,0:T(8,128)(2,1)S(1)}, bf16[256,1024]{1,0:T(8,128)(2,1)S(1)}, u32[]{:S(2)}, u32[]{:S(2)}) collective-permute-start(bf16[256,1024]{1,0:T(8,128)(2,1)S(1)} %attend_new.4.refs_0_), channel_id=1, source_target_pairs={{1,2},{2,1},{5,6},{6,5},{9,10},{10,9},{13,14},{14,13},{17,18},{18,... | collective-permute-start | bytes 1572872 | tf_op jit(solution)/shard_map/ppermute | solution.py:433
  123.4 34.4 %collective-permute-start.15 = (bf16[256,1024]{1,0:T(8,128)(2,1)S(1)}, bf16[256,1024]{1,0:T(8,128)(2,1)S(1)}, u32[]{:S(2)}, u32[]{:S(2)}) collective-permute-start(bf16[256,1024]{1,0:T(8,128)(2,1)S(1)} %collective-permute-done.12.refs_1_), channel_id=1, source_target_pairs={{1,0},{2,3},{5,4},{6,7},{9,8},{10,11},{13,12},{14,15},{17,16},{18,... | collective-permute-start | bytes 1572872 | tf_op jit(solution)/shard_map/ppermute | solution.py:434
  132.2 16.7 %collective-permute-start.10 = (bf16[128,1024]{1,0:T(8,128)(2,1)S(1)}, bf16[128,1024]{1,0:T(8,128)(2,1)S(1)}, u32[]{:S(2)}, u32[]{:S(2)}) collective-permute-start(bf16[128,1024]{1,0:T(8,128)(2,1)S(1)} %attend_new.3.refs_0_), channel_id=1, source_target_pairs={{0,2},{1,3},{2,0},{3,1},{4,6},{5,7},{6,4},{7,5},{8,10},{9,11},{10,... | collective-permute-start | bytes 786440 | tf_op jit(solution)/shard_map/ppermute | solution.py:301
  142.8 23.2 %collective-permute-start.8 = (bf16[128,1024]{1,0:T(8,128)(2,1)S(1)}, bf16[128,1024]{1,0:T(8,128)(2,1)S(1)}, u32[]{:S(2)}, u32[]{:S(2)}) collective-permute-start(bf16[128,1024]{1,0:T(8,128)(2,1)S(1)} %attend_new.3.refs_0_), channel_id=1, source_target_pairs={{0,1},{1,0},{2,3},{3,2},{4,5},{5,4},{6,7},{7,6},{8,9},{9,8},{10,11... | collective-permute-start | bytes 786440 | tf_op jit(solution)/shard_map/ppermute | solution.py:301
  148.9 17.1 %collective-permute-start.9 = (bf16[128,1024]{1,0:T(8,128)(2,1)S(1)}, bf16[128,1024]{1,0:T(8,128)(2,1)S(1)}, u32[]{:S(2)}, u32[]{:S(2)}) collective-permute-start(bf16[128,1024]{1,0:T(8,128)(2,1)S(1)} %attend_new.3.refs_0_), channel_id=1, source_target_pairs={{1,2},{2,1},{5,6},{6,5},{9,10},{10,9},{13,14},{14,13},{17,18},{18,... | collective-permute-start | bytes 786440 | tf_op jit(solution)/shard_map/ppermute | solution.py:433
  153.4 14.7 %collective-permute-start.11 = (bf16[128,1024]{1,0:T(8,128)(2,1)S(1)}, bf16[128,1024]{1,0:T(8,128)(2,1)S(1)}, u32[]{:S(2)}, u32[]{:S(2)}) collective-permute-start(bf16[128,1024]{1,0:T(8,128)(2,1)S(1)} %collective-permute-done.10.refs_1_), channel_id=1, source_target_pairs={{1,0},{2,3},{5,4},{6,7},{9,8},{10,11},{13,12},{14,15},{17,16},{18,... | collective-permute-start | bytes 786440 | tf_op jit(solution)/shard_map/ppermute | solution.py:434
where the time goes:
time: 173 us
  Pallas kernels  67.3 us (39%)
  waiting for transfers between devices  59.7 us (35%)
  starting transfers between devices  31 us (18%)
  other arithmetic  9.3 us (5%)
  local copies, waits for them, and re-layouts  4.88 us (3%)
    ppermute x13, waiting for transfers between devices, swap(): lax.ppermute(x, axis, [(i, i ^ bit) for i in range(lax.axis_size(axis))])  49.4 us
    pallas_call x4, Pallas kernels, out_project(): pl.pallas_call(functools.partial(out_kernel, rels, pick is not None, cuts...  23.6 us
    ppermute x13, starting transfers between devices, swap(): lax.ppermute(x, axis, [(i, i ^ bit) for i in range(lax.axis_size(axis))])  18.7 us
    pallas_call x3, Pallas kernels, attend_cached(): pl.pallas_call(functools.partial(cached_kernel, heads, LOG2E / math.sqrt(...  15.9 us
    pallas_call x3, Pallas kernels, attend_new(): pl.pallas_call(functools.partial(new_kernel, heads, steps, LOG2E / math.s...  13.3 us
    pallas_call x3, Pallas kernels, project(): pl.pallas_call(functools.partial(project_kernel, split, kept, sent), grid...  12.5 us
    ppermute x1, waiting for transfers between devices, chain_sum(): three = lax.ppermute(outward, 'tensor', [(1, 0), (2, 3)])  5.32 us
    ppermute x3, waiting for transfers between devices, gather_heads(): passed = lax.ppermute(far, 'tensor', [(1, 0), (2, 3)])  5 us
  transfers between devices with their start and end apart: 22, of which 9 were waited for; matrix products, arithmetic and copies ran while one was open for 6% of the time, Pallas kernels for 34%

commit v1 on v0

--- a/solution.py
+++ b/solution.py
@@ -66,9 +66,8 @@
     m = qs.shape[0] // heads
     top = None
     at = 0
-    for ref, bias in parts:
-        n = ref.shape[0]
-        s = lax.dot_general(qs, ref[:, :HD], NT, preferred_element_type=jnp.float32)
+    for n, load, bias in parts:
+        s = lax.dot_general(qs, load()[:, :HD], NT, preferred_element_type=jnp.float32)
         s = s.reshape(heads, m, n) * scale2 + bias()[None]
         s_ref[:, :, at : at + n] = s
         most = lane_tiles(jnp.maximum, s)
@@ -77,13 +76,12 @@
     top = jnp.max(top, -1, keepdims=True)
     total = mixed = None
     at = 0
-    for ref, _ in parts:
-        n = ref.shape[0]
+    for n, load, _ in parts:
         w = jnp.exp2(s_ref[:, :, at : at + n] - top)
         summed = lane_tiles(jnp.add, w)
         one = jnp.dot(
             w.astype(jnp.bfloat16).reshape(heads * m, n),
-            ref[:, HD:],
+            load()[:, HD:],
             preferred_element_type=jnp.float32,
         ).reshape(heads, m, HD)
         total = summed if total is None else total + summed
@@ -92,33 +90,74 @@
     return top, jnp.sum(total, -1, keepdims=True), mixed
 
 
-def hidden_unless(prompt, keys):
-    return jnp.where(prompt == keys, 0.0, HIDDEN)
-
-
-def cached_kernel(heads, scale2, q_ref, prompt_ref, keyp_ref, pool_ref, mixed_ref, stat_ref, s_ref):
+def shown(allowed):
+    return jnp.where(allowed, 0.0, HIDDEN)
+
+
+def cached_kernel(
+    heads, cpages, scale2, table_ref, length_ref, q_ref, prompt_ref, pool_ref, mixed_ref, stat_ref, s_ref
+):
     qs = stacked_heads(q_ref, heads)
-    parts = ((pool_ref, lambda: hidden_unless(prompt_ref[...], keyp_ref[...])),)
+    m = qs.shape[0] // heads
+    pages, size = pool_ref.shape[:2]
+    group = 2 * cpages
+
+    def part(at):
+        mine = range(at, min(at + group, pages))
+
+        def load():
+            return jnp.concatenate([pool_ref[table_ref[i]] for i in mine], 0)
+
+        def bias():
+            lane = lax.broadcasted_iota(jnp.int32, (m, size), 1)
+            prompt = prompt_ref[...]
+            return jnp.concatenate(
+                [
+                    shown(
+                        (prompt == i // cpages)
+                        & (lane < length_ref[i // cpages] - (i % cpages) * size)
+                    )
+                    for i in mine
+                ],
+                1,
+            )
+
+        return len(mine) * size, load, bias
+
+    parts = [part(at) for at in range(0, pages, group)]
     top, total, mixed = softmax_parts(qs, heads, parts, scale2, s_ref)
     mixed_ref[...] = mixed
     lane = lax.broadcasted_iota(jnp.int32, mixed.shape, 2)
     stat_ref[...] = jnp.where(lane < HD // 2, top, total)
 
 
-def new_kernel(
-    heads, steps, scale2, q_ref, prompt_ref, keyp_ref, span_ref, tail_ref, mixed_ref, stat_ref, o_ref, s_ref
-):
+def new_kernel(heads, steps, scale2, owner_ref, base_ref, q_ref, prompt_ref, tail_ref, mixed_ref, stat_ref, *refs):
+    span_refs, o_ref, s_ref = refs[:-2], refs[-2], refs[-1]
     qs = stacked_heads(q_ref, heads)
     m = qs.shape[0] // heads
+    span = span_refs[0].shape[0]
+
+    def loaded():
+        return jnp.concatenate([ref[...] for ref in span_refs], 0)
+
+    def owned():
+        prompt = prompt_ref[...]
+        return jnp.concatenate(
+            [
+                jnp.broadcast_to(shown(prompt == owner_ref[base_ref[0] ^ j]), (m, span))
+                for j in range(len(span_refs))
+            ],
+            1,
+        )
 
     def causal():
         row = lax.broadcasted_iota(jnp.int32, (m, m), 0)
         col = lax.broadcasted_iota(jnp.int32, (m, m), 1)
-        return jnp.where((row // steps == col // steps) & (col <= row), 0.0, HIDDEN)
+        return shown((row // steps == col // steps) & (col <= row))
 
     parts = (
-        (span_ref, lambda: hidden_unless(prompt_ref[...], keyp_ref[...])),
-        (tail_ref, causal),
+        (span * len(span_refs), loaded, owned),
+        (m, lambda: tail_ref[...], causal),
     )
     top, total, mixed = softmax_parts(qs, heads, parts, scale2, s_ref)
     old_top = stat_ref[:, :, :1]
@@ -133,24 +172,27 @@
         o_ref[:, h * HD : (h + 1) * HD] = out[h]
 
 
-def attend_cached(q, row_prompt, key_prompt, pool, start, count):
+def attend_cached(q, row_prompt, page_table, prompt_length, pool, start, count):
     steps, width = q.shape[1:]
     heads = width // HD
     block = min(SET_ROWS, q.shape[0])
     m = block * steps
-    cached = pool.shape[0]
+    cached = pool.shape[0] * pool.shape[1]
+    cpages = pool.shape[0] // prompt_length.shape[0]
     return pl.pallas_call(
-        functools.partial(cached_kernel, heads, LOG2E / math.sqrt(HD)),
-        grid=(count,),
-        in_specs=[
-            pl.BlockSpec((block, steps, width), lambda i: (i + start, 0, 0)),
-            pl.BlockSpec((m, 1), lambda i: (i + start, 0)),
-            pl.BlockSpec((1, cached), lambda i: (0, 0)),
-            pl.BlockSpec((cached, 2 * HD), lambda i: (0, 0)),
-        ],
-        out_specs=[pl.BlockSpec((heads, m, HD), lambda i: (0, i, 0))] * 2,
+        functools.partial(cached_kernel, heads, cpages, LOG2E / math.sqrt(HD)),
+        grid_spec=pltpu.PrefetchScalarGridSpec(
+            num_scalar_prefetch=2,
+            grid=(count,),
+            in_specs=[
+                pl.BlockSpec((block, steps, width), lambda i, *_: (i + start, 0, 0)),
+                pl.BlockSpec((m, 1), lambda i, *_: (i + start, 0)),
+                pl.BlockSpec(pool.shape, lambda i, *_: (0, 0, 0)),
+            ],
+            out_specs=[pl.BlockSpec((heads, m, HD), lambda i, *_: (0, i, 0))] * 2,
+            scratch_shapes=[pltpu.VMEM((heads, m, cached), jnp.float32)],
+        ),
         out_shape=[jax.ShapeDtypeStruct((heads, m * count, HD), jnp.float32)] * 2,
-        scratch_shapes=[pltpu.VMEM((heads, m, cached), jnp.float32)],
         cost_estimate=pl.CostEstimate(
             flops=4 * count * heads * m * cached * HD,
             transcendentals=count * heads * m * cached,
@@ -158,31 +200,34 @@
         ),
         compiler_params=SMALL,
         name="attend_cached",
-    )(q, row_prompt, key_prompt, pool)
-
-
-def attend_new(q, row_prompt, key_prompt, span_pairs, tail_pairs, mixed, stat, start, count):
+    )(page_table, prompt_length, q, row_prompt, pool)
+
+
+def attend_new(q, row_prompt, owner, base, span_pairs, tail_pairs, mixed, stat, start, count):
     steps, width = q.shape[1:]
     heads = width // HD
     block = min(SET_ROWS, q.shape[0])
     m = block * steps
-    keys = span_pairs.shape[0]
-    part = pl.BlockSpec((heads, m, HD), lambda i: (0, i, 0))
+    span = span_pairs[0].shape[0]
+    keys = span * len(span_pairs)
+    part = pl.BlockSpec((heads, m, HD), lambda i, *_: (0, i, 0))
     return pl.pallas_call(
         functools.partial(new_kernel, heads, steps, LOG2E / math.sqrt(HD)),
-        grid=(count,),
-        in_specs=[
-            pl.BlockSpec((block, steps, width), lambda i: (i + start, 0, 0)),
-            pl.BlockSpec((m, 1), lambda i: (i + start, 0)),
-            pl.BlockSpec((1, keys), lambda i: (0, 0)),
-            pl.BlockSpec((keys, 2 * HD), lambda i: (0, 0)),
-            pl.BlockSpec((m, 2 * HD), lambda i: (i, 0)),
-            part,
-            part,
-        ],
-        out_specs=pl.BlockSpec((m, width), lambda i: (i, 0)),
+        grid_spec=pltpu.PrefetchScalarGridSpec(
+            num_scalar_prefetch=2,
+            grid=(count,),
+            in_specs=[
+                pl.BlockSpec((block, steps, width), lambda i, *_: (i + start, 0, 0)),
+                pl.BlockSpec((m, 1), lambda i, *_: (i + start, 0)),
+                pl.BlockSpec((m, 2 * HD), lambda i, *_: (i, 0)),
+                part,
+                part,
+            ]
+            + [pl.BlockSpec((span, 2 * HD), lambda i, *_: (0, 0))] * len(span_pairs),
+            out_specs=pl.BlockSpec((m, width), lambda i, *_: (i, 0)),
+            scratch_shapes=[pltpu.VMEM((heads, m, keys + m), jnp.float32)],
+        ),
         out_shape=jax.ShapeDtypeStruct((m * count, width), jnp.bfloat16),
-        scratch_shapes=[pltpu.VMEM((heads, m, keys + m), jnp.float32)],
         cost_estimate=pl.CostEstimate(
             flops=4 * count * heads * m * (keys + m) * HD,
             transcendentals=count * heads * m * (keys + m),
@@ -190,13 +235,15 @@
         ),
         compiler_params=SMALL,
         name="attend_new",
-    )(q, row_prompt, key_prompt, span_pairs, tail_pairs, mixed, stat)
-
-
-def project_kernel(split, kept, sent, rank_ref, x_ref, *refs):
+    )(owner, base, q, row_prompt, tail_pairs, mixed, stat, *span_pairs)
+
+
+def project_kernel(groups, split, kept, sent, rank_ref, *refs):
     keep_ref, send_ref, acc = refs[-3:]
     s = pl.program_id(0)
-    x = x_ref[...].reshape(-1, x_ref.shape[-1])
+    rows = [ref[...].reshape(-1, ref.shape[-1]) for ref in refs[:groups]]
+    x = rows[0] if groups == 1 else jnp.concatenate(rows, 0)
+    refs = refs[groups:]
     w = jnp.concatenate(
         [jnp.concatenate([refs[2 * i][...], refs[2 * i + 1][...]], 1) for i in range(split)], 0
     )
@@ -220,23 +267,25 @@
                 ref[i, :, HD:] = acc[:, pl.ds(pl.multiple_of(at + keys, HD), HD)].astype(ref.dtype)
 
 
-def project(rank, x, start, rows, key_weight, value_weight, kept, sent):
+def project(rank, groups, key_weight, value_weight, kept, sent):
     width, columns = key_weight.shape
     depth, split = width // 2, 2
-    lead = (rows,) + x.shape[1:-1]
-    n = math.prod(lead)
-    zeros = (0,) * (len(lead) - 1)
-    in_specs = [
-        pl.BlockSpec(
-            tuple(pl.Element(d) for d in lead + (depth,)),
-            lambda s, r: (start,) + zeros + (s * depth,),
-        )
-    ]
+    in_specs = []
+    n = 0
+    for x, start, rows in groups:
+        lead = (rows,) + x.shape[1:-1]
+        n += math.prod(lead)
+        in_specs.append(
+            pl.BlockSpec(
+                tuple(pl.Element(d) for d in lead + (depth,)),
+                lambda s, r, start=start, lead=lead: (start,) + (0,) * (len(lead) - 1) + (s * depth,),
+            )
+        )
     for i in range(split):
         piece = pl.BlockSpec((depth // split, columns), lambda s, r, i=i: (s * split + i, 0))
         in_specs += [piece, piece]
     return pl.pallas_call(
-        functools.partial(project_kernel, split, kept, sent),
+        functools.partial(project_kernel, len(groups), split, kept, sent),
         grid_spec=pltpu.PrefetchScalarGridSpec(
             num_scalar_prefetch=1,
             grid=(width // depth,),
@@ -255,32 +304,40 @@
         ),
         compiler_params=SMALL,
         name="project",
-    )(rank, in_hbm(x), *([in_hbm(key_weight), in_hbm(value_weight)] * split))
-
-
-def finish_kernel(keep_ref, *refs):
-    cos_ref, sin_ref, o_ref = refs[-3:]
+    )(
+        rank,
+        *[in_hbm(x) for x, _, _ in groups],
+        *([in_hbm(key_weight), in_hbm(value_weight)] * split),
+    )
+
+
+def finish_kernel(sizes, keep_ref, *refs):
+    outs = refs[-len(sizes) :]
+    refs = refs[: -len(sizes)]
+    cos_ref, sin_ref = refs[-2:]
     summed = keep_ref[0]
-    for ref in refs[:-3]:
+    for ref in refs[:-2]:
         summed = summed + (ref[0] if len(ref.shape) == 3 else ref[...]).astype(jnp.float32)
     keys = summed[:, :HD]
     turned = keys * cos_ref[...] + pltpu.roll(keys, HD // 2, 1) * sin_ref[...]
-    o_ref[:, :HD] = turned.astype(jnp.bfloat16)
-    o_ref[:, HD:] = summed[:, HD:].astype(jnp.bfloat16)
-
-
-def finish(keep, others, tables):
+    at = 0
+    for size, o_ref in zip(sizes, outs):
+        o_ref[:, :HD] = turned[at : at + size].astype(jnp.bfloat16)
+        o_ref[:, HD:] = summed[at : at + size, HD:].astype(jnp.bfloat16)
+        at += size
+
+
+def finish(keep, others, tables, start, sizes):
     n = keep.shape[1]
     first = pl.BlockSpec((1, n, 2 * HD), lambda i: (0, 0, 0))
-    flat = lambda w: pl.BlockSpec((n, w), lambda i: (0, 0))
+    flat = lambda rows: pl.BlockSpec((rows, 2 * HD), lambda i: (0, 0))
+    table = pl.BlockSpec((pl.Element(n), pl.Element(HD)), lambda i: (start, 0))
     return pl.pallas_call(
-        finish_kernel,
+        functools.partial(finish_kernel, sizes),
         grid=(1,),
-        in_specs=[first]
-        + [first if x.ndim == 3 else flat(2 * HD) for x in others]
-        + [flat(HD), flat(HD)],
-        out_specs=flat(2 * HD),
-        out_shape=jax.ShapeDtypeStruct((n, 2 * HD), jnp.bfloat16),
+        in_specs=[first] + [first if x.ndim == 3 else flat(n) for x in others] + [table, table],
+        out_specs=[flat(size) for size in sizes],
+        out_shape=[jax.ShapeDtypeStruct((size, 2 * HD), jnp.bfloat16) for size in sizes],
         compiler_params=SMALL,
         name="finish",
     )(keep, *others, *tables)
@@ -301,20 +358,20 @@
     return lax.ppermute(x, axis, [(i, i ^ bit) for i in range(lax.axis_size(axis))])
 
 
-def swap_sum(keep, send, tables):
+def swap_sum(keep, send, tables, start, sizes):
     got = swap(send, "tensor", 1)
     half = (keep[1] + got[1].astype(jnp.float32)).astype(jnp.bfloat16)
     last = swap(half, "tensor", 2)
-    return finish(keep, (got, last), tables)
-
-
-def chain_sum(keep, send, tables):
+    return finish(keep, (got, last), tables, start, sizes)
+
+
+def chain_sum(keep, send, tables, start, sizes):
     one = lax.ppermute(send, "tensor", [(0, 1), (3, 2)])
     inward = jnp.stack([keep[3] + one[1].astype(jnp.float32), keep[2] + one[2].astype(jnp.float32)])
     two = lax.ppermute(inward.astype(jnp.bfloat16), "tensor", [(1, 2), (2, 1)])
     outward = (keep[1] + two[1].astype(jnp.float32)).astype(jnp.bfloat16)
     three = lax.ppermute(outward, "tensor", [(1, 0), (2, 3)])
-    return finish(keep, (one, two, three), tables)
+    return finish(keep, (one, two, three), tables, start, sizes)
 
 
 def out_kernel(rels, pick, cuts, add, final, rank_ref, *refs):
@@ -406,27 +463,6 @@
     )(rank, *args)
 
 
-def mask_tables(prompt_owner, page_table, prompt_length, page_size, span, order):
-    n_replica = order.shape[0]
-    prompts = jnp.arange(n_replica, dtype=jnp.int32)
-    pool_pages = page_table.shape[0]
-    cpages = pool_pages // n_replica
-    entries = jnp.arange(pool_pages, dtype=jnp.int32)
-    page_hits = page_table[None, :] == entries[:, None]
-    page_prompt = jnp.sum(jnp.where(page_hits, entries[None, :] // cpages, 0), 1)
-    page_slot = jnp.sum(jnp.where(page_hits, entries[None, :] % cpages, 0), 1)
-    page_length = jnp.sum(
-        jnp.where(page_prompt[:, None] == prompts[None, :], prompt_length[None, :], 0), 1
-    )
-    visible = (
-        page_slot[:, None] * page_size + jnp.arange(page_size, dtype=jnp.int32)[None, :]
-        < page_length[:, None]
-    )
-    pool_prompt = jnp.where(visible, page_prompt[:, None], -1).reshape(-1)
-    owners = jnp.sum(jnp.where(order[:, None] == prompts[None, :], prompt_owner[None, :], 0), 1)
-    return jnp.concatenate([pool_prompt, jnp.repeat(owners, span)])[None, :]
-
-
 def gather_heads(own):
     far = swap(own, "tensor", 2)
     near = swap(own, "tensor", 1)
@@ -466,8 +502,7 @@
         row_length[:, None] + span + jnp.arange(steps, dtype=jnp.int32)[None, :]
     ).reshape(-1)
     row_prompt = jnp.repeat(fork_map, steps)[:, None]
-    pool = page_pool.reshape(-1, 2 * HD)
-    cached = pool.shape[0]
+    pool = page_pool.reshape(page_pool.shape[1:])
     short_line = n_tensor == kv_heads == 4 and n_replica == 4
     first = min(SET_ROWS, rows)
     blocks = rows // first
@@ -490,14 +525,20 @@
             outgoing, "tensor", split_axis=0, concat_axis=1, tiled=True
         ).reshape(-1, 2 * HD)
         arrived = lax.all_gather(paired[:span], "replica", axis=0, tiled=True)
-        key_prompt = mask_tables(
-            prompt_owner, page_table, prompt_length, page_pool.shape[2], span, prompts
-        )
         mixed, stat = attend_cached(
-            decode_queries, row_prompt, key_prompt[:, :cached], pool, 0, blocks
+            decode_queries, row_prompt, page_table, prompt_length, pool, 0, blocks
         )
         own = attend_new(
-            decode_queries, row_prompt, key_prompt[:, cached:], arrived, paired[span:], mixed, stat, 0, blocks
+            decode_queries,
+            row_prompt,
+            prompt_owner,
+            jnp.zeros((1,), jnp.int32),
+            jnp.split(arrived, n_replica),
+            paired[span:],
+            mixed,
+            stat,
+            0,
+            blocks,
         )
         decoded = jnp.dot(
             lax.all_gather(own, "tensor", axis=1, tiled=True),
@@ -507,66 +548,80 @@
         return decoded.astype(jnp.bfloat16).reshape(rows, steps, out_weight.shape[1])
 
     rank = device_rank.reshape(1).astype(jnp.int32)
-    order = replica ^ prompts
-    key_prompt = mask_tables(
-        prompt_owner, page_table, prompt_length, page_pool.shape[2], span, order
-    )
-    pool_prompt, span_prompt = key_prompt[:, :cached], key_prompt[:, cached:]
     return line_of_four(
-        rank, span_states, decode_states, decode_queries, key_weight, value_weight,
-        out_weight, pool, row_prompt, pool_prompt, span_prompt, span_places, tail_places,
+        rank, replica.reshape(1).astype(jnp.int32), prompt_owner, fork_map, page_table,
+        prompt_length, span_states, decode_states, decode_queries, key_weight, value_weight,
+        out_weight, pool,
     )
 
 
 def line_of_four(
-    rank, span_states, decode_states, decode_queries, key_weight, value_weight,
-    out_weight, pool, row_prompt, pool_prompt, span_prompt, span_places, tail_places,
+    rank, replica, prompt_owner, fork_map, page_table, prompt_length, span_states, decode_states,
+    decode_queries, key_weight, value_weight, out_weight, pool,
 ):
     n_replica = lax.axis_size("replica")
     span = span_states.shape[0]
     rows, steps, _ = decode_states.shape
     first = min(SET_ROWS, rows)
     blocks = rows // first
+    middle = blocks - 2
     cut = first * steps
 
-    def units(x, start, count, kept, sent):
-        return project(rank, x, start, count, key_weight, value_weight, kept, sent)
-
-    span_units = units(span_states, 0, span, (0, 2), (1, 3))
-    first_units = units(decode_states, 0, first, (0, 2), (1, 3))
-    rest_units = units(decode_states, first, rows - first, (0, 1, 2, 3), (1, 2, 3))
-    span_tables = turn_tables(span_places)
-    cos, sin = turn_tables(tail_places)
-    own_span = swap_sum(*span_units, span_tables)
+    first_units = project(
+        rank, ((span_states, 0, span), (decode_states, 0, first)), key_weight, value_weight,
+        (0, 2), (1, 3),
+    )
+    rest_units = project(
+        rank, ((decode_states, first, rows - first),), key_weight, value_weight,
+        (0, 1, 2, 3), (1, 2, 3),
+    )
+    late_owner, late_fork, late_length, rest_send = lax.optimization_barrier(
+        (prompt_owner, fork_map, prompt_length, rest_units[1])
+    )
+    prompts = jnp.arange(n_replica, dtype=jnp.int32)
+    own_prompt = jnp.sum(jnp.where(prompts == replica, late_owner, 0))
+    own_length = jnp.sum(jnp.where(prompts == own_prompt, late_length, 0))
+    row_hits = late_fork[:, None] == prompts[None, :]
+    row_length = jnp.sum(jnp.where(row_hits, late_length[None, :], 0), 1)
+    places = jnp.concatenate(
+        [
+            own_length + jnp.arange(span, dtype=jnp.int32),
+            (row_length[:, None] + span + jnp.arange(steps, dtype=jnp.int32)[None, :]).reshape(-1),
+        ]
+    )
+    tables = turn_tables(places)
+    row_prompt = jnp.repeat(late_fork, steps)[:, None]
+
+    own_span, first_tail = swap_sum(*first_units, tables, 0, (span, cut))
     arrived = [own_span]
     for j in range(1, n_replica):
         arrived.append(swap(own_span, "replica", j))
-    arrived = jnp.concatenate(arrived, 0)
-    first_tail = swap_sum(*first_units, (cos[:cut], sin[:cut]))
-    rest_tail = chain_sum(*rest_units, (cos[cut:], sin[cut:]))
-
-    def cached_part(start, count):
-        return attend_cached(decode_queries, row_prompt, pool_prompt, pool, start, count)
-
-    def new_part(tail, parts, start, count):
+    middle_tail, last_tail = chain_sum(
+        rest_units[0], rest_send, tables, span + cut, (middle * cut, cut)
+    )
+
+    def attended(tail, start, count):
+        old = attend_cached(
+            decode_queries, row_prompt, page_table, prompt_length, pool, start, count
+        )
         return attend_new(
-            decode_queries, row_prompt, span_prompt, arrived, tail, *parts, start, count
-        )
-
-    middle = blocks - 2
+            decode_queries, row_prompt, prompt_owner, replica, arrived, tail, *old, start, count
+        )
+
     shape = (rows, steps, out_weight.shape[1])
-    first_own = new_part(first_tail, cached_part(0, 1), 0, 1)
-    middle_own = new_part(rest_tail[: middle * cut], cached_part(1, middle), 1, middle)
-    last_own = new_part(rest_tail[middle * cut :], cached_part(blocks - 1, 1), blocks - 1, 1)
-    every = (0, 2, 1, 3)
+    first_own = attended(first_tail, 0, 1)
+    middle_own = attended(middle_tail, 1, middle)
+    last_own = attended(last_tail, blocks - 1, 1)
     far, near, across, passed = gather_heads(first_own)
     decoded = out_project(
-        rank, [first_own, far, near, across], every, out_weight, shape, 0, pick=passed
+        rank, [first_own, far, near, across], (0, 2, 1, 3), out_weight, shape, 0, pick=passed
     )
     far, near, across, passed = gather_heads(middle_own)
+    partial = out_project(
+        rank, [middle_own, far, near], (0, 2, 1), out_weight, shape, 0, final=False
+    )
     decoded = out_project(
-        rank, [middle_own, far, near, across], every, out_weight, shape, first,
-        pick=passed, into=decoded,
+        rank, [across], (3,), out_weight, shape, first, pick=passed, partial=partial, into=decoded
     )
     far, near, across, passed = gather_heads(last_own)
     partial = out_project(rank, [last_own, far], (0, 2), out_weight, shape, 0, final=False)

time: 173 us -> 172 us (level)
  waiting for transfers between devices: 59.7 us -> 49.3 us
  starting transfers between devices: 31 us -> 40.8 us
  other arithmetic: 9.3 us -> 7.17 us
    ppermute x13 -> x11, waiting for transfers between devices: 49.4 us -> 35.1 us  [swap(): lax.ppermute(x, axis, [(i, i ^ bit) for i in range(lax.axis_size(axis))])]
    ppermute x13 -> x11, starting transfers between devices: 18.7 us -> 29.7 us  [swap(): lax.ppermute(x, axis, [(i, i ^ bit) for i in range(lax.axis_size(axis))])]
    ppermute x1, waiting for transfers between devices: 0.01 us -> 9.53 us  [chain_sum(): one = lax.ppermute(send, 'tensor', [(0, 1), (3, 2)])]
    ppermute x1, waiting for transfers between devices: 5.32 us -> 0.01 us  [chain_sum(): three = lax.ppermute(outward, 'tensor', [(1, 0), (2, 3)])]
    pallas_call x9 -> x7, Pallas kernels: 30.4 us -> 28.5 us  [the longest x3 17.8 us: attend_cached(): pl.pallas_call(functools.partial(cached_kernel, heads, cpages, LOG2E / ma...]
    pallas_call x3, Pallas kernels: 13.3 us -> 15.2 us  [attend_new(): pl.pallas_call(functools.partial(new_kernel, heads, steps, LOG2E / math.s...]
    ppermute x1, starting transfers between devices: 3.72 us -> 1.98 us  [chain_sum(): one = lax.ppermute(send, 'tensor', [(0, 1), (3, 2)])]
    pallas_call x4 -> x5, Pallas kernels: 23.6 us -> 25 us  [out_project(): pl.pallas_call(functools.partial(out_kernel, rels, pick is not None, cuts...]
  transfers between devices with their start and end apart: 22 -> 20, of which waited for: 9 -> 6; matrix products, arithmetic and copies ran while one was open for 6% -> 5% of each run, Pallas kernels for 34% -> 30%
where the time goes in v1:
time: 172 us; the launch traced here: 171 us
  Pallas kernels  68.7 us (40%)
  waiting for transfers between devices  49.3 us (29%)
  starting transfers between devices  40.8 us (24%)
  other arithmetic  7.17 us (4%)
  local copies, waits for them, and re-layouts  4.43 us (3%)
    ppermute x11, waiting for transfers between devices, swap(): lax.ppermute(x, axis, [(i, i ^ bit) for i in range(lax.axis_size(axis))])  35.1 us
    ppermute x11, starting transfers between devices, swap(): lax.ppermute(x, axis, [(i, i ^ bit) for i in range(lax.axis_size(axis))])  29.7 us
    pallas_call x5, Pallas kernels, out_project(): pl.pallas_call(functools.partial(out_kernel, rels, pick is not None, cuts...  25 us
    pallas_call x3, Pallas kernels, attend_cached(): pl.pallas_call(functools.partial(cached_kernel, heads, cpages, LOG2E / ma...  17.8 us
    pallas_call x3, Pallas kernels, attend_new(): pl.pallas_call(functools.partial(new_kernel, heads, steps, LOG2E / math.s...  15.2 us
    ppermute x1, waiting for transfers between devices, chain_sum(): one = lax.ppermute(send, 'tensor', [(0, 1), (3, 2)])  9.53 us
    pallas_call x2, Pallas kernels, project(): pl.pallas_call(functools.partial(project_kernel, len(groups), split, kept...  8.59 us
    ppermute x3, waiting for transfers between devices, gather_heads(): passed = lax.ppermute(far, 'tensor', [(1, 0), (2, 3)])  4.72 us
  transfers between devices with their start and end apart: 20, of which 6 were waited for; matrix products, arithmetic and copies ran while one was open for 5% of the time, Pallas kernels for 30%

profile of v1, /device:TPU:0, one launch (start us, length us, event | category | flops | bytes accessed | tf_op | source)
XLA Modules:
  0.0 171.0 jit_solution(10064241765031128341)
XLA Ops:
  0.0 4.2 %project.3 = (f32[2,256,256]{2,1,0:T(8,128)S(1)}, bf16[2,256,256]{2,1,0:T(8,128)(2,1)}) custom-call(s32[1]{0:T(128)} %bitcast.rank_ref, bf16[128,2048]{1,0:T(8,128)(2,1)} %refs_0_.3, bf16[128,4,2048]{2,1,0:T(4,128)(2,1)} %refs_1_.3, bf16[2048,512]{1,0:T(8,128)(2,1)} %refs_4_.4, bf16[2048,512]{1,0:T(8,128)(2,1)} %refs_5_.2, bf16[2048,512]{1,0:T(8,128)(2,1)} %refs_4_.4, ...), custom_call_target="tpu_custom_call" | custom-call | flops 1073741824 | bytes 4194304 | tf_op jit(solution)/shard_map/project/pallas_call | solution.py:287
  4.2 0.8 copy-done.3
  5.0 3.1 %collective-permute-start.3 = (bf16[2,256,256]{2,1,0:T(8,128)(2,1)}, bf16[2,256,256]{2,1,0:T(8,128)(2,1)}, u32[]{:S(2)}, u32[]{:S(2)}) collective-permute-start(bf16[2,256,256]{2,1,0:T(8,128)(2,1)} %get-tuple-element.37), channel_id=1, source_target_pairs={{0,1},{1,0},{2,3},{3,2},{4,5},{5,4},{6,7},{7,6},{8,9},{9,8},{10,11... | collective-permute-start | bytes 786440 | tf_op jit(solution)/shard_map/ppermute | solution.py:358
  8.0 4.4 %project.2 = (f32[4,384,256]{2,1,0:T(8,128)S(1)}, bf16[3,384,256]{2,1,0:T(8,128)(2,1)S(1)}) custom-call(s32[1]{0:T(128)} %bitcast.rank_ref, bf16[128,4,2048]{2,1,0:T(4,128)(2,1)} %refs_1_.3, bf16[2048,512]{1,0:T(8,128)(2,1)} %refs_4_.4, bf16[2048,512]{1,0:T(8,128)(2,1)} %refs_5_.2, bf16[2048,512]{1,0:T(8,128)(2,1)} %refs_4_.4, bf16[2048,512]{1,0:T(8,128)(2,1)} %refs_5_.2), custom_call_target="tpu_custom_call" | custom-call | flops 1610612736 | bytes 4194304 | tf_op jit(solution)/shard_map/project/pallas_call | solution.py:287
  12.5 2.0 %collective-permute-start = (bf16[3,384,256]{2,1,0:T(8,128)(2,1)S(1)}, bf16[3,384,256]{2,1,0:T(8,128)(2,1)S(1)}, u32[]{:S(2)}, u32[]{:S(2)}) collective-permute-start(bf16[3,384,256]{2,1,0:T(8,128)(2,1)S(1)} %get-tuple-element.28), channel_id=1, source_target_pairs={{0,1},{3,2},{4,5},{7,6},{8,9},{11,10},{12,13},{15,14},{16,17},{19,... | collective-permute-start | bytes 1769480 | tf_op jit(solution)/shard_map/ppermute | solution.py:369
  14.9 0.6 fusion.3
  15.5 1.3 fusion.4
  16.8 0.6 iota_add_fusion.1
  17.5 9.5 %collective-permute-done.refs_0_ = bf16[3,384,256]{2,1,0:T(8,128)(2,1)S(1)} collective-permute-done((bf16[3,384,256]{2,1,0:T(8,128)(2,1)S(1)}, bf16[3,384,256]{2,1,0:T(8,128)(2,1)S(1)}, u32[]{:S(2)}, u32[]{:S(2)}) %collective-permute-start) | collective-permute-done | bytes 589856 | tf_op jit(solution)/shard_map/ppermute | solution.py:369
  27.1 0.7 copy-done.1
  27.8 0.8 pad_maximum_fusion
  28.6 1.5 collective-permute-start.1
  30.2 1.2 fusion.2
  31.6 0.7 broadcast_in_dim.27
  32.3 0.9 broadcast_in_dim_reshape.4.prompt_ref
  33.3 1.0 fusion.1
  34.3 5.3 %collective-permute-start.4 = (bf16[256,256]{1,0:T(8,128)(2,1)S(1)}, bf16[256,256]{1,0:T(8,128)(2,1)S(1)}, u32[]{:S(2)}, u32[]{:S(2)}) collective-permute-start(bf16[256,256]{1,0:T(8,128)(2,1)S(1)} %fusion.1), channel_id=1, source_target_pairs={{0,2},{1,3},{2,0},{3,1},{4,6},{5,7},{6,4},{7,5},{8,10},{9,11},{10,... | collective-permute-start | bytes 393224 | tf_op jit(solution)/shard_map/ppermute | solution.py:358
  39.6 1.0 fusion
  40.6 1.5 collective-permute-start.2
  42.1 1.1 copy-done.6
  43.2 8.7 %attend_cached.4 = (f32[8,256,128]{2,1,0:T(8,128)S(1)}, f32[8,256,128]{2,1,0:T(8,128)S(1)}) custom-call(s32[12]{0:T(128)S(1)} %copy-done.9, s32[4]{0:T(128)S(1)} %copy-done.8, bf16[128,4,1024]{2,1,0:T(4,128)(2,1)S(1)} %copy-done, s32[512,1]{1,0:T(8,128)S(1)} %broadcast_in_dim_reshape.4.prompt_ref, bf16[12,128,256]{2,1,0:T(8,128)(2,1)S(1)} %bitcast.7), custom_call_target="tpu_custom_call" | custom-call | flops 1610612736 | bytes 2097152 | tf_op jit(solution)/shard_map/attend_cached/pallas_call | solution.py:182
  52.0 1.0 finish.3
  53.1 1.6 collective-permute-start.6
  54.9 4.6 %attend_cached.5 = (f32[8,128,128]{2,1,0:T(8,128)S(1)}, f32[8,128,128]{2,1,0:T(8,128)S(1)}) custom-call(s32[12]{0:T(128)S(1)} %copy-done.9, s32[4]{0:T(128)S(1)} %copy-done.8, bf16[128,4,1024]{2,1,0:T(4,128)(2,1)S(1)} %copy-done, s32[512,1]{1,0:T(8,128)S(1)} %broadcast_in_dim_reshape.4.prompt_ref, bf16[12,128,256]{2,1,0:T(8,128)(2,1)S(1)} %bitcast.8), custom_call_target="tpu_custom_call" | custom-call | flops 805306368 | bytes 1048576 | tf_op jit(solution)/shard_map/attend_cached/pallas_call | solution.py:182
  59.5 3.8 %attend_new.5.refs_0_ = bf16[128,1024]{1,0:T(8,128)(2,1)S(1)} custom-call(s32[4]{0:T(128)S(1)} %copy-done.5, s32[1]{0:T(128)} %bitcast.1.base_ref, bf16[128,4,1024]{2,1,0:T(4,128)(2,1)S(1)} %copy-done, s32[512,1]{1,0:T(8,128)S(1)} %broadcast_in_dim_reshape.4.prompt_ref, bf16[128,256]{1,0:T(8,128)(2,1)S(1)} %get-tuple-element.42.tail_ref, ...), custom_call_target="tpu_custom_call" | custom-call | flops 335544320 | bytes 1310720 | tf_op jit(solution)/shard_map/attend_new/pallas_call | solution.py:214
  63.4 1.1 finish.2
  64.5 7.5 %attend_new.4.refs_0_ = bf16[256,1024]{1,0:T(8,128)(2,1)S(1)} custom-call(s32[4]{0:T(128)S(1)} %copy-done.5, s32[1]{0:T(128)} %bitcast.1.base_ref, bf16[128,4,1024]{2,1,0:T(4,128)(2,1)S(1)} %copy-done, s32[512,1]{1,0:T(8,128)S(1)} %broadcast_in_dim_reshape.4.prompt_ref, bf16[256,256]{1,0:T(8,128)(2,1)S(1)} %get-tuple-element.39.tail_ref, ...), custom_call_target="tpu_custom_call" | custom-call | flops 671088640 | bytes 2621440 | tf_op jit(solution)/shard_map/attend_new/pallas_call | solution.py:214
  72.0 10.1 %collective-permute-start.13 = (bf16[256,1024]{1,0:T(8,128)(2,1)S(1)}, bf16[256,1024]{1,0:T(8,128)(2,1)S(1)}, u32[]{:S(2)}, u32[]{:S(2)}) collective-permute-start(bf16[256,1024]{1,0:T(8,128)(2,1)S(1)} %attend_new.4.refs_0_), channel_id=1, source_target_pairs={{0,2},{1,3},{2,0},{3,1},{4,6},{5,7},{6,4},{7,5},{8,10},{9,11},{10,... | collective-permute-start | bytes 1572872 | tf_op jit(solution)/shard_map/ppermute | solution.py:358
  82.2 1.7 collective-permute-start.17
  83.8 0.7 collective-permute-start.18
  84.5 32.8 %collective-permute-done.16.refs_1_ = bf16[128,1024]{1,0:T(8,128)(2,1)S(1)} collective-permute-done((bf16[128,1024]{1,0:T(8,128)(2,1)S(1)}, bf16[128,1024]{1,0:T(8,128)(2,1)S(1)}, u32[]{:S(2)}, u32[]{:S(2)}) %collective-permute-start.16) | collective-permute-done | bytes 262176 | tf_op jit(solution)/shard_map/ppermute | solution.py:358
  117.3 1.3 collective-permute-start.19
  118.6 2.7 %collective-permute-start.15 = (bf16[256,1024]{1,0:T(8,128)(2,1)S(1)}, bf16[256,1024]{1,0:T(8,128)(2,1)S(1)}, u32[]{:S(2)}, u32[]{:S(2)}) collective-permute-start(bf16[256,1024]{1,0:T(8,128)(2,1)S(1)} %attend_new.4.refs_0_), channel_id=1, source_target_pairs={{0,1},{1,0},{2,3},{3,2},{4,5},{5,4},{6,7},{7,6},{8,9},{9,8},{10,11... | collective-permute-start | bytes 1572872 | tf_op jit(solution)/shard_map/ppermute | solution.py:358
  121.3 4.6 %attend_cached.3 = (f32[8,128,128]{2,1,0:T(8,128)S(1)}, f32[8,128,128]{2,1,0:T(8,128)S(1)}) custom-call(s32[12]{0:T(128)S(1)} %copy-done.9, s32[4]{0:T(128)S(1)} %copy-done.8, bf16[128,4,1024]{2,1,0:T(4,128)(2,1)S(1)} %copy-done, s32[512,1]{1,0:T(8,128)S(1)} %broadcast_in_dim_reshape.4.prompt_ref, bf16[12,128,256]{2,1,0:T(8,128)(2,1)S(1)} %bitcast.9), custom_call_target="tpu_custom_call" | custom-call | flops 805306368 | bytes 1048576 | tf_op jit(solution)/shard_map/attend_cached/pallas_call | solution.py:182
  125.9 3.8 %attend_new.3.refs_0_ = bf16[128,1024]{1,0:T(8,128)(2,1)S(1)} custom-call(s32[4]{0:T(128)S(1)} %copy-done.5, s32[1]{0:T(128)} %bitcast.1.base_ref, bf16[128,4,1024]{2,1,0:T(4,128)(2,1)S(1)} %copy-done, s32[512,1]{1,0:T(8,128)S(1)} %broadcast_in_dim_reshape.4.prompt_ref, bf16[128,256]{1,0:T(8,128)(2,1)S(1)} %get-tuple-element.33.tail_ref, ...), custom_call_target="tpu_custom_call" | custom-call | flops 335544320 | bytes 1310720 | tf_op jit(solution)/shard_map/attend_new/pallas_call | solution.py:214
  129.8 0.7 collective-permute-start.12
  130.5 1.6 collective-permute-start.14
  132.1 7.1 %out_project.7.refs_4_ = bf16[128,4,2048]{2,1,0:T(4,128)(2,1)} custom-call(s32[1]{0:T(128)} %bitcast.rank_ref, bf16[128,1024]{1,0:T(8,128)(2,1)S(1)} %attend_new.5.refs_0_, bf16[128,1024]{1,0:T(8,128)(2,1)S(1)} %collective-permute-done.16.refs_1_, bf16[128,1024]{1,0:T(8,128)(2,1)S(1)} %collective-permute-done.17.refs_2_, ...), custom_call_target="tpu_custom_call" | custom-call | flops 2147483648 | bytes 16777216 | tf_op jit(solution)/shard_map/out_project/pallas_call | solution.py:442
  139.2 4.8 %collective-permute-start.8 = (bf16[128,1024]{1,0:T(8,128)(2,1)S(1)}, bf16[128,1024]{1,0:T(8,128)(2,1)S(1)}, u32[]{:S(2)}, u32[]{:S(2)}) collective-permute-start(bf16[128,1024]{1,0:T(8,128)(2,1)S(1)} %attend_new.3.refs_0_), channel_id=1, source_target_pairs={{0,1},{1,0},{2,3},{3,2},{4,5},{5,4},{6,7},{7,6},{8,9},{9,8},{10,11... | collective-permute-start | bytes 786440 | tf_op jit(solution)/shard_map/ppermute | solution.py:358
  144.4 0.7 collective-permute-start.9
  145.1 3.8 %out_project.5.refs_3_ = f32[128,2048]{1,0:T(8,128)S(1)} custom-call(s32[1]{0:T(128)} %bitcast.rank_ref, bf16[128,1024]{1,0:T(8,128)(2,1)S(1)} %attend_new.3.refs_0_, bf16[128,1024]{1,0:T(8,128)(2,1)S(1)} %collective-permute-done.10.refs_1_, bf16[4096,2048]{1,0:T(8,128)(2,1)} %refs_4_.5), custom_call_target="tpu_custom_call" | custom-call | flops 1073741824 | bytes 8388608 | tf_op jit(solution)/shard_map/out_project/pallas_call | solution.py:442
  148.9 1.3 collective-permute-start.11
  150.2 5.7 %out_project.6.refs_2_ = f32[256,2048]{1,0:T(8,128)S(1)} custom-call(s32[1]{0:T(128)} %bitcast.rank_ref, bf16[256,1024]{1,0:T(8,128)(2,1)S(1)} %attend_new.4.refs_0_, bf16[256,1024]{1,0:T(8,128)(2,1)S(1)} %collective-permute-done.13.refs_1_, bf16[256,1024]{1,0:T(8,128)(2,1)S(1)} %collective-permute-done.15.refs_2_, bf16[4096,2048]{1,0:T(8,128)(2,1)} %refs_4_.5), custom_call_target="tpu_custom_call" | custom-call | flops 3221225472 | bytes 12582912 | tf_op jit(solution)/shard_map/out_project/pallas_call | solution.py:442
  155.9 0.6 collective-permute-done.14.refs_1_
  156.5 3.8 %out_project.8.refs_5_ = bf16[128,4,2048]{2,1,0:T(4,128)(2,1)} custom-call(s32[1]{0:T(128)} %bitcast.rank_ref, bf16[256,1024]{1,0:T(8,128)(2,1)S(1)} %collective-permute-done.12.refs_0_, bf16[256,1024]{1,0:T(8,128)(2,1)S(1)} %collective-permute-done.14.refs_1_, f32[256,2048]{1,0:T(8,128)S(1)} %out_project.6.refs_2_, ...), custom_call_target="tpu_custom_call", output_to_operand_aliasing={{}: (5, {})} | custom-call | flops 1073741824 | bytes 4194304 | tf_op jit(solution)/shard_map/out_project/pallas_call | solution.py:442
  160.3 1.8 %collective-permute-done.8.refs_0_ = bf16[128,1024]{1,0:T(8,128)(2,1)S(1)} collective-permute-done((bf16[128,1024]{1,0:T(8,128)(2,1)S(1)}, bf16[128,1024]{1,0:T(8,128)(2,1)S(1)}, u32[]{:S(2)}, u32[]{:S(2)}) %collective-permute-start.8) | collective-permute-done | bytes 262176 | tf_op jit(solution)/shard_map/ppermute | solution.py:358
  162.1 4.1 %collective-permute-done.11.refs_2_ = bf16[128,1024]{1,0:T(8,128)(2,1)S(1)} collective-permute-done((bf16[128,1024]{1,0:T(8,128)(2,1)S(1)}, bf16[128,1024]{1,0:T(8,128)(2,1)S(1)}, u32[]{:S(2)}, u32[]{:S(2)}) %collective-permute-start.11) | collective-permute-done | bytes 262176 | tf_op jit(solution)/shard_map/ppermute | solution.py:470
  166.2 4.6 %out_project.9 = bf16[128,4,2048]{2,1,0:T(4,128)(2,1)} custom-call(s32[1]{0:T(128)} %bitcast.rank_ref, bf16[128,1024]{1,0:T(8,128)(2,1)S(1)} %collective-permute-done.8.refs_0_, bf16[128,1024]{1,0:T(8,128)(2,1)S(1)} %collective-permute-done.9.refs_1_, bf16[128,1024]{1,0:T(8,128)(2,1)S(1)} %collective-permute-done.11.refs_2_, ...), custom_call_target="tpu_custom_call", output_to_operand_aliasing={{}: (6, {})} | custom-call | flops 1073741824 | bytes 8388608 | tf_op jit(solution)/shard_map/out_project/pallas_call | solution.py:442
  (46 shorter events, 1.7 us)
Async XLA Ops:
  4.2 0.8 copy-start.3
  5.0 9.5 %copy-start.8 = (s32[4]{0:T(128)S(1)}, s32[4]{0:T(128)}, u32[]{:S(2)}) copy-start(s32[4]{0:T(128)} %length_ref.5) | copy-start | bytes 52
  5.0 9.5 %copy-start.10 = (s32[128]{0:T(128)S(1)}, s32[128]{0:T(128)}, u32[]{:S(2)}) copy-start(s32[128]{0:T(128)} %param.12) | copy-start | bytes 1540
  5.0 9.9 %copy-start.5 = (s32[4]{0:T(128)S(1)}, s32[4]{0:T(128)}, u32[]{:S(2)}) copy-start(s32[4]{0:T(128)} %owner_ref.5) | copy-start | bytes 52
  5.0 28.3 %collective-permute-start.3 = (bf16[2,256,256]{2,1,0:T(8,128)(2,1)}, bf16[2,256,256]{2,1,0:T(8,128)(2,1)}, u32[]{:S(2)}, u32[]{:S(2)}) collective-permute-start(bf16[2,256,256]{2,1,0:T(8,128)(2,1)} %get-tuple-element.37), channel_id=1, source_target_pairs={{0,1},{1,0},{2,3},{3,2},{4,5},{5,4},{6,7},{7,6},{8,9},{9,8},{10,11... | collective-permute-start | bytes 786440 | tf_op jit(solution)/shard_map/ppermute | solution.py:358
  12.5 14.5 %collective-permute-start = (bf16[3,384,256]{2,1,0:T(8,128)(2,1)S(1)}, bf16[3,384,256]{2,1,0:T(8,128)(2,1)S(1)}, u32[]{:S(2)}, u32[]{:S(2)}) collective-permute-start(bf16[3,384,256]{2,1,0:T(8,128)(2,1)S(1)} %get-tuple-element.28), channel_id=1, source_target_pairs={{0,1},{3,2},{4,5},{7,6},{8,9},{11,10},{12,13},{15,14},{16,17},{19,... | collective-permute-start | bytes 1769480 | tf_op jit(solution)/shard_map/ppermute | solution.py:369
  27.0 0.8 copy-start.1
  28.6 13.5 %copy-start = (bf16[128,4,1024]{2,1,0:T(4,128)(2,1)S(1)}, bf16[128,4,1024]{2,1,0:T(4,128)(2,1)}, u32[]{:S(2)}) copy-start(bf16[128,4,1024]{2,1,0:T(4,128)(2,1)} %q_ref.11) | copy-start | bytes 3145732
  28.6 13.5 %copy-start.9 = (s32[12]{0:T(128)S(1)}, s32[12]{0:T(128)}, u32[]{:S(2)}) copy-start(s32[12]{0:T(128)} %table_ref.5) | copy-start | bytes 148
  28.6 11.0 %collective-permute-start.1 = (bf16[2,384,256]{2,1,0:T(8,128)(2,1)}, bf16[2,384,256]{2,1,0:T(8,128)(2,1)}, u32[]{:S(2)}, u32[]{:S(2)}) collective-permute-start(bf16[2,384,256]{2,1,0:T(8,128)(2,1)} %pad_maximum_fusion), channel_id=1, source_target_pairs={{1,2},{2,1},{5,6},{6,5},{9,10},{10,9},{13,14},{14,13},{17,18},{18,... | collective-permute-start | bytes 1179656 | tf_op jit(solution)/shard_map/ppermute | solution.py:371
  34.3 17.7 %collective-permute-start.4 = (bf16[256,256]{1,0:T(8,128)(2,1)S(1)}, bf16[256,256]{1,0:T(8,128)(2,1)S(1)}, u32[]{:S(2)}, u32[]{:S(2)}) collective-permute-start(bf16[256,256]{1,0:T(8,128)(2,1)S(1)} %fusion.1), channel_id=1, source_target_pairs={{0,2},{1,3},{2,0},{3,1},{4,6},{5,7},{6,4},{7,5},{8,10},{9,11},{10,... | collective-permute-start | bytes 393224 | tf_op jit(solution)/shard_map/ppermute | solution.py:358
  40.6 22.8 %collective-permute-start.2 = (bf16[384,256]{1,0:T(8,128)(2,1)S(1)}, bf16[384,256]{1,0:T(8,128)(2,1)S(1)}, u32[]{:S(2)}, u32[]{:S(2)}) collective-permute-start(bf16[384,256]{1,0:T(8,128)(2,1)S(1)} %fusion), channel_id=1, source_target_pairs={{1,0},{2,3},{5,4},{6,7},{9,8},{10,11},{13,12},{14,15},{17,16},{18,... | collective-permute-start | bytes 589832 | tf_op jit(solution)/shard_map/ppermute | solution.py:373
  42.1 1.1 copy-start.6
  43.2 8.7 %copy-start.4 = (f32[2,256,256]{2,1,0:T(8,128)S(1)}, f32[2,256,256]{2,1,0:T(8,128)}, u32[]{:S(2)}) copy-start(f32[2,256,256]{2,1,0:T(8,128)} %copy-done.3) | copy-start | bytes 1572868
  43.2 11.7 %copy-start.7 = (bf16[1,12,128,256]{3,2,1,0:T(8,128)(2,1)S(1)}, bf16[1,12,128,256]{3,2,1,0:T(8,128)(2,1)}, u32[]{:S(2)}) copy-start(bf16[1,12,128,256]{3,2,1,0:T(8,128)(2,1)} %param.21) | copy-start | bytes 2359300
  53.0 6.5 %collective-permute-start.5 = (bf16[128,256]{1,0:T(8,128)(2,1)S(1)}, bf16[128,256]{1,0:T(8,128)(2,1)S(1)}, u32[]{:S(2)}, u32[]{:S(2)}) collective-permute-start(bf16[128,256]{1,0:T(8,128)(2,1)S(1)} %get-tuple-element.38.refs_0_), channel_id=1, source_target_pairs={{0,4},{4,0},{8,12},{12,8},{1,5},{5,1},{9,13},{13,9},{2,6},{6,2},{1... | collective-permute-start | bytes 196616 | tf_op jit(solution)/shard_map/ppermute | solution.py:358
  53.1 6.4 %collective-permute-start.6 = (bf16[128,256]{1,0:T(8,128)(2,1)S(1)}, bf16[128,256]{1,0:T(8,128)(2,1)S(1)}, u32[]{:S(2)}, u32[]{:S(2)}) collective-permute-start(bf16[128,256]{1,0:T(8,128)(2,1)S(1)} %get-tuple-element.38.refs_0_), channel_id=1, source_target_pairs={{0,8},{4,12},{8,0},{12,4},{1,9},{5,13},{9,1},{13,5},{2,10},{6,14},... | collective-permute-start | bytes 196616 | tf_op jit(solution)/shard_map/ppermute | solution.py:358
  54.6 4.9 %collective-permute-start.7 = (bf16[128,256]{1,0:T(8,128)(2,1)S(1)}, bf16[128,256]{1,0:T(8,128)(2,1)S(1)}, u32[]{:S(2)}, u32[]{:S(2)}) collective-permute-start(bf16[128,256]{1,0:T(8,128)(2,1)S(1)} %get-tuple-element.38.refs_0_), channel_id=1, source_target_pairs={{0,12},{4,8},{8,4},{12,0},{1,13},{5,9},{9,5},{13,1},{2,14},{6,10},... | collective-permute-start | bytes 196616 | tf_op jit(solution)/shard_map/ppermute | solution.py:358
  59.5 3.9 %copy-start.2 = (bf16[3,384,256]{2,1,0:T(8,128)(2,1)S(1)}, bf16[3,384,256]{2,1,0:T(8,128)(2,1)}, u32[]{:S(2)}) copy-start(bf16[3,384,256]{2,1,0:T(8,128)(2,1)} %copy-done.1) | copy-start | bytes 1769476
  72.0 58.5 %collective-permute-start.13 = (bf16[256,1024]{1,0:T(8,128)(2,1)S(1)}, bf16[256,1024]{1,0:T(8,128)(2,1)S(1)}, u32[]{:S(2)}, u32[]{:S(2)}) collective-permute-start(bf16[256,1024]{1,0:T(8,128)(2,1)S(1)} %attend_new.4.refs_0_), channel_id=1, source_target_pairs={{0,2},{1,3},{2,0},{3,1},{4,6},{5,7},{6,4},{7,5},{8,10},{9,11},{10,... | collective-permute-start | bytes 1572872 | tf_op jit(solution)/shard_map/ppermute | solution.py:358
  82.1 35.2 %collective-permute-start.16 = (bf16[128,1024]{1,0:T(8,128)(2,1)S(1)}, bf16[128,1024]{1,0:T(8,128)(2,1)S(1)}, u32[]{:S(2)}, u32[]{:S(2)}) collective-permute-start(bf16[128,1024]{1,0:T(8,128)(2,1)S(1)} %attend_new.5.refs_0_), channel_id=1, source_target_pairs={{0,2},{1,3},{2,0},{3,1},{4,6},{5,7},{6,4},{7,5},{8,10},{9,11},{10,... | collective-permute-start | bytes 786440 | tf_op jit(solution)/shard_map/ppermute | solution.py:358
  82.2 47.6 %collective-permute-start.17 = (bf16[128,1024]{1,0:T(8,128)(2,1)S(1)}, bf16[128,1024]{1,0:T(8,128)(2,1)S(1)}, u32[]{:S(2)}, u32[]{:S(2)}) collective-permute-start(bf16[128,1024]{1,0:T(8,128)(2,1)S(1)} %attend_new.5.refs_0_), channel_id=1, source_target_pairs={{0,1},{1,0},{2,3},{3,2},{4,5},{5,4},{6,7},{7,6},{8,9},{9,8},{10,11... | collective-permute-start | bytes 786440 | tf_op jit(solution)/shard_map/ppermute | solution.py:358
  83.8 46.0 %collective-permute-start.18 = (bf16[128,1024]{1,0:T(8,128)(2,1)S(1)}, bf16[128,1024]{1,0:T(8,128)(2,1)S(1)}, u32[]{:S(2)}, u32[]{:S(2)}) collective-permute-start(bf16[128,1024]{1,0:T(8,128)(2,1)S(1)} %attend_new.5.refs_0_), channel_id=1, source_target_pairs={{1,2},{2,1},{5,6},{6,5},{9,10},{10,9},{13,14},{14,13},{17,18},{18,... | collective-permute-start | bytes 786440 | tf_op jit(solution)/shard_map/ppermute | solution.py:469
  117.3 14.8 %collective-permute-start.19 = (bf16[128,1024]{1,0:T(8,128)(2,1)S(1)}, bf16[128,1024]{1,0:T(8,128)(2,1)S(1)}, u32[]{:S(2)}, u32[]{:S(2)}) collective-permute-start(bf16[128,1024]{1,0:T(8,128)(2,1)S(1)} %collective-permute-done.16.refs_1_), channel_id=1, source_target_pairs={{1,0},{2,3},{5,4},{6,7},{9,8},{10,11},{13,12},{14,15},{17,16},{18,... | collective-permute-start | bytes 786440 | tf_op jit(solution)/shard_map/ppermute | solution.py:470
  118.6 30.2 %collective-permute-start.15 = (bf16[256,1024]{1,0:T(8,128)(2,1)S(1)}, bf16[256,1024]{1,0:T(8,128)(2,1)S(1)}, u32[]{:S(2)}, u32[]{:S(2)}) collective-permute-start(bf16[256,1024]{1,0:T(8,128)(2,1)S(1)} %attend_new.4.refs_0_), channel_id=1, source_target_pairs={{0,1},{1,0},{2,3},{3,2},{4,5},{5,4},{6,7},{7,6},{8,9},{9,8},{10,11... | collective-permute-start | bytes 1572872 | tf_op jit(solution)/shard_map/ppermute | solution.py:358
  129.7 14.6 %collective-permute-start.10 = (bf16[128,1024]{1,0:T(8,128)(2,1)S(1)}, bf16[128,1024]{1,0:T(8,128)(2,1)S(1)}, u32[]{:S(2)}, u32[]{:S(2)}) collective-permute-start(bf16[128,1024]{1,0:T(8,128)(2,1)S(1)} %attend_new.3.refs_0_), channel_id=1, source_target_pairs={{0,2},{1,3},{2,0},{3,1},{4,6},{5,7},{6,4},{7,5},{8,10},{9,11},{10,... | collective-permute-start | bytes 786440 | tf_op jit(solution)/shard_map/ppermute | solution.py:358
  129.8 26.0 %collective-permute-start.12 = (bf16[256,1024]{1,0:T(8,128)(2,1)S(1)}, bf16[256,1024]{1,0:T(8,128)(2,1)S(1)}, u32[]{:S(2)}, u32[]{:S(2)}) collective-permute-start(bf16[256,1024]{1,0:T(8,128)(2,1)S(1)} %attend_new.4.refs_0_), channel_id=1, source_target_pairs={{1,2},{2,1},{5,6},{6,5},{9,10},{10,9},{13,14},{14,13},{17,18},{18,... | collective-permute-start | bytes 1572872 | tf_op jit(solution)/shard_map/ppermute | solution.py:469
  130.5 25.9 %collective-permute-start.14 = (bf16[256,1024]{1,0:T(8,128)(2,1)S(1)}, bf16[256,1024]{1,0:T(8,128)(2,1)S(1)}, u32[]{:S(2)}, u32[]{:S(2)}) collective-permute-start(bf16[256,1024]{1,0:T(8,128)(2,1)S(1)} %collective-permute-done.13.refs_1_), channel_id=1, source_target_pairs={{1,0},{2,3},{5,4},{6,7},{9,8},{10,11},{13,12},{14,15},{17,16},{18,... | collective-permute-start | bytes 1572872 | tf_op jit(solution)/shard_map/ppermute | solution.py:470
  139.2 22.9 %collective-permute-start.8 = (bf16[128,1024]{1,0:T(8,128)(2,1)S(1)}, bf16[128,1024]{1,0:T(8,128)(2,1)S(1)}, u32[]{:S(2)}, u32[]{:S(2)}) collective-permute-start(bf16[128,1024]{1,0:T(8,128)(2,1)S(1)} %attend_new.3.refs_0_), channel_id=1, source_target_pairs={{0,1},{1,0},{2,3},{3,2},{4,5},{5,4},{6,7},{7,6},{8,9},{9,8},{10,11... | collective-permute-start | bytes 786440 | tf_op jit(solution)/shard_map/ppermute | solution.py:358
  144.4 17.7 %collective-permute-start.9 = (bf16[128,1024]{1,0:T(8,128)(2,1)S(1)}, bf16[128,1024]{1,0:T(8,128)(2,1)S(1)}, u32[]{:S(2)}, u32[]{:S(2)}) collective-permute-start(bf16[128,1024]{1,0:T(8,128)(2,1)S(1)} %attend_new.3.refs_0_), channel_id=1, source_target_pairs={{1,2},{2,1},{5,6},{6,5},{9,10},{10,9},{13,14},{14,13},{17,18},{18,... | collective-permute-start | bytes 786440 | tf_op jit(solution)/shard_map/ppermute | solution.py:469
  148.9 17.3 %collective-permute-start.11 = (bf16[128,1024]{1,0:T(8,128)(2,1)S(1)}, bf16[128,1024]{1,0:T(8,128)(2,1)S(1)}, u32[]{:S(2)}, u32[]{:S(2)}) collective-permute-start(bf16[128,1024]{1,0:T(8,128)(2,1)S(1)} %collective-permute-done.10.refs_1_), channel_id=1, source_target_pairs={{1,0},{2,3},{5,4},{6,7},{9,8},{10,11},{13,12},{14,15},{17,16},{18,... | collective-permute-start | bytes 786440 | tf_op jit(solution)/shard_map/ppermute | solution.py:470

commit v2 on v1

--- a/solution.py
+++ b/solution.py
@@ -90,15 +90,24 @@
     return top, jnp.sum(total, -1, keepdims=True), mixed
 
 
+def by_row(values, first, rows, steps):
+    lane = lax.broadcasted_iota(jnp.int32, (rows, values.shape[1]), 1)
+    row = lax.broadcasted_iota(jnp.int32, (rows, values.shape[1]), 0)
+    mine = jnp.where(lane == first + row // steps, values.astype(jnp.float32), 0.0)
+    return jnp.sum(mine, 1, keepdims=True)
+
+
 def shown(allowed):
     return jnp.where(allowed, 0.0, HIDDEN)
 
 
 def cached_kernel(
-    heads, cpages, scale2, table_ref, length_ref, q_ref, prompt_ref, pool_ref, mixed_ref, stat_ref, s_ref
+    heads, cpages, scale2, start, table_ref, length_ref, q_ref, fork_ref, pool_ref, mixed_ref, stat_ref, s_ref
 ):
     qs = stacked_heads(q_ref, heads)
     m = qs.shape[0] // heads
+    block, steps = q_ref.shape[:2]
+    prompt = by_row(fork_ref[...], (pl.program_id(0) + start) * block, m, steps)
     pages, size = pool_ref.shape[:2]
     group = 2 * cpages
 
@@ -110,11 +119,10 @@
 
         def bias():
             lane = lax.broadcasted_iota(jnp.int32, (m, size), 1)
-            prompt = prompt_ref[...]
             return jnp.concatenate(
                 [
                     shown(
-                        (prompt == i // cpages)
+                        (prompt == float(i // cpages))
                         & (lane < length_ref[i // cpages] - (i % cpages) * size)
                     )
                     for i in mine
@@ -131,20 +139,24 @@
     stat_ref[...] = jnp.where(lane < HD // 2, top, total)
 
 
-def new_kernel(heads, steps, scale2, owner_ref, base_ref, q_ref, prompt_ref, tail_ref, mixed_ref, stat_ref, *refs):
+def new_kernel(
+    heads, steps, scale2, start, owner_ref, base_ref, q_ref, fork_ref, tail_ref, mixed_ref, stat_ref, *refs
+):
     span_refs, o_ref, s_ref = refs[:-2], refs[-2], refs[-1]
     qs = stacked_heads(q_ref, heads)
     m = qs.shape[0] // heads
     span = span_refs[0].shape[0]
+    prompt = by_row(fork_ref[...], (pl.program_id(0) + start) * q_ref.shape[0], m, steps)
 
     def loaded():
         return jnp.concatenate([ref[...] for ref in span_refs], 0)
 
     def owned():
-        prompt = prompt_ref[...]
         return jnp.concatenate(
             [
-                jnp.broadcast_to(shown(prompt == owner_ref[base_ref[0] ^ j]), (m, span))
+                jnp.broadcast_to(
+                    shown(prompt == owner_ref[base_ref[0] ^ j].astype(jnp.float32)), (m, span)
+                )
                 for j in range(len(span_refs))
             ],
             1,
@@ -172,7 +184,7 @@
         o_ref[:, h * HD : (h + 1) * HD] = out[h]
 
 
-def attend_cached(q, row_prompt, page_table, prompt_length, pool, start, count):
+def attend_cached(q, fork_row, page_table, prompt_length, pool, start, count):
     steps, width = q.shape[1:]
     heads = width // HD
     block = min(SET_ROWS, q.shape[0])
@@ -180,13 +192,13 @@
     cached = pool.shape[0] * pool.shape[1]
     cpages = pool.shape[0] // prompt_length.shape[0]
     return pl.pallas_call(
-        functools.partial(cached_kernel, heads, cpages, LOG2E / math.sqrt(HD)),
+        functools.partial(cached_kernel, heads, cpages, LOG2E / math.sqrt(HD), start),
         grid_spec=pltpu.PrefetchScalarGridSpec(
             num_scalar_prefetch=2,
             grid=(count,),
             in_specs=[
                 pl.BlockSpec((block, steps, width), lambda i, *_: (i + start, 0, 0)),
-                pl.BlockSpec((m, 1), lambda i, *_: (i + start, 0)),
+                pl.BlockSpec(fork_row.shape, lambda i, *_: (0, 0)),
                 pl.BlockSpec(pool.shape, lambda i, *_: (0, 0, 0)),
             ],
             out_specs=[pl.BlockSpec((heads, m, HD), lambda i, *_: (0, i, 0))] * 2,
@@ -200,10 +212,10 @@
         ),
         compiler_params=SMALL,
         name="attend_cached",
-    )(page_table, prompt_length, q, row_prompt, pool)
-
-
-def attend_new(q, row_prompt, owner, base, span_pairs, tail_pairs, mixed, stat, start, count):
+    )(page_table, prompt_length, in_hbm(q), fork_row, in_hbm(pool))
+
+
+def attend_new(q, fork_row, owner, base, span_pairs, tail_pairs, mixed, stat, start, count):
     steps, width = q.shape[1:]
     heads = width // HD
     block = min(SET_ROWS, q.shape[0])
@@ -212,13 +224,13 @@
     keys = span * len(span_pairs)
     part = pl.BlockSpec((heads, m, HD), lambda i, *_: (0, i, 0))
     return pl.pallas_call(
-        functools.partial(new_kernel, heads, steps, LOG2E / math.sqrt(HD)),
+        functools.partial(new_kernel, heads, steps, LOG2E / math.sqrt(HD), start),
         grid_spec=pltpu.PrefetchScalarGridSpec(
             num_scalar_prefetch=2,
             grid=(count,),
             in_specs=[
                 pl.BlockSpec((block, steps, width), lambda i, *_: (i + start, 0, 0)),
-                pl.BlockSpec((m, 1), lambda i, *_: (i + start, 0)),
+                pl.BlockSpec(fork_row.shape, lambda i, *_: (0, 0)),
                 pl.BlockSpec((m, 2 * HD), lambda i, *_: (i, 0)),
                 part,
                 part,
@@ -235,7 +247,7 @@
         ),
         compiler_params=SMALL,
         name="attend_new",
-    )(owner, base, q, row_prompt, tail_pairs, mixed, stat, *span_pairs)
+    )(owner, base, in_hbm(q), fork_row, tail_pairs, mixed, stat, *span_pairs)
 
 
 def project_kernel(groups, split, kept, sent, rank_ref, *refs):
@@ -311,15 +323,36 @@
     )
 
 
-def finish_kernel(sizes, keep_ref, *refs):
+def finish_kernel(
+    span, steps, start, sizes, owner_ref, length_ref, replica_ref, fork_ref, freq_ref, keep_ref, *refs
+):
     outs = refs[-len(sizes) :]
-    refs = refs[: -len(sizes)]
-    cos_ref, sin_ref = refs[-2:]
     summed = keep_ref[0]
-    for ref in refs[:-2]:
+    for ref in refs[: -len(sizes)]:
         summed = summed + (ref[0] if len(ref.shape) == 3 else ref[...]).astype(jnp.float32)
+    n = summed.shape[0]
+    fork = fork_ref[...]
+    lengths = jnp.zeros_like(fork)
+    for p in range(length_ref.shape[0]):
+        lengths = jnp.where(fork == p, length_ref[p], lengths)
+    lead = max(0, span - start)
+    places = []
+    if lead:
+        own = length_ref[owner_ref[replica_ref[0]]]
+        places.append(own + start + lax.broadcasted_iota(jnp.int32, (lead, 1), 0).astype(jnp.int32))
+        places[0] = places[0].astype(jnp.float32)
+    tail = n - lead
+    first = start + lead - span
+    step = lax.broadcasted_iota(jnp.int32, (tail, 1), 0) % steps
+    places.append(
+        by_row(lengths, first // steps, tail, steps) + (span + step).astype(jnp.float32)
+    )
+    places = places[0] if len(places) == 1 else jnp.concatenate(places, 0)
+    angle = places * freq_ref[...]
+    lane = lax.broadcasted_iota(jnp.int32, (n, HD), 1)
+    sine = jnp.where(lane < HD // 2, -jnp.sin(angle), jnp.sin(angle))
     keys = summed[:, :HD]
-    turned = keys * cos_ref[...] + pltpu.roll(keys, HD // 2, 1) * sin_ref[...]
+    turned = keys * jnp.cos(angle) + pltpu.roll(keys, HD // 2, 1) * sine
     at = 0
     for size, o_ref in zip(sizes, outs):
         o_ref[:, :HD] = turned[at : at + size].astype(jnp.bfloat16)
@@ -327,51 +360,35 @@
         at += size
 
 
-def finish(keep, others, tables, start, sizes):
+def finish(keep, others, places, start, sizes):
+    span, steps, owner, length, replica, fork_row, freq = places
     n = keep.shape[1]
-    first = pl.BlockSpec((1, n, 2 * HD), lambda i: (0, 0, 0))
-    flat = lambda rows: pl.BlockSpec((rows, 2 * HD), lambda i: (0, 0))
-    table = pl.BlockSpec((pl.Element(n), pl.Element(HD)), lambda i: (start, 0))
+    unit = pl.BlockSpec((1, n, 2 * HD), lambda i, *_: (0, 0, 0))
+    flat = lambda rows, width: pl.BlockSpec((rows, width), lambda i, *_: (0, 0))
     return pl.pallas_call(
-        functools.partial(finish_kernel, sizes),
-        grid=(1,),
-        in_specs=[first] + [first if x.ndim == 3 else flat(n) for x in others] + [table, table],
-        out_specs=[flat(size) for size in sizes],
+        functools.partial(finish_kernel, span, steps, start, sizes),
+        grid_spec=pltpu.PrefetchScalarGridSpec(
+            num_scalar_prefetch=3,
+            grid=(1,),
+            in_specs=[flat(*fork_row.shape), flat(*freq.shape), unit]
+            + [unit if x.ndim == 3 else flat(n, 2 * HD) for x in others],
+            out_specs=[flat(size, 2 * HD) for size in sizes],
+        ),
         out_shape=[jax.ShapeDtypeStruct((size, 2 * HD), jnp.bfloat16) for size in sizes],
         compiler_params=SMALL,
         name="finish",
-    )(keep, *others, *tables)
-
-
-def turn_tables(places):
-    half = HD // 2
-    freq = rope_base ** (-(2.0 / HD) * jnp.arange(half, dtype=jnp.float32))
-    angle = places.astype(jnp.float32)[:, None] * freq
-    cosine = jnp.cos(angle)
-    sine = jnp.sin(angle)
-    return lax.optimization_barrier(
-        (jnp.concatenate([cosine, cosine], 1), jnp.concatenate([-sine, sine], 1))
-    )
+    )(owner, length, replica, fork_row, freq, keep, *others)
 
 
 def swap(x, axis, bit):
     return lax.ppermute(x, axis, [(i, i ^ bit) for i in range(lax.axis_size(axis))])
 
 
-def swap_sum(keep, send, tables, start, sizes):
+def swap_sum(keep, send, places, start, sizes):
     got = swap(send, "tensor", 1)
     half = (keep[1] + got[1].astype(jnp.float32)).astype(jnp.bfloat16)
     last = swap(half, "tensor", 2)
-    return finish(keep, (got, last), tables, start, sizes)
-
-
-def chain_sum(keep, send, tables, start, sizes):
-    one = lax.ppermute(send, "tensor", [(0, 1), (3, 2)])
-    inward = jnp.stack([keep[3] + one[1].astype(jnp.float32), keep[2] + one[2].astype(jnp.float32)])
-    two = lax.ppermute(inward.astype(jnp.bfloat16), "tensor", [(1, 2), (2, 1)])
-    outward = (keep[1] + two[1].astype(jnp.float32)).astype(jnp.bfloat16)
-    three = lax.ppermute(outward, "tensor", [(1, 0), (2, 3)])
-    return finish(keep, (one, two, three), tables, start, sizes)
+    return finish(keep, (got, last), places, start, sizes)
 
 
 def out_kernel(rels, pick, cuts, add, final, rank_ref, *refs):
@@ -501,7 +518,6 @@
     tail_places = (
         row_length[:, None] + span + jnp.arange(steps, dtype=jnp.int32)[None, :]
     ).reshape(-1)
-    row_prompt = jnp.repeat(fork_map, steps)[:, None]
     pool = page_pool.reshape(page_pool.shape[1:])
     short_line = n_tensor == kv_heads == 4 and n_replica == 4
     first = min(SET_ROWS, rows)
@@ -526,11 +542,11 @@
         ).reshape(-1, 2 * HD)
         arrived = lax.all_gather(paired[:span], "replica", axis=0, tiled=True)
         mixed, stat = attend_cached(
-            decode_queries, row_prompt, page_table, prompt_length, pool, 0, blocks
+            decode_queries, fork_map[None, :], page_table, prompt_length, pool, 0, blocks
         )
         own = attend_new(
             decode_queries,
-            row_prompt,
+            fork_map[None, :],
             prompt_owner,
             jnp.zeros((1,), jnp.int32),
             jnp.split(arrived, n_replica),
@@ -572,40 +588,22 @@
         (0, 2), (1, 3),
     )
     rest_units = project(
-        rank, ((decode_states, first, rows - first),), key_weight, value_weight,
-        (0, 1, 2, 3), (1, 2, 3),
-    )
-    late_owner, late_fork, late_length, rest_send = lax.optimization_barrier(
-        (prompt_owner, fork_map, prompt_length, rest_units[1])
-    )
-    prompts = jnp.arange(n_replica, dtype=jnp.int32)
-    own_prompt = jnp.sum(jnp.where(prompts == replica, late_owner, 0))
-    own_length = jnp.sum(jnp.where(prompts == own_prompt, late_length, 0))
-    row_hits = late_fork[:, None] == prompts[None, :]
-    row_length = jnp.sum(jnp.where(row_hits, late_length[None, :], 0), 1)
-    places = jnp.concatenate(
-        [
-            own_length + jnp.arange(span, dtype=jnp.int32),
-            (row_length[:, None] + span + jnp.arange(steps, dtype=jnp.int32)[None, :]).reshape(-1),
-        ]
-    )
-    tables = turn_tables(places)
-    row_prompt = jnp.repeat(late_fork, steps)[:, None]
-
-    own_span, first_tail = swap_sum(*first_units, tables, 0, (span, cut))
+        rank, ((decode_states, first, rows - first),), key_weight, value_weight, (0, 2), (1, 3)
+    )
+    fork_row = fork_map[None, :]
+    half = rope_base ** (-(2.0 / HD) * jnp.arange(HD // 2, dtype=jnp.float32))
+    freq = jnp.concatenate([half, half])[None, :]
+    places = (span, steps, prompt_owner, prompt_length, replica, fork_row, freq)
+    own_span, first_tail = swap_sum(*first_units, places, 0, (span, cut))
     arrived = [own_span]
     for j in range(1, n_replica):
         arrived.append(swap(own_span, "replica", j))
-    middle_tail, last_tail = chain_sum(
-        rest_units[0], rest_send, tables, span + cut, (middle * cut, cut)
-    )
+    middle_tail, last_tail = swap_sum(*rest_units, places, span + cut, (middle * cut, cut))
 
     def attended(tail, start, count):
-        old = attend_cached(
-            decode_queries, row_prompt, page_table, prompt_length, pool, start, count
-        )
+        old = attend_cached(decode_queries, fork_row, page_table, prompt_length, pool, start, count)
         return attend_new(
-            decode_queries, row_prompt, prompt_owner, replica, arrived, tail, *old, start, count
+            decode_queries, fork_row, prompt_owner, replica, arrived, tail, *old, start, count
         )
 
     shape = (rows, steps, out_weight.shape[1])
@@ -624,9 +622,9 @@
         rank, [across], (3,), out_weight, shape, first, pick=passed, partial=partial, into=decoded
     )
     far, near, across, passed = gather_heads(last_own)
-    partial = out_project(rank, [last_own, far], (0, 2), out_weight, shape, 0, final=False)
+    partial = out_project(rank, [last_own, far, near], (0, 2, 1), out_weight, shape, 0, final=False)
     return out_project(
-        rank, [near, across], (1, 3), out_weight, shape, first * (blocks - 1),
+        rank, [across], (3,), out_weight, shape, first * (blocks - 1),
         pick=passed, partial=partial, into=decoded,
     )
 

time: 172 us -> 142 us (0.83)
  starting transfers between devices: 40.8 us -> 21.9 us
  other arithmetic: 7.17 us -> 0.15 us
  Pallas kernels: 68.7 us -> 74.8 us
  waiting for transfers between devices: 49.3 us -> 44.6 us
  local copies, waits for them, and re-layouts: 4.43 us -> 0.03 us
    ppermute x11 -> x13, starting transfers between devices: 29.7 us -> 16 us  [swap(): lax.ppermute(x, axis, [(i, i ^ bit) for i in range(lax.axis_size(axis))])]
    ppermute x3 -> x0, waiting for transfers between devices: 9.54 us -> none  [the longest x1 9.53 us: chain_sum(): one = lax.ppermute(send, 'tensor', [(0, 1), (3, 2)])]
    ppermute x3 -> x0, starting transfers between devices: 5.01 us -> none  [the longest x1 1.98 us: chain_sum(): one = lax.ppermute(send, 'tensor', [(0, 1), (3, 2)])]
    pallas_call x3, Pallas kernels: 17.8 us -> 21.4 us  [attend_cached(): pl.pallas_call(functools.partial(cached_kernel, heads, cpages, LOG2E / ma...]
    ppermute x3, waiting for transfers between devices: 4.72 us -> 7.82 us  [gather_heads(): passed = lax.ppermute(far, 'tensor', [(1, 0), (2, 3)])]
    pallas_call x3, Pallas kernels: 15.2 us -> 18.1 us  [attend_new(): pl.pallas_call(functools.partial(new_kernel, heads, steps, LOG2E / math.s...]
    unnamed x22 -> x8, local copies, waits for them, and re-layouts: 2.68 us -> 0.03 us
    reduce_sum x3 -> x0, other arithmetic: 2.09 us -> none  [the longest x1 1.29 us: line_of_four(): own_length = jnp.sum(jnp.where(prompts == own_prompt, late_length, 0))]
  transfers between devices with their start and end apart: 20 -> 19, of which waited for: 6 -> 5; matrix products, arithmetic and copies ran while one was open for 5% -> 0% of each run, Pallas kernels for 30% -> 42%
where the time goes in v2:
time: 142 us
  Pallas kernels  74.8 us (53%)
  waiting for transfers between devices  44.6 us (31%)
  starting transfers between devices  21.9 us (15%)
    ppermute x13, waiting for transfers between devices, swap(): lax.ppermute(x, axis, [(i, i ^ bit) for i in range(lax.axis_size(axis))])  36.8 us
    pallas_call x5, Pallas kernels, out_project(): pl.pallas_call(functools.partial(out_kernel, rels, pick is not None, cuts...  25 us
    pallas_call x3, Pallas kernels, attend_cached(): pl.pallas_call(functools.partial(cached_kernel, heads, cpages, LOG2E / ma...  21.4 us
    pallas_call x3, Pallas kernels, attend_new(): pl.pallas_call(functools.partial(new_kernel, heads, steps, LOG2E / math.s...  18.1 us
    ppermute x13, starting transfers between devices, swap(): lax.ppermute(x, axis, [(i, i ^ bit) for i in range(lax.axis_size(axis))])  16 us
    ppermute x3, waiting for transfers between devices, gather_heads(): passed = lax.ppermute(far, 'tensor', [(1, 0), (2, 3)])  7.82 us
    pallas_call x2, Pallas kernels, project(): pl.pallas_call(functools.partial(project_kernel, len(groups), split, kept...  7.73 us
    ppermute x3, starting transfers between devices, gather_heads(): passed = lax.ppermute(far, 'tensor', [(1, 0), (2, 3)])  3.85 us
  transfers between devices with their start and end apart: 19, of which 5 were waited for; matrix products, arithmetic and copies ran while one was open for 0% of the time, Pallas kernels for 42%

profile of v2, /device:TPU:0, one launch (start us, length us, event | category | flops | bytes accessed | tf_op | source)
XLA Modules:
  0.0 141.9 jit_solution(16173216233084941704)
XLA Ops:
  0.0 3.5 %project.3 = (f32[2,256,256]{2,1,0:T(8,128)S(1)}, bf16[2,256,256]{2,1,0:T(8,128)(2,1)S(1)}) custom-call(s32[1]{0:T(128)} %bitcast.rank_ref, bf16[128,2048]{1,0:T(8,128)(2,1)} %refs_0_.3, bf16[128,4,2048]{2,1,0:T(4,128)(2,1)} %refs_1_.3, bf16[2048,512]{1,0:T(8,128)(2,1)} %refs_4_.3, bf16[2048,512]{1,0:T(8,128)(2,1)} %refs_5_.2, bf16[2048,512]{1,0:T(8,128)(2,1)} %refs_4_.3, ...), custom_call_target="tpu_custom_call" | custom-call | flops 1073741824 | bytes 4194304 | tf_op jit(solution)/shard_map/project/pallas_call | solution.py:299
  3.5 0.0 copy-start
  3.5 0.0 copy-start.1
  3.5 0.0 copy-start.2
  3.5 3.1 %collective-permute-start.2 = (bf16[2,256,256]{2,1,0:T(8,128)(2,1)S(1)}, bf16[2,256,256]{2,1,0:T(8,128)(2,1)S(1)}, u32[]{:S(2)}, u32[]{:S(2)}) collective-permute-start(bf16[2,256,256]{2,1,0:T(8,128)(2,1)S(1)} %get-tuple-element.25), channel_id=1, source_target_pairs={{0,1},{1,0},{2,3},{3,2},{4,5},{5,4},{6,7},{7,6},{8,9},{9,8},{10,11... | collective-permute-start | bytes 786440 | tf_op jit(solution)/shard_map/ppermute | solution.py:384
  6.6 4.3 %project.2 = (f32[2,384,256]{2,1,0:T(8,128)S(1)}, bf16[2,384,256]{2,1,0:T(8,128)(2,1)S(1)}) custom-call(s32[1]{0:T(128)} %bitcast.rank_ref, bf16[128,4,2048]{2,1,0:T(4,128)(2,1)} %refs_1_.3, bf16[2048,512]{1,0:T(8,128)(2,1)} %refs_4_.3, bf16[2048,512]{1,0:T(8,128)(2,1)} %refs_5_.2, bf16[2048,512]{1,0:T(8,128)(2,1)} %refs_4_.3, bf16[2048,512]{1,0:T(8,128)(2,1)} %refs_5_.2), custom_call_target="tpu_custom_call" | custom-call | flops 1610612736 | bytes 4194304 | tf_op jit(solution)/shard_map/project/pallas_call | solution.py:299
  10.9 0.0 copy-start.3
  10.9 0.1 collective-permute-start
  11.0 2.3 %collective-permute-done.2.refs_0_ = bf16[2,256,256]{2,1,0:T(8,128)(2,1)S(1)} collective-permute-done((bf16[2,256,256]{2,1,0:T(8,128)(2,1)S(1)}, bf16[2,256,256]{2,1,0:T(8,128)(2,1)S(1)}, u32[]{:S(2)}, u32[]{:S(2)}) %collective-permute-start.2) | collective-permute-done | bytes 262176 | tf_op jit(solution)/shard_map/ppermute | solution.py:384
  13.4 2.6 %collective-permute-start.3 = (bf16[256,256]{1,0:T(8,128)(2,1)S(1)}, bf16[256,256]{1,0:T(8,128)(2,1)S(1)}, u32[]{:S(2)}, u32[]{:S(2)}) collective-permute-start(bf16[256,256]{1,0:T(8,128)(2,1)S(1)} %fusion.1), channel_id=1, source_target_pairs={{0,2},{1,3},{2,0},{3,1},{4,6},{5,7},{6,4},{7,5},{8,10},{9,11},{10,... | collective-permute-start | bytes 393224 | tf_op jit(solution)/shard_map/ppermute | solution.py:384
  16.0 8.4 %collective-permute-done.refs_0_ = bf16[2,384,256]{2,1,0:T(8,128)(2,1)S(1)} collective-permute-done((bf16[2,384,256]{2,1,0:T(8,128)(2,1)S(1)}, bf16[2,384,256]{2,1,0:T(8,128)(2,1)S(1)}, u32[]{:S(2)}, u32[]{:S(2)}) %collective-permute-start) | collective-permute-done | bytes 393248 | tf_op jit(solution)/shard_map/ppermute | solution.py:384
  24.4 1.7 %collective-permute-start.1 = (bf16[384,256]{1,0:T(8,128)(2,1)S(1)}, bf16[384,256]{1,0:T(8,128)(2,1)S(1)}, u32[]{:S(2)}, u32[]{:S(2)}) collective-permute-start(bf16[384,256]{1,0:T(8,128)(2,1)S(1)} %fusion), channel_id=1, source_target_pairs={{0,2},{1,3},{2,0},{3,1},{4,6},{5,7},{6,4},{7,5},{8,10},{9,11},{10,... | collective-permute-start | bytes 589832 | tf_op jit(solution)/shard_map/ppermute | solution.py:384
  26.1 0.1 maximum_bitcast_fusion.freq_ref
  26.2 1.2 finish.3
  27.4 0.1 collective-permute-start.4
  27.5 1.6 %collective-permute-start.5 = (bf16[128,256]{1,0:T(8,128)(2,1)S(1)}, bf16[128,256]{1,0:T(8,128)(2,1)S(1)}, u32[]{:S(2)}, u32[]{:S(2)}) collective-permute-start(bf16[128,256]{1,0:T(8,128)(2,1)S(1)} %get-tuple-element.26.refs_0_), channel_id=1, source_target_pairs={{0,8},{4,12},{8,0},{12,4},{1,9},{5,13},{9,1},{13,5},{2,10},{6,14},... | collective-permute-start | bytes 196616 | tf_op jit(solution)/shard_map/ppermute | solution.py:384
  29.1 0.3 collective-permute-start.6
  29.4 9.9 %attend_cached.4 = (f32[8,256,128]{2,1,0:T(8,128)S(1)}, f32[8,256,128]{2,1,0:T(8,128)S(1)}) custom-call(s32[12]{0:T(128)S(1)} %copy-done.3, s32[4]{0:T(128)S(1)} %copy-done.2, bf16[128,4,1024]{2,1,0:T(4,128)(2,1)} %q_ref.11, s32[1,128]{1,0:T(1,128)S(1)} %bitcast.11, bf16[12,128,256]{2,1,0:T(8,128)(2,1)} %bitcast.18), custom_call_target="tpu_custom_call" | custom-call | flops 1610612736 | bytes 2097152 | tf_op jit(solution)/shard_map/attend_cached/pallas_call | solution.py:194
  39.3 0.0 collective-permute-done.1.refs_1_
  39.3 1.4 %finish.2 = (bf16[256,256]{1,0:T(8,128)(2,1)S(1)}, bf16[128,256]{1,0:T(8,128)(2,1)S(1)}) custom-call(s32[4]{0:T(128)S(1)} %copy-done, s32[4]{0:T(128)S(1)} %copy-done.2, s32[1]{0:T(128)} %bitcast.1.replica_ref.base_ref, s32[1,128]{1,0:T(1,128)S(1)} %bitcast.12, f32[1,128]{1,0:T(1,128)S(1)} %maximum_bitcast_fusion.freq_ref, ...), custom_call_target="tpu_custom_call" | custom-call | tf_op jit(solution)/shard_map/finish/pallas_call | solution.py:368
  40.7 0.0 collective-permute-done.5.refs_2_
  40.7 0.0 collective-permute-done.6.refs_3_
  40.7 8.3 %attend_new.4.refs_0_ = bf16[256,1024]{1,0:T(8,128)(2,1)S(1)} custom-call(s32[4]{0:T(128)S(1)} %copy-done, s32[1]{0:T(128)} %bitcast.1.replica_ref.base_ref, bf16[128,4,1024]{2,1,0:T(4,128)(2,1)} %q_ref.11, s32[1,128]{1,0:T(1,128)S(1)} %bitcast.13, bf16[256,256]{1,0:T(8,128)(2,1)S(1)} %get-tuple-element.27.tail_ref, ...), custom_call_target="tpu_custom_call" | custom-call | flops 671088640 | bytes 2621440 | tf_op jit(solution)/shard_map/attend_new/pallas_call | solution.py:226
  49.0 1.3 collective-permute-start.12
  50.4 5.7 %attend_cached.5 = (f32[8,128,128]{2,1,0:T(8,128)S(1)}, f32[8,128,128]{2,1,0:T(8,128)S(1)}) custom-call(s32[12]{0:T(128)S(1)} %copy-done.3, s32[4]{0:T(128)S(1)} %copy-done.2, bf16[128,4,1024]{2,1,0:T(4,128)(2,1)} %q_ref.11, s32[1,128]{1,0:T(1,128)S(1)} %bitcast.14, bf16[12,128,256]{2,1,0:T(8,128)(2,1)} %bitcast.19), custom_call_target="tpu_custom_call" | custom-call | flops 805306368 | bytes 1048576 | tf_op jit(solution)/shard_map/attend_cached/pallas_call | solution.py:194
  56.1 4.8 %attend_new.5.refs_0_ = bf16[128,1024]{1,0:T(8,128)(2,1)S(1)} custom-call(s32[4]{0:T(128)S(1)} %copy-done, s32[1]{0:T(128)} %bitcast.1.replica_ref.base_ref, bf16[128,4,1024]{2,1,0:T(4,128)(2,1)} %q_ref.11, s32[1,128]{1,0:T(1,128)S(1)} %bitcast.15, bf16[128,256]{1,0:T(8,128)(2,1)S(1)} %get-tuple-element.30.tail_ref, ...), custom_call_target="tpu_custom_call" | custom-call | flops 335544320 | bytes 1310720 | tf_op jit(solution)/shard_map/attend_new/pallas_call | solution.py:226
  60.9 1.7 %collective-permute-start.15 = (bf16[128,1024]{1,0:T(8,128)(2,1)S(1)}, bf16[128,1024]{1,0:T(8,128)(2,1)S(1)}, u32[]{:S(2)}, u32[]{:S(2)}) collective-permute-start(bf16[128,1024]{1,0:T(8,128)(2,1)S(1)} %attend_new.5.refs_0_), channel_id=1, source_target_pairs={{0,2},{1,3},{2,0},{3,1},{4,6},{5,7},{6,4},{7,5},{8,10},{9,11},{10,... | collective-permute-start | bytes 786440 | tf_op jit(solution)/shard_map/ppermute | solution.py:384
  62.6 5.7 %attend_cached.3 = (f32[8,128,128]{2,1,0:T(8,128)S(1)}, f32[8,128,128]{2,1,0:T(8,128)S(1)}) custom-call(s32[12]{0:T(128)S(1)} %copy-done.3, s32[4]{0:T(128)S(1)} %copy-done.2, bf16[128,4,1024]{2,1,0:T(4,128)(2,1)} %q_ref.11, s32[1,128]{1,0:T(1,128)S(1)} %bitcast.16, bf16[12,128,256]{2,1,0:T(8,128)(2,1)} %bitcast.20), custom_call_target="tpu_custom_call" | custom-call | flops 805306368 | bytes 1048576 | tf_op jit(solution)/shard_map/attend_cached/pallas_call | solution.py:194
  68.4 2.5 %collective-permute-start.16 = (bf16[128,1024]{1,0:T(8,128)(2,1)S(1)}, bf16[128,1024]{1,0:T(8,128)(2,1)S(1)}, u32[]{:S(2)}, u32[]{:S(2)}) collective-permute-start(bf16[128,1024]{1,0:T(8,128)(2,1)S(1)} %attend_new.5.refs_0_), channel_id=1, source_target_pairs={{0,1},{1,0},{2,3},{3,2},{4,5},{5,4},{6,7},{7,6},{8,9},{9,8},{10,11... | collective-permute-start | bytes 786440 | tf_op jit(solution)/shard_map/ppermute | solution.py:384
  70.9 5.0 %attend_new.3.refs_0_ = bf16[128,1024]{1,0:T(8,128)(2,1)S(1)} custom-call(s32[4]{0:T(128)S(1)} %copy-done, s32[1]{0:T(128)} %bitcast.1.replica_ref.base_ref, bf16[128,4,1024]{2,1,0:T(4,128)(2,1)} %q_ref.11, s32[1,128]{1,0:T(1,128)S(1)} %bitcast.17, bf16[128,256]{1,0:T(8,128)(2,1)S(1)} %get-tuple-element.21.tail_ref, ...), custom_call_target="tpu_custom_call" | custom-call | flops 335544320 | bytes 1310720 | tf_op jit(solution)/shard_map/attend_new/pallas_call | solution.py:226
  76.0 0.1 collective-permute-start.10
  76.0 0.8 collective-permute-start.8
  76.8 16.2 %collective-permute-done.15.refs_1_ = bf16[128,1024]{1,0:T(8,128)(2,1)S(1)} collective-permute-done((bf16[128,1024]{1,0:T(8,128)(2,1)S(1)}, bf16[128,1024]{1,0:T(8,128)(2,1)S(1)}, u32[]{:S(2)}, u32[]{:S(2)}) %collective-permute-start.15) | collective-permute-done | bytes 262176 | tf_op jit(solution)/shard_map/ppermute | solution.py:384
  93.0 0.7 collective-permute-start.17
  93.7 9.9 %collective-permute-done.10.refs_2_ = bf16[128,1024]{1,0:T(8,128)(2,1)S(1)} collective-permute-done((bf16[128,1024]{1,0:T(8,128)(2,1)S(1)}, bf16[128,1024]{1,0:T(8,128)(2,1)S(1)}, u32[]{:S(2)}, u32[]{:S(2)}) %collective-permute-start.10) | collective-permute-done | bytes 262176 | tf_op jit(solution)/shard_map/ppermute | solution.py:384
  103.6 1.3 collective-permute-start.18
  104.9 0.7 collective-permute-start.11
  105.6 0.0 collective-permute-done.12.refs_1_
  105.6 1.3 collective-permute-start.13
  106.9 5.0 %out_project.5.refs_2_ = f32[128,2048]{1,0:T(8,128)S(1)} custom-call(s32[1]{0:T(128)} %bitcast.rank_ref, bf16[128,1024]{1,0:T(8,128)(2,1)S(1)} %attend_new.3.refs_0_, bf16[128,1024]{1,0:T(8,128)(2,1)S(1)} %collective-permute-done.8.refs_1_, bf16[128,1024]{1,0:T(8,128)(2,1)S(1)} %collective-permute-done.10.refs_2_, bf16[4096,2048]{1,0:T(8,128)(2,1)} %refs_3_.11), custom_call_target="tpu_custom_call" | custom-call | flops 1610612736 | bytes 12582912 | tf_op jit(solution)/shard_map/out_project/pallas_call | solution.py:459
  112.0 0.7 collective-permute-start.7
  112.6 7.8 %collective-permute-done.18.refs_4_ = bf16[128,1024]{1,0:T(8,128)(2,1)S(1)} collective-permute-done((bf16[128,1024]{1,0:T(8,128)(2,1)S(1)}, bf16[128,1024]{1,0:T(8,128)(2,1)S(1)}, u32[]{:S(2)}, u32[]{:S(2)}) %collective-permute-start.18) | collective-permute-done | bytes 262176 | tf_op jit(solution)/shard_map/ppermute | solution.py:487
  120.5 1.3 collective-permute-start.9
  121.8 7.1 %out_project.7.refs_4_ = bf16[128,4,2048]{2,1,0:T(4,128)(2,1)} custom-call(s32[1]{0:T(128)} %bitcast.rank_ref, bf16[128,1024]{1,0:T(8,128)(2,1)S(1)} %attend_new.5.refs_0_, bf16[128,1024]{1,0:T(8,128)(2,1)S(1)} %collective-permute-done.15.refs_1_, bf16[128,1024]{1,0:T(8,128)(2,1)S(1)} %collective-permute-done.16.refs_2_, ...), custom_call_target="tpu_custom_call" | custom-call | flops 2147483648 | bytes 16777216 | tf_op jit(solution)/shard_map/out_project/pallas_call | solution.py:459
  128.8 5.7 %out_project.6.refs_2_ = f32[256,2048]{1,0:T(8,128)S(1)} custom-call(s32[1]{0:T(128)} %bitcast.rank_ref, bf16[256,1024]{1,0:T(8,128)(2,1)S(1)} %attend_new.4.refs_0_, bf16[256,1024]{1,0:T(8,128)(2,1)S(1)} %collective-permute-done.12.refs_1_, bf16[256,1024]{1,0:T(8,128)(2,1)S(1)} %collective-permute-done.14.refs_2_, bf16[4096,2048]{1,0:T(8,128)(2,1)} %refs_3_.11), custom_call_target="tpu_custom_call" | custom-call | flops 3221225472 | bytes 12582912 | tf_op jit(solution)/shard_map/out_project/pallas_call | solution.py:459
  134.5 0.0 collective-permute-done.11.refs_0_
  134.5 3.8 %out_project.8.refs_4_ = bf16[128,4,2048]{2,1,0:T(4,128)(2,1)} custom-call(s32[1]{0:T(128)} %bitcast.rank_ref, bf16[256,1024]{1,0:T(8,128)(2,1)S(1)} %collective-permute-done.11.refs_0_, bf16[256,1024]{1,0:T(8,128)(2,1)S(1)} %collective-permute-done.13.refs_1_, f32[256,2048]{1,0:T(8,128)S(1)} %out_project.6.refs_2_, ...), custom_call_target="tpu_custom_call", output_to_operand_aliasing={{}: (5, {})} | custom-call | flops 1073741824 | bytes 4194304 | tf_op jit(solution)/shard_map/out_project/pallas_call | solution.py:459
  138.4 3.4 %out_project.9 = bf16[128,4,2048]{2,1,0:T(4,128)(2,1)} custom-call(s32[1]{0:T(128)} %bitcast.rank_ref, bf16[128,1024]{1,0:T(8,128)(2,1)S(1)} %collective-permute-done.7.refs_0_, bf16[128,1024]{1,0:T(8,128)(2,1)S(1)} %collective-permute-done.9.refs_1_, f32[128,2048]{1,0:T(8,128)S(1)} %out_project.5.refs_2_, ...), custom_call_target="tpu_custom_call", output_to_operand_aliasing={{}: (5, {})} | custom-call | flops 536870912 | bytes 4194304 | tf_op jit(solution)/shard_map/out_project/pallas_call | solution.py:459
  (17 shorter events, 0.1 us)
Async XLA Ops:
  3.5 22.7 %copy-start = (s32[4]{0:T(128)S(1)}, s32[4]{0:T(128)}, u32[]{:S(2)}) copy-start(s32[4]{0:T(128)} %owner_ref.9) | copy-start | bytes 52
  3.5 22.7 %copy-start.1 = (s32[128]{0:T(128)S(1)}, s32[128]{0:T(128)}, u32[]{:S(2)}) copy-start(s32[128]{0:T(128)} %param.12) | copy-start | bytes 1540
  3.5 22.7 %copy-start.2 = (s32[4]{0:T(128)S(1)}, s32[4]{0:T(128)}, u32[]{:S(2)}) copy-start(s32[4]{0:T(128)} %length_ref.9) | copy-start | bytes 52
  3.5 9.8 %collective-permute-start.2 = (bf16[2,256,256]{2,1,0:T(8,128)(2,1)S(1)}, bf16[2,256,256]{2,1,0:T(8,128)(2,1)S(1)}, u32[]{:S(2)}, u32[]{:S(2)}) collective-permute-start(bf16[2,256,256]{2,1,0:T(8,128)(2,1)S(1)} %get-tuple-element.25), channel_id=1, source_target_pairs={{0,1},{1,0},{2,3},{3,2},{4,5},{5,4},{6,7},{7,6},{8,9},{9,8},{10,11... | collective-permute-start | bytes 786440 | tf_op jit(solution)/shard_map/ppermute | solution.py:384
  10.9 18.5 %copy-start.3 = (s32[12]{0:T(128)S(1)}, s32[12]{0:T(128)}, u32[]{:S(2)}) copy-start(s32[12]{0:T(128)} %table_ref.5) | copy-start | bytes 148
  10.9 13.4 %collective-permute-start = (bf16[2,384,256]{2,1,0:T(8,128)(2,1)S(1)}, bf16[2,384,256]{2,1,0:T(8,128)(2,1)S(1)}, u32[]{:S(2)}, u32[]{:S(2)}) collective-permute-start(bf16[2,384,256]{2,1,0:T(8,128)(2,1)S(1)} %get-tuple-element.20), channel_id=1, source_target_pairs={{0,1},{1,0},{2,3},{3,2},{4,5},{5,4},{6,7},{7,6},{8,9},{9,8},{10,11... | collective-permute-start | bytes 1179656 | tf_op jit(solution)/shard_map/ppermute | solution.py:384
  13.4 12.8 %collective-permute-start.3 = (bf16[256,256]{1,0:T(8,128)(2,1)S(1)}, bf16[256,256]{1,0:T(8,128)(2,1)S(1)}, u32[]{:S(2)}, u32[]{:S(2)}) collective-permute-start(bf16[256,256]{1,0:T(8,128)(2,1)S(1)} %fusion.1), channel_id=1, source_target_pairs={{0,2},{1,3},{2,0},{3,1},{4,6},{5,7},{6,4},{7,5},{8,10},{9,11},{10,... | collective-permute-start | bytes 393224 | tf_op jit(solution)/shard_map/ppermute | solution.py:384
  24.4 14.9 %collective-permute-start.1 = (bf16[384,256]{1,0:T(8,128)(2,1)S(1)}, bf16[384,256]{1,0:T(8,128)(2,1)S(1)}, u32[]{:S(2)}, u32[]{:S(2)}) collective-permute-start(bf16[384,256]{1,0:T(8,128)(2,1)S(1)} %fusion), channel_id=1, source_target_pairs={{0,2},{1,3},{2,0},{3,1},{4,6},{5,7},{6,4},{7,5},{8,10},{9,11},{10,... | collective-permute-start | bytes 589832 | tf_op jit(solution)/shard_map/ppermute | solution.py:384
  27.4 13.3 %collective-permute-start.4 = (bf16[128,256]{1,0:T(8,128)(2,1)S(1)}, bf16[128,256]{1,0:T(8,128)(2,1)S(1)}, u32[]{:S(2)}, u32[]{:S(2)}) collective-permute-start(bf16[128,256]{1,0:T(8,128)(2,1)S(1)} %get-tuple-element.26.refs_0_), channel_id=1, source_target_pairs={{0,4},{4,0},{8,12},{12,8},{1,5},{5,1},{9,13},{13,9},{2,6},{6,2},{1... | collective-permute-start | bytes 196616 | tf_op jit(solution)/shard_map/ppermute | solution.py:384
  27.5 13.2 %collective-permute-start.5 = (bf16[128,256]{1,0:T(8,128)(2,1)S(1)}, bf16[128,256]{1,0:T(8,128)(2,1)S(1)}, u32[]{:S(2)}, u32[]{:S(2)}) collective-permute-start(bf16[128,256]{1,0:T(8,128)(2,1)S(1)} %get-tuple-element.26.refs_0_), channel_id=1, source_target_pairs={{0,8},{4,12},{8,0},{12,4},{1,9},{5,13},{9,1},{13,5},{2,10},{6,14},... | collective-permute-start | bytes 196616 | tf_op jit(solution)/shard_map/ppermute | solution.py:384
  29.1 11.7 %collective-permute-start.6 = (bf16[128,256]{1,0:T(8,128)(2,1)S(1)}, bf16[128,256]{1,0:T(8,128)(2,1)S(1)}, u32[]{:S(2)}, u32[]{:S(2)}) collective-permute-start(bf16[128,256]{1,0:T(8,128)(2,1)S(1)} %get-tuple-element.26.refs_0_), channel_id=1, source_target_pairs={{0,12},{4,8},{8,4},{12,0},{1,13},{5,9},{9,5},{13,1},{2,14},{6,10},... | collective-permute-start | bytes 196616 | tf_op jit(solution)/shard_map/ppermute | solution.py:384
  49.0 56.6 %collective-permute-start.12 = (bf16[256,1024]{1,0:T(8,128)(2,1)S(1)}, bf16[256,1024]{1,0:T(8,128)(2,1)S(1)}, u32[]{:S(2)}, u32[]{:S(2)}) collective-permute-start(bf16[256,1024]{1,0:T(8,128)(2,1)S(1)} %attend_new.4.refs_0_), channel_id=1, source_target_pairs={{0,2},{1,3},{2,0},{3,1},{4,6},{5,7},{6,4},{7,5},{8,10},{9,11},{10,... | collective-permute-start | bytes 1572872 | tf_op jit(solution)/shard_map/ppermute | solution.py:384
  60.9 32.1 %collective-permute-start.15 = (bf16[128,1024]{1,0:T(8,128)(2,1)S(1)}, bf16[128,1024]{1,0:T(8,128)(2,1)S(1)}, u32[]{:S(2)}, u32[]{:S(2)}) collective-permute-start(bf16[128,1024]{1,0:T(8,128)(2,1)S(1)} %attend_new.5.refs_0_), channel_id=1, source_target_pairs={{0,2},{1,3},{2,0},{3,1},{4,6},{5,7},{6,4},{7,5},{8,10},{9,11},{10,... | collective-permute-start | bytes 786440 | tf_op jit(solution)/shard_map/ppermute | solution.py:384
  68.4 24.6 %collective-permute-start.16 = (bf16[128,1024]{1,0:T(8,128)(2,1)S(1)}, bf16[128,1024]{1,0:T(8,128)(2,1)S(1)}, u32[]{:S(2)}, u32[]{:S(2)}) collective-permute-start(bf16[128,1024]{1,0:T(8,128)(2,1)S(1)} %attend_new.5.refs_0_), channel_id=1, source_target_pairs={{0,1},{1,0},{2,3},{3,2},{4,5},{5,4},{6,7},{7,6},{8,9},{9,8},{10,11... | collective-permute-start | bytes 786440 | tf_op jit(solution)/shard_map/ppermute | solution.py:384
  76.0 27.7 %collective-permute-start.10 = (bf16[128,1024]{1,0:T(8,128)(2,1)S(1)}, bf16[128,1024]{1,0:T(8,128)(2,1)S(1)}, u32[]{:S(2)}, u32[]{:S(2)}) collective-permute-start(bf16[128,1024]{1,0:T(8,128)(2,1)S(1)} %attend_new.3.refs_0_), channel_id=1, source_target_pairs={{0,1},{1,0},{2,3},{3,2},{4,5},{5,4},{6,7},{7,6},{8,9},{9,8},{10,11... | collective-permute-start | bytes 786440 | tf_op jit(solution)/shard_map/ppermute | solution.py:384
  76.0 28.9 %collective-permute-start.8 = (bf16[128,1024]{1,0:T(8,128)(2,1)S(1)}, bf16[128,1024]{1,0:T(8,128)(2,1)S(1)}, u32[]{:S(2)}, u32[]{:S(2)}) collective-permute-start(bf16[128,1024]{1,0:T(8,128)(2,1)S(1)} %attend_new.3.refs_0_), channel_id=1, source_target_pairs={{0,2},{1,3},{2,0},{3,1},{4,6},{5,7},{6,4},{7,5},{8,10},{9,11},{10,... | collective-permute-start | bytes 786440 | tf_op jit(solution)/shard_map/ppermute | solution.py:384
  93.0 35.8 %collective-permute-start.14 = (bf16[256,1024]{1,0:T(8,128)(2,1)S(1)}, bf16[256,1024]{1,0:T(8,128)(2,1)S(1)}, u32[]{:S(2)}, u32[]{:S(2)}) collective-permute-start(bf16[256,1024]{1,0:T(8,128)(2,1)S(1)} %attend_new.4.refs_0_), channel_id=1, source_target_pairs={{0,1},{1,0},{2,3},{3,2},{4,5},{5,4},{6,7},{7,6},{8,9},{9,8},{10,11... | collective-permute-start | bytes 1572872 | tf_op jit(solution)/shard_map/ppermute | solution.py:384
  93.0 18.9 %collective-permute-start.17 = (bf16[128,1024]{1,0:T(8,128)(2,1)S(1)}, bf16[128,1024]{1,0:T(8,128)(2,1)S(1)}, u32[]{:S(2)}, u32[]{:S(2)}) collective-permute-start(bf16[128,1024]{1,0:T(8,128)(2,1)S(1)} %attend_new.5.refs_0_), channel_id=1, source_target_pairs={{1,2},{2,1},{5,6},{6,5},{9,10},{10,9},{13,14},{14,13},{17,18},{18,... | collective-permute-start | bytes 786440 | tf_op jit(solution)/shard_map/ppermute | solution.py:486
  103.6 16.9 %collective-permute-start.18 = (bf16[128,1024]{1,0:T(8,128)(2,1)S(1)}, bf16[128,1024]{1,0:T(8,128)(2,1)S(1)}, u32[]{:S(2)}, u32[]{:S(2)}) collective-permute-start(bf16[128,1024]{1,0:T(8,128)(2,1)S(1)} %collective-permute-done.15.refs_1_), channel_id=1, source_target_pairs={{1,0},{2,3},{5,4},{6,7},{9,8},{10,11},{13,12},{14,15},{17,16},{18,... | collective-permute-start | bytes 786440 | tf_op jit(solution)/shard_map/ppermute | solution.py:487
  104.9 29.6 %collective-permute-start.11 = (bf16[256,1024]{1,0:T(8,128)(2,1)S(1)}, bf16[256,1024]{1,0:T(8,128)(2,1)S(1)}, u32[]{:S(2)}, u32[]{:S(2)}) collective-permute-start(bf16[256,1024]{1,0:T(8,128)(2,1)S(1)} %attend_new.4.refs_0_), channel_id=1, source_target_pairs={{1,2},{2,1},{5,6},{6,5},{9,10},{10,9},{13,14},{14,13},{17,18},{18,... | collective-permute-start | bytes 1572872 | tf_op jit(solution)/shard_map/ppermute | solution.py:486
  105.6 28.9 %collective-permute-start.13 = (bf16[256,1024]{1,0:T(8,128)(2,1)S(1)}, bf16[256,1024]{1,0:T(8,128)(2,1)S(1)}, u32[]{:S(2)}, u32[]{:S(2)}) collective-permute-start(bf16[256,1024]{1,0:T(8,128)(2,1)S(1)} %collective-permute-done.12.refs_1_), channel_id=1, source_target_pairs={{1,0},{2,3},{5,4},{6,7},{9,8},{10,11},{13,12},{14,15},{17,16},{18,... | collective-permute-start | bytes 1572872 | tf_op jit(solution)/shard_map/ppermute | solution.py:487
  112.0 26.4 %collective-permute-start.7 = (bf16[128,1024]{1,0:T(8,128)(2,1)S(1)}, bf16[128,1024]{1,0:T(8,128)(2,1)S(1)}, u32[]{:S(2)}, u32[]{:S(2)}) collective-permute-start(bf16[128,1024]{1,0:T(8,128)(2,1)S(1)} %attend_new.3.refs_0_), channel_id=1, source_target_pairs={{1,2},{2,1},{5,6},{6,5},{9,10},{10,9},{13,14},{14,13},{17,18},{18,... | collective-permute-start | bytes 786440 | tf_op jit(solution)/shard_map/ppermute | solution.py:486
  120.5 17.9 %collective-permute-start.9 = (bf16[128,1024]{1,0:T(8,128)(2,1)S(1)}, bf16[128,1024]{1,0:T(8,128)(2,1)S(1)}, u32[]{:S(2)}, u32[]{:S(2)}) collective-permute-start(bf16[128,1024]{1,0:T(8,128)(2,1)S(1)} %collective-permute-done.8.refs_1_), channel_id=1, source_target_pairs={{1,0},{2,3},{5,4},{6,7},{9,8},{10,11},{13,12},{14,15},{17,16},{18,... | collective-permute-start | bytes 786440 | tf_op jit(solution)/shard_map/ppermute | solution.py:487

commit v3 on v2

--- a/solution.py
+++ b/solution.py
@@ -212,7 +212,7 @@
         ),
         compiler_params=SMALL,
         name="attend_cached",
-    )(page_table, prompt_length, in_hbm(q), fork_row, in_hbm(pool))
+    )(page_table, prompt_length, q, fork_row, pool)
 
 
 def attend_new(q, fork_row, owner, base, span_pairs, tail_pairs, mixed, stat, start, count):
@@ -247,7 +247,7 @@
         ),
         compiler_params=SMALL,
         name="attend_new",
-    )(owner, base, in_hbm(q), fork_row, tail_pairs, mixed, stat, *span_pairs)
+    )(owner, base, q, fork_row, tail_pairs, mixed, stat, *span_pairs)
 
 
 def project_kernel(groups, split, kept, sent, rank_ref, *refs):
@@ -391,17 +391,18 @@
     return finish(keep, (got, last), places, start, sizes)
 
 
-def out_kernel(rels, pick, cuts, add, final, rank_ref, *refs):
+def out_kernel(rels, pick, cuts, add, held, rank_ref, *refs):
     refs = list(refs)
     pieces = [refs.pop(0) for _ in rels]
     other = refs.pop(0) if pick else None
     partial = refs.pop(0) if add else None
-    w_ref, o_ref, buf, sem = refs[0], refs[-3], refs[-2], refs[-1]
+    w_ref = refs[0]
+    o_ref, buf, sem = (refs[-1], None, None) if held else refs[-3:]
     width = pieces[0].shape[1]
     depth = width // cuts
     rank = rank_ref[0]
     copies = []
-    for p, rel in enumerate(rels):
+    for p, rel in enumerate(rels if buf is not None else ()):
         for c in range(cuts):
             row = pl.multiple_of((rank ^ rel) * width + c * depth, depth)
             slot = p * cuts + c
@@ -417,15 +418,19 @@
             a = jnp.where(inner, a, other[...])
         for c in range(cuts):
             slot = p * cuts + c
-            copies[slot].wait()
+            if held:
+                w = w_ref[c * depth : (c + 1) * depth, :]
+            else:
+                copies[slot].wait()
+                w = buf[slot]
             one = jnp.dot(
-                a[:, c * depth : (c + 1) * depth], buf[slot], preferred_element_type=jnp.float32
+                a[:, c * depth : (c + 1) * depth], w, preferred_element_type=jnp.float32
             )
             total = one if total is None else total + one
     o_ref[...] = total.reshape(o_ref.shape).astype(o_ref.dtype)
 
 
-def out_project(rank, pieces, rels, weight, shape, start, pick=None, partial=None, into=None, final=True):
+def out_project(rank, pieces, rels, weight, shape, start, pick=None, partial=None, into=None, final=True, held=False):
     m, width = pieces[0].shape
     columns = weight.shape[1]
     steps = shape[1]
@@ -439,8 +444,8 @@
     if partial is not None:
         args.append(partial)
         in_specs.append(flat(columns))
-    args.append(in_hbm(weight))
-    in_specs.append(pl.BlockSpec(memory_space=pl.ANY))
+    args.append(weight if held else in_hbm(weight))
+    in_specs.append(pl.BlockSpec(memory_space=pltpu.VMEM if held else pl.ANY))
     aliases = {}
     if into is not None:
         args.append(into)
@@ -457,13 +462,15 @@
         out_shape = jax.ShapeDtypeStruct((m, columns), jnp.float32)
     slots = len(rels) * cuts
     return pl.pallas_call(
-        functools.partial(out_kernel, rels, pick is not None, cuts, partial is not None, final),
+        functools.partial(out_kernel, rels, pick is not None, cuts, partial is not None, held),
         grid_spec=pltpu.PrefetchScalarGridSpec(
             num_scalar_prefetch=1,
             grid=(1,),
             in_specs=in_specs,
             out_specs=out_spec,
-            scratch_shapes=[
+            scratch_shapes=[]
+            if held
+            else [
                 pltpu.VMEM((slots, width // cuts, columns), jnp.bfloat16),
                 pltpu.SemaphoreType.DMA((slots,)),
             ],
@@ -478,6 +485,32 @@
         compiler_params=LARGE,
         name="out_project",
     )(rank, *args)
+
+
+def hold_kernel(rel, rank_ref, w_ref, o_ref, sem):
+    rows = o_ref.shape[0]
+    at = pl.multiple_of((rank_ref[0] ^ rel) * rows, rows)
+    copy = pltpu.make_async_copy(w_ref.at[pl.ds(at, rows), :], o_ref, sem)
+    copy.start()
+    copy.wait()
+
+
+def hold(rank, rel, weight, rows):
+    shape = (rows, weight.shape[1])
+    held = pl.pallas_call(
+        functools.partial(hold_kernel, rel),
+        grid_spec=pltpu.PrefetchScalarGridSpec(
+            num_scalar_prefetch=1,
+            grid=(1,),
+            in_specs=[pl.BlockSpec(memory_space=pl.ANY)],
+            out_specs=pl.BlockSpec(memory_space=pltpu.VMEM),
+            scratch_shapes=[pltpu.SemaphoreType.DMA],
+        ),
+        out_shape=jax.ShapeDtypeStruct(shape, weight.dtype),
+        compiler_params=SMALL,
+        name="hold",
+    )(rank, in_hbm(weight))
+    return pltpu.with_memory_space_constraint(held, pltpu.VMEM)
 
 
 def gather_heads(own):
@@ -618,14 +651,17 @@
     partial = out_project(
         rank, [middle_own, far, near], (0, 2, 1), out_weight, shape, 0, final=False
     )
+    last_rows = hold(rank, 3, out_weight, middle_own.shape[1])
     decoded = out_project(
-        rank, [across], (3,), out_weight, shape, first, pick=passed, partial=partial, into=decoded
+        rank, [across], (3,), last_rows, shape, first,
+        pick=passed, partial=partial, into=decoded, held=True,
     )
     far, near, across, passed = gather_heads(last_own)
-    partial = out_project(rank, [last_own, far, near], (0, 2, 1), out_weight, shape, 0, final=False)
+    partial = out_project(rank, [last_own, far], (0, 2), out_weight, shape, 0, final=False)
+    partial = out_project(rank, [near], (1,), out_weight, shape, 0, partial=partial, final=False)
     return out_project(
-        rank, [across], (3,), out_weight, shape, first * (blocks - 1),
-        pick=passed, partial=partial, into=decoded,
+        rank, [across], (3,), last_rows, shape, first * (blocks - 1),
+        pick=passed, partial=partial, into=decoded, held=True,
     )
 
 

time: 142 us -> 133 us (0.937); the launches traced: 142 us -> 131 us
  waiting for transfers between devices: 44.6 us -> 37.5 us
  Pallas kernels: 74.8 us -> 69.4 us
    ppermute x3, waiting for transfers between devices: 7.82 us -> 0.4 us  [gather_heads(): passed = lax.ppermute(far, 'tensor', [(1, 0), (2, 3)])]
    pallas_call x3, Pallas kernels: 21.4 us -> 18 us  [attend_cached(): pl.pallas_call(functools.partial(cached_kernel, heads, cpages, LOG2E / ma...]
    pallas_call x3, Pallas kernels: 18.1 us -> 15.2 us  [attend_new(): pl.pallas_call(functools.partial(new_kernel, heads, steps, LOG2E / math.s...]
    pallas_call x0 -> x1, Pallas kernels: none -> 2.2 us  [hold(): pl.pallas_call(functools.partial(hold_kernel, rel), grid_spec=pltpu.Prefe...]
    pallas_call x5 -> x6, Pallas kernels: 25 us -> 23 us  [out_project(): pl.pallas_call(functools.partial(out_kernel, rels, pick is not None, cuts...]
  transfers between devices with their start and end apart: 19 -> 19, of which waited for: 5 -> 5; matrix products, arithmetic and copies ran while one was open for 0% -> 0% of each run, Pallas kernels for 42% -> 48%
where the time goes in v3:
time: 133 us; the launch traced here: 131 us
  Pallas kernels  69.4 us (52%)
  waiting for transfers between devices  37.5 us (28%)
  starting transfers between devices  22.9 us (17%)
    ppermute x13, waiting for transfers between devices, swap(): lax.ppermute(x, axis, [(i, i ^ bit) for i in range(lax.axis_size(axis))])  37.1 us
    pallas_call x6, Pallas kernels, out_project(): pl.pallas_call(functools.partial(out_kernel, rels, pick is not None, cuts...  23 us
    pallas_call x3, Pallas kernels, attend_cached(): pl.pallas_call(functools.partial(cached_kernel, heads, cpages, LOG2E / ma...  18 us
    ppermute x13, starting transfers between devices, swap(): lax.ppermute(x, axis, [(i, i ^ bit) for i in range(lax.axis_size(axis))])  16.7 us
    pallas_call x3, Pallas kernels, attend_new(): pl.pallas_call(functools.partial(new_kernel, heads, steps, LOG2E / math.s...  15.2 us
    pallas_call x2, Pallas kernels, project(): pl.pallas_call(functools.partial(project_kernel, len(groups), split, kept...  8.39 us
    ppermute x3, starting transfers between devices, gather_heads(): passed = lax.ppermute(far, 'tensor', [(1, 0), (2, 3)])  4.11 us
  transfers between devices with their start and end apart: 19, of which 5 were waited for; matrix products, arithmetic and copies ran while one was open for 0% of the time, Pallas kernels for 48%

profile of v3, /device:TPU:0, one launch (start us, length us, event | category | flops | bytes accessed | tf_op | source)
XLA Modules:
  0.0 131.4 jit_solution(14513463660064104997)
XLA Ops:
  0.0 4.1 %project.3 = (f32[2,256,256]{2,1,0:T(8,128)S(1)}, bf16[2,256,256]{2,1,0:T(8,128)(2,1)}) custom-call(s32[1]{0:T(128)} %bitcast.rank_ref, bf16[128,2048]{1,0:T(8,128)(2,1)} %refs_0_.3, bf16[128,4,2048]{2,1,0:T(4,128)(2,1)} %refs_1_.3, bf16[2048,512]{1,0:T(8,128)(2,1)} %refs_4_.3, bf16[2048,512]{1,0:T(8,128)(2,1)} %refs_5_.2, bf16[2048,512]{1,0:T(8,128)(2,1)} %refs_4_.3, ...), custom_call_target="tpu_custom_call" | custom-call | flops 1073741824 | bytes 4194304 | tf_op jit(solution)/shard_map/project/pallas_call | solution.py:299
  4.1 0.0 copy-start.3
  4.2 0.0 copy-start.6
  4.2 3.1 %collective-permute-start.2 = (bf16[2,256,256]{2,1,0:T(8,128)(2,1)}, bf16[2,256,256]{2,1,0:T(8,128)(2,1)S(1)}, u32[]{:S(2)}, u32[]{:S(2)}) collective-permute-start(bf16[2,256,256]{2,1,0:T(8,128)(2,1)} %get-tuple-element.25), channel_id=1, source_target_pairs={{0,1},{1,0},{2,3},{3,2},{4,5},{5,4},{6,7},{7,6},{8,9},{9,8},{10,11... | collective-permute-start | bytes 786440 | tf_op jit(solution)/shard_map/ppermute | solution.py:384
  7.3 4.3 %project.2 = (f32[2,384,256]{2,1,0:T(8,128)S(1)}, bf16[2,384,256]{2,1,0:T(8,128)(2,1)S(1)}) custom-call(s32[1]{0:T(128)} %bitcast.rank_ref, bf16[128,4,2048]{2,1,0:T(4,128)(2,1)} %refs_1_.3, bf16[2048,512]{1,0:T(8,128)(2,1)} %refs_4_.3, bf16[2048,512]{1,0:T(8,128)(2,1)} %refs_5_.2, bf16[2048,512]{1,0:T(8,128)(2,1)} %refs_4_.3, bf16[2048,512]{1,0:T(8,128)(2,1)} %refs_5_.2), custom_call_target="tpu_custom_call" | custom-call | flops 1610612736 | bytes 4194304 | tf_op jit(solution)/shard_map/project/pallas_call | solution.py:299
  11.6 0.2 collective-permute-start
  11.8 0.0 copy-start.4
  11.8 1.1 copy-done.4
  12.9 8.9 %attend_cached.4 = (f32[8,256,128]{2,1,0:T(8,128)S(1)}, f32[8,256,128]{2,1,0:T(8,128)S(1)}) custom-call(s32[12]{0:T(128)S(1)} %copy-done.6, s32[4]{0:T(128)S(1)} %copy-done.3, bf16[128,4,1024]{2,1,0:T(4,128)(2,1)S(1)} %copy-done, s32[1,128]{1,0:T(1,128)S(1)} %bitcast.10, bf16[12,128,256]{2,1,0:T(8,128)(2,1)S(1)} %bitcast.18), custom_call_target="tpu_custom_call" | custom-call | flops 1610612736 | bytes 2097152 | tf_op jit(solution)/shard_map/attend_cached/pallas_call | solution.py:194
  21.8 0.0 copy-start.5
  21.8 0.0 collective-permute-done.2.refs_0_
  21.8 3.0 %collective-permute-start.3 = (bf16[256,256]{1,0:T(8,128)(2,1)S(1)}, bf16[256,256]{1,0:T(8,128)(2,1)S(1)}, u32[]{:S(2)}, u32[]{:S(2)}) collective-permute-start(bf16[256,256]{1,0:T(8,128)(2,1)S(1)} %fusion.1), channel_id=1, source_target_pairs={{0,2},{1,3},{2,0},{3,1},{4,6},{5,7},{6,4},{7,5},{8,10},{9,11},{10,... | collective-permute-start | bytes 393224 | tf_op jit(solution)/shard_map/ppermute | solution.py:384
  24.9 0.2 collective-permute-start.1
  25.1 0.1 maximum_bitcast_fusion.freq_ref
  25.2 10.8 %collective-permute-done.3.refs_1_ = bf16[256,256]{1,0:T(8,128)(2,1)S(1)} collective-permute-done((bf16[256,256]{1,0:T(8,128)(2,1)S(1)}, bf16[256,256]{1,0:T(8,128)(2,1)S(1)}, u32[]{:S(2)}, u32[]{:S(2)}) %collective-permute-start.3) | collective-permute-done | bytes 131104 | tf_op jit(solution)/shard_map/ppermute | solution.py:384
  36.0 1.2 finish.3
  37.2 0.1 collective-permute-start.4
  37.2 1.6 %collective-permute-start.5 = (bf16[128,256]{1,0:T(8,128)(2,1)S(1)}, bf16[128,256]{1,0:T(8,128)(2,1)S(1)}, u32[]{:S(2)}, u32[]{:S(2)}) collective-permute-start(bf16[128,256]{1,0:T(8,128)(2,1)S(1)} %get-tuple-element.26.refs_0_), channel_id=1, source_target_pairs={{0,8},{4,12},{8,0},{12,4},{1,9},{5,13},{9,1},{13,5},{2,10},{6,14},... | collective-permute-start | bytes 196616 | tf_op jit(solution)/shard_map/ppermute | solution.py:384
  38.8 0.3 collective-permute-start.6
  39.1 4.5 %attend_cached.5 = (f32[8,128,128]{2,1,0:T(8,128)S(1)}, f32[8,128,128]{2,1,0:T(8,128)S(1)}) custom-call(s32[12]{0:T(128)S(1)} %copy-done.6, s32[4]{0:T(128)S(1)} %copy-done.3, bf16[128,4,1024]{2,1,0:T(4,128)(2,1)S(1)} %copy-done, s32[1,128]{1,0:T(1,128)S(1)} %bitcast.12, bf16[12,128,256]{2,1,0:T(8,128)(2,1)S(1)} %bitcast.19), custom_call_target="tpu_custom_call" | custom-call | flops 805306368 | bytes 1048576 | tf_op jit(solution)/shard_map/attend_cached/pallas_call | solution.py:194
  43.7 3.8 %attend_new.5.refs_0_ = bf16[128,1024]{1,0:T(8,128)(2,1)S(1)} custom-call(s32[4]{0:T(128)S(1)} %copy-done.1, s32[1]{0:T(128)} %bitcast.1.replica_ref.base_ref, bf16[128,4,1024]{2,1,0:T(4,128)(2,1)S(1)} %copy-done, s32[1,128]{1,0:T(1,128)S(1)} %bitcast.13, bf16[128,256]{1,0:T(8,128)(2,1)S(1)} %get-tuple-element.30.tail_ref, ...), custom_call_target="tpu_custom_call" | custom-call | flops 335544320 | bytes 1310720 | tf_op jit(solution)/shard_map/attend_new/pallas_call | solution.py:226
  47.5 0.1 collective-permute-start.15
  47.6 1.4 %finish.2 = (bf16[256,256]{1,0:T(8,128)(2,1)S(1)}, bf16[128,256]{1,0:T(8,128)(2,1)S(1)}) custom-call(s32[4]{0:T(128)S(1)} %copy-done.1, s32[4]{0:T(128)S(1)} %copy-done.3, s32[1]{0:T(128)} %bitcast.1.replica_ref.base_ref, s32[1,128]{1,0:T(1,128)S(1)} %bitcast.14, f32[1,128]{1,0:T(1,128)S(1)} %maximum_bitcast_fusion.freq_ref, ...), custom_call_target="tpu_custom_call" | custom-call | tf_op jit(solution)/shard_map/finish/pallas_call | solution.py:368
  49.0 7.5 %attend_new.4.refs_0_ = bf16[256,1024]{1,0:T(8,128)(2,1)S(1)} custom-call(s32[4]{0:T(128)S(1)} %copy-done.1, s32[1]{0:T(128)} %bitcast.1.replica_ref.base_ref, bf16[128,4,1024]{2,1,0:T(4,128)(2,1)S(1)} %copy-done, s32[1,128]{1,0:T(1,128)S(1)} %bitcast.15, bf16[256,256]{1,0:T(8,128)(2,1)S(1)} %get-tuple-element.27.tail_ref, ...), custom_call_target="tpu_custom_call" | custom-call | flops 671088640 | bytes 2621440 | tf_op jit(solution)/shard_map/attend_new/pallas_call | solution.py:226
  56.6 3.0 %collective-permute-start.12 = (bf16[256,1024]{1,0:T(8,128)(2,1)S(1)}, bf16[256,1024]{1,0:T(8,128)(2,1)S(1)}, u32[]{:S(2)}, u32[]{:S(2)}) collective-permute-start(bf16[256,1024]{1,0:T(8,128)(2,1)S(1)} %attend_new.4.refs_0_), channel_id=1, source_target_pairs={{0,2},{1,3},{2,0},{3,1},{4,6},{5,7},{6,4},{7,5},{8,10},{9,11},{10,... | collective-permute-start | bytes 1572872 | tf_op jit(solution)/shard_map/ppermute | solution.py:384
  59.5 4.5 %attend_cached.3 = (f32[8,128,128]{2,1,0:T(8,128)S(1)}, f32[8,128,128]{2,1,0:T(8,128)S(1)}) custom-call(s32[12]{0:T(128)S(1)} %copy-done.6, s32[4]{0:T(128)S(1)} %copy-done.3, bf16[128,4,1024]{2,1,0:T(4,128)(2,1)S(1)} %copy-done, s32[1,128]{1,0:T(1,128)S(1)} %bitcast.16, bf16[12,128,256]{2,1,0:T(8,128)(2,1)S(1)} %bitcast.20), custom_call_target="tpu_custom_call" | custom-call | flops 805306368 | bytes 1048576 | tf_op jit(solution)/shard_map/attend_cached/pallas_call | solution.py:194
  64.1 0.3 collective-permute-start.16
  64.4 3.8 %attend_new.3.refs_0_ = bf16[128,1024]{1,0:T(8,128)(2,1)S(1)} custom-call(s32[4]{0:T(128)S(1)} %copy-done.1, s32[1]{0:T(128)} %bitcast.1.replica_ref.base_ref, bf16[128,4,1024]{2,1,0:T(4,128)(2,1)S(1)} %copy-done, s32[1,128]{1,0:T(1,128)S(1)} %bitcast.17, bf16[128,256]{1,0:T(8,128)(2,1)S(1)} %get-tuple-element.21.tail_ref, ...), custom_call_target="tpu_custom_call" | custom-call | flops 335544320 | bytes 1310720 | tf_op jit(solution)/shard_map/attend_new/pallas_call | solution.py:226
  68.2 3.0 %collective-permute-start.8 = (bf16[128,1024]{1,0:T(8,128)(2,1)S(1)}, bf16[128,1024]{1,0:T(8,128)(2,1)S(1)}, u32[]{:S(2)}, u32[]{:S(2)}) collective-permute-start(bf16[128,1024]{1,0:T(8,128)(2,1)S(1)} %attend_new.3.refs_0_), channel_id=1, source_target_pairs={{0,2},{1,3},{2,0},{3,1},{4,6},{5,7},{6,4},{7,5},{8,10},{9,11},{10,... | collective-permute-start | bytes 786440 | tf_op jit(solution)/shard_map/ppermute | solution.py:384
  71.2 0.0 collective-permute-start.14
  71.2 2.0 %collective-permute-start.10 = (bf16[128,1024]{1,0:T(8,128)(2,1)S(1)}, bf16[128,1024]{1,0:T(8,128)(2,1)S(1)}, u32[]{:S(2)}, u32[]{:S(2)}) collective-permute-start(bf16[128,1024]{1,0:T(8,128)(2,1)S(1)} %attend_new.3.refs_0_), channel_id=1, source_target_pairs={{0,1},{1,0},{2,3},{3,2},{4,5},{5,4},{6,7},{7,6},{8,9},{9,8},{10,11... | collective-permute-start | bytes 786440 | tf_op jit(solution)/shard_map/ppermute | solution.py:384
  73.2 4.3 %collective-permute-done.16.refs_2_ = bf16[128,1024]{1,0:T(8,128)(2,1)S(1)} collective-permute-done((bf16[128,1024]{1,0:T(8,128)(2,1)S(1)}, bf16[128,1024]{1,0:T(8,128)(2,1)S(1)}, u32[]{:S(2)}, u32[]{:S(2)}) %collective-permute-start.16) | collective-permute-done | bytes 262176 | tf_op jit(solution)/shard_map/ppermute | solution.py:384
  77.5 0.7 collective-permute-start.17
  78.2 18.3 %collective-permute-done.8.refs_1_ = bf16[128,1024]{1,0:T(8,128)(2,1)S(1)} collective-permute-done((bf16[128,1024]{1,0:T(8,128)(2,1)S(1)}, bf16[128,1024]{1,0:T(8,128)(2,1)S(1)}, u32[]{:S(2)}, u32[]{:S(2)}) %collective-permute-start.8) | collective-permute-done | bytes 262176 | tf_op jit(solution)/shard_map/ppermute | solution.py:384
  96.4 1.3 collective-permute-start.18
  97.7 2.2 %hold.1.refs_3_ = bf16[1024,2048]{1,0:T(8,128)(2,1)S(1)} custom-call(s32[1]{0:T(128)} %bitcast.rank_ref, bf16[4096,2048]{1,0:T(8,128)(2,1)} %refs_5_.3), custom_call_target="tpu_custom_call" | custom-call | tf_op jit(solution)/shard_map/hold/pallas_call | solution.py:500
  99.9 3.8 %out_project.6.refs_1_ = f32[128,2048]{1,0:T(8,128)S(1)} custom-call(s32[1]{0:T(128)} %bitcast.rank_ref, bf16[128,1024]{1,0:T(8,128)(2,1)S(1)} %attend_new.3.refs_0_, bf16[128,1024]{1,0:T(8,128)(2,1)S(1)} %collective-permute-done.8.refs_1_, bf16[4096,2048]{1,0:T(8,128)(2,1)} %refs_5_.3), custom_call_target="tpu_custom_call" | custom-call | flops 1073741824 | bytes 8388608 | tf_op jit(solution)/shard_map/out_project/pallas_call | solution.py:464
  103.7 3.7 %collective-permute-done.10.refs_0_ = bf16[128,1024]{1,0:T(8,128)(2,1)S(1)} collective-permute-done((bf16[128,1024]{1,0:T(8,128)(2,1)S(1)}, bf16[128,1024]{1,0:T(8,128)(2,1)S(1)}, u32[]{:S(2)}, u32[]{:S(2)}) %collective-permute-start.10) | collective-permute-done | bytes 262176 | tf_op jit(solution)/shard_map/ppermute | solution.py:384
  107.4 0.7 collective-permute-start.11
  108.1 1.3 collective-permute-start.13
  109.4 2.5 %out_project.7.refs_2_ = f32[128,2048]{1,0:T(8,128)S(1)} custom-call(s32[1]{0:T(128)} %bitcast.rank_ref, bf16[128,1024]{1,0:T(8,128)(2,1)S(1)} %collective-permute-done.10.refs_0_, f32[128,2048]{1,0:T(8,128)S(1)} %out_project.6.refs_1_, bf16[4096,2048]{1,0:T(8,128)(2,1)} %refs_5_.3), custom_call_target="tpu_custom_call" | custom-call | flops 536870912 | bytes 4194304 | tf_op jit(solution)/shard_map/out_project/pallas_call | solution.py:464
  112.0 0.7 collective-permute-start.7
  112.7 0.4 collective-permute-done.18.refs_4_
  113.1 1.5 %collective-permute-start.9 = (bf16[128,1024]{1,0:T(8,128)(2,1)S(1)}, bf16[128,1024]{1,0:T(8,128)(2,1)S(1)}, u32[]{:S(2)}, u32[]{:S(2)}) collective-permute-start(bf16[128,1024]{1,0:T(8,128)(2,1)S(1)} %collective-permute-done.8.refs_1_), channel_id=1, source_target_pairs={{1,0},{2,3},{5,4},{6,7},{9,8},{10,11},{13,12},{14,15},{17,16},{18,... | collective-permute-start | bytes 786440 | tf_op jit(solution)/shard_map/ppermute | solution.py:520
  114.6 7.1 %out_project.9.refs_4_ = bf16[128,4,2048]{2,1,0:T(4,128)(2,1)} custom-call(s32[1]{0:T(128)} %bitcast.rank_ref, bf16[128,1024]{1,0:T(8,128)(2,1)S(1)} %attend_new.5.refs_0_, bf16[128,1024]{1,0:T(8,128)(2,1)S(1)} %collective-permute-done.15.refs_1_, bf16[128,1024]{1,0:T(8,128)(2,1)S(1)} %collective-permute-done.16.refs_2_, ...), custom_call_target="tpu_custom_call" | custom-call | flops 2147483648 | bytes 16777216 | tf_op jit(solution)/shard_map/out_project/pallas_call | solution.py:464
  121.7 5.7 %out_project.8.refs_2_ = f32[256,2048]{1,0:T(8,128)S(1)} custom-call(s32[1]{0:T(128)} %bitcast.rank_ref, bf16[256,1024]{1,0:T(8,128)(2,1)S(1)} %attend_new.4.refs_0_, bf16[256,1024]{1,0:T(8,128)(2,1)S(1)} %collective-permute-done.12.refs_1_, bf16[256,1024]{1,0:T(8,128)(2,1)S(1)} %collective-permute-done.14.refs_2_, bf16[4096,2048]{1,0:T(8,128)(2,1)} %refs_5_.3), custom_call_target="tpu_custom_call" | custom-call | flops 3221225472 | bytes 12582912 | tf_op jit(solution)/shard_map/out_project/pallas_call | solution.py:464
  127.4 2.4 %out_project.10.refs_4_ = bf16[128,4,2048]{2,1,0:T(4,128)(2,1)} custom-call(s32[1]{0:T(128)} %bitcast.rank_ref, bf16[256,1024]{1,0:T(8,128)(2,1)S(1)} %collective-permute-done.11.refs_0_, bf16[256,1024]{1,0:T(8,128)(2,1)S(1)} %collective-permute-done.13.refs_1_, f32[256,2048]{1,0:T(8,128)S(1)} %out_project.8.refs_2_, ...), custom_call_target="tpu_custom_call", output_to_operand_aliasing={{}: (5, {})} | custom-call | flops 1073741824 | bytes 4194304 | tf_op jit(solution)/shard_map/out_project/pallas_call | solution.py:464
  129.8 1.6 %out_project.11 = bf16[128,4,2048]{2,1,0:T(4,128)(2,1)} custom-call(s32[1]{0:T(128)} %bitcast.rank_ref, bf16[128,1024]{1,0:T(8,128)(2,1)S(1)} %collective-permute-done.7.refs_0_, bf16[128,1024]{1,0:T(8,128)(2,1)S(1)} %collective-permute-done.9.refs_1_, f32[128,2048]{1,0:T(8,128)S(1)} %out_project.7.refs_2_, ...), custom_call_target="tpu_custom_call", output_to_operand_aliasing={{}: (5, {})} | custom-call | flops 536870912 | bytes 4194304 | tf_op jit(solution)/shard_map/out_project/pallas_call | solution.py:464
  (25 shorter events, 0.1 us)
Async XLA Ops:
  4.1 7.6 %copy-start = (bf16[128,4,1024]{2,1,0:T(4,128)(2,1)S(1)}, bf16[128,4,1024]{2,1,0:T(4,128)(2,1)}, u32[]{:S(2)}) copy-start(bf16[128,4,1024]{2,1,0:T(4,128)(2,1)} %q_ref.11) | copy-start | bytes 3145732
  4.1 7.6 %copy-start.2 = (s32[128]{0:T(128)S(1)}, s32[128]{0:T(128)}, u32[]{:S(2)}) copy-start(s32[128]{0:T(128)} %param.12) | copy-start | bytes 1540
  4.1 7.6 %copy-start.3 = (s32[4]{0:T(128)S(1)}, s32[4]{0:T(128)}, u32[]{:S(2)}) copy-start(s32[4]{0:T(128)} %length_ref.9) | copy-start | bytes 52
  4.2 7.6 %copy-start.6 = (s32[12]{0:T(128)S(1)}, s32[12]{0:T(128)}, u32[]{:S(2)}) copy-start(s32[12]{0:T(128)} %table_ref.5) | copy-start | bytes 148
  4.2 17.6 %collective-permute-start.2 = (bf16[2,256,256]{2,1,0:T(8,128)(2,1)}, bf16[2,256,256]{2,1,0:T(8,128)(2,1)S(1)}, u32[]{:S(2)}, u32[]{:S(2)}) collective-permute-start(bf16[2,256,256]{2,1,0:T(8,128)(2,1)} %get-tuple-element.25), channel_id=1, source_target_pairs={{0,1},{1,0},{2,3},{3,2},{4,5},{5,4},{6,7},{7,6},{8,9},{9,8},{10,11... | collective-permute-start | bytes 786440 | tf_op jit(solution)/shard_map/ppermute | solution.py:384
  11.6 13.3 %collective-permute-start = (bf16[2,384,256]{2,1,0:T(8,128)(2,1)S(1)}, bf16[2,384,256]{2,1,0:T(8,128)(2,1)S(1)}, u32[]{:S(2)}, u32[]{:S(2)}) collective-permute-start(bf16[2,384,256]{2,1,0:T(8,128)(2,1)S(1)} %get-tuple-element.20), channel_id=1, source_target_pairs={{0,1},{1,0},{2,3},{3,2},{4,5},{5,4},{6,7},{7,6},{8,9},{9,8},{10,11... | collective-permute-start | bytes 1179656 | tf_op jit(solution)/shard_map/ppermute | solution.py:384
  11.8 1.1 copy-start.4
  12.9 23.1 %copy-start.1 = (s32[4]{0:T(128)S(1)}, s32[4]{0:T(128)}, u32[]{:S(2)}) copy-start(s32[4]{0:T(128)} %owner_ref.9) | copy-start | bytes 52
  21.8 17.3 %copy-start.5 = (bf16[1,12,128,256]{3,2,1,0:T(8,128)(2,1)S(1)}, bf16[1,12,128,256]{3,2,1,0:T(8,128)(2,1)}, u32[]{:S(2)}) copy-start(bf16[1,12,128,256]{3,2,1,0:T(8,128)(2,1)} %param.21) | copy-start | bytes 2359300
  21.8 14.1 %collective-permute-start.3 = (bf16[256,256]{1,0:T(8,128)(2,1)S(1)}, bf16[256,256]{1,0:T(8,128)(2,1)S(1)}, u32[]{:S(2)}, u32[]{:S(2)}) collective-permute-start(bf16[256,256]{1,0:T(8,128)(2,1)S(1)} %fusion.1), channel_id=1, source_target_pairs={{0,2},{1,3},{2,0},{3,1},{4,6},{5,7},{6,4},{7,5},{8,10},{9,11},{10,... | collective-permute-start | bytes 393224 | tf_op jit(solution)/shard_map/ppermute | solution.py:384
  24.9 22.7 %collective-permute-start.1 = (bf16[384,256]{1,0:T(8,128)(2,1)S(1)}, bf16[384,256]{1,0:T(8,128)(2,1)S(1)}, u32[]{:S(2)}, u32[]{:S(2)}) collective-permute-start(bf16[384,256]{1,0:T(8,128)(2,1)S(1)} %fusion), channel_id=1, source_target_pairs={{0,2},{1,3},{2,0},{3,1},{4,6},{5,7},{6,4},{7,5},{8,10},{9,11},{10,... | collective-permute-start | bytes 589832 | tf_op jit(solution)/shard_map/ppermute | solution.py:384
  37.2 6.5 %collective-permute-start.4 = (bf16[128,256]{1,0:T(8,128)(2,1)S(1)}, bf16[128,256]{1,0:T(8,128)(2,1)S(1)}, u32[]{:S(2)}, u32[]{:S(2)}) collective-permute-start(bf16[128,256]{1,0:T(8,128)(2,1)S(1)} %get-tuple-element.26.refs_0_), channel_id=1, source_target_pairs={{0,4},{4,0},{8,12},{12,8},{1,5},{5,1},{9,13},{13,9},{2,6},{6,2},{1... | collective-permute-start | bytes 196616 | tf_op jit(solution)/shard_map/ppermute | solution.py:384
  37.2 6.4 %collective-permute-start.5 = (bf16[128,256]{1,0:T(8,128)(2,1)S(1)}, bf16[128,256]{1,0:T(8,128)(2,1)S(1)}, u32[]{:S(2)}, u32[]{:S(2)}) collective-permute-start(bf16[128,256]{1,0:T(8,128)(2,1)S(1)} %get-tuple-element.26.refs_0_), channel_id=1, source_target_pairs={{0,8},{4,12},{8,0},{12,4},{1,9},{5,13},{9,1},{13,5},{2,10},{6,14},... | collective-permute-start | bytes 196616 | tf_op jit(solution)/shard_map/ppermute | solution.py:384
  38.8 4.9 %collective-permute-start.6 = (bf16[128,256]{1,0:T(8,128)(2,1)S(1)}, bf16[128,256]{1,0:T(8,128)(2,1)S(1)}, u32[]{:S(2)}, u32[]{:S(2)}) collective-permute-start(bf16[128,256]{1,0:T(8,128)(2,1)S(1)} %get-tuple-element.26.refs_0_), channel_id=1, source_target_pairs={{0,12},{4,8},{8,4},{12,0},{1,13},{5,9},{9,5},{13,1},{2,14},{6,10},... | collective-permute-start | bytes 196616 | tf_op jit(solution)/shard_map/ppermute | solution.py:384
  47.5 23.7 %collective-permute-start.15 = (bf16[128,1024]{1,0:T(8,128)(2,1)S(1)}, bf16[128,1024]{1,0:T(8,128)(2,1)S(1)}, u32[]{:S(2)}, u32[]{:S(2)}) collective-permute-start(bf16[128,1024]{1,0:T(8,128)(2,1)S(1)} %attend_new.5.refs_0_), channel_id=1, source_target_pairs={{0,2},{1,3},{2,0},{3,1},{4,6},{5,7},{6,4},{7,5},{8,10},{9,11},{10,... | collective-permute-start | bytes 786440 | tf_op jit(solution)/shard_map/ppermute | solution.py:384
  56.6 51.6 %collective-permute-start.12 = (bf16[256,1024]{1,0:T(8,128)(2,1)S(1)}, bf16[256,1024]{1,0:T(8,128)(2,1)S(1)}, u32[]{:S(2)}, u32[]{:S(2)}) collective-permute-start(bf16[256,1024]{1,0:T(8,128)(2,1)S(1)} %attend_new.4.refs_0_), channel_id=1, source_target_pairs={{0,2},{1,3},{2,0},{3,1},{4,6},{5,7},{6,4},{7,5},{8,10},{9,11},{10,... | collective-permute-start | bytes 1572872 | tf_op jit(solution)/shard_map/ppermute | solution.py:384
  64.1 13.4 %collective-permute-start.16 = (bf16[128,1024]{1,0:T(8,128)(2,1)S(1)}, bf16[128,1024]{1,0:T(8,128)(2,1)S(1)}, u32[]{:S(2)}, u32[]{:S(2)}) collective-permute-start(bf16[128,1024]{1,0:T(8,128)(2,1)S(1)} %attend_new.5.refs_0_), channel_id=1, source_target_pairs={{0,1},{1,0},{2,3},{3,2},{4,5},{5,4},{6,7},{7,6},{8,9},{9,8},{10,11... | collective-permute-start | bytes 786440 | tf_op jit(solution)/shard_map/ppermute | solution.py:384
  68.2 28.2 %collective-permute-start.8 = (bf16[128,1024]{1,0:T(8,128)(2,1)S(1)}, bf16[128,1024]{1,0:T(8,128)(2,1)S(1)}, u32[]{:S(2)}, u32[]{:S(2)}) collective-permute-start(bf16[128,1024]{1,0:T(8,128)(2,1)S(1)} %attend_new.3.refs_0_), channel_id=1, source_target_pairs={{0,2},{1,3},{2,0},{3,1},{4,6},{5,7},{6,4},{7,5},{8,10},{9,11},{10,... | collective-permute-start | bytes 786440 | tf_op jit(solution)/shard_map/ppermute | solution.py:384
  71.2 50.5 %collective-permute-start.14 = (bf16[256,1024]{1,0:T(8,128)(2,1)S(1)}, bf16[256,1024]{1,0:T(8,128)(2,1)S(1)}, u32[]{:S(2)}, u32[]{:S(2)}) collective-permute-start(bf16[256,1024]{1,0:T(8,128)(2,1)S(1)} %attend_new.4.refs_0_), channel_id=1, source_target_pairs={{0,1},{1,0},{2,3},{3,2},{4,5},{5,4},{6,7},{7,6},{8,9},{9,8},{10,11... | collective-permute-start | bytes 1572872 | tf_op jit(solution)/shard_map/ppermute | solution.py:384
  71.2 36.3 %collective-permute-start.10 = (bf16[128,1024]{1,0:T(8,128)(2,1)S(1)}, bf16[128,1024]{1,0:T(8,128)(2,1)S(1)}, u32[]{:S(2)}, u32[]{:S(2)}) collective-permute-start(bf16[128,1024]{1,0:T(8,128)(2,1)S(1)} %attend_new.3.refs_0_), channel_id=1, source_target_pairs={{0,1},{1,0},{2,3},{3,2},{4,5},{5,4},{6,7},{7,6},{8,9},{9,8},{10,11... | collective-permute-start | bytes 786440 | tf_op jit(solution)/shard_map/ppermute | solution.py:384
  77.5 34.5 %collective-permute-start.17 = (bf16[128,1024]{1,0:T(8,128)(2,1)S(1)}, bf16[128,1024]{1,0:T(8,128)(2,1)S(1)}, u32[]{:S(2)}, u32[]{:S(2)}) collective-permute-start(bf16[128,1024]{1,0:T(8,128)(2,1)S(1)} %attend_new.5.refs_0_), channel_id=1, source_target_pairs={{1,2},{2,1},{5,6},{6,5},{9,10},{10,9},{13,14},{14,13},{17,18},{18,... | collective-permute-start | bytes 786440 | tf_op jit(solution)/shard_map/ppermute | solution.py:519
  96.4 16.6 %collective-permute-start.18 = (bf16[128,1024]{1,0:T(8,128)(2,1)S(1)}, bf16[128,1024]{1,0:T(8,128)(2,1)S(1)}, u32[]{:S(2)}, u32[]{:S(2)}) collective-permute-start(bf16[128,1024]{1,0:T(8,128)(2,1)S(1)} %collective-permute-done.15.refs_1_), channel_id=1, source_target_pairs={{1,0},{2,3},{5,4},{6,7},{9,8},{10,11},{13,12},{14,15},{17,16},{18,... | collective-permute-start | bytes 786440 | tf_op jit(solution)/shard_map/ppermute | solution.py:520
  107.4 19.9 %collective-permute-start.11 = (bf16[256,1024]{1,0:T(8,128)(2,1)S(1)}, bf16[256,1024]{1,0:T(8,128)(2,1)S(1)}, u32[]{:S(2)}, u32[]{:S(2)}) collective-permute-start(bf16[256,1024]{1,0:T(8,128)(2,1)S(1)} %attend_new.4.refs_0_), channel_id=1, source_target_pairs={{1,2},{2,1},{5,6},{6,5},{9,10},{10,9},{13,14},{14,13},{17,18},{18,... | collective-permute-start | bytes 1572872 | tf_op jit(solution)/shard_map/ppermute | solution.py:519
  108.1 19.2 %collective-permute-start.13 = (bf16[256,1024]{1,0:T(8,128)(2,1)S(1)}, bf16[256,1024]{1,0:T(8,128)(2,1)S(1)}, u32[]{:S(2)}, u32[]{:S(2)}) collective-permute-start(bf16[256,1024]{1,0:T(8,128)(2,1)S(1)} %collective-permute-done.12.refs_1_), channel_id=1, source_target_pairs={{1,0},{2,3},{5,4},{6,7},{9,8},{10,11},{13,12},{14,15},{17,16},{18,... | collective-permute-start | bytes 1572872 | tf_op jit(solution)/shard_map/ppermute | solution.py:520
  112.0 17.8 %collective-permute-start.7 = (bf16[128,1024]{1,0:T(8,128)(2,1)S(1)}, bf16[128,1024]{1,0:T(8,128)(2,1)S(1)}, u32[]{:S(2)}, u32[]{:S(2)}) collective-permute-start(bf16[128,1024]{1,0:T(8,128)(2,1)S(1)} %attend_new.3.refs_0_), channel_id=1, source_target_pairs={{1,2},{2,1},{5,6},{6,5},{9,10},{10,9},{13,14},{14,13},{17,18},{18,... | collective-permute-start | bytes 786440 | tf_op jit(solution)/shard_map/ppermute | solution.py:519
  113.1 16.7 %collective-permute-start.9 = (bf16[128,1024]{1,0:T(8,128)(2,1)S(1)}, bf16[128,1024]{1,0:T(8,128)(2,1)S(1)}, u32[]{:S(2)}, u32[]{:S(2)}) collective-permute-start(bf16[128,1024]{1,0:T(8,128)(2,1)S(1)} %collective-permute-done.8.refs_1_), channel_id=1, source_target_pairs={{1,0},{2,3},{5,4},{6,7},{9,8},{10,11},{13,12},{14,15},{17,16},{18,... | collective-permute-start | bytes 786440 | tf_op jit(solution)/shard_map/ppermute | solution.py:520

commit v4 on v3

--- a/solution.py
+++ b/solution.py
@@ -109,7 +109,7 @@
     block, steps = q_ref.shape[:2]
     prompt = by_row(fork_ref[...], (pl.program_id(0) + start) * block, m, steps)
     pages, size = pool_ref.shape[:2]
-    group = 2 * cpages
+    group = cpages
 
     def part(at):
         mine = range(at, min(at + group, pages))
@@ -215,14 +215,14 @@
     )(page_table, prompt_length, q, fork_row, pool)
 
 
-def attend_new(q, fork_row, owner, base, span_pairs, tail_pairs, mixed, stat, start, count):
+def attend_new(q, fork_row, owner, base, span_pairs, tail_pairs, mixed, stat, start, count, skip=0):
     steps, width = q.shape[1:]
     heads = width // HD
     block = min(SET_ROWS, q.shape[0])
     m = block * steps
     span = span_pairs[0].shape[0]
     keys = span * len(span_pairs)
-    part = pl.BlockSpec((heads, m, HD), lambda i, *_: (0, i, 0))
+    part = pl.BlockSpec((heads, m, HD), lambda i, *_: (0, i + skip, 0))
     return pl.pallas_call(
         functools.partial(new_kernel, heads, steps, LOG2E / math.sqrt(HD), start),
         grid_spec=pltpu.PrefetchScalarGridSpec(
@@ -391,18 +391,18 @@
     return finish(keep, (got, last), places, start, sizes)
 
 
-def out_kernel(rels, pick, cuts, add, held, rank_ref, *refs):
+def out_kernel(rels, shapes, cuts, add, held, rank_ref, *refs):
     refs = list(refs)
-    pieces = [refs.pop(0) for _ in rels]
-    other = refs.pop(0) if pick else None
+    pieces = [([refs.pop(0) for _ in range(n)], refs.pop(0) if outer else None) for n, outer in shapes]
     partial = refs.pop(0) if add else None
     w_ref = refs[0]
     o_ref, buf, sem = (refs[-1], None, None) if held else refs[-3:]
-    width = pieces[0].shape[1]
+    width = pieces[0][0][0].shape[1]
     depth = width // cuts
     rank = rank_ref[0]
+    inner = (rank == 1) | (rank == 2)
     copies = []
-    for p, rel in enumerate(rels if buf is not None else ()):
+    for p, rel in enumerate(() if held else rels):
         for c in range(cuts):
             row = pl.multiple_of((rank ^ rel) * width + c * depth, depth)
             slot = p * cuts + c
@@ -411,18 +411,18 @@
             )
             copies[-1].start()
     total = partial[...] if add else None
-    for p in range(len(rels)):
-        a = pieces[p][...]
-        if pick and p == len(rels) - 1:
-            inner = (rank == 1) | (rank == 2)
-            a = jnp.where(inner, a, other[...])
+    for p, (groups, outer) in enumerate(pieces):
+        a = [ref[...] for ref in groups]
+        a = a[0] if len(a) == 1 else jnp.concatenate(a, 0)
+        if outer is not None:
+            a = jnp.where(inner, a, outer[...])
         for c in range(cuts):
-            slot = p * cuts + c
             if held:
-                w = w_ref[c * depth : (c + 1) * depth, :]
+                at = held.index(rels[p]) * width + c * depth
+                w = w_ref[at : at + depth, :]
             else:
-                copies[slot].wait()
-                w = buf[slot]
+                copies[p * cuts + c].wait()
+                w = buf[p * cuts + c]
             one = jnp.dot(
                 a[:, c * depth : (c + 1) * depth], w, preferred_element_type=jnp.float32
             )
@@ -430,20 +430,19 @@
     o_ref[...] = total.reshape(o_ref.shape).astype(o_ref.dtype)
 
 
-def out_project(rank, pieces, rels, weight, shape, start, pick=None, partial=None, into=None, final=True, held=False):
-    m, width = pieces[0].shape
+def out_project(rank, pieces, weight, shape, start, partial=None, into=None, final=True, held=()):
+    width = pieces[0][1][0].shape[1]
+    m = sum(x.shape[0] for x in pieces[0][1])
     columns = weight.shape[1]
     steps = shape[1]
-    cuts = 4
-    flat = lambda w: pl.BlockSpec((m, w), lambda i, r: (0, 0))
-    args = list(pieces)
-    in_specs = [flat(width) for _ in pieces]
-    if pick is not None:
-        args.append(pick)
-        in_specs.append(flat(width))
+    cuts = 1 if held else 4
+    flat = lambda x: pl.BlockSpec(x.shape, lambda i, r: (0, 0))
+    args = []
+    for _, groups, outer in pieces:
+        args += list(groups) + ([] if outer is None else [outer])
     if partial is not None:
         args.append(partial)
-        in_specs.append(flat(columns))
+    in_specs = [flat(x) for x in args]
     args.append(weight if held else in_hbm(weight))
     in_specs.append(pl.BlockSpec(memory_space=pltpu.VMEM if held else pl.ANY))
     aliases = {}
@@ -458,11 +457,13 @@
         )
         out_shape = jax.ShapeDtypeStruct(shape, jnp.bfloat16)
     else:
-        out_spec = flat(columns)
+        out_spec = pl.BlockSpec((m, columns), lambda i, r: (0, 0))
         out_shape = jax.ShapeDtypeStruct((m, columns), jnp.float32)
+    rels = tuple(rel for rel, _, _ in pieces)
+    shapes = tuple((len(groups), outer is not None) for _, groups, outer in pieces)
     slots = len(rels) * cuts
     return pl.pallas_call(
-        functools.partial(out_kernel, rels, pick is not None, cuts, partial is not None, held),
+        functools.partial(out_kernel, rels, shapes, cuts, partial is not None, held),
         grid_spec=pltpu.PrefetchScalarGridSpec(
             num_scalar_prefetch=1,
             grid=(1,),
@@ -487,26 +488,32 @@
     )(rank, *args)
 
 
-def hold_kernel(rel, rank_ref, w_ref, o_ref, sem):
-    rows = o_ref.shape[0]
-    at = pl.multiple_of((rank_ref[0] ^ rel) * rows, rows)
-    copy = pltpu.make_async_copy(w_ref.at[pl.ds(at, rows), :], o_ref, sem)
-    copy.start()
-    copy.wait()
-
-
-def hold(rank, rel, weight, rows):
-    shape = (rows, weight.shape[1])
+def hold_kernel(rels, rank_ref, w_ref, o_ref, sem):
+    rows = o_ref.shape[0] // len(rels)
+    copies = []
+    for i, rel in enumerate(rels):
+        at = pl.multiple_of((rank_ref[0] ^ rel) * rows, rows)
+        copies.append(
+            pltpu.make_async_copy(
+                w_ref.at[pl.ds(at, rows), :], o_ref.at[i * rows : (i + 1) * rows, :], sem.at[i]
+            )
+        )
+        copies[-1].start()
+    for copy in copies:
+        copy.wait()
+
+
+def hold(rank, rels, weight, rows):
     held = pl.pallas_call(
-        functools.partial(hold_kernel, rel),
+        functools.partial(hold_kernel, rels),
         grid_spec=pltpu.PrefetchScalarGridSpec(
             num_scalar_prefetch=1,
             grid=(1,),
             in_specs=[pl.BlockSpec(memory_space=pl.ANY)],
             out_specs=pl.BlockSpec(memory_space=pltpu.VMEM),
-            scratch_shapes=[pltpu.SemaphoreType.DMA],
-        ),
-        out_shape=jax.ShapeDtypeStruct(shape, weight.dtype),
+            scratch_shapes=[pltpu.SemaphoreType.DMA((len(rels),))],
+        ),
+        out_shape=jax.ShapeDtypeStruct((len(rels) * rows, weight.shape[1]), weight.dtype),
         compiler_params=SMALL,
         name="hold",
     )(rank, in_hbm(weight))
@@ -519,6 +526,19 @@
     across = lax.ppermute(own, "tensor", [(1, 2), (2, 1)])
     passed = lax.ppermute(far, "tensor", [(1, 0), (2, 3)])
     return far, near, across, passed
+
+
+def relay_heads(groups):
+    near = []
+    for group in groups:
+        near.append(swap(group, "tensor", 1))
+    own = jnp.concatenate(groups, 0)
+    across = lax.ppermute(own, "tensor", [(1, 2), (2, 1)])
+    far = lax.ppermute(own, "tensor", [(0, 2), (3, 1)])
+    outward = [(1, 0), (2, 3)]
+    forward = lax.ppermute(across, "tensor", outward)
+    passed = lax.ppermute(far, "tensor", outward)
+    return near, far, across, forward, passed
 
 
 def on_device(
@@ -631,37 +651,44 @@
     arrived = [own_span]
     for j in range(1, n_replica):
         arrived.append(swap(own_span, "replica", j))
-    middle_tail, last_tail = swap_sum(*rest_units, places, span + cut, (middle * cut, cut))
-
-    def attended(tail, start, count):
-        old = attend_cached(decode_queries, fork_row, page_table, prompt_length, pool, start, count)
+    rest_tails = swap_sum(*rest_units, places, span + cut, (cut,) * (blocks - 1))
+
+    def old_part(start, count):
+        return attend_cached(
+            decode_queries, fork_row, page_table, prompt_length, pool, start, count
+        )
+
+    def new_part(tail, old, start, skip=0):
         return attend_new(
-            decode_queries, fork_row, prompt_owner, replica, arrived, tail, *old, start, count
+            decode_queries, fork_row, prompt_owner, replica, arrived, tail, *old, start, 1, skip
         )
 
     shape = (rows, steps, out_weight.shape[1])
-    first_own = attended(first_tail, 0, 1)
-    middle_own = attended(middle_tail, 1, middle)
-    last_own = attended(last_tail, blocks - 1, 1)
+    first_own = new_part(first_tail, old_part(0, 1), 0)
+    middle_old = old_part(1, middle)
+    middle_own = [new_part(rest_tails[i], middle_old, 1 + i, i) for i in range(middle)]
+    last_own = new_part(rest_tails[-1], old_part(blocks - 1, 1), blocks - 1)
     far, near, across, passed = gather_heads(first_own)
+    pieces = ((0, [first_own], None), (2, [far], None), (1, [near], None), (3, [across], passed))
+    decoded = out_project(rank, pieces, out_weight, shape, 0)
+    near, far, across, forward, passed = relay_heads(middle_own)
+    held = (2, 3)
+    held_rows = hold(rank, held, out_weight, first_own.shape[1])
+    pieces = ((0, middle_own, None), (1, near, None))
+    partial = out_project(rank, pieces, out_weight, shape, 0, final=False)
+    pieces = ((2, [far], forward), (3, [across], passed))
     decoded = out_project(
-        rank, [first_own, far, near, across], (0, 2, 1, 3), out_weight, shape, 0, pick=passed
-    )
-    far, near, across, passed = gather_heads(middle_own)
+        rank, pieces, held_rows, shape, first, partial=partial, into=decoded, held=held
+    )
+    far, near, across, passed = gather_heads(last_own)
+    pieces = ((0, [last_own], None), (2, [far], None))
+    partial = out_project(rank, pieces, out_weight, shape, 0, final=False)
     partial = out_project(
-        rank, [middle_own, far, near], (0, 2, 1), out_weight, shape, 0, final=False
-    )
-    last_rows = hold(rank, 3, out_weight, middle_own.shape[1])
-    decoded = out_project(
-        rank, [across], (3,), last_rows, shape, first,
-        pick=passed, partial=partial, into=decoded, held=True,
-    )
-    far, near, across, passed = gather_heads(last_own)
-    partial = out_project(rank, [last_own, far], (0, 2), out_weight, shape, 0, final=False)
-    partial = out_project(rank, [near], (1,), out_weight, shape, 0, partial=partial, final=False)
+        rank, ((1, [near], None),), out_weight, shape, 0, partial=partial, final=False
+    )
     return out_project(
-        rank, [across], (3,), last_rows, shape, first * (blocks - 1),
-        pick=passed, partial=partial, into=decoded, held=True,
+        rank, ((3, [across], passed),), held_rows, shape, first * (blocks - 1),
+        partial=partial, into=decoded, held=held,
     )
 
 

time: 133 us -> 135 us (1.015)
  starting transfers between devices: 22.9 us -> 31.1 us
  Pallas kernels: 69.4 us -> 66.4 us
  waiting for transfers between devices: 37.5 us -> 35 us
    ppermute x13, waiting for transfers between devices: 37.1 us -> 25.2 us  [swap(): lax.ppermute(x, axis, [(i, i ^ bit) for i in range(lax.axis_size(axis))])]
    ppermute x0 -> x4, waiting for transfers between devices: none -> 9.62 us  [the longest x1 9.61 us: relay_heads(): passed = lax.ppermute(far, 'tensor', outward)]
    ppermute x0 -> x4, starting transfers between devices: none -> 7.91 us  [the longest x1 4.63 us: relay_heads(): far = lax.ppermute(own, 'tensor', [(0, 2), (3, 1)])]
    pallas_call x3, Pallas kernels: 18 us -> 13.6 us  [attend_cached(): pl.pallas_call(functools.partial(cached_kernel, heads, cpages, LOG2E / ma...]
    ppermute x13, starting transfers between devices: 16.7 us -> 19 us  [swap(): lax.ppermute(x, axis, [(i, i ^ bit) for i in range(lax.axis_size(axis))])]
    ppermute x3 -> x2, starting transfers between devices: 4.11 us -> 2.84 us  [gather_heads(): passed = lax.ppermute(far, 'tensor', [(1, 0), (2, 3)])]
    pallas_call x3 -> x4, Pallas kernels: 15.2 us -> 15.6 us  [attend_new(): pl.pallas_call(functools.partial(new_kernel, heads, steps, LOG2E / math.s...]
  transfers between devices with their start and end apart: 19 -> 21, of which waited for: 5 -> 6; matrix products, arithmetic and copies ran while one was open for 0% -> 0% of each run, Pallas kernels for 48% -> 45%
where the time goes in v4:
time: 135 us; the launch traced here: 134 us
  Pallas kernels  66.4 us (49%)
  waiting for transfers between devices  35 us (26%)
  starting transfers between devices  31.1 us (23%)
    ppermute x13, waiting for transfers between devices, swap(): lax.ppermute(x, axis, [(i, i ^ bit) for i in range(lax.axis_size(axis))])  25.2 us
    pallas_call x6, Pallas kernels, out_project(): pl.pallas_call(functools.partial(out_kernel, rels, shapes, cuts, partial...  22.8 us
    ppermute x13, starting transfers between devices, swap(): lax.ppermute(x, axis, [(i, i ^ bit) for i in range(lax.axis_size(axis))])  19 us
    pallas_call x4, Pallas kernels, attend_new(): pl.pallas_call(functools.partial(new_kernel, heads, steps, LOG2E / math.s...  15.6 us
    pallas_call x3, Pallas kernels, attend_cached(): pl.pallas_call(functools.partial(cached_kernel, heads, cpages, LOG2E / ma...  13.6 us
    ppermute x1, waiting for transfers between devices, relay_heads(): passed = lax.ppermute(far, 'tensor', outward)  9.61 us
    pallas_call x2, Pallas kernels, project(): pl.pallas_call(functools.partial(project_kernel, len(groups), split, kept...  8.39 us
    ppermute x1, starting transfers between devices, relay_heads(): far = lax.ppermute(own, 'tensor', [(0, 2), (3, 1)])  4.63 us
  transfers between devices with their start and end apart: 21, of which 6 were waited for; matrix products, arithmetic and copies ran while one was open for 0% of the time, Pallas kernels for 45%

profile of v4, /device:TPU:0, one launch (start us, length us, event | category | flops | bytes accessed | tf_op | source)
XLA Modules:
  0.0 134.3 jit_solution(16974506601014233179)
XLA Ops:
  0.0 4.1 %project.3 = (f32[2,256,256]{2,1,0:T(8,128)S(1)}, bf16[2,256,256]{2,1,0:T(8,128)(2,1)}) custom-call(s32[1]{0:T(128)} %bitcast.rank_ref, bf16[128,2048]{1,0:T(8,128)(2,1)} %refs_0_.3, bf16[128,4,2048]{2,1,0:T(4,128)(2,1)} %refs_1_.3, bf16[2048,512]{1,0:T(8,128)(2,1)} %refs_4_.4, bf16[2048,512]{1,0:T(8,128)(2,1)} %refs_5_.2, bf16[2048,512]{1,0:T(8,128)(2,1)} %refs_4_.4, ...), custom_call_target="tpu_custom_call" | custom-call | flops 1073741824 | bytes 4194304 | tf_op jit(solution)/shard_map/project/pallas_call | solution.py:299
  4.2 3.1 %collective-permute-start.2 = (bf16[2,256,256]{2,1,0:T(8,128)(2,1)}, bf16[2,256,256]{2,1,0:T(8,128)(2,1)S(1)}, u32[]{:S(2)}, u32[]{:S(2)}) collective-permute-start(bf16[2,256,256]{2,1,0:T(8,128)(2,1)} %get-tuple-element.26), channel_id=1, source_target_pairs={{0,1},{1,0},{2,3},{3,2},{4,5},{5,4},{6,7},{7,6},{8,9},{9,8},{10,11... | collective-permute-start | bytes 786440 | tf_op jit(solution)/shard_map/ppermute | solution.py:384
  7.3 4.3 %project.2 = (f32[2,384,256]{2,1,0:T(8,128)S(1)}, bf16[2,384,256]{2,1,0:T(8,128)(2,1)S(1)}) custom-call(s32[1]{0:T(128)} %bitcast.rank_ref, bf16[128,4,2048]{2,1,0:T(4,128)(2,1)} %refs_1_.3, bf16[2048,512]{1,0:T(8,128)(2,1)} %refs_4_.4, bf16[2048,512]{1,0:T(8,128)(2,1)} %refs_5_.2, bf16[2048,512]{1,0:T(8,128)(2,1)} %refs_4_.4, bf16[2048,512]{1,0:T(8,128)(2,1)} %refs_5_.2), custom_call_target="tpu_custom_call" | custom-call | flops 1610612736 | bytes 4194304 | tf_op jit(solution)/shard_map/project/pallas_call | solution.py:299
  11.6 0.2 collective-permute-start
  11.8 0.0 copy-start.4
  11.8 1.1 copy-done.4
  12.9 6.7 %attend_cached.4 = (f32[8,256,128]{2,1,0:T(8,128)S(1)}, f32[8,256,128]{2,1,0:T(8,128)S(1)}) custom-call(s32[12]{0:T(128)S(1)} %copy-done.6, s32[4]{0:T(128)S(1)} %copy-done.3, bf16[128,4,1024]{2,1,0:T(4,128)(2,1)S(1)} %copy-done, s32[1,128]{1,0:T(1,128)S(1)} %bitcast.10, bf16[12,128,256]{2,1,0:T(8,128)(2,1)S(1)} %bitcast.19), custom_call_target="tpu_custom_call" | custom-call | flops 1610612736 | bytes 2097152 | tf_op jit(solution)/shard_map/attend_cached/pallas_call | solution.py:194
  19.6 3.0 %collective-permute-start.3 = (bf16[256,256]{1,0:T(8,128)(2,1)S(1)}, bf16[256,256]{1,0:T(8,128)(2,1)S(1)}, u32[]{:S(2)}, u32[]{:S(2)}) collective-permute-start(bf16[256,256]{1,0:T(8,128)(2,1)S(1)} %fusion.1), channel_id=1, source_target_pairs={{0,2},{1,3},{2,0},{3,1},{4,6},{5,7},{6,4},{7,5},{8,10},{9,11},{10,... | collective-permute-start | bytes 393224 | tf_op jit(solution)/shard_map/ppermute | solution.py:384
  22.7 3.0 %collective-permute-start.1 = (bf16[384,256]{1,0:T(8,128)(2,1)S(1)}, bf16[384,256]{1,0:T(8,128)(2,1)S(1)}, u32[]{:S(2)}, u32[]{:S(2)}) collective-permute-start(bf16[384,256]{1,0:T(8,128)(2,1)S(1)} %fusion), channel_id=1, source_target_pairs={{0,2},{1,3},{2,0},{3,1},{4,6},{5,7},{6,4},{7,5},{8,10},{9,11},{10,... | collective-permute-start | bytes 589832 | tf_op jit(solution)/shard_map/ppermute | solution.py:384
  25.7 0.1 maximum_bitcast_fusion.freq_ref
  25.7 8.1 %collective-permute-done.3.refs_1_ = bf16[256,256]{1,0:T(8,128)(2,1)S(1)} collective-permute-done((bf16[256,256]{1,0:T(8,128)(2,1)S(1)}, bf16[256,256]{1,0:T(8,128)(2,1)S(1)}, u32[]{:S(2)}, u32[]{:S(2)}) %collective-permute-start.3) | collective-permute-done | bytes 131104 | tf_op jit(solution)/shard_map/ppermute | solution.py:384
  33.9 1.2 finish.3
  35.0 0.1 collective-permute-start.4
  35.1 1.7 %collective-permute-start.5 = (bf16[128,256]{1,0:T(8,128)(2,1)S(1)}, bf16[128,256]{1,0:T(8,128)(2,1)S(1)}, u32[]{:S(2)}, u32[]{:S(2)}) collective-permute-start(bf16[128,256]{1,0:T(8,128)(2,1)S(1)} %get-tuple-element.27.refs_0_), channel_id=1, source_target_pairs={{0,8},{4,12},{8,0},{12,4},{1,9},{5,13},{9,1},{13,5},{2,10},{6,14},... | collective-permute-start | bytes 196616 | tf_op jit(solution)/shard_map/ppermute | solution.py:384
  36.8 0.2 collective-permute-start.6
  37.0 3.4 %attend_cached.5 = (f32[8,128,128]{2,1,0:T(8,128)S(1)}, f32[8,128,128]{2,1,0:T(8,128)S(1)}) custom-call(s32[12]{0:T(128)S(1)} %copy-done.6, s32[4]{0:T(128)S(1)} %copy-done.3, bf16[128,4,1024]{2,1,0:T(4,128)(2,1)S(1)} %copy-done, s32[1,128]{1,0:T(1,128)S(1)} %bitcast.12, bf16[12,128,256]{2,1,0:T(8,128)(2,1)S(1)} %bitcast.20), custom_call_target="tpu_custom_call" | custom-call | flops 805306368 | bytes 1048576 | tf_op jit(solution)/shard_map/attend_cached/pallas_call | solution.py:194
  40.4 0.4 collective-permute-done.6.refs_3_
  40.8 3.8 %attend_new.7.refs_0_ = bf16[128,1024]{1,0:T(8,128)(2,1)S(1)} custom-call(s32[4]{0:T(128)S(1)} %copy-done.1, s32[1]{0:T(128)} %bitcast.1.replica_ref.base_ref, bf16[128,4,1024]{2,1,0:T(4,128)(2,1)S(1)} %copy-done, s32[1,128]{1,0:T(1,128)S(1)} %bitcast.13, bf16[128,256]{1,0:T(8,128)(2,1)S(1)} %get-tuple-element.32.tail_ref, ...), custom_call_target="tpu_custom_call" | custom-call | flops 335544320 | bytes 1310720 | tf_op jit(solution)/shard_map/attend_new/pallas_call | solution.py:226
  44.7 0.1 collective-permute-start.17
  44.8 1.4 %finish.2 = (bf16[128,256]{1,0:T(8,128)(2,1)S(1)}, bf16[128,256]{1,0:T(8,128)(2,1)S(1)}, bf16[128,256]{1,0:T(8,128)(2,1)S(1)}) custom-call(s32[4]{0:T(128)S(1)} %copy-done.1, s32[4]{0:T(128)S(1)} %copy-done.3, s32[1]{0:T(128)} %bitcast.1.replica_ref.base_ref, s32[1,128]{1,0:T(1,128)S(1)} %bitcast.14, f32[1,128]{1,0:T(1,128)S(1)} %maximum_bitcast_fusion.freq_ref, ...), custom_call_target="tpu_custom_call" | custom-call | tf_op jit(solution)/shard_map/finish/pallas_call | solution.py:368
  46.2 3.8 %attend_new.5.refs_0_ = bf16[128,1024]{1,0:T(8,128)(2,1)S(1)} custom-call(s32[4]{0:T(128)S(1)} %copy-done.1, s32[1]{0:T(128)} %bitcast.1.replica_ref.base_ref, bf16[128,4,1024]{2,1,0:T(4,128)(2,1)S(1)} %copy-done, s32[1,128]{1,0:T(1,128)S(1)} %bitcast.15, bf16[128,256]{1,0:T(8,128)(2,1)S(1)} %get-tuple-element.28.tail_ref, ...), custom_call_target="tpu_custom_call" | custom-call | flops 335544320 | bytes 1310720 | tf_op jit(solution)/shard_map/attend_new/pallas_call | solution.py:226
  50.0 3.1 %collective-permute-start.15 = (bf16[128,1024]{1,0:T(8,128)(2,1)S(1)}, bf16[128,1024]{1,0:T(8,128)(2,1)S(1)}, u32[]{:S(2)}, u32[]{:S(2)}) collective-permute-start(bf16[128,1024]{1,0:T(8,128)(2,1)S(1)} %attend_new.5.refs_0_), channel_id=1, source_target_pairs={{0,1},{1,0},{2,3},{3,2},{4,5},{5,4},{6,7},{7,6},{8,9},{9,8},{10,11... | collective-permute-start | bytes 786440 | tf_op jit(solution)/shard_map/ppermute | solution.py:384
  53.1 4.0 %attend_new.6.refs_1_ = bf16[128,1024]{1,0:T(8,128)(2,1)S(1)} custom-call(s32[4]{0:T(128)S(1)} %copy-done.1, s32[1]{0:T(128)} %bitcast.1.replica_ref.base_ref, bf16[128,4,1024]{2,1,0:T(4,128)(2,1)S(1)} %copy-done, s32[1,128]{1,0:T(1,128)S(1)} %bitcast.16, bf16[128,256]{1,0:T(8,128)(2,1)S(1)} %get-tuple-element.31.tail_ref, ...), custom_call_target="tpu_custom_call" | custom-call | flops 335544320 | bytes 1310720 | tf_op jit(solution)/shard_map/attend_new/pallas_call | solution.py:226
  57.2 0.7 collective-permute-start.12
  57.9 4.6 %collective-permute-start.11 = (bf16[256,1024]{1,0:T(8,128)(2,1)S(1)}, bf16[256,1024]{1,0:T(8,128)(2,1)S(1)}, u32[]{:S(2)}, u32[]{:S(2)}) collective-permute-start(bf16[256,1024]{1,0:T(8,128)(2,1)S(1)} %pad_maximum_fusion), channel_id=1, source_target_pairs={{0,2},{3,1},{4,6},{7,5},{8,10},{11,9},{12,14},{15,13},{16,18},{19,... | collective-permute-start | bytes 1572872 | tf_op jit(solution)/shard_map/ppermute | solution.py:537
  62.6 3.4 %attend_cached.3 = (f32[8,128,128]{2,1,0:T(8,128)S(1)}, f32[8,128,128]{2,1,0:T(8,128)S(1)}) custom-call(s32[12]{0:T(128)S(1)} %copy-done.6, s32[4]{0:T(128)S(1)} %copy-done.3, bf16[128,4,1024]{2,1,0:T(4,128)(2,1)S(1)} %copy-done, s32[1,128]{1,0:T(1,128)S(1)} %bitcast.17, bf16[12,128,256]{2,1,0:T(8,128)(2,1)S(1)} %bitcast.21), custom_call_target="tpu_custom_call" | custom-call | flops 805306368 | bytes 1048576 | tf_op jit(solution)/shard_map/attend_cached/pallas_call | solution.py:194
  66.0 0.1 collective-permute-start.16
  66.1 3.8 %attend_new.4.refs_0_ = bf16[128,1024]{1,0:T(8,128)(2,1)S(1)} custom-call(s32[4]{0:T(128)S(1)} %copy-done.1, s32[1]{0:T(128)} %bitcast.1.replica_ref.base_ref, bf16[128,4,1024]{2,1,0:T(4,128)(2,1)S(1)} %copy-done, s32[1,128]{1,0:T(1,128)S(1)} %bitcast.18, bf16[128,256]{1,0:T(8,128)(2,1)S(1)} %get-tuple-element.22.tail_ref, ...), custom_call_target="tpu_custom_call" | custom-call | flops 335544320 | bytes 1310720 | tf_op jit(solution)/shard_map/attend_new/pallas_call | solution.py:226
  70.0 2.1 %collective-permute-start.8 = (bf16[128,1024]{1,0:T(8,128)(2,1)S(1)}, bf16[128,1024]{1,0:T(8,128)(2,1)S(1)}, u32[]{:S(2)}, u32[]{:S(2)}) collective-permute-start(bf16[128,1024]{1,0:T(8,128)(2,1)S(1)} %attend_new.4.refs_0_), channel_id=1, source_target_pairs={{0,2},{1,3},{2,0},{3,1},{4,6},{5,7},{6,4},{7,5},{8,10},{9,11},{10,... | collective-permute-start | bytes 786440 | tf_op jit(solution)/shard_map/ppermute | solution.py:384
  72.0 0.1 collective-permute-start.10
  72.1 3.5 %hold.1.refs_5_.refs_3_ = bf16[2048,2048]{1,0:T(8,128)(2,1)S(1)} custom-call(s32[1]{0:T(128)} %bitcast.rank_ref, bf16[4096,2048]{1,0:T(8,128)(2,1)} %refs_5_.3), custom_call_target="tpu_custom_call" | custom-call | tf_op jit(solution)/shard_map/hold/pallas_call | solution.py:507
  75.6 4.8 %collective-permute-done.16.refs_3_ = bf16[128,1024]{1,0:T(8,128)(2,1)S(1)} collective-permute-done((bf16[128,1024]{1,0:T(8,128)(2,1)S(1)}, bf16[128,1024]{1,0:T(8,128)(2,1)S(1)}, u32[]{:S(2)}, u32[]{:S(2)}) %collective-permute-start.16) | collective-permute-done | bytes 262176 | tf_op jit(solution)/shard_map/ppermute | solution.py:384
  80.4 2.5 %collective-permute-start.18 = (bf16[128,1024]{1,0:T(8,128)(2,1)S(1)}, bf16[128,1024]{1,0:T(8,128)(2,1)S(1)}, u32[]{:S(2)}, u32[]{:S(2)}) collective-permute-start(bf16[128,1024]{1,0:T(8,128)(2,1)S(1)} %attend_new.7.refs_0_), channel_id=1, source_target_pairs={{0,1},{1,0},{2,3},{3,2},{4,5},{5,4},{6,7},{7,6},{8,9},{9,8},{10,11... | collective-permute-start | bytes 786440 | tf_op jit(solution)/shard_map/ppermute | solution.py:384
  82.9 11.8 %collective-permute-done.8.refs_1_ = bf16[128,1024]{1,0:T(8,128)(2,1)S(1)} collective-permute-done((bf16[128,1024]{1,0:T(8,128)(2,1)S(1)}, bf16[128,1024]{1,0:T(8,128)(2,1)S(1)}, u32[]{:S(2)}, u32[]{:S(2)}) %collective-permute-start.8) | collective-permute-done | bytes 262176 | tf_op jit(solution)/shard_map/ppermute | solution.py:384
  94.7 0.7 collective-permute-start.19
  95.4 1.3 collective-permute-start.20
  96.7 1.3 collective-permute-start.13
  98.0 1.3 collective-permute-start.14
  99.3 3.8 %out_project.6.refs_1_ = f32[128,2048]{1,0:T(8,128)S(1)} custom-call(s32[1]{0:T(128)} %bitcast.rank_ref, bf16[128,1024]{1,0:T(8,128)(2,1)S(1)} %attend_new.4.refs_0_, bf16[128,1024]{1,0:T(8,128)(2,1)S(1)} %collective-permute-done.8.refs_1_, bf16[4096,2048]{1,0:T(8,128)(2,1)} %refs_5_.3), custom_call_target="tpu_custom_call" | custom-call | flops 1073741824 | bytes 8388608 | tf_op jit(solution)/shard_map/out_project/pallas_call | solution.py:465
  103.1 2.5 %out_project.7.refs_2_ = f32[128,2048]{1,0:T(8,128)S(1)} custom-call(s32[1]{0:T(128)} %bitcast.rank_ref, bf16[128,1024]{1,0:T(8,128)(2,1)S(1)} %collective-permute-done.10.refs_0_, f32[128,2048]{1,0:T(8,128)S(1)} %out_project.6.refs_1_, bf16[4096,2048]{1,0:T(8,128)(2,1)} %refs_5_.3), custom_call_target="tpu_custom_call" | custom-call | flops 536870912 | bytes 4194304 | tf_op jit(solution)/shard_map/out_project/pallas_call | solution.py:465
  105.7 4.3 %out_project.8.refs_4_ = f32[256,2048]{1,0:T(8,128)S(1)} custom-call(s32[1]{0:T(128)} %bitcast.rank_ref, bf16[128,1024]{1,0:T(8,128)(2,1)S(1)} %attend_new.5.refs_0_, bf16[128,1024]{1,0:T(8,128)(2,1)S(1)} %attend_new.6.refs_1_, bf16[128,1024]{1,0:T(8,128)(2,1)S(1)} %collective-permute-done.15.refs_2_, bf16[128,1024]{1,0:T(8,128)(2,1)S(1)} %collective-permute-done.16.refs_3_, ...), custom_call_target="tpu_custom_call" | custom-call | flops 2147483648 | bytes 8388608 | tf_op jit(solution)/shard_map/out_project/pallas_call | solution.py:465
  110.0 0.7 collective-permute-start.7
  110.7 1.6 %collective-permute-start.9 = (bf16[128,1024]{1,0:T(8,128)(2,1)S(1)}, bf16[128,1024]{1,0:T(8,128)(2,1)S(1)}, u32[]{:S(2)}, u32[]{:S(2)}) collective-permute-start(bf16[128,1024]{1,0:T(8,128)(2,1)S(1)} %collective-permute-done.8.refs_1_), channel_id=1, source_target_pairs={{1,0},{2,3},{5,4},{6,7},{9,8},{10,11},{13,12},{14,15},{17,16},{18,... | collective-permute-start | bytes 786440 | tf_op jit(solution)/shard_map/ppermute | solution.py:527
  112.3 7.1 %out_project.9.refs_6_ = bf16[128,4,2048]{2,1,0:T(4,128)(2,1)} custom-call(s32[1]{0:T(128)} %bitcast.rank_ref, bf16[128,1024]{1,0:T(8,128)(2,1)S(1)} %attend_new.7.refs_0_, bf16[128,1024]{1,0:T(8,128)(2,1)S(1)} %collective-permute-done.17.refs_1_, bf16[128,1024]{1,0:T(8,128)(2,1)S(1)} %collective-permute-done.18.refs_2_, ...), custom_call_target="tpu_custom_call" | custom-call | flops 2147483648 | bytes 16777216 | tf_op jit(solution)/shard_map/out_project/pallas_call | solution.py:465
  119.4 9.6 %collective-permute-done.14.refs_3_ = bf16[256,1024]{1,0:T(8,128)(2,1)S(1)} collective-permute-done((bf16[256,1024]{1,0:T(8,128)(2,1)S(1)}, bf16[256,1024]{1,0:T(8,128)(2,1)S(1)}, u32[]{:S(2)}, u32[]{:S(2)}) %collective-permute-start.14) | collective-permute-done | bytes 524320 | tf_op jit(solution)/shard_map/ppermute | solution.py:540
  129.0 3.5 %out_project.10.refs_4_ = bf16[128,4,2048]{2,1,0:T(4,128)(2,1)} custom-call(s32[1]{0:T(128)} %bitcast.rank_ref, bf16[256,1024]{1,0:T(8,128)(2,1)S(1)} %collective-permute-done.11.refs_0_, bf16[256,1024]{1,0:T(8,128)(2,1)S(1)} %collective-permute-done.13.refs_1_, ...), custom_call_target="tpu_custom_call", output_to_operand_aliasing={{}: (7, {})} | custom-call | flops 2147483648 | bytes 8388608 | tf_op jit(solution)/shard_map/out_project/pallas_call | solution.py:465
  132.5 0.2 collective-permute-done.9.refs_1_
  132.6 1.6 %out_project.11 = bf16[128,4,2048]{2,1,0:T(4,128)(2,1)} custom-call(s32[1]{0:T(128)} %bitcast.rank_ref, bf16[128,1024]{1,0:T(8,128)(2,1)S(1)} %collective-permute-done.7.refs_0_, bf16[128,1024]{1,0:T(8,128)(2,1)S(1)} %collective-permute-done.9.refs_1_, f32[128,2048]{1,0:T(8,128)S(1)} %out_project.7.refs_2_, ...), custom_call_target="tpu_custom_call", output_to_operand_aliasing={{}: (5, {})} | custom-call | flops 536870912 | bytes 4194304 | tf_op jit(solution)/shard_map/out_project/pallas_call | solution.py:465
  (31 shorter events, 0.2 us)
Async XLA Ops:
  4.1 7.6 %copy-start = (bf16[128,4,1024]{2,1,0:T(4,128)(2,1)S(1)}, bf16[128,4,1024]{2,1,0:T(4,128)(2,1)}, u32[]{:S(2)}) copy-start(bf16[128,4,1024]{2,1,0:T(4,128)(2,1)} %q_ref.13) | copy-start | bytes 3145732
  4.1 7.6 %copy-start.2 = (s32[128]{0:T(128)S(1)}, s32[128]{0:T(128)}, u32[]{:S(2)}) copy-start(s32[128]{0:T(128)} %param.12) | copy-start | bytes 1540
  4.1 7.6 %copy-start.3 = (s32[4]{0:T(128)S(1)}, s32[4]{0:T(128)}, u32[]{:S(2)}) copy-start(s32[4]{0:T(128)} %length_ref.9) | copy-start | bytes 52
  4.2 7.6 %copy-start.6 = (s32[12]{0:T(128)S(1)}, s32[12]{0:T(128)}, u32[]{:S(2)}) copy-start(s32[12]{0:T(128)} %table_ref.5) | copy-start | bytes 148
  4.2 15.4 %collective-permute-start.2 = (bf16[2,256,256]{2,1,0:T(8,128)(2,1)}, bf16[2,256,256]{2,1,0:T(8,128)(2,1)S(1)}, u32[]{:S(2)}, u32[]{:S(2)}) collective-permute-start(bf16[2,256,256]{2,1,0:T(8,128)(2,1)} %get-tuple-element.26), channel_id=1, source_target_pairs={{0,1},{1,0},{2,3},{3,2},{4,5},{5,4},{6,7},{7,6},{8,9},{9,8},{10,11... | collective-permute-start | bytes 786440 | tf_op jit(solution)/shard_map/ppermute | solution.py:384
  11.6 11.1 %collective-permute-start = (bf16[2,384,256]{2,1,0:T(8,128)(2,1)S(1)}, bf16[2,384,256]{2,1,0:T(8,128)(2,1)S(1)}, u32[]{:S(2)}, u32[]{:S(2)}) collective-permute-start(bf16[2,384,256]{2,1,0:T(8,128)(2,1)S(1)} %get-tuple-element.21), channel_id=1, source_target_pairs={{0,1},{1,0},{2,3},{3,2},{4,5},{5,4},{6,7},{7,6},{8,9},{9,8},{10,11... | collective-permute-start | bytes 1179656 | tf_op jit(solution)/shard_map/ppermute | solution.py:384
  11.8 1.1 copy-start.4
  12.9 21.0 %copy-start.1 = (s32[4]{0:T(128)S(1)}, s32[4]{0:T(128)}, u32[]{:S(2)}) copy-start(s32[4]{0:T(128)} %owner_ref.11) | copy-start | bytes 52
  19.6 17.4 %copy-start.5 = (bf16[1,12,128,256]{3,2,1,0:T(8,128)(2,1)S(1)}, bf16[1,12,128,256]{3,2,1,0:T(8,128)(2,1)}, u32[]{:S(2)}) copy-start(bf16[1,12,128,256]{3,2,1,0:T(8,128)(2,1)} %param.21) | copy-start | bytes 2359300
  19.6 14.2 %collective-permute-start.3 = (bf16[256,256]{1,0:T(8,128)(2,1)S(1)}, bf16[256,256]{1,0:T(8,128)(2,1)S(1)}, u32[]{:S(2)}, u32[]{:S(2)}) collective-permute-start(bf16[256,256]{1,0:T(8,128)(2,1)S(1)} %fusion.1), channel_id=1, source_target_pairs={{0,2},{1,3},{2,0},{3,1},{4,6},{5,7},{6,4},{7,5},{8,10},{9,11},{10,... | collective-permute-start | bytes 393224 | tf_op jit(solution)/shard_map/ppermute | solution.py:384
  22.7 22.1 %collective-permute-start.1 = (bf16[384,256]{1,0:T(8,128)(2,1)S(1)}, bf16[384,256]{1,0:T(8,128)(2,1)S(1)}, u32[]{:S(2)}, u32[]{:S(2)}) collective-permute-start(bf16[384,256]{1,0:T(8,128)(2,1)S(1)} %fusion), channel_id=1, source_target_pairs={{0,2},{1,3},{2,0},{3,1},{4,6},{5,7},{6,4},{7,5},{8,10},{9,11},{10,... | collective-permute-start | bytes 589832 | tf_op jit(solution)/shard_map/ppermute | solution.py:384
  35.0 5.4 %collective-permute-start.4 = (bf16[128,256]{1,0:T(8,128)(2,1)S(1)}, bf16[128,256]{1,0:T(8,128)(2,1)S(1)}, u32[]{:S(2)}, u32[]{:S(2)}) collective-permute-start(bf16[128,256]{1,0:T(8,128)(2,1)S(1)} %get-tuple-element.27.refs_0_), channel_id=1, source_target_pairs={{0,4},{4,0},{8,12},{12,8},{1,5},{5,1},{9,13},{13,9},{2,6},{6,2},{1... | collective-permute-start | bytes 196616 | tf_op jit(solution)/shard_map/ppermute | solution.py:384
  35.1 5.3 %collective-permute-start.5 = (bf16[128,256]{1,0:T(8,128)(2,1)S(1)}, bf16[128,256]{1,0:T(8,128)(2,1)S(1)}, u32[]{:S(2)}, u32[]{:S(2)}) collective-permute-start(bf16[128,256]{1,0:T(8,128)(2,1)S(1)} %get-tuple-element.27.refs_0_), channel_id=1, source_target_pairs={{0,8},{4,12},{8,0},{12,4},{1,9},{5,13},{9,1},{13,5},{2,10},{6,14},... | collective-permute-start | bytes 196616 | tf_op jit(solution)/shard_map/ppermute | solution.py:384
  36.8 4.1 %collective-permute-start.6 = (bf16[128,256]{1,0:T(8,128)(2,1)S(1)}, bf16[128,256]{1,0:T(8,128)(2,1)S(1)}, u32[]{:S(2)}, u32[]{:S(2)}) collective-permute-start(bf16[128,256]{1,0:T(8,128)(2,1)S(1)} %get-tuple-element.27.refs_0_), channel_id=1, source_target_pairs={{0,12},{4,8},{8,4},{12,0},{1,13},{5,9},{9,5},{13,1},{2,14},{6,10},... | collective-permute-start | bytes 196616 | tf_op jit(solution)/shard_map/ppermute | solution.py:384
  44.7 25.3 %collective-permute-start.17 = (bf16[128,1024]{1,0:T(8,128)(2,1)S(1)}, bf16[128,1024]{1,0:T(8,128)(2,1)S(1)}, u32[]{:S(2)}, u32[]{:S(2)}) collective-permute-start(bf16[128,1024]{1,0:T(8,128)(2,1)S(1)} %attend_new.7.refs_0_), channel_id=1, source_target_pairs={{0,2},{1,3},{2,0},{3,1},{4,6},{5,7},{6,4},{7,5},{8,10},{9,11},{10,... | collective-permute-start | bytes 786440 | tf_op jit(solution)/shard_map/ppermute | solution.py:384
  50.0 22.0 %collective-permute-start.15 = (bf16[128,1024]{1,0:T(8,128)(2,1)S(1)}, bf16[128,1024]{1,0:T(8,128)(2,1)S(1)}, u32[]{:S(2)}, u32[]{:S(2)}) collective-permute-start(bf16[128,1024]{1,0:T(8,128)(2,1)S(1)} %attend_new.5.refs_0_), channel_id=1, source_target_pairs={{0,1},{1,0},{2,3},{3,2},{4,5},{5,4},{6,7},{7,6},{8,9},{9,8},{10,11... | collective-permute-start | bytes 786440 | tf_op jit(solution)/shard_map/ppermute | solution.py:384
  57.2 39.5 %collective-permute-start.12 = (bf16[256,1024]{1,0:T(8,128)(2,1)S(1)}, bf16[256,1024]{1,0:T(8,128)(2,1)S(1)}, u32[]{:S(2)}, u32[]{:S(2)}) collective-permute-start(bf16[256,1024]{1,0:T(8,128)(2,1)S(1)} %pad_maximum_fusion), channel_id=1, source_target_pairs={{1,2},{2,1},{5,6},{6,5},{9,10},{10,9},{13,14},{14,13},{17,18},{18,... | collective-permute-start | bytes 1572872 | tf_op jit(solution)/shard_map/ppermute | solution.py:536
  57.9 40.1 %collective-permute-start.11 = (bf16[256,1024]{1,0:T(8,128)(2,1)S(1)}, bf16[256,1024]{1,0:T(8,128)(2,1)S(1)}, u32[]{:S(2)}, u32[]{:S(2)}) collective-permute-start(bf16[256,1024]{1,0:T(8,128)(2,1)S(1)} %pad_maximum_fusion), channel_id=1, source_target_pairs={{0,2},{3,1},{4,6},{7,5},{8,10},{11,9},{12,14},{15,13},{16,18},{19,... | collective-permute-start | bytes 1572872 | tf_op jit(solution)/shard_map/ppermute | solution.py:537
  66.0 14.4 %collective-permute-start.16 = (bf16[128,1024]{1,0:T(8,128)(2,1)S(1)}, bf16[128,1024]{1,0:T(8,128)(2,1)S(1)}, u32[]{:S(2)}, u32[]{:S(2)}) collective-permute-start(bf16[128,1024]{1,0:T(8,128)(2,1)S(1)} %attend_new.6.refs_1_), channel_id=1, source_target_pairs={{0,1},{1,0},{2,3},{3,2},{4,5},{5,4},{6,7},{7,6},{8,9},{9,8},{10,11... | collective-permute-start | bytes 786440 | tf_op jit(solution)/shard_map/ppermute | solution.py:384
  70.0 24.8 %collective-permute-start.8 = (bf16[128,1024]{1,0:T(8,128)(2,1)S(1)}, bf16[128,1024]{1,0:T(8,128)(2,1)S(1)}, u32[]{:S(2)}, u32[]{:S(2)}) collective-permute-start(bf16[128,1024]{1,0:T(8,128)(2,1)S(1)} %attend_new.4.refs_0_), channel_id=1, source_target_pairs={{0,2},{1,3},{2,0},{3,1},{4,6},{5,7},{6,4},{7,5},{8,10},{9,11},{10,... | collective-permute-start | bytes 786440 | tf_op jit(solution)/shard_map/ppermute | solution.py:384
  72.0 23.4 %collective-permute-start.10 = (bf16[128,1024]{1,0:T(8,128)(2,1)S(1)}, bf16[128,1024]{1,0:T(8,128)(2,1)S(1)}, u32[]{:S(2)}, u32[]{:S(2)}) collective-permute-start(bf16[128,1024]{1,0:T(8,128)(2,1)S(1)} %attend_new.4.refs_0_), channel_id=1, source_target_pairs={{0,1},{1,0},{2,3},{3,2},{4,5},{5,4},{6,7},{7,6},{8,9},{9,8},{10,11... | collective-permute-start | bytes 786440 | tf_op jit(solution)/shard_map/ppermute | solution.py:384
  80.4 29.6 %collective-permute-start.18 = (bf16[128,1024]{1,0:T(8,128)(2,1)S(1)}, bf16[128,1024]{1,0:T(8,128)(2,1)S(1)}, u32[]{:S(2)}, u32[]{:S(2)}) collective-permute-start(bf16[128,1024]{1,0:T(8,128)(2,1)S(1)} %attend_new.7.refs_0_), channel_id=1, source_target_pairs={{0,1},{1,0},{2,3},{3,2},{4,5},{5,4},{6,7},{7,6},{8,9},{9,8},{10,11... | collective-permute-start | bytes 786440 | tf_op jit(solution)/shard_map/ppermute | solution.py:384
  94.7 15.9 %collective-permute-start.19 = (bf16[128,1024]{1,0:T(8,128)(2,1)S(1)}, bf16[128,1024]{1,0:T(8,128)(2,1)S(1)}, u32[]{:S(2)}, u32[]{:S(2)}) collective-permute-start(bf16[128,1024]{1,0:T(8,128)(2,1)S(1)} %attend_new.7.refs_0_), channel_id=1, source_target_pairs={{1,2},{2,1},{5,6},{6,5},{9,10},{10,9},{13,14},{14,13},{17,18},{18,... | collective-permute-start | bytes 786440 | tf_op jit(solution)/shard_map/ppermute | solution.py:526
  95.4 16.8 %collective-permute-start.20 = (bf16[128,1024]{1,0:T(8,128)(2,1)S(1)}, bf16[128,1024]{1,0:T(8,128)(2,1)S(1)}, u32[]{:S(2)}, u32[]{:S(2)}) collective-permute-start(bf16[128,1024]{1,0:T(8,128)(2,1)S(1)} %collective-permute-done.17.refs_1_), channel_id=1, source_target_pairs={{1,0},{2,3},{5,4},{6,7},{9,8},{10,11},{13,12},{14,15},{17,16},{18,... | collective-permute-start | bytes 786440 | tf_op jit(solution)/shard_map/ppermute | solution.py:527
  96.7 22.6 %collective-permute-start.13 = (bf16[256,1024]{1,0:T(8,128)(2,1)S(1)}, bf16[256,1024]{1,0:T(8,128)(2,1)S(1)}, u32[]{:S(2)}, u32[]{:S(2)}) collective-permute-start(bf16[256,1024]{1,0:T(8,128)(2,1)S(1)} %collective-permute-done.12.refs_2_), channel_id=1, source_target_pairs={{1,0},{2,3},{5,4},{6,7},{9,8},{10,11},{13,12},{14,15},{17,16},{18,... | collective-permute-start | bytes 1572872 | tf_op jit(solution)/shard_map/ppermute | solution.py:539
  98.0 30.9 %collective-permute-start.14 = (bf16[256,1024]{1,0:T(8,128)(2,1)S(1)}, bf16[256,1024]{1,0:T(8,128)(2,1)S(1)}, u32[]{:S(2)}, u32[]{:S(2)}) collective-permute-start(bf16[256,1024]{1,0:T(8,128)(2,1)S(1)} %collective-permute-done.11.refs_0_), channel_id=1, source_target_pairs={{1,0},{2,3},{5,4},{6,7},{9,8},{10,11},{13,12},{14,15},{17,16},{18,... | collective-permute-start | bytes 1572872 | tf_op jit(solution)/shard_map/ppermute | solution.py:540
  110.0 22.5 %collective-permute-start.7 = (bf16[128,1024]{1,0:T(8,128)(2,1)S(1)}, bf16[128,1024]{1,0:T(8,128)(2,1)S(1)}, u32[]{:S(2)}, u32[]{:S(2)}) collective-permute-start(bf16[128,1024]{1,0:T(8,128)(2,1)S(1)} %attend_new.4.refs_0_), channel_id=1, source_target_pairs={{1,2},{2,1},{5,6},{6,5},{9,10},{10,9},{13,14},{14,13},{17,18},{18,... | collective-permute-start | bytes 786440 | tf_op jit(solution)/shard_map/ppermute | solution.py:526
  110.7 21.9 %collective-permute-start.9 = (bf16[128,1024]{1,0:T(8,128)(2,1)S(1)}, bf16[128,1024]{1,0:T(8,128)(2,1)S(1)}, u32[]{:S(2)}, u32[]{:S(2)}) collective-permute-start(bf16[128,1024]{1,0:T(8,128)(2,1)S(1)} %collective-permute-done.8.refs_1_), channel_id=1, source_target_pairs={{1,0},{2,3},{5,4},{6,7},{9,8},{10,11},{13,12},{14,15},{17,16},{18,... | collective-permute-start | bytes 786440 | tf_op jit(solution)/shard_map/ppermute | solution.py:527

commit v5 on v4

--- a/solution.py
+++ b/solution.py
@@ -520,25 +520,22 @@
     return pltpu.with_memory_space_constraint(held, pltpu.VMEM)
 
 
-def gather_heads(own):
-    far = swap(own, "tensor", 2)
-    near = swap(own, "tensor", 1)
-    across = lax.ppermute(own, "tensor", [(1, 2), (2, 1)])
-    passed = lax.ppermute(far, "tensor", [(1, 0), (2, 3)])
-    return far, near, across, passed
-
-
-def relay_heads(groups):
+def near_heads(groups):
     near = []
     for group in groups:
         near.append(swap(group, "tensor", 1))
-    own = jnp.concatenate(groups, 0)
+    return near
+
+
+def far_heads(own, relay):
+    outward = [(1, 0), (2, 3)]
+    far = lax.ppermute(own, "tensor", [(0, 2), (3, 1)]) if relay else swap(own, "tensor", 2)
     across = lax.ppermute(own, "tensor", [(1, 2), (2, 1)])
-    far = lax.ppermute(own, "tensor", [(0, 2), (3, 1)])
-    outward = [(1, 0), (2, 3)]
-    forward = lax.ppermute(across, "tensor", outward)
+    forward = None
+    if relay:
+        forward = lax.ppermute(across, "tensor", outward)
     passed = lax.ppermute(far, "tensor", outward)
-    return near, far, across, forward, passed
+    return (2, [far], forward), (3, [across], passed)
 
 
 def on_device(
@@ -668,26 +665,26 @@
     middle_old = old_part(1, middle)
     middle_own = [new_part(rest_tails[i], middle_old, 1 + i, i) for i in range(middle)]
     last_own = new_part(rest_tails[-1], old_part(blocks - 1, 1), blocks - 1)
-    far, near, across, passed = gather_heads(first_own)
-    pieces = ((0, [first_own], None), (2, [far], None), (1, [near], None), (3, [across], passed))
-    decoded = out_project(rank, pieces, out_weight, shape, 0)
-    near, far, across, forward, passed = relay_heads(middle_own)
+    near = near_heads([first_own])
+    two, three = far_heads(first_own, False)
+    decoded = out_project(
+        rank, ((0, [first_own], None), two, (1, near, None), three), out_weight, shape, 0
+    )
     held = (2, 3)
     held_rows = hold(rank, held, out_weight, first_own.shape[1])
-    pieces = ((0, middle_own, None), (1, near, None))
+    near = near_heads(middle_own)
+    two, three = far_heads(jnp.concatenate(middle_own, 0), False)
+    pieces = ((0, middle_own, None), (1, near, None), two)
     partial = out_project(rank, pieces, out_weight, shape, 0, final=False)
-    pieces = ((2, [far], forward), (3, [across], passed))
     decoded = out_project(
-        rank, pieces, held_rows, shape, first, partial=partial, into=decoded, held=held
-    )
-    far, near, across, passed = gather_heads(last_own)
-    pieces = ((0, [last_own], None), (2, [far], None))
+        rank, (three,), held_rows, shape, first, partial=partial, into=decoded, held=held
+    )
+    near = near_heads([last_own])
+    two, three = far_heads(last_own, True)
+    pieces = ((0, [last_own], None), (1, near, None))
     partial = out_project(rank, pieces, out_weight, shape, 0, final=False)
-    partial = out_project(
-        rank, ((1, [near], None),), out_weight, shape, 0, partial=partial, final=False
-    )
     return out_project(
-        rank, ((3, [across], passed),), held_rows, shape, first * (blocks - 1),
+        rank, (two, three), held_rows, shape, first * (blocks - 1),
         partial=partial, into=decoded, held=held,
     )
 

time: 135 us -> 125 us (0.926)
  waiting for transfers between devices: 35 us -> 13.2 us
  starting transfers between devices: 31.1 us -> 45.1 us
  Pallas kernels: 66.4 us -> 64.7 us
    ppermute x13, waiting for transfers between devices: 25.2 us -> 8.54 us  [swap(): lax.ppermute(x, axis, [(i, i ^ bit) for i in range(lax.axis_size(axis))])]
    ppermute x13, starting transfers between devices: 19 us -> 33 us  [swap(): lax.ppermute(x, axis, [(i, i ^ bit) for i in range(lax.axis_size(axis))])]
    ppermute x8, waiting for transfers between devices: 9.8 us -> 4.7 us  [the longest x1 3.92 us: far_heads(): forward = lax.ppermute(across, 'tensor', outward)]
    pallas_call x6 -> x5, Pallas kernels: 22.8 us -> 21.1 us  [out_project(): pl.pallas_call(functools.partial(out_kernel, rels, shapes, cuts, partial...]
  transfers between devices with their start and end apart: 21 -> 21, of which waited for: 6 -> 4; matrix products, arithmetic and copies ran while one was open for 0% -> 0% of each run, Pallas kernels for 45% -> 47%
where the time goes in v5:
time: 125 us
  Pallas kernels  64.7 us (52%)
  starting transfers between devices  45.1 us (36%)
  waiting for transfers between devices  13.2 us (11%)
    ppermute x13, starting transfers between devices, swap(): lax.ppermute(x, axis, [(i, i ^ bit) for i in range(lax.axis_size(axis))])  33 us
    pallas_call x5, Pallas kernels, out_project(): pl.pallas_call(functools.partial(out_kernel, rels, shapes, cuts, partial...  21.1 us
    pallas_call x4, Pallas kernels, attend_new(): pl.pallas_call(functools.partial(new_kernel, heads, steps, LOG2E / math.s...  15.6 us
    pallas_call x3, Pallas kernels, attend_cached(): pl.pallas_call(functools.partial(cached_kernel, heads, cpages, LOG2E / ma...  13.6 us
    ppermute x13, waiting for transfers between devices, swap(): lax.ppermute(x, axis, [(i, i ^ bit) for i in range(lax.axis_size(axis))])  8.54 us
    pallas_call x2, Pallas kernels, project(): pl.pallas_call(functools.partial(project_kernel, len(groups), split, kept...  8.39 us
    ppermute x1, starting transfers between devices, far_heads(): lax.ppermute(own, 'tensor', [(0, 2), (3, 1)])  4.6 us
    ppermute x1, waiting for transfers between devices, far_heads(): forward = lax.ppermute(across, 'tensor', outward)  3.92 us
  transfers between devices with their start and end apart: 21, of which 4 were waited for; matrix products, arithmetic and copies ran while one was open for 0% of the time, Pallas kernels for 47%

profile of v5, /device:TPU:0, one launch (start us, length us, event | category | flops | bytes accessed | tf_op | source)
XLA Modules:
  0.0 124.8 jit_solution(6933019926189554641)
XLA Ops:
  0.0 4.1 %project.3 = (f32[2,256,256]{2,1,0:T(8,128)S(1)}, bf16[2,256,256]{2,1,0:T(8,128)(2,1)}) custom-call(s32[1]{0:T(128)} %bitcast.rank_ref, bf16[128,2048]{1,0:T(8,128)(2,1)} %refs_0_.3, bf16[128,4,2048]{2,1,0:T(4,128)(2,1)} %refs_1_.3, bf16[2048,512]{1,0:T(8,128)(2,1)} %refs_4_.3, bf16[2048,512]{1,0:T(8,128)(2,1)} %refs_5_.3, bf16[2048,512]{1,0:T(8,128)(2,1)} %refs_4_.3, ...), custom_call_target="tpu_custom_call" | custom-call | flops 1073741824 | bytes 4194304 | tf_op jit(solution)/shard_map/project/pallas_call | solution.py:299
  4.1 0.0 copy-start.3
  4.2 0.0 copy-start.6
  4.2 3.1 %collective-permute-start.2 = (bf16[2,256,256]{2,1,0:T(8,128)(2,1)}, bf16[2,256,256]{2,1,0:T(8,128)(2,1)S(1)}, u32[]{:S(2)}, u32[]{:S(2)}) collective-permute-start(bf16[2,256,256]{2,1,0:T(8,128)(2,1)} %get-tuple-element.26), channel_id=1, source_target_pairs={{0,1},{1,0},{2,3},{3,2},{4,5},{5,4},{6,7},{7,6},{8,9},{9,8},{10,11... | collective-permute-start | bytes 786440 | tf_op jit(solution)/shard_map/ppermute | solution.py:384
  7.3 4.3 %project.2 = (f32[2,384,256]{2,1,0:T(8,128)S(1)}, bf16[2,384,256]{2,1,0:T(8,128)(2,1)S(1)}) custom-call(s32[1]{0:T(128)} %bitcast.rank_ref, bf16[128,4,2048]{2,1,0:T(4,128)(2,1)} %refs_1_.3, bf16[2048,512]{1,0:T(8,128)(2,1)} %refs_4_.3, bf16[2048,512]{1,0:T(8,128)(2,1)} %refs_5_.3, bf16[2048,512]{1,0:T(8,128)(2,1)} %refs_4_.3, bf16[2048,512]{1,0:T(8,128)(2,1)} %refs_5_.3), custom_call_target="tpu_custom_call" | custom-call | flops 1610612736 | bytes 4194304 | tf_op jit(solution)/shard_map/project/pallas_call | solution.py:299
  11.6 0.2 collective-permute-start
  11.8 0.0 copy-start.4
  11.8 1.1 copy-done.4
  12.9 6.7 %attend_cached.4 = (f32[8,256,128]{2,1,0:T(8,128)S(1)}, f32[8,256,128]{2,1,0:T(8,128)S(1)}) custom-call(s32[12]{0:T(128)S(1)} %copy-done.6, s32[4]{0:T(128)S(1)} %copy-done.3, bf16[128,4,1024]{2,1,0:T(4,128)(2,1)S(1)} %copy-done, s32[1,128]{1,0:T(1,128)S(1)} %bitcast.10, bf16[12,128,256]{2,1,0:T(8,128)(2,1)S(1)} %bitcast.19), custom_call_target="tpu_custom_call" | custom-call | flops 1610612736 | bytes 2097152 | tf_op jit(solution)/shard_map/attend_cached/pallas_call | solution.py:194
  19.6 0.0 copy-start.5
  19.6 3.0 %collective-permute-start.3 = (bf16[256,256]{1,0:T(8,128)(2,1)S(1)}, bf16[256,256]{1,0:T(8,128)(2,1)S(1)}, u32[]{:S(2)}, u32[]{:S(2)}) collective-permute-start(bf16[256,256]{1,0:T(8,128)(2,1)S(1)} %fusion.1), channel_id=1, source_target_pairs={{0,2},{1,3},{2,0},{3,1},{4,6},{5,7},{6,4},{7,5},{8,10},{9,11},{10,... | collective-permute-start | bytes 393224 | tf_op jit(solution)/shard_map/ppermute | solution.py:384
  22.7 3.0 %collective-permute-start.1 = (bf16[384,256]{1,0:T(8,128)(2,1)S(1)}, bf16[384,256]{1,0:T(8,128)(2,1)S(1)}, u32[]{:S(2)}, u32[]{:S(2)}) collective-permute-start(bf16[384,256]{1,0:T(8,128)(2,1)S(1)} %fusion), channel_id=1, source_target_pairs={{0,2},{1,3},{2,0},{3,1},{4,6},{5,7},{6,4},{7,5},{8,10},{9,11},{10,... | collective-permute-start | bytes 589832 | tf_op jit(solution)/shard_map/ppermute | solution.py:384
  25.7 0.1 maximum_bitcast_fusion.freq_ref
  25.7 8.1 %collective-permute-done.3.refs_1_ = bf16[256,256]{1,0:T(8,128)(2,1)S(1)} collective-permute-done((bf16[256,256]{1,0:T(8,128)(2,1)S(1)}, bf16[256,256]{1,0:T(8,128)(2,1)S(1)}, u32[]{:S(2)}, u32[]{:S(2)}) %collective-permute-start.3) | collective-permute-done | bytes 131104 | tf_op jit(solution)/shard_map/ppermute | solution.py:384
  33.9 1.2 finish.3
  35.0 0.1 collective-permute-start.4
  35.1 1.7 %collective-permute-start.5 = (bf16[128,256]{1,0:T(8,128)(2,1)S(1)}, bf16[128,256]{1,0:T(8,128)(2,1)S(1)}, u32[]{:S(2)}, u32[]{:S(2)}) collective-permute-start(bf16[128,256]{1,0:T(8,128)(2,1)S(1)} %get-tuple-element.27.refs_0_), channel_id=1, source_target_pairs={{0,8},{4,12},{8,0},{12,4},{1,9},{5,13},{9,1},{13,5},{2,10},{6,14},... | collective-permute-start | bytes 196616 | tf_op jit(solution)/shard_map/ppermute | solution.py:384
  36.8 0.2 collective-permute-start.6
  37.0 3.4 %attend_cached.5 = (f32[8,128,128]{2,1,0:T(8,128)S(1)}, f32[8,128,128]{2,1,0:T(8,128)S(1)}) custom-call(s32[12]{0:T(128)S(1)} %copy-done.6, s32[4]{0:T(128)S(1)} %copy-done.3, bf16[128,4,1024]{2,1,0:T(4,128)(2,1)S(1)} %copy-done, s32[1,128]{1,0:T(1,128)S(1)} %bitcast.12, bf16[12,128,256]{2,1,0:T(8,128)(2,1)S(1)} %bitcast.20), custom_call_target="tpu_custom_call" | custom-call | flops 805306368 | bytes 1048576 | tf_op jit(solution)/shard_map/attend_cached/pallas_call | solution.py:194
  40.4 0.4 collective-permute-done.6.refs_3_
  40.8 3.8 %attend_new.7.refs_0_ = bf16[128,1024]{1,0:T(8,128)(2,1)S(1)} custom-call(s32[4]{0:T(128)S(1)} %copy-done.1, s32[1]{0:T(128)} %bitcast.1.replica_ref.base_ref, bf16[128,4,1024]{2,1,0:T(4,128)(2,1)S(1)} %copy-done, s32[1,128]{1,0:T(1,128)S(1)} %bitcast.13, bf16[128,256]{1,0:T(8,128)(2,1)S(1)} %get-tuple-element.32.tail_ref, ...), custom_call_target="tpu_custom_call" | custom-call | flops 335544320 | bytes 1310720 | tf_op jit(solution)/shard_map/attend_new/pallas_call | solution.py:226
  44.7 0.1 collective-permute-start.17
  44.8 3.0 %collective-permute-start.18 = (bf16[128,1024]{1,0:T(8,128)(2,1)S(1)}, bf16[128,1024]{1,0:T(8,128)(2,1)S(1)}, u32[]{:S(2)}, u32[]{:S(2)}) collective-permute-start(bf16[128,1024]{1,0:T(8,128)(2,1)S(1)} %attend_new.7.refs_0_), channel_id=1, source_target_pairs={{0,1},{1,0},{2,3},{3,2},{4,5},{5,4},{6,7},{7,6},{8,9},{9,8},{10,11... | collective-permute-start | bytes 786440 | tf_op jit(solution)/shard_map/ppermute | solution.py:384
  47.8 1.4 %finish.2 = (bf16[128,256]{1,0:T(8,128)(2,1)S(1)}, bf16[128,256]{1,0:T(8,128)(2,1)S(1)}, bf16[128,256]{1,0:T(8,128)(2,1)S(1)}) custom-call(s32[4]{0:T(128)S(1)} %copy-done.1, s32[4]{0:T(128)S(1)} %copy-done.3, s32[1]{0:T(128)} %bitcast.1.replica_ref.base_ref, s32[1,128]{1,0:T(1,128)S(1)} %bitcast.14, f32[1,128]{1,0:T(1,128)S(1)} %maximum_bitcast_fusion.freq_ref, ...), custom_call_target="tpu_custom_call" | custom-call | tf_op jit(solution)/shard_map/finish/pallas_call | solution.py:368
  49.2 3.8 %attend_new.5.refs_0_ = bf16[128,1024]{1,0:T(8,128)(2,1)S(1)} custom-call(s32[4]{0:T(128)S(1)} %copy-done.1, s32[1]{0:T(128)} %bitcast.1.replica_ref.base_ref, bf16[128,4,1024]{2,1,0:T(4,128)(2,1)S(1)} %copy-done, s32[1,128]{1,0:T(1,128)S(1)} %bitcast.15, bf16[128,256]{1,0:T(8,128)(2,1)S(1)} %get-tuple-element.28.tail_ref, ...), custom_call_target="tpu_custom_call" | custom-call | flops 335544320 | bytes 1310720 | tf_op jit(solution)/shard_map/attend_new/pallas_call | solution.py:226
  53.1 4.1 %attend_new.6.refs_1_ = bf16[128,1024]{1,0:T(8,128)(2,1)S(1)} custom-call(s32[4]{0:T(128)S(1)} %copy-done.1, s32[1]{0:T(128)} %bitcast.1.replica_ref.base_ref, bf16[128,4,1024]{2,1,0:T(4,128)(2,1)S(1)} %copy-done, s32[1,128]{1,0:T(1,128)S(1)} %bitcast.16, bf16[128,256]{1,0:T(8,128)(2,1)S(1)} %get-tuple-element.31.tail_ref, ...), custom_call_target="tpu_custom_call" | custom-call | flops 335544320 | bytes 1310720 | tf_op jit(solution)/shard_map/attend_new/pallas_call | solution.py:226
  57.2 0.1 collective-permute-start.13
  57.3 3.4 %attend_cached.3 = (f32[8,128,128]{2,1,0:T(8,128)S(1)}, f32[8,128,128]{2,1,0:T(8,128)S(1)}) custom-call(s32[12]{0:T(128)S(1)} %copy-done.6, s32[4]{0:T(128)S(1)} %copy-done.3, bf16[128,4,1024]{2,1,0:T(4,128)(2,1)S(1)} %copy-done, s32[1,128]{1,0:T(1,128)S(1)} %bitcast.17, bf16[12,128,256]{2,1,0:T(8,128)(2,1)S(1)} %bitcast.21), custom_call_target="tpu_custom_call" | custom-call | flops 805306368 | bytes 1048576 | tf_op jit(solution)/shard_map/attend_cached/pallas_call | solution.py:194
  60.8 0.7 collective-permute-start.19
  61.4 4.7 %collective-permute-start.15 = (bf16[128,1024]{1,0:T(8,128)(2,1)S(1)}, bf16[128,1024]{1,0:T(8,128)(2,1)S(1)}, u32[]{:S(2)}, u32[]{:S(2)}) collective-permute-start(bf16[128,1024]{1,0:T(8,128)(2,1)S(1)} %attend_new.5.refs_0_), channel_id=1, source_target_pairs={{0,1},{1,0},{2,3},{3,2},{4,5},{5,4},{6,7},{7,6},{8,9},{9,8},{10,11... | collective-permute-start | bytes 786440 | tf_op jit(solution)/shard_map/ppermute | solution.py:384
  66.1 3.8 %attend_new.4.refs_0_ = bf16[128,1024]{1,0:T(8,128)(2,1)S(1)} custom-call(s32[4]{0:T(128)S(1)} %copy-done.1, s32[1]{0:T(128)} %bitcast.1.replica_ref.base_ref, bf16[128,4,1024]{2,1,0:T(4,128)(2,1)S(1)} %copy-done, s32[1,128]{1,0:T(1,128)S(1)} %bitcast.18, bf16[128,256]{1,0:T(8,128)(2,1)S(1)} %get-tuple-element.22.tail_ref, ...), custom_call_target="tpu_custom_call" | custom-call | flops 335544320 | bytes 1310720 | tf_op jit(solution)/shard_map/attend_new/pallas_call | solution.py:226
  70.0 0.1 collective-permute-start.11
  70.1 1.3 %collective-permute-start.20 = (bf16[128,1024]{1,0:T(8,128)(2,1)S(1)}, bf16[128,1024]{1,0:T(8,128)(2,1)S(1)}, u32[]{:S(2)}, u32[]{:S(2)}) collective-permute-start(bf16[128,1024]{1,0:T(8,128)(2,1)S(1)} %collective-permute-done.17.refs_1_), channel_id=1, source_target_pairs={{1,0},{2,3},{5,4},{6,7},{9,8},{10,11},{13,12},{14,15},{17,16},{18,... | collective-permute-start | bytes 786440 | tf_op jit(solution)/shard_map/ppermute | solution.py:537
  71.4 3.5 %hold.1.refs_3_.refs_5_ = bf16[2048,2048]{1,0:T(8,128)(2,1)S(1)} custom-call(s32[1]{0:T(128)} %bitcast.rank_ref, bf16[4096,2048]{1,0:T(8,128)(2,1)} %refs_5_.5), custom_call_target="tpu_custom_call" | custom-call | tf_op jit(solution)/shard_map/hold/pallas_call | solution.py:507
  74.9 13.8 %collective-permute-start.16 = (bf16[128,1024]{1,0:T(8,128)(2,1)S(1)}, bf16[128,1024]{1,0:T(8,128)(2,1)S(1)}, u32[]{:S(2)}, u32[]{:S(2)}) collective-permute-start(bf16[128,1024]{1,0:T(8,128)(2,1)S(1)} %attend_new.6.refs_1_), channel_id=1, source_target_pairs={{0,1},{1,0},{2,3},{3,2},{4,5},{5,4},{6,7},{7,6},{8,9},{9,8},{10,11... | collective-permute-start | bytes 786440 | tf_op jit(solution)/shard_map/ppermute | solution.py:384
  88.7 0.7 collective-permute-start.12
  89.4 4.6 %collective-permute-start.7 = (bf16[128,1024]{1,0:T(8,128)(2,1)S(1)}, bf16[128,1024]{1,0:T(8,128)(2,1)S(1)}, u32[]{:S(2)}, u32[]{:S(2)}) collective-permute-start(bf16[128,1024]{1,0:T(8,128)(2,1)S(1)} %attend_new.4.refs_0_), channel_id=1, source_target_pairs={{0,2},{3,1},{4,6},{7,5},{8,10},{11,9},{12,14},{15,13},{16,18},{19,... | collective-permute-start | bytes 786440 | tf_op jit(solution)/shard_map/ppermute | solution.py:532
  94.0 0.8 collective-permute-done.20.refs_4_
  94.8 0.7 collective-permute-start.8
  95.5 1.3 %collective-permute-start.14 = (bf16[256,1024]{1,0:T(8,128)(2,1)S(1)}, bf16[256,1024]{1,0:T(8,128)(2,1)S(1)}, u32[]{:S(2)}, u32[]{:S(2)}) collective-permute-start(bf16[256,1024]{1,0:T(8,128)(2,1)S(1)} %collective-permute-done.13.refs_4_), channel_id=1, source_target_pairs={{1,0},{2,3},{5,4},{6,7},{9,8},{10,11},{13,12},{14,15},{17,16},{18,... | collective-permute-start | bytes 1572872 | tf_op jit(solution)/shard_map/ppermute | solution.py:537
  96.8 3.8 %out_project.5.refs_4_ = f32[128,2048]{1,0:T(8,128)S(1)} custom-call(s32[1]{0:T(128)} %bitcast.rank_ref, bf16[128,1024]{1,0:T(8,128)(2,1)S(1)} %attend_new.4.refs_0_, bf16[128,1024]{1,0:T(8,128)(2,1)S(1)} %collective-permute-done.11.refs_1_, bf16[4096,2048]{1,0:T(8,128)(2,1)} %refs_5_.5), custom_call_target="tpu_custom_call" | custom-call | flops 1073741824 | bytes 8388608 | tf_op jit(solution)/shard_map/out_project/pallas_call | solution.py:465
  100.6 7.1 %out_project.7.refs_4_ = bf16[128,4,2048]{2,1,0:T(4,128)(2,1)} custom-call(s32[1]{0:T(128)} %bitcast.rank_ref, bf16[128,1024]{1,0:T(8,128)(2,1)S(1)} %attend_new.7.refs_0_, bf16[128,1024]{1,0:T(8,128)(2,1)S(1)} %collective-permute-done.17.refs_1_, bf16[128,1024]{1,0:T(8,128)(2,1)S(1)} %collective-permute-done.18.refs_2_, ...), custom_call_target="tpu_custom_call" | custom-call | flops 2147483648 | bytes 16777216 | tf_op jit(solution)/shard_map/out_project/pallas_call | solution.py:465
  107.7 1.3 %collective-permute-start.10 = (bf16[128,1024]{1,0:T(8,128)(2,1)S(1)}, bf16[128,1024]{1,0:T(8,128)(2,1)S(1)}, u32[]{:S(2)}, u32[]{:S(2)}) collective-permute-start(bf16[128,1024]{1,0:T(8,128)(2,1)S(1)} %collective-permute-done.7.refs_0_), channel_id=1, source_target_pairs={{1,0},{2,3},{5,4},{6,7},{9,8},{10,11},{13,12},{14,15},{17,16},{18,... | collective-permute-start | bytes 786440 | tf_op jit(solution)/shard_map/ppermute | solution.py:537
  109.0 1.6 %collective-permute-start.9 = (bf16[128,1024]{1,0:T(8,128)(2,1)S(1)}, bf16[128,1024]{1,0:T(8,128)(2,1)S(1)}, u32[]{:S(2)}, u32[]{:S(2)}) collective-permute-start(bf16[128,1024]{1,0:T(8,128)(2,1)S(1)} %collective-permute-done.8.refs_2_), channel_id=1, source_target_pairs={{1,0},{2,3},{5,4},{6,7},{9,8},{10,11},{13,12},{14,15},{17,16},{18,... | collective-permute-start | bytes 786440 | tf_op jit(solution)/shard_map/ppermute | solution.py:536
  110.6 5.7 %out_project.6.refs_2_ = f32[256,2048]{1,0:T(8,128)S(1)} custom-call(s32[1]{0:T(128)} %bitcast.rank_ref, bf16[128,1024]{1,0:T(8,128)(2,1)S(1)} %attend_new.5.refs_0_, bf16[128,1024]{1,0:T(8,128)(2,1)S(1)} %attend_new.6.refs_1_, bf16[128,1024]{1,0:T(8,128)(2,1)S(1)} %collective-permute-done.15.refs_2_, bf16[128,1024]{1,0:T(8,128)(2,1)S(1)} %collective-permute-done.16.refs_3_, ...), custom_call_target="tpu_custom_call" | custom-call | flops 3221225472 | bytes 12582912 | tf_op jit(solution)/shard_map/out_project/pallas_call | solution.py:465
  116.3 2.4 %out_project.8.refs_6_ = bf16[128,4,2048]{2,1,0:T(4,128)(2,1)} custom-call(s32[1]{0:T(128)} %bitcast.rank_ref, bf16[256,1024]{1,0:T(8,128)(2,1)S(1)} %collective-permute-done.12.refs_0_, bf16[256,1024]{1,0:T(8,128)(2,1)S(1)} %collective-permute-done.14.refs_1_, f32[256,2048]{1,0:T(8,128)S(1)} %out_project.6.refs_2_, ...), custom_call_target="tpu_custom_call", output_to_operand_aliasing={{}: (5, {})} | custom-call | flops 1073741824 | bytes 4194304 | tf_op jit(solution)/shard_map/out_project/pallas_call | solution.py:465
  118.7 3.9 %collective-permute-done.9.refs_1_ = bf16[128,1024]{1,0:T(8,128)(2,1)S(1)} collective-permute-done((bf16[128,1024]{1,0:T(8,128)(2,1)S(1)}, bf16[128,1024]{1,0:T(8,128)(2,1)S(1)}, u32[]{:S(2)}, u32[]{:S(2)}) %collective-permute-start.9) | collective-permute-done | bytes 262176 | tf_op jit(solution)/shard_map/ppermute | solution.py:536
  122.6 2.2 %out_project.9 = bf16[128,4,2048]{2,1,0:T(4,128)(2,1)} custom-call(s32[1]{0:T(128)} %bitcast.rank_ref, bf16[128,1024]{1,0:T(8,128)(2,1)S(1)} %collective-permute-done.7.refs_0_, bf16[128,1024]{1,0:T(8,128)(2,1)S(1)} %collective-permute-done.9.refs_1_, bf16[128,1024]{1,0:T(8,128)(2,1)S(1)} %collective-permute-done.8.refs_2_, ...), custom_call_target="tpu_custom_call", output_to_operand_aliasing={{}: (7, {})} | custom-call | flops 1073741824 | bytes 8388608 | tf_op jit(solution)/shard_map/out_project/pallas_call | solution.py:465
  (30 shorter events, 0.2 us)
Async XLA Ops:
  4.1 7.6 %copy-start = (bf16[128,4,1024]{2,1,0:T(4,128)(2,1)S(1)}, bf16[128,4,1024]{2,1,0:T(4,128)(2,1)}, u32[]{:S(2)}) copy-start(bf16[128,4,1024]{2,1,0:T(4,128)(2,1)} %q_ref.13) | copy-start | bytes 3145732
  4.1 7.6 %copy-start.2 = (s32[128]{0:T(128)S(1)}, s32[128]{0:T(128)}, u32[]{:S(2)}) copy-start(s32[128]{0:T(128)} %param.12) | copy-start | bytes 1540
  4.1 7.6 %copy-start.3 = (s32[4]{0:T(128)S(1)}, s32[4]{0:T(128)}, u32[]{:S(2)}) copy-start(s32[4]{0:T(128)} %length_ref.9) | copy-start | bytes 52
  4.2 7.6 %copy-start.6 = (s32[12]{0:T(128)S(1)}, s32[12]{0:T(128)}, u32[]{:S(2)}) copy-start(s32[12]{0:T(128)} %table_ref.5) | copy-start | bytes 148
  4.2 15.4 %collective-permute-start.2 = (bf16[2,256,256]{2,1,0:T(8,128)(2,1)}, bf16[2,256,256]{2,1,0:T(8,128)(2,1)S(1)}, u32[]{:S(2)}, u32[]{:S(2)}) collective-permute-start(bf16[2,256,256]{2,1,0:T(8,128)(2,1)} %get-tuple-element.26), channel_id=1, source_target_pairs={{0,1},{1,0},{2,3},{3,2},{4,5},{5,4},{6,7},{7,6},{8,9},{9,8},{10,11... | collective-permute-start | bytes 786440 | tf_op jit(solution)/shard_map/ppermute | solution.py:384
  11.6 11.1 %collective-permute-start = (bf16[2,384,256]{2,1,0:T(8,128)(2,1)S(1)}, bf16[2,384,256]{2,1,0:T(8,128)(2,1)S(1)}, u32[]{:S(2)}, u32[]{:S(2)}) collective-permute-start(bf16[2,384,256]{2,1,0:T(8,128)(2,1)S(1)} %get-tuple-element.21), channel_id=1, source_target_pairs={{0,1},{1,0},{2,3},{3,2},{4,5},{5,4},{6,7},{7,6},{8,9},{9,8},{10,11... | collective-permute-start | bytes 1179656 | tf_op jit(solution)/shard_map/ppermute | solution.py:384
  11.8 1.1 copy-start.4
  12.9 21.0 %copy-start.1 = (s32[4]{0:T(128)S(1)}, s32[4]{0:T(128)}, u32[]{:S(2)}) copy-start(s32[4]{0:T(128)} %owner_ref.11) | copy-start | bytes 52
  19.6 17.4 %copy-start.5 = (bf16[1,12,128,256]{3,2,1,0:T(8,128)(2,1)S(1)}, bf16[1,12,128,256]{3,2,1,0:T(8,128)(2,1)}, u32[]{:S(2)}) copy-start(bf16[1,12,128,256]{3,2,1,0:T(8,128)(2,1)} %param.21) | copy-start | bytes 2359300
  19.6 14.2 %collective-permute-start.3 = (bf16[256,256]{1,0:T(8,128)(2,1)S(1)}, bf16[256,256]{1,0:T(8,128)(2,1)S(1)}, u32[]{:S(2)}, u32[]{:S(2)}) collective-permute-start(bf16[256,256]{1,0:T(8,128)(2,1)S(1)} %fusion.1), channel_id=1, source_target_pairs={{0,2},{1,3},{2,0},{3,1},{4,6},{5,7},{6,4},{7,5},{8,10},{9,11},{10,... | collective-permute-start | bytes 393224 | tf_op jit(solution)/shard_map/ppermute | solution.py:384
  22.7 25.1 %collective-permute-start.1 = (bf16[384,256]{1,0:T(8,128)(2,1)S(1)}, bf16[384,256]{1,0:T(8,128)(2,1)S(1)}, u32[]{:S(2)}, u32[]{:S(2)}) collective-permute-start(bf16[384,256]{1,0:T(8,128)(2,1)S(1)} %fusion), channel_id=1, source_target_pairs={{0,2},{1,3},{2,0},{3,1},{4,6},{5,7},{6,4},{7,5},{8,10},{9,11},{10,... | collective-permute-start | bytes 589832 | tf_op jit(solution)/shard_map/ppermute | solution.py:384
  35.0 5.4 %collective-permute-start.4 = (bf16[128,256]{1,0:T(8,128)(2,1)S(1)}, bf16[128,256]{1,0:T(8,128)(2,1)S(1)}, u32[]{:S(2)}, u32[]{:S(2)}) collective-permute-start(bf16[128,256]{1,0:T(8,128)(2,1)S(1)} %get-tuple-element.27.refs_0_), channel_id=1, source_target_pairs={{0,4},{4,0},{8,12},{12,8},{1,5},{5,1},{9,13},{13,9},{2,6},{6,2},{1... | collective-permute-start | bytes 196616 | tf_op jit(solution)/shard_map/ppermute | solution.py:384
  35.1 5.3 %collective-permute-start.5 = (bf16[128,256]{1,0:T(8,128)(2,1)S(1)}, bf16[128,256]{1,0:T(8,128)(2,1)S(1)}, u32[]{:S(2)}, u32[]{:S(2)}) collective-permute-start(bf16[128,256]{1,0:T(8,128)(2,1)S(1)} %get-tuple-element.27.refs_0_), channel_id=1, source_target_pairs={{0,8},{4,12},{8,0},{12,4},{1,9},{5,13},{9,1},{13,5},{2,10},{6,14},... | collective-permute-start | bytes 196616 | tf_op jit(solution)/shard_map/ppermute | solution.py:384
  36.8 4.1 %collective-permute-start.6 = (bf16[128,256]{1,0:T(8,128)(2,1)S(1)}, bf16[128,256]{1,0:T(8,128)(2,1)S(1)}, u32[]{:S(2)}, u32[]{:S(2)}) collective-permute-start(bf16[128,256]{1,0:T(8,128)(2,1)S(1)} %get-tuple-element.27.refs_0_), channel_id=1, source_target_pairs={{0,12},{4,8},{8,4},{12,0},{1,13},{5,9},{9,5},{13,1},{2,14},{6,10},... | collective-permute-start | bytes 196616 | tf_op jit(solution)/shard_map/ppermute | solution.py:384
  44.7 25.3 %collective-permute-start.17 = (bf16[128,1024]{1,0:T(8,128)(2,1)S(1)}, bf16[128,1024]{1,0:T(8,128)(2,1)S(1)}, u32[]{:S(2)}, u32[]{:S(2)}) collective-permute-start(bf16[128,1024]{1,0:T(8,128)(2,1)S(1)} %attend_new.7.refs_0_), channel_id=1, source_target_pairs={{0,2},{1,3},{2,0},{3,1},{4,6},{5,7},{6,4},{7,5},{8,10},{9,11},{10,... | collective-permute-start | bytes 786440 | tf_op jit(solution)/shard_map/ppermute | solution.py:384
  44.8 25.3 %collective-permute-start.18 = (bf16[128,1024]{1,0:T(8,128)(2,1)S(1)}, bf16[128,1024]{1,0:T(8,128)(2,1)S(1)}, u32[]{:S(2)}, u32[]{:S(2)}) collective-permute-start(bf16[128,1024]{1,0:T(8,128)(2,1)S(1)} %attend_new.7.refs_0_), channel_id=1, source_target_pairs={{0,1},{1,0},{2,3},{3,2},{4,5},{5,4},{6,7},{7,6},{8,9},{9,8},{10,11... | collective-permute-start | bytes 786440 | tf_op jit(solution)/shard_map/ppermute | solution.py:384
  57.2 38.3 %collective-permute-start.13 = (bf16[256,1024]{1,0:T(8,128)(2,1)S(1)}, bf16[256,1024]{1,0:T(8,128)(2,1)S(1)}, u32[]{:S(2)}, u32[]{:S(2)}) collective-permute-start(bf16[256,1024]{1,0:T(8,128)(2,1)S(1)} %pad_maximum_fusion), channel_id=1, source_target_pairs={{0,2},{1,3},{2,0},{3,1},{4,6},{5,7},{6,4},{7,5},{8,10},{9,11},{10,... | collective-permute-start | bytes 1572872 | tf_op jit(solution)/shard_map/ppermute | solution.py:384
  60.8 14.1 %collective-permute-start.19 = (bf16[128,1024]{1,0:T(8,128)(2,1)S(1)}, bf16[128,1024]{1,0:T(8,128)(2,1)S(1)}, u32[]{:S(2)}, u32[]{:S(2)}) collective-permute-start(bf16[128,1024]{1,0:T(8,128)(2,1)S(1)} %attend_new.7.refs_0_), channel_id=1, source_target_pairs={{1,2},{2,1},{5,6},{6,5},{9,10},{10,9},{13,14},{14,13},{17,18},{18,... | collective-permute-start | bytes 786440 | tf_op jit(solution)/shard_map/ppermute | solution.py:533
  61.4 27.3 %collective-permute-start.15 = (bf16[128,1024]{1,0:T(8,128)(2,1)S(1)}, bf16[128,1024]{1,0:T(8,128)(2,1)S(1)}, u32[]{:S(2)}, u32[]{:S(2)}) collective-permute-start(bf16[128,1024]{1,0:T(8,128)(2,1)S(1)} %attend_new.5.refs_0_), channel_id=1, source_target_pairs={{0,1},{1,0},{2,3},{3,2},{4,5},{5,4},{6,7},{7,6},{8,9},{9,8},{10,11... | collective-permute-start | bytes 786440 | tf_op jit(solution)/shard_map/ppermute | solution.py:384
  70.0 19.4 %collective-permute-start.11 = (bf16[128,1024]{1,0:T(8,128)(2,1)S(1)}, bf16[128,1024]{1,0:T(8,128)(2,1)S(1)}, u32[]{:S(2)}, u32[]{:S(2)}) collective-permute-start(bf16[128,1024]{1,0:T(8,128)(2,1)S(1)} %attend_new.4.refs_0_), channel_id=1, source_target_pairs={{0,1},{1,0},{2,3},{3,2},{4,5},{5,4},{6,7},{7,6},{8,9},{9,8},{10,11... | collective-permute-start | bytes 786440 | tf_op jit(solution)/shard_map/ppermute | solution.py:384
  70.1 24.7 %collective-permute-start.20 = (bf16[128,1024]{1,0:T(8,128)(2,1)S(1)}, bf16[128,1024]{1,0:T(8,128)(2,1)S(1)}, u32[]{:S(2)}, u32[]{:S(2)}) collective-permute-start(bf16[128,1024]{1,0:T(8,128)(2,1)S(1)} %collective-permute-done.17.refs_1_), channel_id=1, source_target_pairs={{1,0},{2,3},{5,4},{6,7},{9,8},{10,11},{13,12},{14,15},{17,16},{18,... | collective-permute-start | bytes 786440 | tf_op jit(solution)/shard_map/ppermute | solution.py:537
  74.9 35.6 %collective-permute-start.16 = (bf16[128,1024]{1,0:T(8,128)(2,1)S(1)}, bf16[128,1024]{1,0:T(8,128)(2,1)S(1)}, u32[]{:S(2)}, u32[]{:S(2)}) collective-permute-start(bf16[128,1024]{1,0:T(8,128)(2,1)S(1)} %attend_new.6.refs_1_), channel_id=1, source_target_pairs={{0,1},{1,0},{2,3},{3,2},{4,5},{5,4},{6,7},{7,6},{8,9},{9,8},{10,11... | collective-permute-start | bytes 786440 | tf_op jit(solution)/shard_map/ppermute | solution.py:384
  88.7 27.5 %collective-permute-start.12 = (bf16[256,1024]{1,0:T(8,128)(2,1)S(1)}, bf16[256,1024]{1,0:T(8,128)(2,1)S(1)}, u32[]{:S(2)}, u32[]{:S(2)}) collective-permute-start(bf16[256,1024]{1,0:T(8,128)(2,1)S(1)} %pad_maximum_fusion), channel_id=1, source_target_pairs={{1,2},{2,1},{5,6},{6,5},{9,10},{10,9},{13,14},{14,13},{17,18},{18,... | collective-permute-start | bytes 1572872 | tf_op jit(solution)/shard_map/ppermute | solution.py:533
  89.4 18.2 %collective-permute-start.7 = (bf16[128,1024]{1,0:T(8,128)(2,1)S(1)}, bf16[128,1024]{1,0:T(8,128)(2,1)S(1)}, u32[]{:S(2)}, u32[]{:S(2)}) collective-permute-start(bf16[128,1024]{1,0:T(8,128)(2,1)S(1)} %attend_new.4.refs_0_), channel_id=1, source_target_pairs={{0,2},{3,1},{4,6},{7,5},{8,10},{11,9},{12,14},{15,13},{16,18},{19,... | collective-permute-start | bytes 786440 | tf_op jit(solution)/shard_map/ppermute | solution.py:532
  94.8 14.2 %collective-permute-start.8 = (bf16[128,1024]{1,0:T(8,128)(2,1)S(1)}, bf16[128,1024]{1,0:T(8,128)(2,1)S(1)}, u32[]{:S(2)}, u32[]{:S(2)}) collective-permute-start(bf16[128,1024]{1,0:T(8,128)(2,1)S(1)} %attend_new.4.refs_0_), channel_id=1, source_target_pairs={{1,2},{2,1},{5,6},{6,5},{9,10},{10,9},{13,14},{14,13},{17,18},{18,... | collective-permute-start | bytes 786440 | tf_op jit(solution)/shard_map/ppermute | solution.py:533
  95.5 20.8 %collective-permute-start.14 = (bf16[256,1024]{1,0:T(8,128)(2,1)S(1)}, bf16[256,1024]{1,0:T(8,128)(2,1)S(1)}, u32[]{:S(2)}, u32[]{:S(2)}) collective-permute-start(bf16[256,1024]{1,0:T(8,128)(2,1)S(1)} %collective-permute-done.13.refs_4_), channel_id=1, source_target_pairs={{1,0},{2,3},{5,4},{6,7},{9,8},{10,11},{13,12},{14,15},{17,16},{18,... | collective-permute-start | bytes 1572872 | tf_op jit(solution)/shard_map/ppermute | solution.py:537
  107.7 11.0 %collective-permute-start.10 = (bf16[128,1024]{1,0:T(8,128)(2,1)S(1)}, bf16[128,1024]{1,0:T(8,128)(2,1)S(1)}, u32[]{:S(2)}, u32[]{:S(2)}) collective-permute-start(bf16[128,1024]{1,0:T(8,128)(2,1)S(1)} %collective-permute-done.7.refs_0_), channel_id=1, source_target_pairs={{1,0},{2,3},{5,4},{6,7},{9,8},{10,11},{13,12},{14,15},{17,16},{18,... | collective-permute-start | bytes 786440 | tf_op jit(solution)/shard_map/ppermute | solution.py:537
  109.0 13.6 %collective-permute-start.9 = (bf16[128,1024]{1,0:T(8,128)(2,1)S(1)}, bf16[128,1024]{1,0:T(8,128)(2,1)S(1)}, u32[]{:S(2)}, u32[]{:S(2)}) collective-permute-start(bf16[128,1024]{1,0:T(8,128)(2,1)S(1)} %collective-permute-done.8.refs_2_), channel_id=1, source_target_pairs={{1,0},{2,3},{5,4},{6,7},{9,8},{10,11},{13,12},{14,15},{17,16},{18,... | collective-permute-start | bytes 786440 | tf_op jit(solution)/shard_map/ppermute | solution.py:536

commit v6 on v5

--- a/solution.py
+++ b/solution.py
@@ -56,9 +56,13 @@
     return out
 
 
-def stacked_heads(q_ref, heads):
-    m = q_ref.shape[0] * q_ref.shape[1]
-    q = q_ref[...].reshape(m, heads * HD)
+ON_CHIP = pl.BlockSpec(memory_space=pltpu.VMEM)
+
+
+def stacked_heads(q_ref, heads, block, direct, start):
+    at = start * block if direct else 0
+    m = block * q_ref.shape[1]
+    q = q_ref[at : at + block].reshape(m, heads * HD)
     return jnp.concatenate([q[:, h * HD : (h + 1) * HD] for h in range(heads)], 0)
 
 
@@ -102,11 +106,11 @@
 
 
 def cached_kernel(
-    heads, cpages, scale2, start, table_ref, length_ref, q_ref, fork_ref, pool_ref, mixed_ref, stat_ref, s_ref
+    heads, block, direct, cpages, scale2, start, table_ref, length_ref, q_ref, fork_ref, pool_ref, mixed_ref, stat_ref, s_ref
 ):
-    qs = stacked_heads(q_ref, heads)
+    qs = stacked_heads(q_ref, heads, block, direct, start)
     m = qs.shape[0] // heads
-    block, steps = q_ref.shape[:2]
+    steps = q_ref.shape[1]
     prompt = by_row(fork_ref[...], (pl.program_id(0) + start) * block, m, steps)
     pages, size = pool_ref.shape[:2]
     group = cpages
@@ -140,13 +144,15 @@
 
 
 def new_kernel(
-    heads, steps, scale2, start, owner_ref, base_ref, q_ref, fork_ref, tail_ref, mixed_ref, stat_ref, *refs
+    heads, block, direct, skip, steps, scale2, start, owner_ref, base_ref, q_ref, fork_ref, tail_ref, mixed_ref, stat_ref, *refs
 ):
     span_refs, o_ref, s_ref = refs[:-2], refs[-2], refs[-1]
-    qs = stacked_heads(q_ref, heads)
+    qs = stacked_heads(q_ref, heads, block, direct, start)
     m = qs.shape[0] // heads
     span = span_refs[0].shape[0]
-    prompt = by_row(fork_ref[...], (pl.program_id(0) + start) * q_ref.shape[0], m, steps)
+    prompt = by_row(fork_ref[...], (pl.program_id(0) + start) * block, m, steps)
+    at = skip * m if direct else 0
+    mine = slice(at, at + m)
 
     def loaded():
         return jnp.concatenate([ref[...] for ref in span_refs], 0)
@@ -172,13 +178,13 @@
         (m, lambda: tail_ref[...], causal),
     )
     top, total, mixed = softmax_parts(qs, heads, parts, scale2, s_ref)
-    old_top = stat_ref[:, :, :1]
-    old_total = stat_ref[:, :, HD // 2 : HD // 2 + 1]
+    old_top = stat_ref[:, mine, :1]
+    old_total = stat_ref[:, mine, HD // 2 : HD // 2 + 1]
     both = jnp.maximum(top, old_top)
     new_share = jnp.exp2(top - both)
     old_share = jnp.exp2(old_top - both)
     total = total * new_share + old_total * old_share
-    mixed = mixed * new_share + mixed_ref[...] * old_share
+    mixed = mixed * new_share + mixed_ref[:, mine, :] * old_share
     out = (mixed / total).astype(jnp.bfloat16)
     for h in range(heads):
         o_ref[:, h * HD : (h + 1) * HD] = out[h]
@@ -191,17 +197,22 @@
     m = block * steps
     cached = pool.shape[0] * pool.shape[1]
     cpages = pool.shape[0] // prompt_length.shape[0]
+    direct = count == 1
     return pl.pallas_call(
-        functools.partial(cached_kernel, heads, cpages, LOG2E / math.sqrt(HD), start),
+        functools.partial(cached_kernel, heads, block, direct, cpages, LOG2E / math.sqrt(HD), start),
         grid_spec=pltpu.PrefetchScalarGridSpec(
             num_scalar_prefetch=2,
             grid=(count,),
-            in_specs=[
+            in_specs=[ON_CHIP] * 3
+            if direct
+            else [
                 pl.BlockSpec((block, steps, width), lambda i, *_: (i + start, 0, 0)),
                 pl.BlockSpec(fork_row.shape, lambda i, *_: (0, 0)),
                 pl.BlockSpec(pool.shape, lambda i, *_: (0, 0, 0)),
             ],
-            out_specs=[pl.BlockSpec((heads, m, HD), lambda i, *_: (0, i, 0))] * 2,
+            out_specs=[ON_CHIP] * 2
+            if direct
+            else [pl.BlockSpec((heads, m, HD), lambda i, *_: (0, i, 0))] * 2,
             scratch_shapes=[pltpu.VMEM((heads, m, cached), jnp.float32)],
         ),
         out_shape=[jax.ShapeDtypeStruct((heads, m * count, HD), jnp.float32)] * 2,
@@ -222,13 +233,16 @@
     m = block * steps
     span = span_pairs[0].shape[0]
     keys = span * len(span_pairs)
+    direct = count == 1
     part = pl.BlockSpec((heads, m, HD), lambda i, *_: (0, i + skip, 0))
     return pl.pallas_call(
-        functools.partial(new_kernel, heads, steps, LOG2E / math.sqrt(HD), start),
+        functools.partial(new_kernel, heads, block, direct, skip, steps, LOG2E / math.sqrt(HD), start),
         grid_spec=pltpu.PrefetchScalarGridSpec(
             num_scalar_prefetch=2,
             grid=(count,),
-            in_specs=[
+            in_specs=[ON_CHIP] * (5 + len(span_pairs))
+            if direct
+            else [
                 pl.BlockSpec((block, steps, width), lambda i, *_: (i + start, 0, 0)),
                 pl.BlockSpec(fork_row.shape, lambda i, *_: (0, 0)),
                 pl.BlockSpec((m, 2 * HD), lambda i, *_: (i, 0)),
@@ -236,7 +250,7 @@
                 part,
             ]
             + [pl.BlockSpec((span, 2 * HD), lambda i, *_: (0, 0))] * len(span_pairs),
-            out_specs=pl.BlockSpec((m, width), lambda i, *_: (i, 0)),
+            out_specs=ON_CHIP if direct else pl.BlockSpec((m, width), lambda i, *_: (i, 0)),
             scratch_shapes=[pltpu.VMEM((heads, m, keys + m), jnp.float32)],
         ),
         out_shape=jax.ShapeDtypeStruct((m * count, width), jnp.bfloat16),
@@ -362,17 +376,13 @@
 
 def finish(keep, others, places, start, sizes):
     span, steps, owner, length, replica, fork_row, freq = places
-    n = keep.shape[1]
-    unit = pl.BlockSpec((1, n, 2 * HD), lambda i, *_: (0, 0, 0))
-    flat = lambda rows, width: pl.BlockSpec((rows, width), lambda i, *_: (0, 0))
     return pl.pallas_call(
         functools.partial(finish_kernel, span, steps, start, sizes),
         grid_spec=pltpu.PrefetchScalarGridSpec(
             num_scalar_prefetch=3,
             grid=(1,),
-            in_specs=[flat(*fork_row.shape), flat(*freq.shape), unit]
-            + [unit if x.ndim == 3 else flat(n, 2 * HD) for x in others],
-            out_specs=[flat(size, 2 * HD) for size in sizes],
+            in_specs=[ON_CHIP] * (3 + len(others)),
+            out_specs=[ON_CHIP] * len(sizes),
         ),
         out_shape=[jax.ShapeDtypeStruct((size, 2 * HD), jnp.bfloat16) for size in sizes],
         compiler_params=SMALL,

time: 125 us -> 125 us (level)
  no operation moved by 1% of the time
where the time goes in v6:
time: 125 us
  Pallas kernels  64.7 us (52%)
  starting transfers between devices  45.1 us (36%)
  waiting for transfers between devices  13.2 us (11%)
    ppermute x13, starting transfers between devices, swap(): lax.ppermute(x, axis, [(i, i ^ bit) for i in range(lax.axis_size(axis))])  33 us
    pallas_call x5, Pallas kernels, out_project(): pl.pallas_call(functools.partial(out_kernel, rels, shapes, cuts, partial...  21.1 us
    pallas_call x4, Pallas kernels, attend_new(): pl.pallas_call(functools.partial(new_kernel, heads, block, direct, skip,...  15.6 us
    pallas_call x3, Pallas kernels, attend_cached(): pl.pallas_call(functools.partial(cached_kernel, heads, block, direct, cpa...  13.6 us
    ppermute x13, waiting for transfers between devices, swap(): lax.ppermute(x, axis, [(i, i ^ bit) for i in range(lax.axis_size(axis))])  8.54 us
    pallas_call x2, Pallas kernels, project(): pl.pallas_call(functools.partial(project_kernel, len(groups), split, kept...  8.39 us
    ppermute x1, starting transfers between devices, far_heads(): lax.ppermute(own, 'tensor', [(0, 2), (3, 1)])  4.6 us
    ppermute x1, waiting for transfers between devices, far_heads(): forward = lax.ppermute(across, 'tensor', outward)  3.92 us
  transfers between devices with their start and end apart: 21, of which 4 were waited for; matrix products, arithmetic and copies ran while one was open for 0% of the time, Pallas kernels for 47%

profile of v6, /device:TPU:0, one launch (start us, length us, event | category | flops | bytes accessed | tf_op | source)
XLA Modules:
  0.0 124.8 jit_solution(8525828560850864410)
XLA Ops:
  0.0 4.1 %project.3 = (f32[2,256,256]{2,1,0:T(8,128)S(1)}, bf16[2,256,256]{2,1,0:T(8,128)(2,1)}) custom-call(s32[1]{0:T(128)} %bitcast.rank_ref, bf16[128,2048]{1,0:T(8,128)(2,1)} %refs_0_.3, bf16[128,4,2048]{2,1,0:T(4,128)(2,1)} %refs_1_.3, bf16[2048,512]{1,0:T(8,128)(2,1)} %refs_4_.3, bf16[2048,512]{1,0:T(8,128)(2,1)} %refs_5_.3, bf16[2048,512]{1,0:T(8,128)(2,1)} %refs_4_.3, ...), custom_call_target="tpu_custom_call" | custom-call | flops 1073741824 | bytes 4194304 | tf_op jit(solution)/shard_map/project/pallas_call | solution.py:313
  4.1 0.0 copy-start.3
  4.2 0.0 copy-start.6
  4.2 3.1 %collective-permute-start.2 = (bf16[2,256,256]{2,1,0:T(8,128)(2,1)}, bf16[2,256,256]{2,1,0:T(8,128)(2,1)S(1)}, u32[]{:S(2)}, u32[]{:S(2)}) collective-permute-start(bf16[2,256,256]{2,1,0:T(8,128)(2,1)} %get-tuple-element.26), channel_id=1, source_target_pairs={{0,1},{1,0},{2,3},{3,2},{4,5},{5,4},{6,7},{7,6},{8,9},{9,8},{10,11... | collective-permute-start | bytes 786440 | tf_op jit(solution)/shard_map/ppermute | solution.py:394
  7.3 4.3 %project.2 = (f32[2,384,256]{2,1,0:T(8,128)S(1)}, bf16[2,384,256]{2,1,0:T(8,128)(2,1)S(1)}) custom-call(s32[1]{0:T(128)} %bitcast.rank_ref, bf16[128,4,2048]{2,1,0:T(4,128)(2,1)} %refs_1_.3, bf16[2048,512]{1,0:T(8,128)(2,1)} %refs_4_.3, bf16[2048,512]{1,0:T(8,128)(2,1)} %refs_5_.3, bf16[2048,512]{1,0:T(8,128)(2,1)} %refs_4_.3, bf16[2048,512]{1,0:T(8,128)(2,1)} %refs_5_.3), custom_call_target="tpu_custom_call" | custom-call | flops 1610612736 | bytes 4194304 | tf_op jit(solution)/shard_map/project/pallas_call | solution.py:313
  11.6 0.2 collective-permute-start
  11.8 0.0 copy-start.4
  11.8 1.1 copy-done.4
  12.9 6.7 %attend_cached.4 = (f32[8,256,128]{2,1,0:T(8,128)S(1)}, f32[8,256,128]{2,1,0:T(8,128)S(1)}) custom-call(s32[12]{0:T(128)S(1)} %copy-done.6, s32[4]{0:T(128)S(1)} %copy-done.3, bf16[128,4,1024]{2,1,0:T(4,128)(2,1)S(1)} %copy-done, s32[1,128]{1,0:T(1,128)S(1)} %bitcast.10, bf16[12,128,256]{2,1,0:T(8,128)(2,1)S(1)} %bitcast.19), custom_call_target="tpu_custom_call" | custom-call | flops 1610612736 | bytes 2097152 | tf_op jit(solution)/shard_map/attend_cached/pallas_call | solution.py:201
  19.6 0.0 copy-start.5
  19.6 3.0 %collective-permute-start.3 = (bf16[256,256]{1,0:T(8,128)(2,1)S(1)}, bf16[256,256]{1,0:T(8,128)(2,1)S(1)}, u32[]{:S(2)}, u32[]{:S(2)}) collective-permute-start(bf16[256,256]{1,0:T(8,128)(2,1)S(1)} %fusion.1), channel_id=1, source_target_pairs={{0,2},{1,3},{2,0},{3,1},{4,6},{5,7},{6,4},{7,5},{8,10},{9,11},{10,... | collective-permute-start | bytes 393224 | tf_op jit(solution)/shard_map/ppermute | solution.py:394
  22.7 3.0 %collective-permute-start.1 = (bf16[384,256]{1,0:T(8,128)(2,1)S(1)}, bf16[384,256]{1,0:T(8,128)(2,1)S(1)}, u32[]{:S(2)}, u32[]{:S(2)}) collective-permute-start(bf16[384,256]{1,0:T(8,128)(2,1)S(1)} %fusion), channel_id=1, source_target_pairs={{0,2},{1,3},{2,0},{3,1},{4,6},{5,7},{6,4},{7,5},{8,10},{9,11},{10,... | collective-permute-start | bytes 589832 | tf_op jit(solution)/shard_map/ppermute | solution.py:394
  25.7 0.1 maximum_bitcast_fusion.freq_ref
  25.7 8.1 %collective-permute-done.3.refs_1_ = bf16[256,256]{1,0:T(8,128)(2,1)S(1)} collective-permute-done((bf16[256,256]{1,0:T(8,128)(2,1)S(1)}, bf16[256,256]{1,0:T(8,128)(2,1)S(1)}, u32[]{:S(2)}, u32[]{:S(2)}) %collective-permute-start.3) | collective-permute-done | bytes 131104 | tf_op jit(solution)/shard_map/ppermute | solution.py:394
  33.9 1.2 finish.3
  35.0 0.1 collective-permute-start.4
  35.1 1.7 %collective-permute-start.5 = (bf16[128,256]{1,0:T(8,128)(2,1)S(1)}, bf16[128,256]{1,0:T(8,128)(2,1)S(1)}, u32[]{:S(2)}, u32[]{:S(2)}) collective-permute-start(bf16[128,256]{1,0:T(8,128)(2,1)S(1)} %get-tuple-element.27.refs_0_), channel_id=1, source_target_pairs={{0,8},{4,12},{8,0},{12,4},{1,9},{5,13},{9,1},{13,5},{2,10},{6,14},... | collective-permute-start | bytes 196616 | tf_op jit(solution)/shard_map/ppermute | solution.py:394
  36.8 0.2 collective-permute-start.6
  37.0 3.4 %attend_cached.5 = (f32[8,128,128]{2,1,0:T(8,128)S(1)}, f32[8,128,128]{2,1,0:T(8,128)S(1)}) custom-call(s32[12]{0:T(128)S(1)} %copy-done.6, s32[4]{0:T(128)S(1)} %copy-done.3, bf16[128,4,1024]{2,1,0:T(4,128)(2,1)S(1)} %copy-done, s32[1,128]{1,0:T(1,128)S(1)} %bitcast.12, bf16[12,128,256]{2,1,0:T(8,128)(2,1)S(1)} %bitcast.20), custom_call_target="tpu_custom_call" | custom-call | flops 805306368 | bytes 1048576 | tf_op jit(solution)/shard_map/attend_cached/pallas_call | solution.py:201
  40.4 0.4 collective-permute-done.6.refs_3_
  40.8 3.8 %attend_new.7.refs_0_ = bf16[128,1024]{1,0:T(8,128)(2,1)S(1)} custom-call(s32[4]{0:T(128)S(1)} %copy-done.1, s32[1]{0:T(128)} %bitcast.1.replica_ref.base_ref, bf16[128,4,1024]{2,1,0:T(4,128)(2,1)S(1)} %copy-done, s32[1,128]{1,0:T(1,128)S(1)} %bitcast.13, bf16[128,256]{1,0:T(8,128)(2,1)S(1)} %get-tuple-element.32.tail_ref, ...), custom_call_target="tpu_custom_call" | custom-call | flops 335544320 | bytes 1310720 | tf_op jit(solution)/shard_map/attend_new/pallas_call | solution.py:238
  44.7 0.1 collective-permute-start.17
  44.8 3.0 %collective-permute-start.18 = (bf16[128,1024]{1,0:T(8,128)(2,1)S(1)}, bf16[128,1024]{1,0:T(8,128)(2,1)S(1)}, u32[]{:S(2)}, u32[]{:S(2)}) collective-permute-start(bf16[128,1024]{1,0:T(8,128)(2,1)S(1)} %attend_new.7.refs_0_), channel_id=1, source_target_pairs={{0,1},{1,0},{2,3},{3,2},{4,5},{5,4},{6,7},{7,6},{8,9},{9,8},{10,11... | collective-permute-start | bytes 786440 | tf_op jit(solution)/shard_map/ppermute | solution.py:394
  47.8 1.4 %finish.2 = (bf16[128,256]{1,0:T(8,128)(2,1)S(1)}, bf16[128,256]{1,0:T(8,128)(2,1)S(1)}, bf16[128,256]{1,0:T(8,128)(2,1)S(1)}) custom-call(s32[4]{0:T(128)S(1)} %copy-done.1, s32[4]{0:T(128)S(1)} %copy-done.3, s32[1]{0:T(128)} %bitcast.1.replica_ref.base_ref, s32[1,128]{1,0:T(1,128)S(1)} %bitcast.14, f32[1,128]{1,0:T(1,128)S(1)} %maximum_bitcast_fusion.freq_ref, ...), custom_call_target="tpu_custom_call" | custom-call | tf_op jit(solution)/shard_map/finish/pallas_call | solution.py:379
  49.2 3.8 %attend_new.5.refs_0_ = bf16[128,1024]{1,0:T(8,128)(2,1)S(1)} custom-call(s32[4]{0:T(128)S(1)} %copy-done.1, s32[1]{0:T(128)} %bitcast.1.replica_ref.base_ref, bf16[128,4,1024]{2,1,0:T(4,128)(2,1)S(1)} %copy-done, s32[1,128]{1,0:T(1,128)S(1)} %bitcast.15, bf16[128,256]{1,0:T(8,128)(2,1)S(1)} %get-tuple-element.28.tail_ref, ...), custom_call_target="tpu_custom_call" | custom-call | flops 335544320 | bytes 1310720 | tf_op jit(solution)/shard_map/attend_new/pallas_call | solution.py:238
  53.1 4.1 %attend_new.6.refs_1_ = bf16[128,1024]{1,0:T(8,128)(2,1)S(1)} custom-call(s32[4]{0:T(128)S(1)} %copy-done.1, s32[1]{0:T(128)} %bitcast.1.replica_ref.base_ref, bf16[128,4,1024]{2,1,0:T(4,128)(2,1)S(1)} %copy-done, s32[1,128]{1,0:T(1,128)S(1)} %bitcast.16, bf16[128,256]{1,0:T(8,128)(2,1)S(1)} %get-tuple-element.31.tail_ref, ...), custom_call_target="tpu_custom_call" | custom-call | flops 335544320 | bytes 1310720 | tf_op jit(solution)/shard_map/attend_new/pallas_call | solution.py:238
  57.2 0.1 collective-permute-start.13
  57.3 3.4 %attend_cached.3 = (f32[8,128,128]{2,1,0:T(8,128)S(1)}, f32[8,128,128]{2,1,0:T(8,128)S(1)}) custom-call(s32[12]{0:T(128)S(1)} %copy-done.6, s32[4]{0:T(128)S(1)} %copy-done.3, bf16[128,4,1024]{2,1,0:T(4,128)(2,1)S(1)} %copy-done, s32[1,128]{1,0:T(1,128)S(1)} %bitcast.17, bf16[12,128,256]{2,1,0:T(8,128)(2,1)S(1)} %bitcast.21), custom_call_target="tpu_custom_call" | custom-call | flops 805306368 | bytes 1048576 | tf_op jit(solution)/shard_map/attend_cached/pallas_call | solution.py:201
  60.8 0.7 collective-permute-start.19
  61.4 4.7 %collective-permute-start.15 = (bf16[128,1024]{1,0:T(8,128)(2,1)S(1)}, bf16[128,1024]{1,0:T(8,128)(2,1)S(1)}, u32[]{:S(2)}, u32[]{:S(2)}) collective-permute-start(bf16[128,1024]{1,0:T(8,128)(2,1)S(1)} %attend_new.5.refs_0_), channel_id=1, source_target_pairs={{0,1},{1,0},{2,3},{3,2},{4,5},{5,4},{6,7},{7,6},{8,9},{9,8},{10,11... | collective-permute-start | bytes 786440 | tf_op jit(solution)/shard_map/ppermute | solution.py:394
  66.2 3.8 %attend_new.4.refs_0_ = bf16[128,1024]{1,0:T(8,128)(2,1)S(1)} custom-call(s32[4]{0:T(128)S(1)} %copy-done.1, s32[1]{0:T(128)} %bitcast.1.replica_ref.base_ref, bf16[128,4,1024]{2,1,0:T(4,128)(2,1)S(1)} %copy-done, s32[1,128]{1,0:T(1,128)S(1)} %bitcast.18, bf16[128,256]{1,0:T(8,128)(2,1)S(1)} %get-tuple-element.22.tail_ref, ...), custom_call_target="tpu_custom_call" | custom-call | flops 335544320 | bytes 1310720 | tf_op jit(solution)/shard_map/attend_new/pallas_call | solution.py:238
  70.0 0.1 collective-permute-start.11
  70.1 1.3 %collective-permute-start.20 = (bf16[128,1024]{1,0:T(8,128)(2,1)S(1)}, bf16[128,1024]{1,0:T(8,128)(2,1)S(1)}, u32[]{:S(2)}, u32[]{:S(2)}) collective-permute-start(bf16[128,1024]{1,0:T(8,128)(2,1)S(1)} %collective-permute-done.17.refs_1_), channel_id=1, source_target_pairs={{1,0},{2,3},{5,4},{6,7},{9,8},{10,11},{13,12},{14,15},{17,16},{18,... | collective-permute-start | bytes 786440 | tf_op jit(solution)/shard_map/ppermute | solution.py:547
  71.4 3.5 %hold.1.refs_3_.refs_5_ = bf16[2048,2048]{1,0:T(8,128)(2,1)S(1)} custom-call(s32[1]{0:T(128)} %bitcast.rank_ref, bf16[4096,2048]{1,0:T(8,128)(2,1)} %refs_5_.5), custom_call_target="tpu_custom_call" | custom-call | tf_op jit(solution)/shard_map/hold/pallas_call | solution.py:517
  74.9 13.8 %collective-permute-start.16 = (bf16[128,1024]{1,0:T(8,128)(2,1)S(1)}, bf16[128,1024]{1,0:T(8,128)(2,1)S(1)}, u32[]{:S(2)}, u32[]{:S(2)}) collective-permute-start(bf16[128,1024]{1,0:T(8,128)(2,1)S(1)} %attend_new.6.refs_1_), channel_id=1, source_target_pairs={{0,1},{1,0},{2,3},{3,2},{4,5},{5,4},{6,7},{7,6},{8,9},{9,8},{10,11... | collective-permute-start | bytes 786440 | tf_op jit(solution)/shard_map/ppermute | solution.py:394
  88.7 0.7 collective-permute-start.12
  89.4 4.6 %collective-permute-start.7 = (bf16[128,1024]{1,0:T(8,128)(2,1)S(1)}, bf16[128,1024]{1,0:T(8,128)(2,1)S(1)}, u32[]{:S(2)}, u32[]{:S(2)}) collective-permute-start(bf16[128,1024]{1,0:T(8,128)(2,1)S(1)} %attend_new.4.refs_0_), channel_id=1, source_target_pairs={{0,2},{3,1},{4,6},{7,5},{8,10},{11,9},{12,14},{15,13},{16,18},{19,... | collective-permute-start | bytes 786440 | tf_op jit(solution)/shard_map/ppermute | solution.py:542
  94.0 0.8 collective-permute-done.20.refs_4_
  94.8 0.7 collective-permute-start.8
  95.5 1.3 %collective-permute-start.14 = (bf16[256,1024]{1,0:T(8,128)(2,1)S(1)}, bf16[256,1024]{1,0:T(8,128)(2,1)S(1)}, u32[]{:S(2)}, u32[]{:S(2)}) collective-permute-start(bf16[256,1024]{1,0:T(8,128)(2,1)S(1)} %collective-permute-done.13.refs_4_), channel_id=1, source_target_pairs={{1,0},{2,3},{5,4},{6,7},{9,8},{10,11},{13,12},{14,15},{17,16},{18,... | collective-permute-start | bytes 1572872 | tf_op jit(solution)/shard_map/ppermute | solution.py:547
  96.8 3.8 %out_project.5.refs_4_ = f32[128,2048]{1,0:T(8,128)S(1)} custom-call(s32[1]{0:T(128)} %bitcast.rank_ref, bf16[128,1024]{1,0:T(8,128)(2,1)S(1)} %attend_new.4.refs_0_, bf16[128,1024]{1,0:T(8,128)(2,1)S(1)} %collective-permute-done.11.refs_1_, bf16[4096,2048]{1,0:T(8,128)(2,1)} %refs_5_.5), custom_call_target="tpu_custom_call" | custom-call | flops 1073741824 | bytes 8388608 | tf_op jit(solution)/shard_map/out_project/pallas_call | solution.py:475
  100.6 7.1 %out_project.7.refs_4_ = bf16[128,4,2048]{2,1,0:T(4,128)(2,1)} custom-call(s32[1]{0:T(128)} %bitcast.rank_ref, bf16[128,1024]{1,0:T(8,128)(2,1)S(1)} %attend_new.7.refs_0_, bf16[128,1024]{1,0:T(8,128)(2,1)S(1)} %collective-permute-done.17.refs_1_, bf16[128,1024]{1,0:T(8,128)(2,1)S(1)} %collective-permute-done.18.refs_2_, ...), custom_call_target="tpu_custom_call" | custom-call | flops 2147483648 | bytes 16777216 | tf_op jit(solution)/shard_map/out_project/pallas_call | solution.py:475
  107.7 1.3 %collective-permute-start.10 = (bf16[128,1024]{1,0:T(8,128)(2,1)S(1)}, bf16[128,1024]{1,0:T(8,128)(2,1)S(1)}, u32[]{:S(2)}, u32[]{:S(2)}) collective-permute-start(bf16[128,1024]{1,0:T(8,128)(2,1)S(1)} %collective-permute-done.7.refs_0_), channel_id=1, source_target_pairs={{1,0},{2,3},{5,4},{6,7},{9,8},{10,11},{13,12},{14,15},{17,16},{18,... | collective-permute-start | bytes 786440 | tf_op jit(solution)/shard_map/ppermute | solution.py:547
  109.0 1.6 %collective-permute-start.9 = (bf16[128,1024]{1,0:T(8,128)(2,1)S(1)}, bf16[128,1024]{1,0:T(8,128)(2,1)S(1)}, u32[]{:S(2)}, u32[]{:S(2)}) collective-permute-start(bf16[128,1024]{1,0:T(8,128)(2,1)S(1)} %collective-permute-done.8.refs_2_), channel_id=1, source_target_pairs={{1,0},{2,3},{5,4},{6,7},{9,8},{10,11},{13,12},{14,15},{17,16},{18,... | collective-permute-start | bytes 786440 | tf_op jit(solution)/shard_map/ppermute | solution.py:546
  110.6 5.7 %out_project.6.refs_2_ = f32[256,2048]{1,0:T(8,128)S(1)} custom-call(s32[1]{0:T(128)} %bitcast.rank_ref, bf16[128,1024]{1,0:T(8,128)(2,1)S(1)} %attend_new.5.refs_0_, bf16[128,1024]{1,0:T(8,128)(2,1)S(1)} %attend_new.6.refs_1_, bf16[128,1024]{1,0:T(8,128)(2,1)S(1)} %collective-permute-done.15.refs_2_, bf16[128,1024]{1,0:T(8,128)(2,1)S(1)} %collective-permute-done.16.refs_3_, ...), custom_call_target="tpu_custom_call" | custom-call | flops 3221225472 | bytes 12582912 | tf_op jit(solution)/shard_map/out_project/pallas_call | solution.py:475
  116.3 2.4 %out_project.8.refs_6_ = bf16[128,4,2048]{2,1,0:T(4,128)(2,1)} custom-call(s32[1]{0:T(128)} %bitcast.rank_ref, bf16[256,1024]{1,0:T(8,128)(2,1)S(1)} %collective-permute-done.12.refs_0_, bf16[256,1024]{1,0:T(8,128)(2,1)S(1)} %collective-permute-done.14.refs_1_, f32[256,2048]{1,0:T(8,128)S(1)} %out_project.6.refs_2_, ...), custom_call_target="tpu_custom_call", output_to_operand_aliasing={{}: (5, {})} | custom-call | flops 1073741824 | bytes 4194304 | tf_op jit(solution)/shard_map/out_project/pallas_call | solution.py:475
  118.7 3.9 %collective-permute-done.9.refs_1_ = bf16[128,1024]{1,0:T(8,128)(2,1)S(1)} collective-permute-done((bf16[128,1024]{1,0:T(8,128)(2,1)S(1)}, bf16[128,1024]{1,0:T(8,128)(2,1)S(1)}, u32[]{:S(2)}, u32[]{:S(2)}) %collective-permute-start.9) | collective-permute-done | bytes 262176 | tf_op jit(solution)/shard_map/ppermute | solution.py:546
  122.6 2.2 %out_project.9 = bf16[128,4,2048]{2,1,0:T(4,128)(2,1)} custom-call(s32[1]{0:T(128)} %bitcast.rank_ref, bf16[128,1024]{1,0:T(8,128)(2,1)S(1)} %collective-permute-done.7.refs_0_, bf16[128,1024]{1,0:T(8,128)(2,1)S(1)} %collective-permute-done.9.refs_1_, bf16[128,1024]{1,0:T(8,128)(2,1)S(1)} %collective-permute-done.8.refs_2_, ...), custom_call_target="tpu_custom_call", output_to_operand_aliasing={{}: (7, {})} | custom-call | flops 1073741824 | bytes 8388608 | tf_op jit(solution)/shard_map/out_project/pallas_call | solution.py:475
  (30 shorter events, 0.2 us)
Async XLA Ops:
  4.1 7.6 %copy-start = (bf16[128,4,1024]{2,1,0:T(4,128)(2,1)S(1)}, bf16[128,4,1024]{2,1,0:T(4,128)(2,1)}, u32[]{:S(2)}) copy-start(bf16[128,4,1024]{2,1,0:T(4,128)(2,1)} %q_ref.13) | copy-start | bytes 3145732
  4.1 7.6 %copy-start.2 = (s32[128]{0:T(128)S(1)}, s32[128]{0:T(128)}, u32[]{:S(2)}) copy-start(s32[128]{0:T(128)} %param.12) | copy-start | bytes 1540
  4.1 7.6 %copy-start.3 = (s32[4]{0:T(128)S(1)}, s32[4]{0:T(128)}, u32[]{:S(2)}) copy-start(s32[4]{0:T(128)} %length_ref.9) | copy-start | bytes 52
  4.2 7.6 %copy-start.6 = (s32[12]{0:T(128)S(1)}, s32[12]{0:T(128)}, u32[]{:S(2)}) copy-start(s32[12]{0:T(128)} %table_ref.5) | copy-start | bytes 148
  4.2 15.4 %collective-permute-start.2 = (bf16[2,256,256]{2,1,0:T(8,128)(2,1)}, bf16[2,256,256]{2,1,0:T(8,128)(2,1)S(1)}, u32[]{:S(2)}, u32[]{:S(2)}) collective-permute-start(bf16[2,256,256]{2,1,0:T(8,128)(2,1)} %get-tuple-element.26), channel_id=1, source_target_pairs={{0,1},{1,0},{2,3},{3,2},{4,5},{5,4},{6,7},{7,6},{8,9},{9,8},{10,11... | collective-permute-start | bytes 786440 | tf_op jit(solution)/shard_map/ppermute | solution.py:394
  11.6 11.1 %collective-permute-start = (bf16[2,384,256]{2,1,0:T(8,128)(2,1)S(1)}, bf16[2,384,256]{2,1,0:T(8,128)(2,1)S(1)}, u32[]{:S(2)}, u32[]{:S(2)}) collective-permute-start(bf16[2,384,256]{2,1,0:T(8,128)(2,1)S(1)} %get-tuple-element.21), channel_id=1, source_target_pairs={{0,1},{1,0},{2,3},{3,2},{4,5},{5,4},{6,7},{7,6},{8,9},{9,8},{10,11... | collective-permute-start | bytes 1179656 | tf_op jit(solution)/shard_map/ppermute | solution.py:394
  11.8 1.1 copy-start.4
  12.9 21.0 %copy-start.1 = (s32[4]{0:T(128)S(1)}, s32[4]{0:T(128)}, u32[]{:S(2)}) copy-start(s32[4]{0:T(128)} %owner_ref.11) | copy-start | bytes 52
  19.6 17.4 %copy-start.5 = (bf16[1,12,128,256]{3,2,1,0:T(8,128)(2,1)S(1)}, bf16[1,12,128,256]{3,2,1,0:T(8,128)(2,1)}, u32[]{:S(2)}) copy-start(bf16[1,12,128,256]{3,2,1,0:T(8,128)(2,1)} %param.21) | copy-start | bytes 2359300
  19.6 14.2 %collective-permute-start.3 = (bf16[256,256]{1,0:T(8,128)(2,1)S(1)}, bf16[256,256]{1,0:T(8,128)(2,1)S(1)}, u32[]{:S(2)}, u32[]{:S(2)}) collective-permute-start(bf16[256,256]{1,0:T(8,128)(2,1)S(1)} %fusion.1), channel_id=1, source_target_pairs={{0,2},{1,3},{2,0},{3,1},{4,6},{5,7},{6,4},{7,5},{8,10},{9,11},{10,... | collective-permute-start | bytes 393224 | tf_op jit(solution)/shard_map/ppermute | solution.py:394
  22.7 25.1 %collective-permute-start.1 = (bf16[384,256]{1,0:T(8,128)(2,1)S(1)}, bf16[384,256]{1,0:T(8,128)(2,1)S(1)}, u32[]{:S(2)}, u32[]{:S(2)}) collective-permute-start(bf16[384,256]{1,0:T(8,128)(2,1)S(1)} %fusion), channel_id=1, source_target_pairs={{0,2},{1,3},{2,0},{3,1},{4,6},{5,7},{6,4},{7,5},{8,10},{9,11},{10,... | collective-permute-start | bytes 589832 | tf_op jit(solution)/shard_map/ppermute | solution.py:394
  35.0 5.4 %collective-permute-start.4 = (bf16[128,256]{1,0:T(8,128)(2,1)S(1)}, bf16[128,256]{1,0:T(8,128)(2,1)S(1)}, u32[]{:S(2)}, u32[]{:S(2)}) collective-permute-start(bf16[128,256]{1,0:T(8,128)(2,1)S(1)} %get-tuple-element.27.refs_0_), channel_id=1, source_target_pairs={{0,4},{4,0},{8,12},{12,8},{1,5},{5,1},{9,13},{13,9},{2,6},{6,2},{1... | collective-permute-start | bytes 196616 | tf_op jit(solution)/shard_map/ppermute | solution.py:394
  35.1 5.3 %collective-permute-start.5 = (bf16[128,256]{1,0:T(8,128)(2,1)S(1)}, bf16[128,256]{1,0:T(8,128)(2,1)S(1)}, u32[]{:S(2)}, u32[]{:S(2)}) collective-permute-start(bf16[128,256]{1,0:T(8,128)(2,1)S(1)} %get-tuple-element.27.refs_0_), channel_id=1, source_target_pairs={{0,8},{4,12},{8,0},{12,4},{1,9},{5,13},{9,1},{13,5},{2,10},{6,14},... | collective-permute-start | bytes 196616 | tf_op jit(solution)/shard_map/ppermute | solution.py:394
  36.8 4.1 %collective-permute-start.6 = (bf16[128,256]{1,0:T(8,128)(2,1)S(1)}, bf16[128,256]{1,0:T(8,128)(2,1)S(1)}, u32[]{:S(2)}, u32[]{:S(2)}) collective-permute-start(bf16[128,256]{1,0:T(8,128)(2,1)S(1)} %get-tuple-element.27.refs_0_), channel_id=1, source_target_pairs={{0,12},{4,8},{8,4},{12,0},{1,13},{5,9},{9,5},{13,1},{2,14},{6,10},... | collective-permute-start | bytes 196616 | tf_op jit(solution)/shard_map/ppermute | solution.py:394
  44.7 25.3 %collective-permute-start.17 = (bf16[128,1024]{1,0:T(8,128)(2,1)S(1)}, bf16[128,1024]{1,0:T(8,128)(2,1)S(1)}, u32[]{:S(2)}, u32[]{:S(2)}) collective-permute-start(bf16[128,1024]{1,0:T(8,128)(2,1)S(1)} %attend_new.7.refs_0_), channel_id=1, source_target_pairs={{0,2},{1,3},{2,0},{3,1},{4,6},{5,7},{6,4},{7,5},{8,10},{9,11},{10,... | collective-permute-start | bytes 786440 | tf_op jit(solution)/shard_map/ppermute | solution.py:394
  44.8 25.3 %collective-permute-start.18 = (bf16[128,1024]{1,0:T(8,128)(2,1)S(1)}, bf16[128,1024]{1,0:T(8,128)(2,1)S(1)}, u32[]{:S(2)}, u32[]{:S(2)}) collective-permute-start(bf16[128,1024]{1,0:T(8,128)(2,1)S(1)} %attend_new.7.refs_0_), channel_id=1, source_target_pairs={{0,1},{1,0},{2,3},{3,2},{4,5},{5,4},{6,7},{7,6},{8,9},{9,8},{10,11... | collective-permute-start | bytes 786440 | tf_op jit(solution)/shard_map/ppermute | solution.py:394
  57.2 38.3 %collective-permute-start.13 = (bf16[256,1024]{1,0:T(8,128)(2,1)S(1)}, bf16[256,1024]{1,0:T(8,128)(2,1)S(1)}, u32[]{:S(2)}, u32[]{:S(2)}) collective-permute-start(bf16[256,1024]{1,0:T(8,128)(2,1)S(1)} %pad_maximum_fusion), channel_id=1, source_target_pairs={{0,2},{1,3},{2,0},{3,1},{4,6},{5,7},{6,4},{7,5},{8,10},{9,11},{10,... | collective-permute-start | bytes 1572872 | tf_op jit(solution)/shard_map/ppermute | solution.py:394
  60.8 14.1 %collective-permute-start.19 = (bf16[128,1024]{1,0:T(8,128)(2,1)S(1)}, bf16[128,1024]{1,0:T(8,128)(2,1)S(1)}, u32[]{:S(2)}, u32[]{:S(2)}) collective-permute-start(bf16[128,1024]{1,0:T(8,128)(2,1)S(1)} %attend_new.7.refs_0_), channel_id=1, source_target_pairs={{1,2},{2,1},{5,6},{6,5},{9,10},{10,9},{13,14},{14,13},{17,18},{18,... | collective-permute-start | bytes 786440 | tf_op jit(solution)/shard_map/ppermute | solution.py:543
  61.4 27.3 %collective-permute-start.15 = (bf16[128,1024]{1,0:T(8,128)(2,1)S(1)}, bf16[128,1024]{1,0:T(8,128)(2,1)S(1)}, u32[]{:S(2)}, u32[]{:S(2)}) collective-permute-start(bf16[128,1024]{1,0:T(8,128)(2,1)S(1)} %attend_new.5.refs_0_), channel_id=1, source_target_pairs={{0,1},{1,0},{2,3},{3,2},{4,5},{5,4},{6,7},{7,6},{8,9},{9,8},{10,11... | collective-permute-start | bytes 786440 | tf_op jit(solution)/shard_map/ppermute | solution.py:394
  70.0 19.4 %collective-permute-start.11 = (bf16[128,1024]{1,0:T(8,128)(2,1)S(1)}, bf16[128,1024]{1,0:T(8,128)(2,1)S(1)}, u32[]{:S(2)}, u32[]{:S(2)}) collective-permute-start(bf16[128,1024]{1,0:T(8,128)(2,1)S(1)} %attend_new.4.refs_0_), channel_id=1, source_target_pairs={{0,1},{1,0},{2,3},{3,2},{4,5},{5,4},{6,7},{7,6},{8,9},{9,8},{10,11... | collective-permute-start | bytes 786440 | tf_op jit(solution)/shard_map/ppermute | solution.py:394
  70.1 24.7 %collective-permute-start.20 = (bf16[128,1024]{1,0:T(8,128)(2,1)S(1)}, bf16[128,1024]{1,0:T(8,128)(2,1)S(1)}, u32[]{:S(2)}, u32[]{:S(2)}) collective-permute-start(bf16[128,1024]{1,0:T(8,128)(2,1)S(1)} %collective-permute-done.17.refs_1_), channel_id=1, source_target_pairs={{1,0},{2,3},{5,4},{6,7},{9,8},{10,11},{13,12},{14,15},{17,16},{18,... | collective-permute-start | bytes 786440 | tf_op jit(solution)/shard_map/ppermute | solution.py:547
  74.9 35.6 %collective-permute-start.16 = (bf16[128,1024]{1,0:T(8,128)(2,1)S(1)}, bf16[128,1024]{1,0:T(8,128)(2,1)S(1)}, u32[]{:S(2)}, u32[]{:S(2)}) collective-permute-start(bf16[128,1024]{1,0:T(8,128)(2,1)S(1)} %attend_new.6.refs_1_), channel_id=1, source_target_pairs={{0,1},{1,0},{2,3},{3,2},{4,5},{5,4},{6,7},{7,6},{8,9},{9,8},{10,11... | collective-permute-start | bytes 786440 | tf_op jit(solution)/shard_map/ppermute | solution.py:394
  88.7 27.5 %collective-permute-start.12 = (bf16[256,1024]{1,0:T(8,128)(2,1)S(1)}, bf16[256,1024]{1,0:T(8,128)(2,1)S(1)}, u32[]{:S(2)}, u32[]{:S(2)}) collective-permute-start(bf16[256,1024]{1,0:T(8,128)(2,1)S(1)} %pad_maximum_fusion), channel_id=1, source_target_pairs={{1,2},{2,1},{5,6},{6,5},{9,10},{10,9},{13,14},{14,13},{17,18},{18,... | collective-permute-start | bytes 1572872 | tf_op jit(solution)/shard_map/ppermute | solution.py:543
  89.4 18.2 %collective-permute-start.7 = (bf16[128,1024]{1,0:T(8,128)(2,1)S(1)}, bf16[128,1024]{1,0:T(8,128)(2,1)S(1)}, u32[]{:S(2)}, u32[]{:S(2)}) collective-permute-start(bf16[128,1024]{1,0:T(8,128)(2,1)S(1)} %attend_new.4.refs_0_), channel_id=1, source_target_pairs={{0,2},{3,1},{4,6},{7,5},{8,10},{11,9},{12,14},{15,13},{16,18},{19,... | collective-permute-start | bytes 786440 | tf_op jit(solution)/shard_map/ppermute | solution.py:542
  94.8 14.2 %collective-permute-start.8 = (bf16[128,1024]{1,0:T(8,128)(2,1)S(1)}, bf16[128,1024]{1,0:T(8,128)(2,1)S(1)}, u32[]{:S(2)}, u32[]{:S(2)}) collective-permute-start(bf16[128,1024]{1,0:T(8,128)(2,1)S(1)} %attend_new.4.refs_0_), channel_id=1, source_target_pairs={{1,2},{2,1},{5,6},{6,5},{9,10},{10,9},{13,14},{14,13},{17,18},{18,... | collective-permute-start | bytes 786440 | tf_op jit(solution)/shard_map/ppermute | solution.py:543
  95.5 20.8 %collective-permute-start.14 = (bf16[256,1024]{1,0:T(8,128)(2,1)S(1)}, bf16[256,1024]{1,0:T(8,128)(2,1)S(1)}, u32[]{:S(2)}, u32[]{:S(2)}) collective-permute-start(bf16[256,1024]{1,0:T(8,128)(2,1)S(1)} %collective-permute-done.13.refs_4_), channel_id=1, source_target_pairs={{1,0},{2,3},{5,4},{6,7},{9,8},{10,11},{13,12},{14,15},{17,16},{18,... | collective-permute-start | bytes 1572872 | tf_op jit(solution)/shard_map/ppermute | solution.py:547
  107.7 11.0 %collective-permute-start.10 = (bf16[128,1024]{1,0:T(8,128)(2,1)S(1)}, bf16[128,1024]{1,0:T(8,128)(2,1)S(1)}, u32[]{:S(2)}, u32[]{:S(2)}) collective-permute-start(bf16[128,1024]{1,0:T(8,128)(2,1)S(1)} %collective-permute-done.7.refs_0_), channel_id=1, source_target_pairs={{1,0},{2,3},{5,4},{6,7},{9,8},{10,11},{13,12},{14,15},{17,16},{18,... | collective-permute-start | bytes 786440 | tf_op jit(solution)/shard_map/ppermute | solution.py:547
  109.0 13.6 %collective-permute-start.9 = (bf16[128,1024]{1,0:T(8,128)(2,1)S(1)}, bf16[128,1024]{1,0:T(8,128)(2,1)S(1)}, u32[]{:S(2)}, u32[]{:S(2)}) collective-permute-start(bf16[128,1024]{1,0:T(8,128)(2,1)S(1)} %collective-permute-done.8.refs_2_), channel_id=1, source_target_pairs={{1,0},{2,3},{5,4},{6,7},{9,8},{10,11},{13,12},{14,15},{17,16},{18,... | collective-permute-start | bytes 786440 | tf_op jit(solution)/shard_map/ppermute | solution.py:546

commit v7 on v6

--- a/solution.py
+++ b/solution.py
@@ -43,6 +43,8 @@
 SMALL = pltpu.CompilerParams(vmem_limit_bytes=24 << 20)
 LARGE = pltpu.CompilerParams(vmem_limit_bytes=36 << 20)
 SET_ROWS = 32
+SPAN_GROUP = 2
+PAGE_GROUP = 3
 
 
 def in_hbm(x):
@@ -113,7 +115,7 @@
     steps = q_ref.shape[1]
     prompt = by_row(fork_ref[...], (pl.program_id(0) + start) * block, m, steps)
     pages, size = pool_ref.shape[:2]
-    group = cpages
+    group = PAGE_GROUP
 
     def part(at):
         mine = range(at, min(at + group, pages))
@@ -154,29 +156,28 @@
     at = skip * m if direct else 0
     mine = slice(at, at + m)
 
-    def loaded():
-        return jnp.concatenate([ref[...] for ref in span_refs], 0)
-
-    def owned():
-        return jnp.concatenate(
-            [
-                jnp.broadcast_to(
-                    shown(prompt == owner_ref[base_ref[0] ^ j].astype(jnp.float32)), (m, span)
-                )
-                for j in range(len(span_refs))
-            ],
-            1,
-        )
+    def spans(mine):
+        def load():
+            return jnp.concatenate([span_refs[j][...] for j in mine], 0)
+
+        def bias():
+            owners = [owner_ref[base_ref[0] ^ j].astype(jnp.float32) for j in mine]
+            return jnp.concatenate(
+                [jnp.broadcast_to(shown(prompt == owner), (m, span)) for owner in owners], 1
+            )
+
+        return span * len(mine), load, bias
 
     def causal():
         row = lax.broadcasted_iota(jnp.int32, (m, m), 0)
         col = lax.broadcasted_iota(jnp.int32, (m, m), 1)
         return shown((row // steps == col // steps) & (col <= row))
 
-    parts = (
-        (span * len(span_refs), loaded, owned),
-        (m, lambda: tail_ref[...], causal),
-    )
+    count = len(span_refs)
+    parts = [
+        spans(range(at, min(at + SPAN_GROUP, count))) for at in range(0, count, SPAN_GROUP)
+    ]
+    parts.append((m, lambda: tail_ref[...], causal))
     top, total, mixed = softmax_parts(qs, heads, parts, scale2, s_ref)
     old_top = stat_ref[:, mine, :1]
     old_total = stat_ref[:, mine, HD // 2 : HD // 2 + 1]
@@ -693,8 +694,11 @@
     two, three = far_heads(last_own, True)
     pieces = ((0, [last_own], None), (1, near, None))
     partial = out_project(rank, pieces, out_weight, shape, 0, final=False)
+    partial = out_project(
+        rank, (two,), held_rows, shape, 0, partial=partial, final=False, held=held
+    )
     return out_project(
-        rank, (two, three), held_rows, shape, first * (blocks - 1),
+        rank, (three,), held_rows, shape, first * (blocks - 1),
         partial=partial, into=decoded, held=held,
     )
 

time: 125 us -> 126 us (level)
  Pallas kernels: 64.7 us -> 63.1 us
  waiting for transfers between devices: 13.2 us -> 14.8 us
    pallas_call x4, Pallas kernels: 15.6 us -> 13.7 us  [attend_new(): pl.pallas_call(functools.partial(new_kernel, heads, block, direct, skip,...]
    ppermute x1, waiting for transfers between devices: 3.92 us -> 5.35 us  [far_heads(): forward = lax.ppermute(across, 'tensor', outward)]
    pallas_call x5 -> x6, Pallas kernels: 21.1 us -> 21.3 us  [out_project(): pl.pallas_call(functools.partial(out_kernel, rels, shapes, cuts, partial...]
  transfers between devices with their start and end apart: 21 -> 21, of which waited for: 4 -> 4; matrix products, arithmetic and copies ran while one was open for 0% -> 0% of each run, Pallas kernels for 47% -> 46%
where the time goes in v7:
time: 126 us
  Pallas kernels  63.1 us (50%)
  starting transfers between devices  46 us (37%)
  waiting for transfers between devices  14.8 us (12%)
    ppermute x13, starting transfers between devices, swap(): lax.ppermute(x, axis, [(i, i ^ bit) for i in range(lax.axis_size(axis))])  33.9 us
    pallas_call x6, Pallas kernels, out_project(): pl.pallas_call(functools.partial(out_kernel, rels, shapes, cuts, partial...  21.3 us
    pallas_call x4, Pallas kernels, attend_new(): pl.pallas_call(functools.partial(new_kernel, heads, block, direct, skip,...  13.7 us
    pallas_call x3, Pallas kernels, attend_cached(): pl.pallas_call(functools.partial(cached_kernel, heads, block, direct, cpa...  13.6 us
    ppermute x13, waiting for transfers between devices, swap(): lax.ppermute(x, axis, [(i, i ^ bit) for i in range(lax.axis_size(axis))])  8.54 us
    pallas_call x2, Pallas kernels, project(): pl.pallas_call(functools.partial(project_kernel, len(groups), split, kept...  8.39 us
    ppermute x1, waiting for transfers between devices, far_heads(): forward = lax.ppermute(across, 'tensor', outward)  5.35 us
    ppermute x1, starting transfers between devices, far_heads(): lax.ppermute(own, 'tensor', [(0, 2), (3, 1)])  4.62 us
  transfers between devices with their start and end apart: 21, of which 4 were waited for; matrix products, arithmetic and copies ran while one was open for 0% of the time, Pallas kernels for 46%

profile of v7, /device:TPU:0, one launch (start us, length us, event | category | flops | bytes accessed | tf_op | source)
XLA Modules:
  0.0 125.6 jit_solution(2330090942514127390)
XLA Ops:
  0.0 4.1 %project.3 = (f32[2,256,256]{2,1,0:T(8,128)S(1)}, bf16[2,256,256]{2,1,0:T(8,128)(2,1)}) custom-call(s32[1]{0:T(128)} %bitcast.rank_ref, bf16[128,2048]{1,0:T(8,128)(2,1)} %refs_0_.3, bf16[128,4,2048]{2,1,0:T(4,128)(2,1)} %refs_1_.3, bf16[2048,512]{1,0:T(8,128)(2,1)} %refs_4_.3, bf16[2048,512]{1,0:T(8,128)(2,1)} %refs_5_.3, bf16[2048,512]{1,0:T(8,128)(2,1)} %refs_4_.3, ...), custom_call_target="tpu_custom_call" | custom-call | flops 1073741824 | bytes 4194304 | tf_op jit(solution)/shard_map/project/pallas_call | solution.py:314
  4.1 0.0 copy-start.3
  4.2 0.0 copy-start.6
  4.2 3.1 %collective-permute-start.2 = (bf16[2,256,256]{2,1,0:T(8,128)(2,1)}, bf16[2,256,256]{2,1,0:T(8,128)(2,1)S(1)}, u32[]{:S(2)}, u32[]{:S(2)}) collective-permute-start(bf16[2,256,256]{2,1,0:T(8,128)(2,1)} %get-tuple-element.26), channel_id=1, source_target_pairs={{0,1},{1,0},{2,3},{3,2},{4,5},{5,4},{6,7},{7,6},{8,9},{9,8},{10,11... | collective-permute-start | bytes 786440 | tf_op jit(solution)/shard_map/ppermute | solution.py:395
  7.3 4.3 %project.2 = (f32[2,384,256]{2,1,0:T(8,128)S(1)}, bf16[2,384,256]{2,1,0:T(8,128)(2,1)S(1)}) custom-call(s32[1]{0:T(128)} %bitcast.rank_ref, bf16[128,4,2048]{2,1,0:T(4,128)(2,1)} %refs_1_.3, bf16[2048,512]{1,0:T(8,128)(2,1)} %refs_4_.3, bf16[2048,512]{1,0:T(8,128)(2,1)} %refs_5_.3, bf16[2048,512]{1,0:T(8,128)(2,1)} %refs_4_.3, bf16[2048,512]{1,0:T(8,128)(2,1)} %refs_5_.3), custom_call_target="tpu_custom_call" | custom-call | flops 1610612736 | bytes 4194304 | tf_op jit(solution)/shard_map/project/pallas_call | solution.py:314
  11.6 0.2 collective-permute-start
  11.8 0.0 copy-start.4
  11.8 1.1 copy-done.4
  12.9 6.7 %attend_cached.4 = (f32[8,256,128]{2,1,0:T(8,128)S(1)}, f32[8,256,128]{2,1,0:T(8,128)S(1)}) custom-call(s32[12]{0:T(128)S(1)} %copy-done.6, s32[4]{0:T(128)S(1)} %copy-done.3, bf16[128,4,1024]{2,1,0:T(4,128)(2,1)S(1)} %copy-done, s32[1,128]{1,0:T(1,128)S(1)} %bitcast.10, bf16[12,128,256]{2,1,0:T(8,128)(2,1)S(1)} %bitcast.19), custom_call_target="tpu_custom_call" | custom-call | flops 1610612736 | bytes 2097152 | tf_op jit(solution)/shard_map/attend_cached/pallas_call | solution.py:202
  19.6 3.0 %collective-permute-start.3 = (bf16[256,256]{1,0:T(8,128)(2,1)S(1)}, bf16[256,256]{1,0:T(8,128)(2,1)S(1)}, u32[]{:S(2)}, u32[]{:S(2)}) collective-permute-start(bf16[256,256]{1,0:T(8,128)(2,1)S(1)} %fusion.1), channel_id=1, source_target_pairs={{0,2},{1,3},{2,0},{3,1},{4,6},{5,7},{6,4},{7,5},{8,10},{9,11},{10,... | collective-permute-start | bytes 393224 | tf_op jit(solution)/shard_map/ppermute | solution.py:395
  22.7 3.0 %collective-permute-start.1 = (bf16[384,256]{1,0:T(8,128)(2,1)S(1)}, bf16[384,256]{1,0:T(8,128)(2,1)S(1)}, u32[]{:S(2)}, u32[]{:S(2)}) collective-permute-start(bf16[384,256]{1,0:T(8,128)(2,1)S(1)} %fusion), channel_id=1, source_target_pairs={{0,2},{1,3},{2,0},{3,1},{4,6},{5,7},{6,4},{7,5},{8,10},{9,11},{10,... | collective-permute-start | bytes 589832 | tf_op jit(solution)/shard_map/ppermute | solution.py:395
  25.7 0.1 maximum_bitcast_fusion.freq_ref
  25.7 8.1 %collective-permute-done.3.refs_1_ = bf16[256,256]{1,0:T(8,128)(2,1)S(1)} collective-permute-done((bf16[256,256]{1,0:T(8,128)(2,1)S(1)}, bf16[256,256]{1,0:T(8,128)(2,1)S(1)}, u32[]{:S(2)}, u32[]{:S(2)}) %collective-permute-start.3) | collective-permute-done | bytes 131104 | tf_op jit(solution)/shard_map/ppermute | solution.py:395
  33.9 1.2 finish.3
  35.0 0.1 collective-permute-start.4
  35.1 1.7 %collective-permute-start.5 = (bf16[128,256]{1,0:T(8,128)(2,1)S(1)}, bf16[128,256]{1,0:T(8,128)(2,1)S(1)}, u32[]{:S(2)}, u32[]{:S(2)}) collective-permute-start(bf16[128,256]{1,0:T(8,128)(2,1)S(1)} %get-tuple-element.27.refs_0_), channel_id=1, source_target_pairs={{0,8},{4,12},{8,0},{12,4},{1,9},{5,13},{9,1},{13,5},{2,10},{6,14},... | collective-permute-start | bytes 196616 | tf_op jit(solution)/shard_map/ppermute | solution.py:395
  36.8 0.2 collective-permute-start.6
  37.0 3.4 %attend_cached.5 = (f32[8,128,128]{2,1,0:T(8,128)S(1)}, f32[8,128,128]{2,1,0:T(8,128)S(1)}) custom-call(s32[12]{0:T(128)S(1)} %copy-done.6, s32[4]{0:T(128)S(1)} %copy-done.3, bf16[128,4,1024]{2,1,0:T(4,128)(2,1)S(1)} %copy-done, s32[1,128]{1,0:T(1,128)S(1)} %bitcast.12, bf16[12,128,256]{2,1,0:T(8,128)(2,1)S(1)} %bitcast.20), custom_call_target="tpu_custom_call" | custom-call | flops 805306368 | bytes 1048576 | tf_op jit(solution)/shard_map/attend_cached/pallas_call | solution.py:202
  40.4 0.4 collective-permute-done.6.refs_3_
  40.8 3.3 %attend_new.7.refs_0_ = bf16[128,1024]{1,0:T(8,128)(2,1)S(1)} custom-call(s32[4]{0:T(128)S(1)} %copy-done.1, s32[1]{0:T(128)} %bitcast.1.replica_ref.base_ref, bf16[128,4,1024]{2,1,0:T(4,128)(2,1)S(1)} %copy-done, s32[1,128]{1,0:T(1,128)S(1)} %bitcast.13, bf16[128,256]{1,0:T(8,128)(2,1)S(1)} %get-tuple-element.32.tail_ref, ...), custom_call_target="tpu_custom_call" | custom-call | flops 335544320 | bytes 1310720 | tf_op jit(solution)/shard_map/attend_new/pallas_call | solution.py:239
  44.2 0.1 collective-permute-start.17
  44.3 3.0 %collective-permute-start.18 = (bf16[128,1024]{1,0:T(8,128)(2,1)S(1)}, bf16[128,1024]{1,0:T(8,128)(2,1)S(1)}, u32[]{:S(2)}, u32[]{:S(2)}) collective-permute-start(bf16[128,1024]{1,0:T(8,128)(2,1)S(1)} %attend_new.7.refs_0_), channel_id=1, source_target_pairs={{0,1},{1,0},{2,3},{3,2},{4,5},{5,4},{6,7},{7,6},{8,9},{9,8},{10,11... | collective-permute-start | bytes 786440 | tf_op jit(solution)/shard_map/ppermute | solution.py:395
  47.3 1.4 %finish.2 = (bf16[128,256]{1,0:T(8,128)(2,1)S(1)}, bf16[128,256]{1,0:T(8,128)(2,1)S(1)}, bf16[128,256]{1,0:T(8,128)(2,1)S(1)}) custom-call(s32[4]{0:T(128)S(1)} %copy-done.1, s32[4]{0:T(128)S(1)} %copy-done.3, s32[1]{0:T(128)} %bitcast.1.replica_ref.base_ref, s32[1,128]{1,0:T(1,128)S(1)} %bitcast.14, f32[1,128]{1,0:T(1,128)S(1)} %maximum_bitcast_fusion.freq_ref, ...), custom_call_target="tpu_custom_call" | custom-call | tf_op jit(solution)/shard_map/finish/pallas_call | solution.py:380
  48.7 3.4 %attend_new.5.refs_0_ = bf16[128,1024]{1,0:T(8,128)(2,1)S(1)} custom-call(s32[4]{0:T(128)S(1)} %copy-done.1, s32[1]{0:T(128)} %bitcast.1.replica_ref.base_ref, bf16[128,4,1024]{2,1,0:T(4,128)(2,1)S(1)} %copy-done, s32[1,128]{1,0:T(1,128)S(1)} %bitcast.15, bf16[128,256]{1,0:T(8,128)(2,1)S(1)} %get-tuple-element.28.tail_ref, ...), custom_call_target="tpu_custom_call" | custom-call | flops 335544320 | bytes 1310720 | tf_op jit(solution)/shard_map/attend_new/pallas_call | solution.py:239
  52.1 3.6 %attend_new.6.refs_1_ = bf16[128,1024]{1,0:T(8,128)(2,1)S(1)} custom-call(s32[4]{0:T(128)S(1)} %copy-done.1, s32[1]{0:T(128)} %bitcast.1.replica_ref.base_ref, bf16[128,4,1024]{2,1,0:T(4,128)(2,1)S(1)} %copy-done, s32[1,128]{1,0:T(1,128)S(1)} %bitcast.16, bf16[128,256]{1,0:T(8,128)(2,1)S(1)} %get-tuple-element.31.tail_ref, ...), custom_call_target="tpu_custom_call" | custom-call | flops 335544320 | bytes 1310720 | tf_op jit(solution)/shard_map/attend_new/pallas_call | solution.py:239
  55.8 0.1 collective-permute-start.13
  55.9 3.4 %attend_cached.3 = (f32[8,128,128]{2,1,0:T(8,128)S(1)}, f32[8,128,128]{2,1,0:T(8,128)S(1)}) custom-call(s32[12]{0:T(128)S(1)} %copy-done.6, s32[4]{0:T(128)S(1)} %copy-done.3, bf16[128,4,1024]{2,1,0:T(4,128)(2,1)S(1)} %copy-done, s32[1,128]{1,0:T(1,128)S(1)} %bitcast.17, bf16[12,128,256]{2,1,0:T(8,128)(2,1)S(1)} %bitcast.21), custom_call_target="tpu_custom_call" | custom-call | flops 805306368 | bytes 1048576 | tf_op jit(solution)/shard_map/attend_cached/pallas_call | solution.py:202
  59.4 0.7 collective-permute-start.19
  60.0 4.7 %collective-permute-start.15 = (bf16[128,1024]{1,0:T(8,128)(2,1)S(1)}, bf16[128,1024]{1,0:T(8,128)(2,1)S(1)}, u32[]{:S(2)}, u32[]{:S(2)}) collective-permute-start(bf16[128,1024]{1,0:T(8,128)(2,1)S(1)} %attend_new.5.refs_0_), channel_id=1, source_target_pairs={{0,1},{1,0},{2,3},{3,2},{4,5},{5,4},{6,7},{7,6},{8,9},{9,8},{10,11... | collective-permute-start | bytes 786440 | tf_op jit(solution)/shard_map/ppermute | solution.py:395
  64.7 3.4 %attend_new.4.refs_0_ = bf16[128,1024]{1,0:T(8,128)(2,1)S(1)} custom-call(s32[4]{0:T(128)S(1)} %copy-done.1, s32[1]{0:T(128)} %bitcast.1.replica_ref.base_ref, bf16[128,4,1024]{2,1,0:T(4,128)(2,1)S(1)} %copy-done, s32[1,128]{1,0:T(1,128)S(1)} %bitcast.18, bf16[128,256]{1,0:T(8,128)(2,1)S(1)} %get-tuple-element.22.tail_ref, ...), custom_call_target="tpu_custom_call" | custom-call | flops 335544320 | bytes 1310720 | tf_op jit(solution)/shard_map/attend_new/pallas_call | solution.py:239
  68.1 0.1 collective-permute-start.11
  68.2 1.3 %collective-permute-start.20 = (bf16[128,1024]{1,0:T(8,128)(2,1)S(1)}, bf16[128,1024]{1,0:T(8,128)(2,1)S(1)}, u32[]{:S(2)}, u32[]{:S(2)}) collective-permute-start(bf16[128,1024]{1,0:T(8,128)(2,1)S(1)} %collective-permute-done.17.refs_1_), channel_id=1, source_target_pairs={{1,0},{2,3},{5,4},{6,7},{9,8},{10,11},{13,12},{14,15},{17,16},{18,... | collective-permute-start | bytes 786440 | tf_op jit(solution)/shard_map/ppermute | solution.py:548
  69.5 3.5 %hold.1.refs_3_ = bf16[2048,2048]{1,0:T(8,128)(2,1)S(1)} custom-call(s32[1]{0:T(128)} %bitcast.rank_ref, bf16[4096,2048]{1,0:T(8,128)(2,1)} %refs_5_.5), custom_call_target="tpu_custom_call" | custom-call | tf_op jit(solution)/shard_map/hold/pallas_call | solution.py:518
  73.0 14.7 %collective-permute-start.16 = (bf16[128,1024]{1,0:T(8,128)(2,1)S(1)}, bf16[128,1024]{1,0:T(8,128)(2,1)S(1)}, u32[]{:S(2)}, u32[]{:S(2)}) collective-permute-start(bf16[128,1024]{1,0:T(8,128)(2,1)S(1)} %attend_new.6.refs_1_), channel_id=1, source_target_pairs={{0,1},{1,0},{2,3},{3,2},{4,5},{5,4},{6,7},{7,6},{8,9},{9,8},{10,11... | collective-permute-start | bytes 786440 | tf_op jit(solution)/shard_map/ppermute | solution.py:395
  87.7 0.7 collective-permute-start.7
  88.4 4.6 %collective-permute-start.8 = (bf16[128,1024]{1,0:T(8,128)(2,1)S(1)}, bf16[128,1024]{1,0:T(8,128)(2,1)S(1)}, u32[]{:S(2)}, u32[]{:S(2)}) collective-permute-start(bf16[128,1024]{1,0:T(8,128)(2,1)S(1)} %attend_new.4.refs_0_), channel_id=1, source_target_pairs={{0,2},{3,1},{4,6},{7,5},{8,10},{11,9},{12,14},{15,13},{16,18},{19,... | collective-permute-start | bytes 786440 | tf_op jit(solution)/shard_map/ppermute | solution.py:543
  93.0 3.8 %out_project.6.refs_2_ = f32[128,2048]{1,0:T(8,128)S(1)} custom-call(s32[1]{0:T(128)} %bitcast.rank_ref, bf16[128,1024]{1,0:T(8,128)(2,1)S(1)} %attend_new.4.refs_0_, bf16[128,1024]{1,0:T(8,128)(2,1)S(1)} %collective-permute-done.11.refs_1_, bf16[4096,2048]{1,0:T(8,128)(2,1)} %refs_5_.5), custom_call_target="tpu_custom_call" | custom-call | flops 1073741824 | bytes 8388608 | tf_op jit(solution)/shard_map/out_project/pallas_call | solution.py:476
  96.9 0.7 collective-permute-start.12
  97.6 1.3 %collective-permute-start.14 = (bf16[256,1024]{1,0:T(8,128)(2,1)S(1)}, bf16[256,1024]{1,0:T(8,128)(2,1)S(1)}, u32[]{:S(2)}, u32[]{:S(2)}) collective-permute-start(bf16[256,1024]{1,0:T(8,128)(2,1)S(1)} %collective-permute-done.13.refs_4_), channel_id=1, source_target_pairs={{1,0},{2,3},{5,4},{6,7},{9,8},{10,11},{13,12},{14,15},{17,16},{18,... | collective-permute-start | bytes 1572872 | tf_op jit(solution)/shard_map/ppermute | solution.py:548
  98.9 7.1 %out_project.9.refs_4_ = bf16[128,4,2048]{2,1,0:T(4,128)(2,1)} custom-call(s32[1]{0:T(128)} %bitcast.rank_ref, bf16[128,1024]{1,0:T(8,128)(2,1)S(1)} %attend_new.7.refs_0_, bf16[128,1024]{1,0:T(8,128)(2,1)S(1)} %collective-permute-done.17.refs_1_, bf16[128,1024]{1,0:T(8,128)(2,1)S(1)} %collective-permute-done.18.refs_2_, ...), custom_call_target="tpu_custom_call" | custom-call | flops 2147483648 | bytes 16777216 | tf_op jit(solution)/shard_map/out_project/pallas_call | solution.py:476
  106.0 1.3 %collective-permute-start.10 = (bf16[128,1024]{1,0:T(8,128)(2,1)S(1)}, bf16[128,1024]{1,0:T(8,128)(2,1)S(1)}, u32[]{:S(2)}, u32[]{:S(2)}) collective-permute-start(bf16[128,1024]{1,0:T(8,128)(2,1)S(1)} %collective-permute-done.7.refs_0_), channel_id=1, source_target_pairs={{1,0},{2,3},{5,4},{6,7},{9,8},{10,11},{13,12},{14,15},{17,16},{18,... | collective-permute-start | bytes 786440 | tf_op jit(solution)/shard_map/ppermute | solution.py:547
  107.3 1.6 %collective-permute-start.9 = (bf16[128,1024]{1,0:T(8,128)(2,1)S(1)}, bf16[128,1024]{1,0:T(8,128)(2,1)S(1)}, u32[]{:S(2)}, u32[]{:S(2)}) collective-permute-start(bf16[128,1024]{1,0:T(8,128)(2,1)S(1)} %collective-permute-done.8.refs_0_), channel_id=1, source_target_pairs={{1,0},{2,3},{5,4},{6,7},{9,8},{10,11},{13,12},{14,15},{17,16},{18,... | collective-permute-start | bytes 786440 | tf_op jit(solution)/shard_map/ppermute | solution.py:548
  108.8 5.7 %out_project.8.refs_2_ = f32[256,2048]{1,0:T(8,128)S(1)} custom-call(s32[1]{0:T(128)} %bitcast.rank_ref, bf16[128,1024]{1,0:T(8,128)(2,1)S(1)} %attend_new.5.refs_0_, bf16[128,1024]{1,0:T(8,128)(2,1)S(1)} %attend_new.6.refs_1_, bf16[128,1024]{1,0:T(8,128)(2,1)S(1)} %collective-permute-done.15.refs_2_, bf16[128,1024]{1,0:T(8,128)(2,1)S(1)} %collective-permute-done.16.refs_3_, ...), custom_call_target="tpu_custom_call" | custom-call | flops 3221225472 | bytes 12582912 | tf_op jit(solution)/shard_map/out_project/pallas_call | solution.py:476
  114.5 5.3 %collective-permute-done.10.refs_1_ = bf16[128,1024]{1,0:T(8,128)(2,1)S(1)} collective-permute-done((bf16[128,1024]{1,0:T(8,128)(2,1)S(1)}, bf16[128,1024]{1,0:T(8,128)(2,1)S(1)}, u32[]{:S(2)}, u32[]{:S(2)}) %collective-permute-start.10) | collective-permute-done | bytes 262176 | tf_op jit(solution)/shard_map/ppermute | solution.py:547
  119.9 0.7 out_project.7.refs_2_
  120.6 2.4 %out_project.10.refs_4_ = bf16[128,4,2048]{2,1,0:T(4,128)(2,1)} custom-call(s32[1]{0:T(128)} %bitcast.rank_ref, bf16[256,1024]{1,0:T(8,128)(2,1)S(1)} %collective-permute-done.12.refs_0_, bf16[256,1024]{1,0:T(8,128)(2,1)S(1)} %collective-permute-done.14.refs_1_, f32[256,2048]{1,0:T(8,128)S(1)} %out_project.8.refs_2_, ...), custom_call_target="tpu_custom_call", output_to_operand_aliasing={{}: (5, {})} | custom-call | flops 1073741824 | bytes 4194304 | tf_op jit(solution)/shard_map/out_project/pallas_call | solution.py:476
  123.0 0.9 collective-permute-done.9.refs_1_
  124.0 1.6 %out_project.11 = bf16[128,4,2048]{2,1,0:T(4,128)(2,1)} custom-call(s32[1]{0:T(128)} %bitcast.rank_ref, bf16[128,1024]{1,0:T(8,128)(2,1)S(1)} %collective-permute-done.7.refs_0_, bf16[128,1024]{1,0:T(8,128)(2,1)S(1)} %collective-permute-done.9.refs_1_, f32[128,2048]{1,0:T(8,128)S(1)} %out_project.7.refs_2_, ...), custom_call_target="tpu_custom_call", output_to_operand_aliasing={{}: (5, {})} | custom-call | flops 536870912 | bytes 4194304 | tf_op jit(solution)/shard_map/out_project/pallas_call | solution.py:476
  (31 shorter events, 0.2 us)
Async XLA Ops:
  4.1 7.6 %copy-start = (bf16[128,4,1024]{2,1,0:T(4,128)(2,1)S(1)}, bf16[128,4,1024]{2,1,0:T(4,128)(2,1)}, u32[]{:S(2)}) copy-start(bf16[128,4,1024]{2,1,0:T(4,128)(2,1)} %q_ref.13) | copy-start | bytes 3145732
  4.1 7.6 %copy-start.2 = (s32[128]{0:T(128)S(1)}, s32[128]{0:T(128)}, u32[]{:S(2)}) copy-start(s32[128]{0:T(128)} %param.12) | copy-start | bytes 1540
  4.1 7.6 %copy-start.3 = (s32[4]{0:T(128)S(1)}, s32[4]{0:T(128)}, u32[]{:S(2)}) copy-start(s32[4]{0:T(128)} %length_ref.9) | copy-start | bytes 52
  4.2 7.6 %copy-start.6 = (s32[12]{0:T(128)S(1)}, s32[12]{0:T(128)}, u32[]{:S(2)}) copy-start(s32[12]{0:T(128)} %table_ref.5) | copy-start | bytes 148
  4.2 15.4 %collective-permute-start.2 = (bf16[2,256,256]{2,1,0:T(8,128)(2,1)}, bf16[2,256,256]{2,1,0:T(8,128)(2,1)S(1)}, u32[]{:S(2)}, u32[]{:S(2)}) collective-permute-start(bf16[2,256,256]{2,1,0:T(8,128)(2,1)} %get-tuple-element.26), channel_id=1, source_target_pairs={{0,1},{1,0},{2,3},{3,2},{4,5},{5,4},{6,7},{7,6},{8,9},{9,8},{10,11... | collective-permute-start | bytes 786440 | tf_op jit(solution)/shard_map/ppermute | solution.py:395
  11.6 11.1 %collective-permute-start = (bf16[2,384,256]{2,1,0:T(8,128)(2,1)S(1)}, bf16[2,384,256]{2,1,0:T(8,128)(2,1)S(1)}, u32[]{:S(2)}, u32[]{:S(2)}) collective-permute-start(bf16[2,384,256]{2,1,0:T(8,128)(2,1)S(1)} %get-tuple-element.21), channel_id=1, source_target_pairs={{0,1},{1,0},{2,3},{3,2},{4,5},{5,4},{6,7},{7,6},{8,9},{9,8},{10,11... | collective-permute-start | bytes 1179656 | tf_op jit(solution)/shard_map/ppermute | solution.py:395
  11.8 1.1 copy-start.4
  12.9 21.0 %copy-start.1 = (s32[4]{0:T(128)S(1)}, s32[4]{0:T(128)}, u32[]{:S(2)}) copy-start(s32[4]{0:T(128)} %owner_ref.11) | copy-start | bytes 52
  19.6 17.4 %copy-start.5 = (bf16[1,12,128,256]{3,2,1,0:T(8,128)(2,1)S(1)}, bf16[1,12,128,256]{3,2,1,0:T(8,128)(2,1)}, u32[]{:S(2)}) copy-start(bf16[1,12,128,256]{3,2,1,0:T(8,128)(2,1)} %param.21) | copy-start | bytes 2359300
  19.6 14.2 %collective-permute-start.3 = (bf16[256,256]{1,0:T(8,128)(2,1)S(1)}, bf16[256,256]{1,0:T(8,128)(2,1)S(1)}, u32[]{:S(2)}, u32[]{:S(2)}) collective-permute-start(bf16[256,256]{1,0:T(8,128)(2,1)S(1)} %fusion.1), channel_id=1, source_target_pairs={{0,2},{1,3},{2,0},{3,1},{4,6},{5,7},{6,4},{7,5},{8,10},{9,11},{10,... | collective-permute-start | bytes 393224 | tf_op jit(solution)/shard_map/ppermute | solution.py:395
  22.7 24.6 %collective-permute-start.1 = (bf16[384,256]{1,0:T(8,128)(2,1)S(1)}, bf16[384,256]{1,0:T(8,128)(2,1)S(1)}, u32[]{:S(2)}, u32[]{:S(2)}) collective-permute-start(bf16[384,256]{1,0:T(8,128)(2,1)S(1)} %fusion), channel_id=1, source_target_pairs={{0,2},{1,3},{2,0},{3,1},{4,6},{5,7},{6,4},{7,5},{8,10},{9,11},{10,... | collective-permute-start | bytes 589832 | tf_op jit(solution)/shard_map/ppermute | solution.py:395
  35.0 5.4 %collective-permute-start.4 = (bf16[128,256]{1,0:T(8,128)(2,1)S(1)}, bf16[128,256]{1,0:T(8,128)(2,1)S(1)}, u32[]{:S(2)}, u32[]{:S(2)}) collective-permute-start(bf16[128,256]{1,0:T(8,128)(2,1)S(1)} %get-tuple-element.27.refs_0_), channel_id=1, source_target_pairs={{0,4},{4,0},{8,12},{12,8},{1,5},{5,1},{9,13},{13,9},{2,6},{6,2},{1... | collective-permute-start | bytes 196616 | tf_op jit(solution)/shard_map/ppermute | solution.py:395
  35.1 5.3 %collective-permute-start.5 = (bf16[128,256]{1,0:T(8,128)(2,1)S(1)}, bf16[128,256]{1,0:T(8,128)(2,1)S(1)}, u32[]{:S(2)}, u32[]{:S(2)}) collective-permute-start(bf16[128,256]{1,0:T(8,128)(2,1)S(1)} %get-tuple-element.27.refs_0_), channel_id=1, source_target_pairs={{0,8},{4,12},{8,0},{12,4},{1,9},{5,13},{9,1},{13,5},{2,10},{6,14},... | collective-permute-start | bytes 196616 | tf_op jit(solution)/shard_map/ppermute | solution.py:395
  36.8 4.1 %collective-permute-start.6 = (bf16[128,256]{1,0:T(8,128)(2,1)S(1)}, bf16[128,256]{1,0:T(8,128)(2,1)S(1)}, u32[]{:S(2)}, u32[]{:S(2)}) collective-permute-start(bf16[128,256]{1,0:T(8,128)(2,1)S(1)} %get-tuple-element.27.refs_0_), channel_id=1, source_target_pairs={{0,12},{4,8},{8,4},{12,0},{1,13},{5,9},{9,5},{13,1},{2,14},{6,10},... | collective-permute-start | bytes 196616 | tf_op jit(solution)/shard_map/ppermute | solution.py:395
  44.2 23.9 %collective-permute-start.17 = (bf16[128,1024]{1,0:T(8,128)(2,1)S(1)}, bf16[128,1024]{1,0:T(8,128)(2,1)S(1)}, u32[]{:S(2)}, u32[]{:S(2)}) collective-permute-start(bf16[128,1024]{1,0:T(8,128)(2,1)S(1)} %attend_new.7.refs_0_), channel_id=1, source_target_pairs={{0,2},{1,3},{2,0},{3,1},{4,6},{5,7},{6,4},{7,5},{8,10},{9,11},{10,... | collective-permute-start | bytes 786440 | tf_op jit(solution)/shard_map/ppermute | solution.py:395
  44.3 23.9 %collective-permute-start.18 = (bf16[128,1024]{1,0:T(8,128)(2,1)S(1)}, bf16[128,1024]{1,0:T(8,128)(2,1)S(1)}, u32[]{:S(2)}, u32[]{:S(2)}) collective-permute-start(bf16[128,1024]{1,0:T(8,128)(2,1)S(1)} %attend_new.7.refs_0_), channel_id=1, source_target_pairs={{0,1},{1,0},{2,3},{3,2},{4,5},{5,4},{6,7},{7,6},{8,9},{9,8},{10,11... | collective-permute-start | bytes 786440 | tf_op jit(solution)/shard_map/ppermute | solution.py:395
  55.8 41.8 %collective-permute-start.13 = (bf16[256,1024]{1,0:T(8,128)(2,1)S(1)}, bf16[256,1024]{1,0:T(8,128)(2,1)S(1)}, u32[]{:S(2)}, u32[]{:S(2)}) collective-permute-start(bf16[256,1024]{1,0:T(8,128)(2,1)S(1)} %pad_maximum_fusion), channel_id=1, source_target_pairs={{0,2},{1,3},{2,0},{3,1},{4,6},{5,7},{6,4},{7,5},{8,10},{9,11},{10,... | collective-permute-start | bytes 1572872 | tf_op jit(solution)/shard_map/ppermute | solution.py:395
  59.4 13.7 %collective-permute-start.19 = (bf16[128,1024]{1,0:T(8,128)(2,1)S(1)}, bf16[128,1024]{1,0:T(8,128)(2,1)S(1)}, u32[]{:S(2)}, u32[]{:S(2)}) collective-permute-start(bf16[128,1024]{1,0:T(8,128)(2,1)S(1)} %attend_new.7.refs_0_), channel_id=1, source_target_pairs={{1,2},{2,1},{5,6},{6,5},{9,10},{10,9},{13,14},{14,13},{17,18},{18,... | collective-permute-start | bytes 786440 | tf_op jit(solution)/shard_map/ppermute | solution.py:544
  60.0 27.7 %collective-permute-start.15 = (bf16[128,1024]{1,0:T(8,128)(2,1)S(1)}, bf16[128,1024]{1,0:T(8,128)(2,1)S(1)}, u32[]{:S(2)}, u32[]{:S(2)}) collective-permute-start(bf16[128,1024]{1,0:T(8,128)(2,1)S(1)} %attend_new.5.refs_0_), channel_id=1, source_target_pairs={{0,1},{1,0},{2,3},{3,2},{4,5},{5,4},{6,7},{7,6},{8,9},{9,8},{10,11... | collective-permute-start | bytes 786440 | tf_op jit(solution)/shard_map/ppermute | solution.py:395
  68.1 20.3 %collective-permute-start.11 = (bf16[128,1024]{1,0:T(8,128)(2,1)S(1)}, bf16[128,1024]{1,0:T(8,128)(2,1)S(1)}, u32[]{:S(2)}, u32[]{:S(2)}) collective-permute-start(bf16[128,1024]{1,0:T(8,128)(2,1)S(1)} %attend_new.4.refs_0_), channel_id=1, source_target_pairs={{0,1},{1,0},{2,3},{3,2},{4,5},{5,4},{6,7},{7,6},{8,9},{9,8},{10,11... | collective-permute-start | bytes 786440 | tf_op jit(solution)/shard_map/ppermute | solution.py:395
  68.2 28.6 %collective-permute-start.20 = (bf16[128,1024]{1,0:T(8,128)(2,1)S(1)}, bf16[128,1024]{1,0:T(8,128)(2,1)S(1)}, u32[]{:S(2)}, u32[]{:S(2)}) collective-permute-start(bf16[128,1024]{1,0:T(8,128)(2,1)S(1)} %collective-permute-done.17.refs_1_), channel_id=1, source_target_pairs={{1,0},{2,3},{5,4},{6,7},{9,8},{10,11},{13,12},{14,15},{17,16},{18,... | collective-permute-start | bytes 786440 | tf_op jit(solution)/shard_map/ppermute | solution.py:548
  73.0 35.8 %collective-permute-start.16 = (bf16[128,1024]{1,0:T(8,128)(2,1)S(1)}, bf16[128,1024]{1,0:T(8,128)(2,1)S(1)}, u32[]{:S(2)}, u32[]{:S(2)}) collective-permute-start(bf16[128,1024]{1,0:T(8,128)(2,1)S(1)} %attend_new.6.refs_1_), channel_id=1, source_target_pairs={{0,1},{1,0},{2,3},{3,2},{4,5},{5,4},{6,7},{7,6},{8,9},{9,8},{10,11... | collective-permute-start | bytes 786440 | tf_op jit(solution)/shard_map/ppermute | solution.py:395
  87.7 18.2 %collective-permute-start.7 = (bf16[128,1024]{1,0:T(8,128)(2,1)S(1)}, bf16[128,1024]{1,0:T(8,128)(2,1)S(1)}, u32[]{:S(2)}, u32[]{:S(2)}) collective-permute-start(bf16[128,1024]{1,0:T(8,128)(2,1)S(1)} %attend_new.4.refs_0_), channel_id=1, source_target_pairs={{1,2},{2,1},{5,6},{6,5},{9,10},{10,9},{13,14},{14,13},{17,18},{18,... | collective-permute-start | bytes 786440 | tf_op jit(solution)/shard_map/ppermute | solution.py:544
  88.4 18.8 %collective-permute-start.8 = (bf16[128,1024]{1,0:T(8,128)(2,1)S(1)}, bf16[128,1024]{1,0:T(8,128)(2,1)S(1)}, u32[]{:S(2)}, u32[]{:S(2)}) collective-permute-start(bf16[128,1024]{1,0:T(8,128)(2,1)S(1)} %attend_new.4.refs_0_), channel_id=1, source_target_pairs={{0,2},{3,1},{4,6},{7,5},{8,10},{11,9},{12,14},{15,13},{16,18},{19,... | collective-permute-start | bytes 786440 | tf_op jit(solution)/shard_map/ppermute | solution.py:543
  96.9 23.8 %collective-permute-start.12 = (bf16[256,1024]{1,0:T(8,128)(2,1)S(1)}, bf16[256,1024]{1,0:T(8,128)(2,1)S(1)}, u32[]{:S(2)}, u32[]{:S(2)}) collective-permute-start(bf16[256,1024]{1,0:T(8,128)(2,1)S(1)} %pad_maximum_fusion), channel_id=1, source_target_pairs={{1,2},{2,1},{5,6},{6,5},{9,10},{10,9},{13,14},{14,13},{17,18},{18,... | collective-permute-start | bytes 1572872 | tf_op jit(solution)/shard_map/ppermute | solution.py:544
  97.6 23.1 %collective-permute-start.14 = (bf16[256,1024]{1,0:T(8,128)(2,1)S(1)}, bf16[256,1024]{1,0:T(8,128)(2,1)S(1)}, u32[]{:S(2)}, u32[]{:S(2)}) collective-permute-start(bf16[256,1024]{1,0:T(8,128)(2,1)S(1)} %collective-permute-done.13.refs_4_), channel_id=1, source_target_pairs={{1,0},{2,3},{5,4},{6,7},{9,8},{10,11},{13,12},{14,15},{17,16},{18,... | collective-permute-start | bytes 1572872 | tf_op jit(solution)/shard_map/ppermute | solution.py:548
  106.0 13.9 %collective-permute-start.10 = (bf16[128,1024]{1,0:T(8,128)(2,1)S(1)}, bf16[128,1024]{1,0:T(8,128)(2,1)S(1)}, u32[]{:S(2)}, u32[]{:S(2)}) collective-permute-start(bf16[128,1024]{1,0:T(8,128)(2,1)S(1)} %collective-permute-done.7.refs_0_), channel_id=1, source_target_pairs={{1,0},{2,3},{5,4},{6,7},{9,8},{10,11},{13,12},{14,15},{17,16},{18,... | collective-permute-start | bytes 786440 | tf_op jit(solution)/shard_map/ppermute | solution.py:547
  107.3 16.7 %collective-permute-start.9 = (bf16[128,1024]{1,0:T(8,128)(2,1)S(1)}, bf16[128,1024]{1,0:T(8,128)(2,1)S(1)}, u32[]{:S(2)}, u32[]{:S(2)}) collective-permute-start(bf16[128,1024]{1,0:T(8,128)(2,1)S(1)} %collective-permute-done.8.refs_0_), channel_id=1, source_target_pairs={{1,0},{2,3},{5,4},{6,7},{9,8},{10,11},{13,12},{14,15},{17,16},{18,... | collective-permute-start | bytes 786440 | tf_op jit(solution)/shard_map/ppermute | solution.py:548

commit v8 on v7

--- a/solution.py
+++ b/solution.py
@@ -641,7 +641,6 @@
     rows, steps, _ = decode_states.shape
     first = min(SET_ROWS, rows)
     blocks = rows // first
-    middle = blocks - 2
     cut = first * steps
 
     first_units = project(
@@ -673,9 +672,11 @@
 
     shape = (rows, steps, out_weight.shape[1])
     first_own = new_part(first_tail, old_part(0, 1), 0)
-    middle_old = old_part(1, middle)
-    middle_own = [new_part(rest_tails[i], middle_old, 1 + i, i) for i in range(middle)]
-    last_own = new_part(rest_tails[-1], old_part(blocks - 1, 1), blocks - 1)
+    later_old = old_part(2, blocks - 2)
+    middle_own = [new_part(rest_tails[0], old_part(1, 1), 1)] + [
+        new_part(rest_tails[i - 1], later_old, i, i - 2) for i in range(2, blocks - 1)
+    ]
+    last_own = new_part(rest_tails[-1], later_old, blocks - 1, blocks - 3)
     near = near_heads([first_own])
     two, three = far_heads(first_own, False)
     decoded = out_project(

time: 126 us -> 143 us (1.13)
  waiting for transfers between devices: 14.8 us -> 22.3 us
  starting transfers between devices: 46 us -> 52.3 us
    ppermute x1, starting transfers between devices: 4.62 us -> 17.6 us  [far_heads(): lax.ppermute(own, 'tensor', [(0, 2), (3, 1)])]
    ppermute x1, waiting for transfers between devices: 5.35 us -> 13.1 us  [far_heads(): forward = lax.ppermute(across, 'tensor', outward)]
    ppermute x13, starting transfers between devices: 33.9 us -> 27.2 us  [swap(): lax.ppermute(x, axis, [(i, i ^ bit) for i in range(lax.axis_size(axis))])]
    pallas_call x2, Pallas kernels: 2.6 us -> 4.44 us  [finish(): pl.pallas_call(functools.partial(finish_kernel, span, steps, start, sizes...]
  transfers between devices with their start and end apart: 21 -> 21, of which waited for: 4 -> 4; matrix products, arithmetic and copies ran while one was open for 0% -> 1% of each run, Pallas kernels for 46% -> 41%
where the time goes in v8:
time: 143 us
  Pallas kernels  64.2 us (45%)
  starting transfers between devices  52.3 us (37%)
  waiting for transfers between devices  22.3 us (16%)
  local copies, waits for them, and re-layouts  1.85 us (1%)
  other arithmetic  1.58 us (1%)
    ppermute x13, starting transfers between devices, swap(): lax.ppermute(x, axis, [(i, i ^ bit) for i in range(lax.axis_size(axis))])  27.2 us
    pallas_call x6, Pallas kernels, out_project(): pl.pallas_call(functools.partial(out_kernel, rels, shapes, cuts, partial...  21.3 us
    ppermute x1, starting transfers between devices, far_heads(): lax.ppermute(own, 'tensor', [(0, 2), (3, 1)])  17.6 us
    pallas_call x4, Pallas kernels, attend_new(): pl.pallas_call(functools.partial(new_kernel, heads, block, direct, skip,...  13.7 us
    pallas_call x3, Pallas kernels, attend_cached(): pl.pallas_call(functools.partial(cached_kernel, heads, block, direct, cpa...  13.6 us
    ppermute x1, waiting for transfers between devices, far_heads(): forward = lax.ppermute(across, 'tensor', outward)  13.1 us
    ppermute x13, waiting for transfers between devices, swap(): lax.ppermute(x, axis, [(i, i ^ bit) for i in range(lax.axis_size(axis))])  9.25 us
    pallas_call x2, Pallas kernels, project(): pl.pallas_call(functools.partial(project_kernel, len(groups), split, kept...  7.73 us
  transfers between devices with their start and end apart: 21, of which 4 were waited for; matrix products, arithmetic and copies ran while one was open for 1% of the time, Pallas kernels for 41%

profile of v8, /device:TPU:0, one launch (start us, length us, event | category | flops | bytes accessed | tf_op | source)
XLA Modules:
  0.0 142.7 jit_solution(1954018916265900498)
XLA Ops:
  0.0 4.3 %project.2 = (f32[2,384,256]{2,1,0:T(8,128)S(1)}, bf16[2,384,256]{2,1,0:T(8,128)(2,1)S(1)}) custom-call(s32[1]{0:T(128)} %bitcast.rank_ref, bf16[128,4,2048]{2,1,0:T(4,128)(2,1)} %refs_1_.3, bf16[2048,512]{1,0:T(8,128)(2,1)} %refs_4_.3, bf16[2048,512]{1,0:T(8,128)(2,1)} %refs_5_.3, bf16[2048,512]{1,0:T(8,128)(2,1)} %refs_4_.3, bf16[2048,512]{1,0:T(8,128)(2,1)} %refs_5_.3), custom_call_target="tpu_custom_call" | custom-call | flops 1610612736 | bytes 4194304 | tf_op jit(solution)/shard_map/project/pallas_call | solution.py:314
  4.3 3.1 %collective-permute-start = (bf16[2,384,256]{2,1,0:T(8,128)(2,1)S(1)}, bf16[2,384,256]{2,1,0:T(8,128)(2,1)S(1)}, u32[]{:S(2)}, u32[]{:S(2)}) collective-permute-start(bf16[2,384,256]{2,1,0:T(8,128)(2,1)S(1)} %get-tuple-element.21), channel_id=1, source_target_pairs={{0,1},{1,0},{2,3},{3,2},{4,5},{5,4},{6,7},{7,6},{8,9},{9,8},{10,11... | collective-permute-start | bytes 1179656 | tf_op jit(solution)/shard_map/ppermute | solution.py:395
  7.5 3.5 %project.3 = (f32[2,256,256]{2,1,0:T(8,128)S(1)}, bf16[2,256,256]{2,1,0:T(8,128)(2,1)S(1)}) custom-call(s32[1]{0:T(128)} %bitcast.rank_ref, bf16[128,2048]{1,0:T(8,128)(2,1)} %refs_0_.3, bf16[128,4,2048]{2,1,0:T(4,128)(2,1)} %refs_1_.3, bf16[2048,512]{1,0:T(8,128)(2,1)} %refs_4_.3, bf16[2048,512]{1,0:T(8,128)(2,1)} %refs_5_.3, bf16[2048,512]{1,0:T(8,128)(2,1)} %refs_4_.3, ...), custom_call_target="tpu_custom_call" | custom-call | flops 1073741824 | bytes 4194304 | tf_op jit(solution)/shard_map/project/pallas_call | solution.py:314
  10.9 0.5 collective-permute-start.2
  11.5 6.7 %attend_cached.3 = (f32[8,256,128]{2,1,0:T(8,128)S(1)}, f32[8,256,128]{2,1,0:T(8,128)S(1)}) custom-call(s32[12]{0:T(128)S(1)} %copy-done.12, s32[4]{0:T(128)S(1)} %copy-done.9, bf16[128,4,1024]{2,1,0:T(4,128)(2,1)S(1)} %copy-done, s32[1,128]{1,0:T(1,128)S(1)} %bitcast.10, bf16[12,128,256]{2,1,0:T(8,128)(2,1)S(1)} %bitcast.19), custom_call_target="tpu_custom_call" | custom-call | flops 1610612736 | bytes 2097152 | tf_op jit(solution)/shard_map/attend_cached/pallas_call | solution.py:202
  18.2 4.0 %collective-permute-done.2.refs_0_ = bf16[2,256,256]{2,1,0:T(8,128)(2,1)S(1)} collective-permute-done((bf16[2,256,256]{2,1,0:T(8,128)(2,1)S(1)}, bf16[2,256,256]{2,1,0:T(8,128)(2,1)S(1)}, u32[]{:S(2)}, u32[]{:S(2)}) %collective-permute-start.2) | collective-permute-done | bytes 262176 | tf_op jit(solution)/shard_map/ppermute | solution.py:395
  22.2 0.7 fusion.1
  22.9 2.8 %collective-permute-start.3 = (bf16[256,256]{1,0:T(8,128)(2,1)}, bf16[256,256]{1,0:T(8,128)(2,1)}, u32[]{:S(2)}, u32[]{:S(2)}) collective-permute-start(bf16[256,256]{1,0:T(8,128)(2,1)} %fusion.1), channel_id=1, source_target_pairs={{0,2},{1,3},{2,0},{3,1},{4,6},{5,7},{6,4},{7,5},{8,10},{9,11},{10,... | collective-permute-start | bytes 393224 | tf_op jit(solution)/shard_map/ppermute | solution.py:395
  25.7 0.7 fusion
  26.4 0.2 collective-permute-start.1
  26.6 0.1 maximum_bitcast_fusion.freq_ref
  26.7 1.1 copy-done.11
  27.8 0.7 copy-done.13
  28.5 3.4 %attend_cached.4 = (f32[8,128,128]{2,1,0:T(8,128)S(1)}, f32[8,128,128]{2,1,0:T(8,128)S(1)}) custom-call(s32[12]{0:T(128)S(1)} %copy-done.13, s32[4]{0:T(128)S(1)} %copy-done.9, bf16[128,4,1024]{2,1,0:T(4,128)(2,1)S(1)} %copy-done, s32[1,128]{1,0:T(1,128)S(1)} %bitcast.11, bf16[12,128,256]{2,1,0:T(8,128)(2,1)S(1)} %bitcast.20), custom_call_target="tpu_custom_call" | custom-call | flops 805306368 | bytes 1048576 | tf_op jit(solution)/shard_map/attend_cached/pallas_call | solution.py:202
  31.9 4.9 %collective-permute-done.3.refs_1_ = bf16[256,256]{1,0:T(8,128)(2,1)} collective-permute-done((bf16[256,256]{1,0:T(8,128)(2,1)}, bf16[256,256]{1,0:T(8,128)(2,1)}, u32[]{:S(2)}, u32[]{:S(2)}) %collective-permute-start.3) | collective-permute-done | bytes 131104 | tf_op jit(solution)/shard_map/ppermute | solution.py:395
  36.8 2.1 %finish.3 = (bf16[128,256]{1,0:T(8,128)(2,1)S(1)}, bf16[128,256]{1,0:T(8,128)(2,1)S(1)}) custom-call(s32[4]{0:T(128)S(1)} %copy-done.7, s32[4]{0:T(128)S(1)} %copy-done.9, s32[1]{0:T(128)} %bitcast.1.replica_ref.base_ref, s32[1,128]{1,0:T(1,128)S(1)} %bitcast.12, f32[1,128]{1,0:T(1,128)S(1)} %maximum_bitcast_fusion.freq_ref, f32[2,256,256]{2,1,0:T(8,128)S(1)} %copy-done.4, ...), custom_call_target="tpu_custom_call" | custom-call | tf_op jit(solution)/shard_map/finish/pallas_call | solution.py:380
  38.9 0.1 collective-permute-start.4
  39.0 1.6 %collective-permute-start.5 = (bf16[128,256]{1,0:T(8,128)(2,1)S(1)}, bf16[128,256]{1,0:T(8,128)(2,1)S(1)}, u32[]{:S(2)}, u32[]{:S(2)}) collective-permute-start(bf16[128,256]{1,0:T(8,128)(2,1)S(1)} %get-tuple-element.27.refs_0_), channel_id=1, source_target_pairs={{0,8},{4,12},{8,0},{12,4},{1,9},{5,13},{9,1},{13,5},{2,10},{6,14},... | collective-permute-start | bytes 196616 | tf_op jit(solution)/shard_map/ppermute | solution.py:395
  40.6 0.3 collective-permute-start.6
  40.9 3.4 %attend_cached.5 = (f32[8,128,128]{2,1,0:T(8,128)S(1)}, f32[8,128,128]{2,1,0:T(8,128)S(1)}) custom-call(s32[12]{0:T(128)S(1)} %copy-done.13, s32[4]{0:T(128)S(1)} %copy-done.9, bf16[128,4,1024]{2,1,0:T(4,128)(2,1)S(1)} %copy-done, s32[1,128]{1,0:T(1,128)S(1)} %bitcast.13, bf16[12,128,256]{2,1,0:T(8,128)(2,1)S(1)} %bitcast.21), custom_call_target="tpu_custom_call" | custom-call | flops 805306368 | bytes 1048576 | tf_op jit(solution)/shard_map/attend_cached/pallas_call | solution.py:202
  44.3 0.3 collective-permute-done.6.refs_3_
  44.6 3.4 %attend_new.7.refs_0_ = bf16[128,1024]{1,0:T(8,128)(2,1)S(1)} custom-call(s32[4]{0:T(128)S(1)} %copy-done.7, s32[1]{0:T(128)} %bitcast.1.replica_ref.base_ref, bf16[128,4,1024]{2,1,0:T(4,128)(2,1)S(1)} %copy-done, s32[1,128]{1,0:T(1,128)S(1)} %bitcast.14, bf16[128,256]{1,0:T(8,128)(2,1)S(1)} %get-tuple-element.32.tail_ref, ...), custom_call_target="tpu_custom_call" | custom-call | flops 335544320 | bytes 1310720 | tf_op jit(solution)/shard_map/attend_new/pallas_call | solution.py:239
  48.0 0.1 collective-permute-start.17
  48.1 3.0 %collective-permute-start.18 = (bf16[128,1024]{1,0:T(8,128)(2,1)S(1)}, bf16[128,1024]{1,0:T(8,128)(2,1)S(1)}, u32[]{:S(2)}, u32[]{:S(2)}) collective-permute-start(bf16[128,1024]{1,0:T(8,128)(2,1)S(1)} %attend_new.7.refs_0_), channel_id=1, source_target_pairs={{0,1},{1,0},{2,3},{3,2},{4,5},{5,4},{6,7},{7,6},{8,9},{9,8},{10,11... | collective-permute-start | bytes 786440 | tf_op jit(solution)/shard_map/ppermute | solution.py:395
  51.1 2.3 %finish.2 = (bf16[128,256]{1,0:T(8,128)(2,1)S(1)}, bf16[128,256]{1,0:T(8,128)(2,1)S(1)}, bf16[128,256]{1,0:T(8,128)(2,1)S(1)}) custom-call(s32[4]{0:T(128)S(1)} %copy-done.7, s32[4]{0:T(128)S(1)} %copy-done.9, s32[1]{0:T(128)} %bitcast.1.replica_ref.base_ref, s32[1,128]{1,0:T(1,128)S(1)} %bitcast.15, f32[1,128]{1,0:T(1,128)S(1)} %maximum_bitcast_fusion.freq_ref, ...), custom_call_target="tpu_custom_call" | custom-call | tf_op jit(solution)/shard_map/finish/pallas_call | solution.py:380
  53.5 3.6 %attend_new.6.refs_1_ = bf16[128,1024]{1,0:T(8,128)(2,1)S(1)} custom-call(s32[4]{0:T(128)S(1)} %copy-done.7, s32[1]{0:T(128)} %bitcast.1.replica_ref.base_ref, bf16[128,4,1024]{2,1,0:T(4,128)(2,1)S(1)} %copy-done, s32[1,128]{1,0:T(1,128)S(1)} %bitcast.16, bf16[128,256]{1,0:T(8,128)(2,1)S(1)} %get-tuple-element.31.tail_ref, ...), custom_call_target="tpu_custom_call" | custom-call | flops 335544320 | bytes 1310720 | tf_op jit(solution)/shard_map/attend_new/pallas_call | solution.py:239
  57.0 3.4 %attend_new.5.refs_0_ = bf16[128,1024]{1,0:T(8,128)(2,1)S(1)} custom-call(s32[4]{0:T(128)S(1)} %copy-done.7, s32[1]{0:T(128)} %bitcast.1.replica_ref.base_ref, bf16[128,4,1024]{2,1,0:T(4,128)(2,1)S(1)} %copy-done, s32[1,128]{1,0:T(1,128)S(1)} %bitcast.17, bf16[128,256]{1,0:T(8,128)(2,1)S(1)} %get-tuple-element.28.tail_ref, ...), custom_call_target="tpu_custom_call" | custom-call | flops 335544320 | bytes 1310720 | tf_op jit(solution)/shard_map/attend_new/pallas_call | solution.py:239
  60.5 0.1 collective-permute-start.13
  60.6 0.7 collective-permute-start.19
  61.3 3.3 %attend_new.4.refs_0_ = bf16[128,1024]{1,0:T(8,128)(2,1)S(1)} custom-call(s32[4]{0:T(128)S(1)} %copy-done.7, s32[1]{0:T(128)} %bitcast.1.replica_ref.base_ref, bf16[128,4,1024]{2,1,0:T(4,128)(2,1)S(1)} %copy-done, s32[1,128]{1,0:T(1,128)S(1)} %bitcast.18, bf16[128,256]{1,0:T(8,128)(2,1)S(1)} %get-tuple-element.22.tail_ref, ...), custom_call_target="tpu_custom_call" | custom-call | flops 335544320 | bytes 1310720 | tf_op jit(solution)/shard_map/attend_new/pallas_call | solution.py:239
  64.6 0.7 collective-permute-start.7
  65.3 6.4 %collective-permute-start.11 = (bf16[128,1024]{1,0:T(8,128)(2,1)S(1)}, bf16[128,1024]{1,0:T(8,128)(2,1)S(1)}, u32[]{:S(2)}, u32[]{:S(2)}) collective-permute-start(bf16[128,1024]{1,0:T(8,128)(2,1)S(1)} %attend_new.4.refs_0_), channel_id=1, source_target_pairs={{0,1},{1,0},{2,3},{3,2},{4,5},{5,4},{6,7},{7,6},{8,9},{9,8},{10,11... | collective-permute-start | bytes 786440 | tf_op jit(solution)/shard_map/ppermute | solution.py:395
  71.7 1.3 collective-permute-start.20
  73.0 3.5 %hold.1.refs_3_ = bf16[2048,2048]{1,0:T(8,128)(2,1)S(1)} custom-call(s32[1]{0:T(128)} %bitcast.rank_ref, bf16[4096,2048]{1,0:T(8,128)(2,1)} %refs_5_.5), custom_call_target="tpu_custom_call" | custom-call | tf_op jit(solution)/shard_map/hold/pallas_call | solution.py:518
  76.5 17.6 %collective-permute-start.8 = (bf16[128,1024]{1,0:T(8,128)(2,1)S(1)}, bf16[128,1024]{1,0:T(8,128)(2,1)S(1)}, u32[]{:S(2)}, u32[]{:S(2)}) collective-permute-start(bf16[128,1024]{1,0:T(8,128)(2,1)S(1)} %attend_new.4.refs_0_), channel_id=1, source_target_pairs={{0,2},{3,1},{4,6},{7,5},{8,10},{11,9},{12,14},{15,13},{16,18},{19,... | collective-permute-start | bytes 786440 | tf_op jit(solution)/shard_map/ppermute | solution.py:543
  94.1 9.1 %collective-permute-start.15 = (bf16[128,1024]{1,0:T(8,128)(2,1)S(1)}, bf16[128,1024]{1,0:T(8,128)(2,1)S(1)}, u32[]{:S(2)}, u32[]{:S(2)}) collective-permute-start(bf16[128,1024]{1,0:T(8,128)(2,1)S(1)} %attend_new.5.refs_0_), channel_id=1, source_target_pairs={{0,1},{1,0},{2,3},{3,2},{4,5},{5,4},{6,7},{7,6},{8,9},{9,8},{10,11... | collective-permute-start | bytes 786440 | tf_op jit(solution)/shard_map/ppermute | solution.py:395
  103.3 0.0 collective-permute-start.16
  103.3 3.8 %out_project.6.refs_2_ = f32[128,2048]{1,0:T(8,128)S(1)} custom-call(s32[1]{0:T(128)} %bitcast.rank_ref, bf16[128,1024]{1,0:T(8,128)(2,1)S(1)} %attend_new.4.refs_0_, bf16[128,1024]{1,0:T(8,128)(2,1)S(1)} %collective-permute-done.11.refs_1_, bf16[4096,2048]{1,0:T(8,128)(2,1)} %refs_5_.5), custom_call_target="tpu_custom_call" | custom-call | flops 1073741824 | bytes 8388608 | tf_op jit(solution)/shard_map/out_project/pallas_call | solution.py:476
  107.1 0.7 collective-permute-start.12
  107.8 1.3 collective-permute-start.14
  109.1 7.1 %out_project.9.refs_4_ = bf16[128,4,2048]{2,1,0:T(4,128)(2,1)} custom-call(s32[1]{0:T(128)} %bitcast.rank_ref, bf16[128,1024]{1,0:T(8,128)(2,1)S(1)} %attend_new.7.refs_0_, bf16[128,1024]{1,0:T(8,128)(2,1)S(1)} %collective-permute-done.17.refs_1_, bf16[128,1024]{1,0:T(8,128)(2,1)S(1)} %collective-permute-done.18.refs_2_, ...), custom_call_target="tpu_custom_call" | custom-call | flops 2147483648 | bytes 16777216 | tf_op jit(solution)/shard_map/out_project/pallas_call | solution.py:476
  116.2 1.3 collective-permute-start.9
  117.5 1.6 %collective-permute-start.10 = (bf16[128,1024]{1,0:T(8,128)(2,1)S(1)}, bf16[128,1024]{1,0:T(8,128)(2,1)S(1)}, u32[]{:S(2)}, u32[]{:S(2)}) collective-permute-start(bf16[128,1024]{1,0:T(8,128)(2,1)S(1)} %collective-permute-done.7.refs_0_), channel_id=1, source_target_pairs={{1,0},{2,3},{5,4},{6,7},{9,8},{10,11},{13,12},{14,15},{17,16},{18,... | collective-permute-start | bytes 786440 | tf_op jit(solution)/shard_map/ppermute | solution.py:547
  119.1 5.7 %out_project.8.refs_2_ = f32[256,2048]{1,0:T(8,128)S(1)} custom-call(s32[1]{0:T(128)} %bitcast.rank_ref, bf16[128,1024]{1,0:T(8,128)(2,1)S(1)} %attend_new.5.refs_0_, bf16[128,1024]{1,0:T(8,128)(2,1)S(1)} %attend_new.6.refs_1_, bf16[128,1024]{1,0:T(8,128)(2,1)S(1)} %collective-permute-done.15.refs_2_, bf16[128,1024]{1,0:T(8,128)(2,1)S(1)} %collective-permute-done.16.refs_3_, ...), custom_call_target="tpu_custom_call" | custom-call | flops 3221225472 | bytes 12582912 | tf_op jit(solution)/shard_map/out_project/pallas_call | solution.py:476
  124.8 13.1 %collective-permute-done.10.refs_1_ = bf16[128,1024]{1,0:T(8,128)(2,1)S(1)} collective-permute-done((bf16[128,1024]{1,0:T(8,128)(2,1)S(1)}, bf16[128,1024]{1,0:T(8,128)(2,1)S(1)}, u32[]{:S(2)}, u32[]{:S(2)}) %collective-permute-start.10) | collective-permute-done | bytes 262176 | tf_op jit(solution)/shard_map/ppermute | solution.py:547
  137.9 0.7 out_project.7.refs_2_
  138.6 2.4 %out_project.10.refs_4_ = bf16[128,4,2048]{2,1,0:T(4,128)(2,1)} custom-call(s32[1]{0:T(128)} %bitcast.rank_ref, bf16[256,1024]{1,0:T(8,128)(2,1)S(1)} %collective-permute-done.12.refs_0_, bf16[256,1024]{1,0:T(8,128)(2,1)S(1)} %collective-permute-done.14.refs_1_, f32[256,2048]{1,0:T(8,128)S(1)} %out_project.8.refs_2_, ...), custom_call_target="tpu_custom_call", output_to_operand_aliasing={{}: (5, {})} | custom-call | flops 1073741824 | bytes 4194304 | tf_op jit(solution)/shard_map/out_project/pallas_call | solution.py:476
  141.0 1.6 %out_project.11 = bf16[128,4,2048]{2,1,0:T(4,128)(2,1)} custom-call(s32[1]{0:T(128)} %bitcast.rank_ref, bf16[128,1024]{1,0:T(8,128)(2,1)S(1)} %collective-permute-done.7.refs_0_, bf16[128,1024]{1,0:T(8,128)(2,1)S(1)} %collective-permute-done.9.refs_1_, f32[128,2048]{1,0:T(8,128)S(1)} %out_project.7.refs_2_, ...), custom_call_target="tpu_custom_call", output_to_operand_aliasing={{}: (5, {})} | custom-call | flops 536870912 | bytes 4194304 | tf_op jit(solution)/shard_map/out_project/pallas_call | solution.py:476
  (45 shorter events, 0.2 us)
Async XLA Ops:
  4.3 21.4 %copy-start.1 = (f32[2,384,256]{2,1,0:T(8,128)}, f32[2,384,256]{2,1,0:T(8,128)S(1)}, u32[]{:S(2)}) copy-start(f32[2,384,256]{2,1,0:T(8,128)S(1)} %get-tuple-element.20.keep_ref) | copy-start | bytes 2359300
  4.3 7.2 %copy-start = (bf16[128,4,1024]{2,1,0:T(4,128)(2,1)S(1)}, bf16[128,4,1024]{2,1,0:T(4,128)(2,1)}, u32[]{:S(2)}) copy-start(bf16[128,4,1024]{2,1,0:T(4,128)(2,1)} %q_ref.13) | copy-start | bytes 3145732
  4.3 7.1 %copy-start.8 = (s32[128]{0:T(128)S(1)}, s32[128]{0:T(128)}, u32[]{:S(2)}) copy-start(s32[128]{0:T(128)} %param.12) | copy-start | bytes 1540
  4.3 7.1 %copy-start.9 = (s32[4]{0:T(128)S(1)}, s32[4]{0:T(128)}, u32[]{:S(2)}) copy-start(s32[4]{0:T(128)} %length_ref.9) | copy-start | bytes 52
  4.3 7.1 %copy-start.10 = (bf16[1,12,128,256]{3,2,1,0:T(8,128)(2,1)S(1)}, bf16[1,12,128,256]{3,2,1,0:T(8,128)(2,1)}, u32[]{:S(2)}) copy-start(bf16[1,12,128,256]{3,2,1,0:T(8,128)(2,1)} %param.21) | copy-start | bytes 2359300
  4.3 7.1 %copy-start.12 = (s32[12]{0:T(128)S(1)}, s32[12]{0:T(128)}, u32[]{:S(2)}) copy-start(s32[12]{0:T(128)} %table_ref.5) | copy-start | bytes 148
  4.3 21.4 %collective-permute-start = (bf16[2,384,256]{2,1,0:T(8,128)(2,1)S(1)}, bf16[2,384,256]{2,1,0:T(8,128)(2,1)S(1)}, u32[]{:S(2)}, u32[]{:S(2)}) collective-permute-start(bf16[2,384,256]{2,1,0:T(8,128)(2,1)S(1)} %get-tuple-element.21), channel_id=1, source_target_pairs={{0,1},{1,0},{2,3},{3,2},{4,5},{5,4},{6,7},{7,6},{8,9},{9,8},{10,11... | collective-permute-start | bytes 1179656 | tf_op jit(solution)/shard_map/ppermute | solution.py:395
  10.9 11.3 %copy-start.3 = (f32[2,256,256]{2,1,0:T(8,128)}, f32[2,256,256]{2,1,0:T(8,128)S(1)}, u32[]{:S(2)}) copy-start(f32[2,256,256]{2,1,0:T(8,128)S(1)} %get-tuple-element.25.keep_ref) | copy-start | bytes 1572868
  10.9 11.2 %collective-permute-start.2 = (bf16[2,256,256]{2,1,0:T(8,128)(2,1)S(1)}, bf16[2,256,256]{2,1,0:T(8,128)(2,1)S(1)}, u32[]{:S(2)}, u32[]{:S(2)}) collective-permute-start(bf16[2,256,256]{2,1,0:T(8,128)(2,1)S(1)} %get-tuple-element.26), channel_id=1, source_target_pairs={{0,1},{1,0},{2,3},{3,2},{4,5},{5,4},{6,7},{7,6},{8,9},{9,8},{10,11... | collective-permute-start | bytes 786440 | tf_op jit(solution)/shard_map/ppermute | solution.py:395
  22.2 4.2 %copy-start.5 = (bf16[2,256,256]{2,1,0:T(8,128)(2,1)}, bf16[2,256,256]{2,1,0:T(8,128)(2,1)S(1)}, u32[]{:S(2)}) copy-start(bf16[2,256,256]{2,1,0:T(8,128)(2,1)S(1)} %collective-permute-done.2.refs_0_) | copy-start | bytes 786436
  22.2 14.6 %copy-start.7 = (s32[4]{0:T(128)S(1)}, s32[4]{0:T(128)}, u32[]{:S(2)}) copy-start(s32[4]{0:T(128)} %owner_ref.11) | copy-start | bytes 52
  22.9 13.9 %collective-permute-start.3 = (bf16[256,256]{1,0:T(8,128)(2,1)}, bf16[256,256]{1,0:T(8,128)(2,1)}, u32[]{:S(2)}, u32[]{:S(2)}) collective-permute-start(bf16[256,256]{1,0:T(8,128)(2,1)} %fusion.1), channel_id=1, source_target_pairs={{0,2},{1,3},{2,0},{3,1},{4,6},{5,7},{6,4},{7,5},{8,10},{9,11},{10,... | collective-permute-start | bytes 393224 | tf_op jit(solution)/shard_map/ppermute | solution.py:395
  26.4 24.7 %collective-permute-start.1 = (bf16[384,256]{1,0:T(8,128)(2,1)}, bf16[384,256]{1,0:T(8,128)(2,1)}, u32[]{:S(2)}, u32[]{:S(2)}) collective-permute-start(bf16[384,256]{1,0:T(8,128)(2,1)} %fusion), channel_id=1, source_target_pairs={{0,2},{1,3},{2,0},{3,1},{4,6},{5,7},{6,4},{7,5},{8,10},{9,11},{10,... | collective-permute-start | bytes 589832 | tf_op jit(solution)/shard_map/ppermute | solution.py:395
  26.7 1.1 copy-start.11
  27.8 0.7 copy-start.13
  28.5 8.4 %copy-start.4 = (f32[2,256,256]{2,1,0:T(8,128)S(1)}, f32[2,256,256]{2,1,0:T(8,128)}, u32[]{:S(2)}) copy-start(f32[2,256,256]{2,1,0:T(8,128)} %copy-done.3) | copy-start | bytes 1572868
  28.5 8.4 %copy-start.6 = (bf16[2,256,256]{2,1,0:T(8,128)(2,1)S(1)}, bf16[2,256,256]{2,1,0:T(8,128)(2,1)}, u32[]{:S(2)}) copy-start(bf16[2,256,256]{2,1,0:T(8,128)(2,1)} %copy-done.5) | copy-start | bytes 786436
  38.9 12.2 %copy-start.2 = (f32[2,384,256]{2,1,0:T(8,128)S(1)}, f32[2,384,256]{2,1,0:T(8,128)}, u32[]{:S(2)}) copy-start(f32[2,384,256]{2,1,0:T(8,128)} %copy-done.1) | copy-start | bytes 2359300
  38.9 5.4 %collective-permute-start.4 = (bf16[128,256]{1,0:T(8,128)(2,1)S(1)}, bf16[128,256]{1,0:T(8,128)(2,1)S(1)}, u32[]{:S(2)}, u32[]{:S(2)}) collective-permute-start(bf16[128,256]{1,0:T(8,128)(2,1)S(1)} %get-tuple-element.27.refs_0_), channel_id=1, source_target_pairs={{0,4},{4,0},{8,12},{12,8},{1,5},{5,1},{9,13},{13,9},{2,6},{6,2},{1... | collective-permute-start | bytes 196616 | tf_op jit(solution)/shard_map/ppermute | solution.py:395
  39.0 5.3 %collective-permute-start.5 = (bf16[128,256]{1,0:T(8,128)(2,1)S(1)}, bf16[128,256]{1,0:T(8,128)(2,1)S(1)}, u32[]{:S(2)}, u32[]{:S(2)}) collective-permute-start(bf16[128,256]{1,0:T(8,128)(2,1)S(1)} %get-tuple-element.27.refs_0_), channel_id=1, source_target_pairs={{0,8},{4,12},{8,0},{12,4},{1,9},{5,13},{9,1},{13,5},{2,10},{6,14},... | collective-permute-start | bytes 196616 | tf_op jit(solution)/shard_map/ppermute | solution.py:395
  40.6 4.1 %collective-permute-start.6 = (bf16[128,256]{1,0:T(8,128)(2,1)S(1)}, bf16[128,256]{1,0:T(8,128)(2,1)S(1)}, u32[]{:S(2)}, u32[]{:S(2)}) collective-permute-start(bf16[128,256]{1,0:T(8,128)(2,1)S(1)} %get-tuple-element.27.refs_0_), channel_id=1, source_target_pairs={{0,12},{4,8},{8,4},{12,0},{1,13},{5,9},{9,5},{13,1},{2,14},{6,10},... | collective-permute-start | bytes 196616 | tf_op jit(solution)/shard_map/ppermute | solution.py:395
  48.0 17.3 %collective-permute-start.17 = (bf16[128,1024]{1,0:T(8,128)(2,1)S(1)}, bf16[128,1024]{1,0:T(8,128)(2,1)S(1)}, u32[]{:S(2)}, u32[]{:S(2)}) collective-permute-start(bf16[128,1024]{1,0:T(8,128)(2,1)S(1)} %attend_new.7.refs_0_), channel_id=1, source_target_pairs={{0,2},{1,3},{2,0},{3,1},{4,6},{5,7},{6,4},{7,5},{8,10},{9,11},{10,... | collective-permute-start | bytes 786440 | tf_op jit(solution)/shard_map/ppermute | solution.py:395
  48.1 23.6 %collective-permute-start.18 = (bf16[128,1024]{1,0:T(8,128)(2,1)S(1)}, bf16[128,1024]{1,0:T(8,128)(2,1)S(1)}, u32[]{:S(2)}, u32[]{:S(2)}) collective-permute-start(bf16[128,1024]{1,0:T(8,128)(2,1)S(1)} %attend_new.7.refs_0_), channel_id=1, source_target_pairs={{0,1},{1,0},{2,3},{3,2},{4,5},{5,4},{6,7},{7,6},{8,9},{9,8},{10,11... | collective-permute-start | bytes 786440 | tf_op jit(solution)/shard_map/ppermute | solution.py:395
  60.5 47.3 %collective-permute-start.13 = (bf16[256,1024]{1,0:T(8,128)(2,1)S(1)}, bf16[256,1024]{1,0:T(8,128)(2,1)S(1)}, u32[]{:S(2)}, u32[]{:S(2)}) collective-permute-start(bf16[256,1024]{1,0:T(8,128)(2,1)S(1)} %pad_maximum_fusion), channel_id=1, source_target_pairs={{0,2},{1,3},{2,0},{3,1},{4,6},{5,7},{6,4},{7,5},{8,10},{9,11},{10,... | collective-permute-start | bytes 1572872 | tf_op jit(solution)/shard_map/ppermute | solution.py:395
  60.6 15.9 %collective-permute-start.19 = (bf16[128,1024]{1,0:T(8,128)(2,1)S(1)}, bf16[128,1024]{1,0:T(8,128)(2,1)S(1)}, u32[]{:S(2)}, u32[]{:S(2)}) collective-permute-start(bf16[128,1024]{1,0:T(8,128)(2,1)S(1)} %attend_new.7.refs_0_), channel_id=1, source_target_pairs={{1,2},{2,1},{5,6},{6,5},{9,10},{10,9},{13,14},{14,13},{17,18},{18,... | collective-permute-start | bytes 786440 | tf_op jit(solution)/shard_map/ppermute | solution.py:544
  64.6 29.5 %collective-permute-start.7 = (bf16[128,1024]{1,0:T(8,128)(2,1)S(1)}, bf16[128,1024]{1,0:T(8,128)(2,1)S(1)}, u32[]{:S(2)}, u32[]{:S(2)}) collective-permute-start(bf16[128,1024]{1,0:T(8,128)(2,1)S(1)} %attend_new.4.refs_0_), channel_id=1, source_target_pairs={{1,2},{2,1},{5,6},{6,5},{9,10},{10,9},{13,14},{14,13},{17,18},{18,... | collective-permute-start | bytes 786440 | tf_op jit(solution)/shard_map/ppermute | solution.py:544
  65.3 38.0 %collective-permute-start.11 = (bf16[128,1024]{1,0:T(8,128)(2,1)S(1)}, bf16[128,1024]{1,0:T(8,128)(2,1)S(1)}, u32[]{:S(2)}, u32[]{:S(2)}) collective-permute-start(bf16[128,1024]{1,0:T(8,128)(2,1)S(1)} %attend_new.4.refs_0_), channel_id=1, source_target_pairs={{0,1},{1,0},{2,3},{3,2},{4,5},{5,4},{6,7},{7,6},{8,9},{9,8},{10,11... | collective-permute-start | bytes 786440 | tf_op jit(solution)/shard_map/ppermute | solution.py:395
  71.7 35.4 %collective-permute-start.20 = (bf16[128,1024]{1,0:T(8,128)(2,1)S(1)}, bf16[128,1024]{1,0:T(8,128)(2,1)S(1)}, u32[]{:S(2)}, u32[]{:S(2)}) collective-permute-start(bf16[128,1024]{1,0:T(8,128)(2,1)S(1)} %collective-permute-done.17.refs_1_), channel_id=1, source_target_pairs={{1,0},{2,3},{5,4},{6,7},{9,8},{10,11},{13,12},{14,15},{17,16},{18,... | collective-permute-start | bytes 786440 | tf_op jit(solution)/shard_map/ppermute | solution.py:548
  76.5 39.7 %collective-permute-start.8 = (bf16[128,1024]{1,0:T(8,128)(2,1)S(1)}, bf16[128,1024]{1,0:T(8,128)(2,1)S(1)}, u32[]{:S(2)}, u32[]{:S(2)}) collective-permute-start(bf16[128,1024]{1,0:T(8,128)(2,1)S(1)} %attend_new.4.refs_0_), channel_id=1, source_target_pairs={{0,2},{3,1},{4,6},{7,5},{8,10},{11,9},{12,14},{15,13},{16,18},{19,... | collective-permute-start | bytes 786440 | tf_op jit(solution)/shard_map/ppermute | solution.py:543
  94.1 23.4 %collective-permute-start.15 = (bf16[128,1024]{1,0:T(8,128)(2,1)S(1)}, bf16[128,1024]{1,0:T(8,128)(2,1)S(1)}, u32[]{:S(2)}, u32[]{:S(2)}) collective-permute-start(bf16[128,1024]{1,0:T(8,128)(2,1)S(1)} %attend_new.5.refs_0_), channel_id=1, source_target_pairs={{0,1},{1,0},{2,3},{3,2},{4,5},{5,4},{6,7},{7,6},{8,9},{9,8},{10,11... | collective-permute-start | bytes 786440 | tf_op jit(solution)/shard_map/ppermute | solution.py:395
  103.3 15.8 %collective-permute-start.16 = (bf16[128,1024]{1,0:T(8,128)(2,1)S(1)}, bf16[128,1024]{1,0:T(8,128)(2,1)S(1)}, u32[]{:S(2)}, u32[]{:S(2)}) collective-permute-start(bf16[128,1024]{1,0:T(8,128)(2,1)S(1)} %attend_new.6.refs_1_), channel_id=1, source_target_pairs={{0,1},{1,0},{2,3},{3,2},{4,5},{5,4},{6,7},{7,6},{8,9},{9,8},{10,11... | collective-permute-start | bytes 786440 | tf_op jit(solution)/shard_map/ppermute | solution.py:395
  107.1 31.5 %collective-permute-start.12 = (bf16[256,1024]{1,0:T(8,128)(2,1)S(1)}, bf16[256,1024]{1,0:T(8,128)(2,1)S(1)}, u32[]{:S(2)}, u32[]{:S(2)}) collective-permute-start(bf16[256,1024]{1,0:T(8,128)(2,1)S(1)} %pad_maximum_fusion), channel_id=1, source_target_pairs={{1,2},{2,1},{5,6},{6,5},{9,10},{10,9},{13,14},{14,13},{17,18},{18,... | collective-permute-start | bytes 1572872 | tf_op jit(solution)/shard_map/ppermute | solution.py:544
  107.8 30.8 %collective-permute-start.14 = (bf16[256,1024]{1,0:T(8,128)(2,1)S(1)}, bf16[256,1024]{1,0:T(8,128)(2,1)S(1)}, u32[]{:S(2)}, u32[]{:S(2)}) collective-permute-start(bf16[256,1024]{1,0:T(8,128)(2,1)S(1)} %collective-permute-done.13.refs_4_), channel_id=1, source_target_pairs={{1,0},{2,3},{5,4},{6,7},{9,8},{10,11},{13,12},{14,15},{17,16},{18,... | collective-permute-start | bytes 1572872 | tf_op jit(solution)/shard_map/ppermute | solution.py:548
  116.2 24.8 %collective-permute-start.9 = (bf16[128,1024]{1,0:T(8,128)(2,1)S(1)}, bf16[128,1024]{1,0:T(8,128)(2,1)S(1)}, u32[]{:S(2)}, u32[]{:S(2)}) collective-permute-start(bf16[128,1024]{1,0:T(8,128)(2,1)S(1)} %collective-permute-done.8.refs_0_), channel_id=1, source_target_pairs={{1,0},{2,3},{5,4},{6,7},{9,8},{10,11},{13,12},{14,15},{17,16},{18,... | collective-permute-start | bytes 786440 | tf_op jit(solution)/shard_map/ppermute | solution.py:548
  117.5 20.3 %collective-permute-start.10 = (bf16[128,1024]{1,0:T(8,128)(2,1)S(1)}, bf16[128,1024]{1,0:T(8,128)(2,1)S(1)}, u32[]{:S(2)}, u32[]{:S(2)}) collective-permute-start(bf16[128,1024]{1,0:T(8,128)(2,1)S(1)} %collective-permute-done.7.refs_0_), channel_id=1, source_target_pairs={{1,0},{2,3},{5,4},{6,7},{9,8},{10,11},{13,12},{14,15},{17,16},{18,... | collective-permute-start | bytes 786440 | tf_op jit(solution)/shard_map/ppermute | solution.py:547
